TPU v7x, 32 devices: a whole 2x2x4 slice. The times are simulated.
32 devices in a mesh: dp: 16 (over z, y, core), tp: 2 (over x).
Axes of the slice: x: 2, y: 2, z: 4, core: 2. Of those that a mesh axis runs over, the one named last changes fastest.
Arguments:
- layer_in: bfloat16 [16, 1024, 2048], P('dp', 'tp'), may hold values from -6 to 6
- cotangent: bfloat16 [16, 1024, 2048], P('dp', 'tp'), may hold values from -6 to 6
- resets: int32 [16, 1024], P('dp', 'tp'), may hold values 0 or 1
- norm_gains: float32 [2, 2048], replicated, may hold values from 0.5 to 1.5
- w_x: bfloat16 [2048, 2560], P(None, 'tp'), may hold values from -0.125 to 0.125
- w_y: bfloat16 [2048, 2560], P(None, 'tp'), may hold values from -0.125 to 0.125
- conv_w: float32 [4, 2560], replicated, may hold values from -3 to 3
- lru_bias: float32 [3, 2560], replicated, may hold values from -3 to 3
- a_param: float32 [2560], replicated, may hold values from -10.4 to -5.3
- gate_blocks: bfloat16 [2, 10, 256, 256], replicated, may hold values from -0.375 to 0.375
- w_out: bfloat16 [2560, 2048], P('tp'), may hold values from -0.25 to 0.25
- w_gate: bfloat16 [2048, 6144], P(None, 'tp'), may hold values from -0.125 to 0.125
- w_up: bfloat16 [2048, 6144], P(None, 'tp'), may hold values from -0.125 to 0.125
- w_down: bfloat16 [6144, 2048], P('tp'), may hold values from -0.078125 to 0.078125
Outputs:
- layer_out: bfloat16 [16, 1024, 2048], P('dp', 'tp')
- input_grad: float32 [16, 1024, 2048], P('dp', 'tp')
- norm_gains_grad: float32 [2, 2048], P(None, 'dp')
- w_x_grad: float32 [2048, 2560], P('dp', 'tp')
- w_y_grad: float32 [2048, 2560], P('dp', 'tp')
- conv_w_grad: float32 [4, 2560], P(None, 'dp')
- lru_bias_grad: float32 [3, 2560], P(None, 'dp')
- a_param_grad: float32 [2560], P('dp')
- gate_blocks_grad: float32 [2, 10, 256, 256], P(None, None, 'dp')
- w_out_grad: float32 [2560, 2048], P('tp', 'dp')
- w_gate_grad: float32 [2048, 6144], P('dp', 'tp')
- w_up_grad: float32 [2048, 6144], P('dp', 'tp')
- w_down_grad: float32 [6144, 2048], P('tp', 'dp')
All inputs are finite; a program needn't handle non-finite values. No bound on the sum of `resets` on one device may be relied on, other than what follows from the above.
Results may differ from a plain program's by a relative error of at most 0.02.
Values may be sent and summed in bfloat16 or wider, within the bound.
A program may use at most 448 MiB of HBM per device.

v0:
```python
import jax
import jax.numpy as jnp
from jax import lax
from jax.sharding import PartitionSpec as P

EPS = 1e-06


def from_behind(value, axis, steps):
    count = lax.axis_size(axis)
    first, last = (max(0, -steps), min(count, count - steps))
    return lax.ppermute(value, axis, [(source, source + steps) for source in range(first, last)])


def rms_scale(values, gain_vec):
    return values * lax.rsqrt(jnp.mean(values * values, axis=-1, keepdims=True) + EPS) * gain_vec


def gelu_product(gate_val, up_val):
    return jax.nn.gelu(gate_val, approximate=True) * up_val


def lru_terms(conv_out, gate_in, gate_rate, a_param, starts):
    keep_mask = 1.0 - starts
    input_gate = jax.nn.sigmoid(gate_in)
    rate_gate = jax.nn.sigmoid(gate_rate)
    log_decay = -8.0 * rate_gate * jax.nn.softplus(a_param)
    scaling = starts + keep_mask * jnp.sqrt(-jnp.expm1(2.0 * log_decay))
    return (jnp.exp(log_decay) * keep_mask, conv_out * input_gate * scaling)


def matmul(first_mat, second_mat):
    return jnp.dot(first_mat, second_mat, preferred_element_type=jnp.float32)


def matmul_left(first_mat, second_mat):
    return lax.dot_general(
        first_mat, second_mat, (((0,), (0,)), ((), ())), preferred_element_type=jnp.float32
    )


def matmul_right(first_mat, second_mat):
    return lax.dot_general(
        first_mat, second_mat, (((1,), (1,)), ((), ())), preferred_element_type=jnp.float32
    )


def combine_state(first_item, second_item):
    return (first_item[0] * second_item[0], second_item[1] + second_item[0] * first_item[1])


def carry_across(coef_end, state_end, reverse):
    incoming = jnp.zeros_like(state_end)
    direction = -1 if reverse else 1
    for turn_index in range(lax.axis_size("tp") - 1):
        incoming = from_behind(state_end + coef_end * incoming, "tp", direction)
    return incoming


def local(
    layer_in,
    cotangent,
    resets,
    norm_gains,
    w_x,
    w_y,
    conv_w,
    lru_bias,
    a_param,
    gate_blocks,
    w_out,
    w_gate,
    w_up,
    w_down,
):
    inputs = layer_in[0].astype(jnp.float32)
    starts = resets[0].astype(jnp.float32)
    keep_mask = 1.0 - starts
    rim_size = conv_w.shape[0] - 1
    head_count = gate_blocks.shape[1]
    block_size = gate_blocks.shape[2]
    full_width = conv_w.shape[1]
    normed, norm_pull = jax.vjp(rms_scale, inputs, norm_gains[0])
    normed_low = normed.astype(jnp.bfloat16)
    proj_x, proj_y, proj_out = (
        lax.all_gather(w_x, "tp", axis=1, tiled=True),
        lax.all_gather(w_y, "tp", axis=1, tiled=True),
        lax.all_gather(w_out, "tp", axis=0, tiled=True),
    )
    rec_len = normed_low.shape[0]
    branch_x = matmul(normed_low, proj_x).astype(jnp.bfloat16)
    branch_y = matmul(normed_low, proj_y)
    rim_rows, rim_keep = from_behind(
        (branch_x[rec_len - rim_size :], keep_mask[rec_len - rim_size :].astype(jnp.bfloat16)),
        "tp",
        1,
    )
    padded_x = jnp.concatenate([rim_rows, branch_x], axis=0).astype(jnp.float32)
    padded_keep = jnp.concatenate([rim_keep.astype(jnp.float32), keep_mask])
    conv_sum = conv_w[0] * padded_x[rim_size:]
    valid_mask = keep_mask
    valid_list = []
    for offset in range(1, rim_size + 1):
        valid_list.append(valid_mask)
        conv_sum = (
            conv_sum
            + valid_mask[:, None]
            * conv_w[offset]
            * padded_x[rim_size - offset : rim_size - offset + rec_len]
        )
        valid_mask = valid_mask * padded_keep[rim_size - offset : rim_size - offset + rec_len]
    conv_out = (conv_sum + lru_bias[0]).astype(jnp.bfloat16)
    row_count = conv_out.shape[0]
    conv_blocks = conv_out.reshape(row_count, head_count, block_size)
    pre_rows = (
        jnp.einsum(
            "lhb,ghbc->glhc", conv_blocks, gate_blocks, preferred_element_type=jnp.float32
        ).reshape(2, row_count, full_width)
        + lru_bias[1:3][:, None, :]
    )
    gate_in = pre_rows[0]
    gate_rate = pre_rows[1]
    conv_float = conv_out.astype(jnp.float32)

    def lru_local(conv_in, in_pre, rate_pre, decay_in):
        return lru_terms(conv_in, in_pre, rate_pre, decay_in, starts[:, None])

    (decay_rate, pushed), lru_pull = jax.vjp(lru_local, conv_float, gate_in, gate_rate, a_param)
    decay_cum, local_states = lax.associative_scan(combine_state, (decay_rate, pushed), axis=0)
    incoming = carry_across(decay_cum[-1], local_states[-1], False)
    states = local_states + decay_cum * incoming
    gated_val, gated_pull = jax.vjp(gelu_product, branch_y, states)
    gated_low = gated_val.astype(jnp.bfloat16)
    recurrent = matmul(gated_low, proj_out)
    middle = inputs + recurrent
    normed_two, norm_two_pull = jax.vjp(rms_scale, middle, norm_gains[1])
    normed_two_low = normed_two.astype(jnp.bfloat16)
    group_rows = lax.all_gather(normed_two_low, "tp", axis=0, tiled=True)
    gate_val = matmul(group_rows, w_gate)
    up_val = matmul(group_rows, w_up)
    hidden_val, mlp_pull = jax.vjp(gelu_product, gate_val, up_val)
    hidden = hidden_val.astype(jnp.bfloat16)
    mlp_out = lax.psum_scatter(
        matmul(hidden, w_down).astype(jnp.bfloat16), "tp", scatter_dimension=0, tiled=True
    ).astype(jnp.float32)
    layer_out = (middle + mlp_out).astype(jnp.bfloat16)
    grad_out = cotangent[0].astype(jnp.float32)
    group_grad = lax.all_gather(cotangent[0], "tp", axis=0, tiled=True)
    w_down_grad = matmul_left(hidden, group_grad)
    grad_hidden = matmul_right(group_grad, w_down)
    grad_gate, grad_up = mlp_pull(grad_hidden)
    grad_gate = grad_gate.astype(jnp.bfloat16)
    grad_up = grad_up.astype(jnp.bfloat16)
    w_gate_grad = matmul_left(group_rows, grad_gate)
    w_up_grad = matmul_left(group_rows, grad_up)
    grad_normed_two = lax.psum_scatter(
        (matmul_right(grad_gate, w_gate) + matmul_right(grad_up, w_up)).astype(jnp.bfloat16),
        "tp",
        scatter_dimension=0,
        tiled=True,
    ).astype(jnp.float32)
    grad_middle, gain_two_grad = norm_two_pull(grad_normed_two)
    grad_middle = grad_middle + grad_out
    grad_rec = grad_middle.astype(jnp.bfloat16)
    grad_gated = matmul_right(grad_rec, proj_out)
    grad_branch_y, grad_direct = gated_pull(grad_gated)
    grad_branch_y = grad_branch_y.astype(jnp.bfloat16)
    decay_next = jnp.concatenate([decay_rate[1:], jnp.ones_like(decay_rate[:1])], axis=0)
    reach_back, local_grads = lax.associative_scan(
        combine_state, (decay_next, grad_direct), reverse=True, axis=0
    )
    outgoing = carry_across(decay_rate[0] * reach_back[0], decay_rate[0] * local_grads[0], True)
    state_grads = local_grads + reach_back * outgoing
    prior_states = jnp.concatenate([incoming[None], states[:-1]], axis=0)
    grad_conv, grad_in, grad_rate, a_local_grad = lru_pull(
        (state_grads * prior_states, state_grads)
    )
    grad_pre = jnp.stack([grad_in, grad_rate]).astype(jnp.bfloat16)
    pre_sums = jnp.sum(grad_pre.astype(jnp.float32), axis=1)
    pre_blocks = grad_pre.reshape(2, row_count, head_count, block_size)
    gate_blocks_grad = jnp.einsum(
        "lhb,glhc->ghbc", conv_blocks, pre_blocks, preferred_element_type=jnp.float32
    )
    gate_back = jnp.einsum(
        "glhc,ghbc->lhb", pre_blocks, gate_blocks, preferred_element_type=jnp.float32
    ).reshape(row_count, full_width)
    grad_conv = grad_conv + gate_back
    conv_w_rows = [jnp.sum(grad_conv * padded_x[rim_size:], axis=0)]
    grad_padded = (
        jnp.zeros((rec_len + rim_size, full_width), jnp.float32)
        .at[rim_size:]
        .add(conv_w[0] * grad_conv)
    )
    for offset in range(1, rim_size + 1):
        masked = valid_list[offset - 1][:, None] * grad_conv
        conv_w_rows.append(
            jnp.sum(masked * padded_x[rim_size - offset : rim_size - offset + rec_len], axis=0)
        )
        grad_padded = grad_padded.at[rim_size - offset : rim_size - offset + rec_len].add(
            conv_w[offset] * masked
        )
    returned = from_behind(grad_padded[:rim_size], "tp", -1)
    grad_x_branch = (
        grad_padded[rim_size:].at[rec_len - rim_size :].add(returned).astype(jnp.bfloat16)
    )
    conv_w_grad = jnp.stack(conv_w_rows)
    lru_bias_grad = jnp.concatenate([jnp.sum(grad_conv, axis=0)[None], pre_sums], axis=0)
    grad_normed = matmul_right(grad_x_branch, proj_x) + matmul_right(grad_branch_y, proj_y)
    grad_inputs, gain_one_grad = norm_pull(grad_normed)
    input_grad = grad_middle + grad_inputs
    w_x_grad, w_y_grad, w_out_grad = (
        lax.psum_scatter(
            matmul_left(normed_low, grad_x_branch).astype(jnp.bfloat16),
            "tp",
            scatter_dimension=1,
            tiled=True,
        ).astype(jnp.float32),
        lax.psum_scatter(
            matmul_left(normed_low, grad_branch_y).astype(jnp.bfloat16),
            "tp",
            scatter_dimension=1,
            tiled=True,
        ).astype(jnp.float32),
        lax.psum_scatter(
            matmul_left(gated_low, grad_rec).astype(jnp.bfloat16),
            "tp",
            scatter_dimension=0,
            tiled=True,
        ).astype(jnp.float32),
    )
    norm_gains_grad = jnp.stack([gain_one_grad, gain_two_grad])
    totals = (
        lax.psum_scatter(
            w_x_grad.astype(jnp.bfloat16), "dp", scatter_dimension=0, tiled=True
        ).astype(jnp.float32),
        lax.psum_scatter(
            w_y_grad.astype(jnp.bfloat16), "dp", scatter_dimension=0, tiled=True
        ).astype(jnp.float32),
        lax.psum_scatter(
            w_out_grad.astype(jnp.bfloat16), "dp", scatter_dimension=1, tiled=True
        ).astype(jnp.float32),
        lax.psum_scatter(
            w_gate_grad.astype(jnp.bfloat16), "dp", scatter_dimension=0, tiled=True
        ).astype(jnp.float32),
        lax.psum_scatter(
            w_up_grad.astype(jnp.bfloat16), "dp", scatter_dimension=0, tiled=True
        ).astype(jnp.float32),
        lax.psum_scatter(
            w_down_grad.astype(jnp.bfloat16), "dp", scatter_dimension=1, tiled=True
        ).astype(jnp.float32),
        lax.psum_scatter(
            norm_gains_grad.astype(jnp.bfloat16), "dp", scatter_dimension=1, tiled=True
        ).astype(jnp.float32),
        lax.psum_scatter(
            conv_w_grad.astype(jnp.bfloat16), "dp", scatter_dimension=1, tiled=True
        ).astype(jnp.float32),
        lax.psum_scatter(
            lru_bias_grad.astype(jnp.bfloat16), "dp", scatter_dimension=1, tiled=True
        ).astype(jnp.float32),
        lax.psum_scatter(
            a_local_grad.astype(jnp.bfloat16), "dp", scatter_dimension=0, tiled=True
        ).astype(jnp.float32),
        lax.psum_scatter(
            gate_blocks_grad.astype(jnp.bfloat16), "dp", scatter_dimension=2, tiled=True
        ).astype(jnp.float32),
    )
    reduced_small = (
        lax.psum(totals[6].astype(jnp.bfloat16), "tp").astype(jnp.float32),
        lax.psum(totals[7].astype(jnp.bfloat16), "tp").astype(jnp.float32),
        lax.psum(totals[8].astype(jnp.bfloat16), "tp").astype(jnp.float32),
        lax.psum(totals[9].astype(jnp.bfloat16), "tp").astype(jnp.float32),
        lax.psum(totals[10].astype(jnp.bfloat16), "tp").astype(jnp.float32),
    )
    return (
        layer_out[None],
        input_grad[None],
        reduced_small[0],
        totals[0],
        totals[1],
        reduced_small[1],
        reduced_small[2],
        reduced_small[3],
        reduced_small[4],
        totals[2],
        totals[3],
        totals[4],
        totals[5],
    )


def solution(mesh):
    return jax.shard_map(
        local,
        mesh=mesh,
        in_specs=(
            P("dp", "tp", None),
            P("dp", "tp", None),
            P("dp", "tp"),
            P(),
            P(None, "tp"),
            P(None, "tp"),
            P(),
            P(),
            P(),
            P(),
            P("tp", None),
            P(None, "tp"),
            P(None, "tp"),
            P("tp", None),
        ),
        out_specs=(
            P("dp", "tp", None),
            P("dp", "tp", None),
            P(None, "dp"),
            P("dp", "tp"),
            P("dp", "tp"),
            P(None, "dp"),
            P(None, "dp"),
            P("dp"),
            P(None, None, "dp", None),
            P("tp", "dp"),
            P("dp", "tp"),
            P("dp", "tp"),
            P("tp", "dp"),
        ),
        check_vma=False,
    )
```

profile of v0, /device:TPU:0, one launch (start us, length us, event | category | flops | bytes accessed | tf_op | source)
XLA Modules:
  0.0 2920.7 jit_solution(7331917937362932643)
XLA Ops:
  17.3 124.5 %all-gather.9.cloned.1.call-done = bf16[2048,2560]{1,0:T(8,128)(2,1)} async-done(((bf16[2048,1280]{1,0:T(8,128)(2,1)}), bf16[2048,2560]{1,0:T(8,128)(2,1)}) %all-gather.9.cloned.1.call-update) | async-done | bytes 10485776 | tf_op jit(solution)/shard_map/all_gather | solution.py:86
  197.1 21.5 fusion.45
  504.2 17.6 pad.268
  556.6 17.5 pad.267
  574.1 17.5 pad.250
  595.1 17.7 pad.249
  619.5 17.9 multiply_convert_fusion.2
  651.5 58.3 %all-gather.13.cloned.1.call-done = bf16[1024,2048]{1,0:T(8,128)(2,1)} async-done(((bf16[512,2048]{1,0:T(8,128)(2,1)}), bf16[1024,2048]{1,0:T(8,128)(2,1)}) %all-gather.13.cloned.1.call-update) | async-done | bytes 4194320 | tf_op jit(solution)/shard_map/all_gather | solution.py:138
  709.8 20.5 fusion.113
  730.2 17.8 fusion.114
  748.0 19.9 all-gather.15.cloned.1.call-done
  767.9 32.0 %multiply_convert_fusion = (bf16[1024,3072]{1,0:T(8,128)(2,1)}, bf16[1024,3072]{1,0:T(8,128)(2,1)}, bf16[1024,3072]{1,0:T(8,128)(2,1)}) fusion(f32[1024,3072]{1,0:T(8,128)} %fusion.113, f32[1024,3072]{1,0:T(8,128)} %fusion.114, bf16[3072,2048]{1,0:T(8,128)(2,1)} %param.37, bf16[1,1024,2048]{2,1,0:T(8,128)(2,1)} %all-gather.15.cloned.1.call-done), kind=kOutput, calls=%fused_computation.9 | convolution fusion | flops 12966690816 | bytes 60817408 | tf_op jit(solution)/shard_map/dot_general | solution.py:43
  800.0 18.9 fusion.115
  818.9 20.7 add_convert_fusion
  839.7 19.3 convolution_convert_fusion.7
  895.6 21.3 slice.832
  916.9 20.9 slice.842
  937.8 20.8 slice.836
  969.3 18.0 fusion.51
  1007.5 20.8 slice.834
  1028.3 20.8 slice.838
  1278.6 21.2 slice.829
  1338.6 17.6 pad.285
  1356.3 17.6 pad.286
  1377.4 17.6 pad.303
  1394.9 17.6 pad.304
  1427.2 40.6 %rev.8 = f32[512,2560]{1,0:T(8,128)} reverse(f32[512,2560]{1,0:T(8,128)} %add.641), dimensions={0} | reverse | bytes 10485760 | tf_op jit(solution)/shard_map/rev | solution.py:169
  1467.9 40.5 %rev.9 = f32[512,2560]{1,0:T(8,128)} reverse(f32[512,2560]{1,0:T(8,128)} %add.650), dimensions={0} | reverse | bytes 10485760 | tf_op jit(solution)/shard_map/rev | solution.py:169
  1508.5 28.1 fusion.8
  1608.7 15.2 multiply_reduce_fusion.4
  1652.0 12.6 scatter-add.20
  1723.8 19.6 convolution_convert_fusion
  1743.4 16.8 copy.84
  1760.3 19.9 convolution_convert_fusion.2
  1780.2 19.6 convolution_convert_fusion.1
  1807.9 116.0 %reduce-scatter.33.cloned.1.call-done = bf16[2048,1280]{1,0:T(8,128)(2,1)} async-done(((bf16[2048,2560]{1,0:T(8,128)(2,1)}), bf16[2048,1280]{1,0:T(8,128)(2,1)}) %reduce-scatter.33.cloned.1.call-update) | async-done | bytes 5242896 | tf_op jit(solution)/shard_map/reduce_scatter | solution.py:218
  1923.9 124.1 %reduce-scatter.29.cloned.1.call-done = bf16[2048,1280]{1,0:T(8,128)(2,1)} async-done(((bf16[2048,2560]{1,0:T(8,128)(2,1)}), bf16[2048,1280]{1,0:T(8,128)(2,1)}) %reduce-scatter.29.cloned.1.call-update) | async-done | bytes 5242896 | tf_op jit(solution)/shard_map/reduce_scatter | solution.py:212
  2048.7 33.8 %all-reduce.75 = bf16[2560]{0:T(1024)(128)(2,1)S(1)} all-reduce(bf16[2560]{0:T(1024)(128)(2,1)S(1)} %copy-done.92), channel_id=12, replica_groups=mesh['dp'=16,'tp'=2] {'dp'}, use_global_device_ids=true, to_apply=%region_25.26.clone | all-reduce | flops 2560 | bytes 10240
  2082.6 25.7 reduce-scatter.47.cloned.1.call-done
  2109.2 59.0 %reduce-scatter.45.cloned.1.call-done = bf16[160,4]{1,0:T(8,128)(2,1)} async-done(((bf16[2560,4]{1,0:T(8,128)(2,1)}), bf16[160,4]{1,0:T(8,128)(2,1)}) %reduce-scatter.45.cloned.1.call-update) | async-done | bytes 1296
  2176.2 50.8 %reduce-scatter.43.cloned.1.call-done = bf16[128,2]{1,0:T(8,128)(2,1)} async-done(((bf16[2048,2]{1,0:T(8,128)(2,1)}), bf16[128,2]{1,0:T(8,128)(2,1)}) %reduce-scatter.43.cloned.1.call-update) | async-done | bytes 528
  2235.1 15.6 all-reduce.81.cloned.1.call-done
  2252.4 137.4 %reduce-scatter.51.cloned.1.call-done = bf16[128,3072]{1,0:T(8,128)(2,1)} async-done(((bf16[2048,3072]{1,0:T(8,128)(2,1)}), bf16[128,3072]{1,0:T(8,128)(2,1)}) %reduce-scatter.51.cloned.1.call-update) | async-done | bytes 786448
  2392.6 135.5 %reduce-scatter.39.cloned.1.call-done = bf16[128,3072]{1,0:T(8,128)(2,1)} async-done(((bf16[2048,3072]{1,0:T(8,128)(2,1)}), bf16[128,3072]{1,0:T(8,128)(2,1)}) %reduce-scatter.39.cloned.1.call-update) | async-done | bytes 786448 | tf_op jit(solution)/shard_map/reduce_scatter | solution.py:242
  2530.5 136.0 %reduce-scatter.41.cloned.1.call-done = bf16[128,3072]{1,0:T(8,128)(2,1)} async-done(((bf16[2048,3072]{1,0:T(8,128)(2,1)}), bf16[128,3072]{1,0:T(8,128)(2,1)}) %reduce-scatter.41.cloned.1.call-update) | async-done | bytes 786448 | tf_op jit(solution)/shard_map/reduce_scatter | solution.py:245
  2668.9 79.5 %reduce-scatter.49.cloned.1.call-done = bf16[128,1280]{1,0:T(8,128)(2,1)} async-done(((bf16[2048,1280]{1,0:T(8,128)(2,1)}), bf16[128,1280]{1,0:T(8,128)(2,1)}) %reduce-scatter.49.cloned.1.call-update) | async-done | bytes 327696
  2750.5 79.5 %reduce-scatter.35.cloned.1.call-done = bf16[128,1280]{1,0:T(8,128)(2,1)} async-done(((bf16[2048,1280]{1,0:T(8,128)(2,1)}), bf16[128,1280]{1,0:T(8,128)(2,1)}) %reduce-scatter.35.cloned.1.call-update) | async-done | bytes 327696 | tf_op jit(solution)/shard_map/reduce_scatter | solution.py:236
  2831.9 79.9 %reduce-scatter.31.cloned.1.call-done = bf16[128,1280]{1,0:T(8,128)(2,1)} async-done(((bf16[2048,1280]{1,0:T(8,128)(2,1)}), bf16[128,1280]{1,0:T(8,128)(2,1)}) %reduce-scatter.31.cloned.1.call-update) | async-done | bytes 327696 | tf_op jit(solution)/shard_map/reduce_scatter | solution.py:233
  (642 shorter events, 961.5 us)
Async XLA Ops:
  7.2 160.2 %copy-start = (bf16[2,10,256,256]{3,2,1,0:T(8,128)(2,1)S(1)}, bf16[2,10,256,256]{3,2,1,0:T(8,128)(2,1)}, u32[]{:S(2)}) copy-start(bf16[2,10,256,256]{3,2,1,0:T(8,128)(2,1)} %param.33) | copy-start | bytes 7864324
  7.2 134.6 %all-gather.9.cloned.1.call-start = ((), (), s32[]{:S(2)}) async-start(), calls=%async_computation.15 | async-start | bytes 15728640 | tf_op jit(solution)/shard_map/all_gather | solution.py:86
  8.0 610.1 %all-gather.7.cloned.1.call-start = ((), (), s32[]{:S(2)}) async-start(), calls=%async_computation.14 | async-start | bytes 15728640 | tf_op jit(solution)/shard_map/all_gather | solution.py:87
  8.7 628.7 %all-gather.11.cloned.1.call-start = ((), (), s32[]{:S(2)}) async-start(), calls=%async_computation.16 | async-start | bytes 15728640 | tf_op jit(solution)/shard_map/all_gather | solution.py:88
  8.8 188.3 %copy-start.57 = (f32[1,512]{1,0:T(1,128)}, f32[1,512]{1,0:T(1,128)S(1)}, u32[]{:S(2)}) copy-start(f32[1,512]{1,0:T(1,128)S(1)} %convert_element_type.170) | copy-start | bytes 6148
  8.8 188.2 %copy-start.49 = (f32[512]{0:T(512)}, f32[512]{0:T(512)S(1)}, u32[]{:S(2)}) copy-start(f32[512]{0:T(512)S(1)} %get-tuple-element.232) | copy-start | bytes 6148
  8.9 8.3 collective-permute-start.1
  13.8 696.0 %all-gather.13.cloned.1.call-start = ((), (), s32[]{:S(2)}) async-start(), calls=%async_computation.17 | async-start | bytes 6291456 | tf_op jit(solution)/shard_map/all_gather | solution.py:138
  13.9 183.2 %copy-start.39 = (f32[2560]{0:T(1024)}, f32[2560]{0:T(1024)S(1)}, u32[]{:S(2)}) copy-start(f32[2560]{0:T(1024)S(1)} %slice_reduce_fusion) | copy-start | bytes 30724
  13.9 183.1 %copy-start.47 = (f32[2560]{0:T(1024)}, f32[2560]{0:T(1024)S(1)}, u32[]{:S(2)}) copy-start(f32[2560]{0:T(1024)S(1)} %broadcast_multiply_fusion.1) | copy-start | bytes 30724
  14.6 136.3 %copy-start.89 = (f32[1,2048]{1,0:T(1,128)}, f32[1,2048]{1,0:T(1,128)S(1)}, u32[]{:S(2)}) copy-start(f32[1,2048]{1,0:T(1,128)S(1)} %get-tuple-element.228) | copy-start | bytes 24580
  16.7 134.2 %copy-start.102 = (f32[512]{0:T(512)}, f32[512]{0:T(512)S(1)}, u32[]{:S(2)}) copy-start(f32[512]{0:T(512)S(1)} %fusion.89) | copy-start | bytes 6148
  17.2 179.8 %copy-start.31 = (f32[2560]{0:T(1024)}, f32[2560]{0:T(1024)S(1)}, u32[]{:S(2)}) copy-start(f32[2560]{0:T(1024)S(1)} %get-tuple-element.123) | copy-start | bytes 30724
  17.2 179.8 %copy-start.33 = (f32[2560]{0:T(1024)}, f32[2560]{0:T(1024)S(1)}, u32[]{:S(2)}) copy-start(f32[2560]{0:T(1024)S(1)} %get-tuple-element.124) | copy-start | bytes 30724
  17.2 179.9 %copy-start.35 = (f32[2560]{0:T(1024)}, f32[2560]{0:T(1024)S(1)}, u32[]{:S(2)}) copy-start(f32[2560]{0:T(1024)S(1)} %get-tuple-element.122) | copy-start | bytes 30724
  17.2 179.9 %copy-start.37 = (f32[2560]{0:T(1024)}, f32[2560]{0:T(1024)S(1)}, u32[]{:S(2)}) copy-start(f32[2560]{0:T(1024)S(1)} %get-tuple-element.121) | copy-start | bytes 30724
  150.9 3.7 collective-permute-start
  153.2 43.9 %copy-start.53 = (f32[512]{0:T(512)}, f32[512]{0:T(512)S(1)}, u32[]{:S(2)}) copy-start(f32[512]{0:T(512)S(1)} %get-tuple-element.138) | copy-start | bytes 6148
  153.2 43.9 %copy-start.55 = (f32[512]{0:T(512)}, f32[512]{0:T(512)S(1)}, u32[]{:S(2)}) copy-start(f32[512]{0:T(512)S(1)} %get-tuple-element.139) | copy-start | bytes 6148
  613.9 5.6 collective-permute-start.2
  650.9 117.1 %all-gather.15.cloned.1.call-start = ((), (), s32[]{:S(2)}) async-start(), calls=%async_computation.28 | async-start | bytes 6291456 | tf_op jit(solution)/shard_map/all_gather | solution.py:148
  651.4 307.1 %reduce-scatter.27.cloned.1.call-start = ((), (), s32[]{:S(2)}) async-start(), calls=%async_computation.19 | async-start | bytes 6291456 | tf_op jit(solution)/shard_map/reduce_scatter | solution.py:156
  839.6 123.8 %reduce-scatter.25.cloned.1.call-start = ((), (), s32[]{:S(2)}) async-start(), calls=%async_computation.18 | async-start | bytes 6291456 | tf_op jit(solution)/shard_map/reduce_scatter | solution.py:143
  859.0 863.0 %all-reduce.83.cloned.1.call-start = ((), (), s32[]{:S(2)}) async-start(), calls=%async_computation.34 | async-start | bytes 5242880
  916.9 41.7 %copy-start.46 = (f32[1,2048]{1,0:T(1,128)S(1)}, f32[1,2048]{1,0:T(1,128)}, u32[]{:S(2)}) copy-start(f32[1,2048]{1,0:T(1,128)} %get-tuple-element.227) | copy-start | bytes 24580
  916.9 41.7 %copy-start.88 = (f32[512]{0:T(512)S(1)}, f32[512]{0:T(512)}, u32[]{:S(2)}) copy-start(f32[512]{0:T(512)} %copy-done.87) | copy-start | bytes 6148
  1413.7 94.8 %collective-permute-start.3 = (f32[2560]{0:T(1024)S(1)}, f32[2560]{0:T(1024)S(1)}, u32[]{:S(2)}, u32[]{:S(2)}) collective-permute-start(f32[2560]{0:T(1024)S(1)} %fusion.88), channel_id=1, source_target_pairs={{1,0},{3,2},{5,4},{7,6},{9,8},{11,10},{13,12},{15,14},{17,16},{19,... | collective-permute-start | bytes 30728 | tf_op jit(solution)/shard_map/ppermute | solution.py:12
  1467.8 40.6 %copy-start.40 = (f32[2560]{0:T(1024)S(1)}, f32[2560]{0:T(1024)}, u32[]{:S(2)}) copy-start(f32[2560]{0:T(1024)} %copy-done.39) | copy-start | bytes 30724
  1467.8 40.6 %copy-start.48 = (f32[2560]{0:T(1024)S(1)}, f32[2560]{0:T(1024)}, u32[]{:S(2)}) copy-start(f32[2560]{0:T(1024)} %copy-done.47) | copy-start | bytes 30724
  1467.8 40.6 %copy-start.50 = (f32[512]{0:T(512)S(1)}, f32[512]{0:T(512)}, u32[]{:S(2)}) copy-start(f32[512]{0:T(512)} %copy-done.49) | copy-start | bytes 6148
  1467.8 40.6 %copy-start.54 = (f32[512]{0:T(512)S(1)}, f32[512]{0:T(512)}, u32[]{:S(2)}) copy-start(f32[512]{0:T(512)} %copy-done.53) | copy-start | bytes 6148
  1467.8 40.6 %copy-start.56 = (f32[512]{0:T(512)S(1)}, f32[512]{0:T(512)}, u32[]{:S(2)}) copy-start(f32[512]{0:T(512)} %copy-done.55) | copy-start | bytes 6148
  1573.6 226.4 %reduce-scatter.37.cloned.1.call-start = ((), (), s32[]{:S(2)}) async-start(), calls=%async_computation.25 | async-start | bytes 15728640 | tf_op jit(solution)/shard_map/reduce_scatter | solution.py:224
  1584.8 339.0 %reduce-scatter.33.cloned.1.call-start = ((), (), s32[]{:S(2)}) async-start(), calls=%async_computation.22 | async-start | bytes 15728640 | tf_op jit(solution)/shard_map/reduce_scatter | solution.py:218
  1596.2 451.9 %reduce-scatter.29.cloned.1.call-start = ((), (), s32[]{:S(2)}) async-start(), calls=%async_computation.20 | async-start | bytes 15728640 | tf_op jit(solution)/shard_map/reduce_scatter | solution.py:212
  1672.8 5.9 collective-permute-start.4
  1691.8 416.5 %reduce-scatter.47.cloned.1.call-start = ((), (), s32[]{:S(2)}) async-start(), calls=%async_computation.31 | async-start | bytes 696320
  1707.0 461.2 %reduce-scatter.45.cloned.1.call-start = ((), (), s32[]{:S(2)}) async-start(), calls=%async_computation.30 | async-start | bytes 696320
  1708.3 518.7 %reduce-scatter.43.cloned.1.call-start = ((), (), s32[]{:S(2)}) async-start(), calls=%async_computation.29 | async-start | bytes 557056
  1721.9 528.8 %all-reduce.81.cloned.1.call-start = ((), (), s32[]{:S(2)}) async-start(), calls=%async_computation.24 | async-start | bytes 327680 | tf_op jit(solution)/shard_map/psum | solution.py:272
  1723.7 666.1 %reduce-scatter.51.cloned.1.call-start = ((), (), s32[]{:S(2)}) async-start(), calls=%async_computation.33 | async-start | bytes 13369344
  1760.2 767.8 %reduce-scatter.39.cloned.1.call-start = ((), (), s32[]{:S(2)}) async-start(), calls=%async_computation.26 | async-start | bytes 13369344 | tf_op jit(solution)/shard_map/reduce_scatter | solution.py:242
  1780.2 886.3 %reduce-scatter.41.cloned.1.call-start = ((), (), s32[]{:S(2)}) async-start(), calls=%async_computation.27 | async-start | bytes 13369344 | tf_op jit(solution)/shard_map/reduce_scatter | solution.py:245
  1799.9 948.6 %reduce-scatter.49.cloned.1.call-start = ((), (), s32[]{:S(2)}) async-start(), calls=%async_computation.32 | async-start | bytes 5570560
  1807.8 1022.2 %reduce-scatter.35.cloned.1.call-start = ((), (), s32[]{:S(2)}) async-start(), calls=%async_computation.23 | async-start | bytes 5570560 | tf_op jit(solution)/shard_map/reduce_scatter | solution.py:236
  1923.8 124.9 %copy-start.92 = (bf16[2560]{0:T(1024)(128)(2,1)S(1)}, bf16[2560]{0:T(1024)(128)(2,1)}, u32[]{:S(2)}) copy-start(bf16[2560]{0:T(1024)(128)(2,1)} %get-tuple-element.229) | copy-start | bytes 15364
  1923.9 245.2 %copy-start.95 = (f32[512]{0:T(512)S(1)}, f32[512]{0:T(512)}, u32[]{:S(2)}) copy-start(f32[512]{0:T(512)} %copy-done.94) | copy-start | bytes 6148
  1923.9 987.9 %reduce-scatter.31.cloned.1.call-start = ((), (), s32[]{:S(2)}) async-start(), calls=%async_computation.21 | async-start | bytes 5570560 | tf_op jit(solution)/shard_map/reduce_scatter | solution.py:233
  (86 other events, 1345.0 us)
Sparse Core Ops, SparseCore 0:
  9.6 132.1 all-gather.8
  143.4 129.4 all-gather.6
  274.5 129.5 all-gather.10
  651.0 58.7 all-gather.12
  711.1 56.7 all-gather.14
  839.7 54.2 reduce-scatter.26
  896.5 54.3 reduce-scatter.24
  1573.7 102.6 all-reduce.82
  1678.7 121.0 reduce-scatter.36
  1802.0 121.8 reduce-scatter.32
  1926.2 121.8 reduce-scatter.28
  2052.0 56.2 reduce-scatter.46
  2112.8 55.2 reduce-scatter.44
  2172.1 54.8 reduce-scatter.42
  2229.8 20.8 all-reduce.80
  2255.2 134.5 reduce-scatter.50
  2394.2 133.7 reduce-scatter.38
  2532.5 133.9 reduce-scatter.40
  2670.8 77.5 reduce-scatter.48
  2752.6 77.3 reduce-scatter.34
  2834.4 77.3 reduce-scatter.30
where the time goes:
time: 2950 us; the launch traced here: 2920 us
  waiting for transfers between devices  1250 us (42%)
  local copies, waits for them, and re-layouts  973 us (33%)
  matrix products  315 us (11%)
  other arithmetic  314 us (11%)
  blocking collectives  38.8 us (1%)
    unnamed x27, waiting for transfers between devices  355 us
    slice x65, local copies, waits for them, and re-layouts, local(): lax.associative_scan(combine_state, (decay_next, grad_direct), reverse=Tr...  293 us
    slice x60, local copies, waits for them, and re-layouts, local(): lax.associative_scan(combine_state, (decay_rate, pushed), axis=0)  169 us
    pad x32, local copies, waits for them, and re-layouts, local(): lax.associative_scan(combine_state, (decay_rate, pushed), axis=0)  143 us
    pad x32, local copies, waits for them, and re-layouts, local(): lax.associative_scan(combine_state, (decay_next, grad_direct), reverse=Tr...  141 us
    reduce_scatter x1, waiting for transfers between devices, local(): lax.psum_scatter(w_up_grad.astype(jnp.bfloat16), 'dp', scatter_dimension=...  136 us
    reduce_scatter x1, waiting for transfers between devices, local(): lax.psum_scatter(w_gate_grad.astype(jnp.bfloat16), 'dp', scatter_dimensio...  135 us
    all_gather x1, waiting for transfers between devices, local(): lax.all_gather(w_x, 'tp', axis=1, tiled=True)  124 us
  transfers between devices with their start and end apart: 26, of which 17 were waited for; matrix products, arithmetic and copies ran while one was open for 34% of the time, Pallas kernels for 0%

commit v1 on v0

--- a/solution.py
+++ b/solution.py
@@ -1,9 +1,548 @@
+import functools
+
 import jax
 import jax.numpy as jnp
 from jax import lax
+from jax.experimental import pallas as pl
+from jax.experimental.pallas import tpu as pltpu
 from jax.sharding import PartitionSpec as P
 
 EPS = 1e-06
+F32, BF16 = jnp.float32, jnp.bfloat16
+STEP = 64
+GELU_A, GELU_B = 0.7978845608028654, 0.044715
+
+
+def one_minus_exp(value, exp_neg):
+    series = 1.0 / 5040.0
+    for term in (-1.0 / 720.0, 1.0 / 120.0, -1.0 / 24.0, 1.0 / 6.0, -0.5, 1.0):
+        series = series * value + term
+    return jnp.where(value < 0.25, series * value, 1.0 - exp_neg)
+
+
+def group_scan(coef, term, carry, reverse):
+    rows, lanes = coef.shape
+    groups = rows // 8
+    coef = coef.reshape(groups, 8, lanes)
+    term = term.reshape(groups, 8, lanes)
+    row = lax.broadcasted_iota(jnp.int32, (1, 8, lanes), 1)
+    for dist in (1, 2, 4):
+        shift = 8 - dist if reverse else dist
+        inside = row < 8 - dist if reverse else row >= dist
+        coef_by = jnp.where(inside, pltpu.roll(coef, shift, 1), 1.0)
+        term_by = jnp.where(inside, pltpu.roll(term, shift, 1), 0.0)
+        term = term + coef * term_by
+        coef = coef * coef_by
+    parts = [None] * groups
+    for group in reversed(range(groups)) if reverse else range(groups):
+        parts[group] = term[group] + coef[group] * carry
+        carry = parts[group][0:1] if reverse else parts[group][7:8]
+    return jnp.concatenate(parts, axis=0), carry
+
+
+def gate_setup(place, bx_own, bx_oth, mask_ref, prm_ref, gate_ref, xs, cs, pre):
+    half = bx_own.shape[0]
+    length = 2 * half
+    lanes = bx_own.shape[1]
+    xs[0:8, :] = jnp.zeros((8, lanes), F32)
+    xs[pl.ds(pl.multiple_of(8 + place * half, 8), half), :] = bx_own[...].astype(F32)
+    xs[pl.ds(pl.multiple_of(8 + (1 - place) * half, 8), half), :] = bx_oth[...].astype(F32)
+    taps = [prm_ref[k : k + 1, :] for k in range(4)]
+    bias = prm_ref[4:5, :]
+
+    def conv_step(index, _):
+        at = pl.multiple_of(index * STEP, STEP)
+        window = xs[pl.ds(at, STEP + 8), :]
+        mask = mask_ref[pl.ds(at, STEP), :]
+        total = taps[0] * window[8 : 8 + STEP] + bias
+        for k in (1, 2, 3):
+            total = total + (mask[:, k : k + 1] * taps[k]) * window[8 - k : 8 - k + STEP]
+        cs[pl.ds(at, STEP), :] = total.astype(BF16)
+        return 0
+
+    lax.fori_loop(0, length // STEP, conv_step, 0)
+
+    def gate_step(index, _):
+        rows = pl.ds(pl.multiple_of(index * 256, 256), 256)
+        conv = cs[rows, :]
+        pre[rows, 0:lanes] = jnp.dot(conv, gate_ref[0, 0], preferred_element_type=F32)
+        pre[rows, lanes:] = jnp.dot(conv, gate_ref[1, 0], preferred_element_type=F32)
+        return 0
+
+    lax.fori_loop(0, length // 256, gate_step, 0)
+
+
+def gate_terms(pre_rows, prm_ref, keep):
+    lanes = pre_rows.shape[1] // 2
+    in_gate = jax.nn.sigmoid(pre_rows[:, :lanes] + prm_ref[5:6, :])
+    rate_gate = jax.nn.sigmoid(pre_rows[:, lanes:] + prm_ref[6:7, :])
+    log_decay = prm_ref[7:8, :] * rate_gate
+    decay = jnp.exp(log_decay)
+    squared = decay * decay
+    gap = one_minus_exp(-2.0 * log_decay, squared)
+    return in_gate, rate_gate, decay, squared, gap
+
+
+def own_rows(place, half):
+    return pl.ds(pl.multiple_of(place * half, half), half), pl.ds(pl.multiple_of((1 - place) * half, half), half)
+
+
+def rec_fwd_kernel(
+    bx_own, bx_oth, by_own, by_oth, mask_ref, prm_ref, gate_ref, gated_own, gated_oth, state_ref, xs, cs, pre, ys, gated,
+):
+    place = lax.axis_index("tp")
+    half, lanes = bx_own.shape
+    own, oth = own_rows(place, half)
+    gate_setup(place, bx_own, bx_oth, mask_ref, prm_ref, gate_ref, xs, cs, pre)
+    ys[own, :] = by_own[...]
+    ys[oth, :] = by_oth[...]
+
+    def step(index, carry):
+        rows = pl.ds(pl.multiple_of(index * STEP, STEP), STEP)
+        keep = mask_ref[rows, :][:, 0:1]
+        in_gate, _, decay, _, gap = gate_terms(pre[rows, :], prm_ref, keep)
+        scaling = (1.0 - keep) + keep * jnp.sqrt(gap)
+        pushed = cs[rows, :].astype(F32) * in_gate * scaling
+        state, carry = group_scan(decay * keep, pushed, carry, False)
+        state_ref[rows, :] = state
+        y = ys[rows, :]
+        tanh = jnp.tanh(GELU_A * (y + GELU_B * (y * y * y)))
+        gated[rows, :] = (state * (0.5 * y * (1.0 + tanh))).astype(BF16)
+        return carry
+
+    lax.fori_loop(0, 2 * half // STEP, step, jnp.zeros((1, lanes), F32))
+    gated_own[...] = gated[own, :]
+    gated_oth[...] = gated[oth, :]
+
+
+def fold(value):
+    return jnp.sum(value.reshape(value.shape[0] // 8, 8, value.shape[1]), axis=0)
+
+
+def rec_bwd_kernel(
+    count, bits, bx_own, bx_oth, by_own, by_oth, state_ref, up_own, up_oth, mask_ref, prm_ref, gate_ref,
+    gx_own, gx_oth, gy_own, gy_oth, gw_ref, sum_ref, xs, cs, pre, ys, up_ref, gx_ref, gy_ref, gw, dg, gc,
+):
+    place = lax.axis_index("tp")
+    half, lanes = bx_own.shape
+    length = 2 * half
+    steps = length // STEP
+    own, oth = own_rows(place, half)
+    gate_setup(place, bx_own, bx_oth, mask_ref, prm_ref, gate_ref, xs, cs, pre)
+    ys[own, :] = by_own[...]
+    ys[oth, :] = by_oth[...]
+    up_ref[own, :] = up_own[...]
+    up_ref[oth, :] = up_oth[...]
+    zero8 = jnp.zeros((8, lanes), F32)
+
+    def step(index, carried):
+        carry, sum_in, sum_rate, sum_log = carried
+        rows = pl.ds(pl.multiple_of((steps - 1 - index) * STEP, STEP), STEP)
+        keep = mask_ref[rows, :][:, 0:1]
+        in_gate, rate_gate, decay, squared, gap = gate_terms(pre[rows, :], prm_ref, keep)
+        inverse = lax.rsqrt(gap)
+        scaling = (1.0 - keep) + keep * (gap * inverse)
+        y = ys[rows, :]
+        y2 = y * y
+        tanh = jnp.tanh(GELU_A * y * (1.0 + GELU_B * y2))
+        lift = 0.5 * (1.0 + tanh)
+        slope = lift + (0.5 * GELU_A) * y * (1.0 - tanh * tanh) * (1.0 + (3.0 * GELU_B) * y2)
+        up = up_ref[rows, :]
+        state = state_ref[rows, :]
+        gy_ref[rows, :] = (up * state * slope).astype(BF16)
+        direct = up * (y * lift)
+        coef = decay * keep
+        sent, below = group_scan(coef, coef * direct, carry, True)
+        shifted = jnp.concatenate([sent[1:], carry], axis=0)
+        grad_state = direct + shifted
+        entered = cs[rows, :].astype(F32) * in_gate
+        pushed = entered * scaling
+        grad_log = grad_state * ((state - pushed) - entered * (keep * squared * inverse))
+        grad_in = (grad_state * pushed * (1.0 - in_gate)).astype(BF16)
+        through = grad_log * rate_gate
+        grad_rate = (through * (1.0 - rate_gate) * prm_ref[7:8, :]).astype(BF16)
+        dg[rows, 0:lanes] = grad_in
+        dg[rows, lanes:] = grad_rate
+        gc[rows, :] = grad_state * in_gate * scaling
+        return (
+            below,
+            sum_in + fold(grad_in.astype(F32)),
+            sum_rate + fold(grad_rate.astype(F32)),
+            sum_log + fold(through),
+        )
+
+    _, sum_in, sum_rate, sum_log = lax.fori_loop(
+        0, steps, step, (jnp.zeros((1, lanes), F32), zero8, zero8, zero8)
+    )
+    gc[length : length + 8, :] = zero8
+
+    def back_step(index, _):
+        rows = pl.ds(pl.multiple_of(index * 256, 256), 256)
+        gc[rows, :] += matmul_right(dg[rows, 0:lanes], gate_ref[0, 0]) + matmul_right(
+            dg[rows, lanes:], gate_ref[1, 0]
+        )
+        return 0
+
+    lax.fori_loop(0, length // 256, back_step, 0)
+    gw[0:lanes, :] = matmul_left(cs[...], dg[:, 0:lanes]).astype(BF16)
+    gw[lanes:, :] = matmul_left(cs[...], dg[:, lanes:]).astype(BF16)
+    rows_each = lanes // count
+    me = lax.axis_index("dp")
+    for spot in range(count):
+        block = block_from(me, spot, bits)
+        for gate in (0, 1):
+            source = pl.ds(pl.multiple_of(gate * lanes + block * rows_each, rows_each), rows_each)
+            gw_ref[spot, 0, gate * rows_each : (gate + 1) * rows_each, :] = gw[source, :]
+    taps = [prm_ref[k : k + 1, :] for k in range(4)]
+
+    def conv_step(index, sums):
+        at = pl.multiple_of(index * STEP, STEP)
+        grad = gc[pl.ds(at, STEP + 8), :]
+        window = xs[pl.ds(at, STEP + 8), :]
+        mask = mask_ref[pl.ds(at, STEP + 8), :]
+        here = grad[0:STEP]
+        total = taps[0] * here
+        sums = [sums[0] + fold(here), sums[1] + fold(here * window[8 : 8 + STEP])] + list(sums[2:])
+        for k in (1, 2, 3):
+            masked = grad * mask[:, k : k + 1]
+            total = total + taps[k] * masked[k : k + STEP]
+            sums[k + 1] = sums[k + 1] + fold(masked[0:STEP] * window[8 - k : 8 - k + STEP])
+        gx_ref[pl.ds(at, STEP), :] = total.astype(BF16)
+        return tuple(sums)
+
+    sums = lax.fori_loop(0, steps, conv_step, (zero8,) * 5)
+    for index, value in enumerate(sums[1:5] + (sums[0], sum_in, sum_rate, sum_log)):
+        sum_ref[index : index + 1, :] = jnp.sum(value, axis=0, keepdims=True)
+    for source, first, second in ((gx_ref, gx_own, gx_oth), (gy_ref, gy_own, gy_oth)):
+        first[...] = source[own, :]
+        second[...] = source[oth, :]
+
+
+def rec_specs(half, lanes, length):
+    piece = pl.BlockSpec((half, lanes), lambda h: (0, h))
+    whole = pl.BlockSpec((length, lanes), lambda h: (0, h))
+    mask = pl.BlockSpec((length + 8, 8), lambda h: (0, 0))
+    prm = pl.BlockSpec((8, lanes), lambda h: (0, h))
+    gate = pl.BlockSpec((2, 1, lanes, lanes), lambda h: (0, h, 0, 0))
+    return piece, whole, mask, prm, gate
+
+
+def rec_scratch(length, lanes):
+    return [
+        pltpu.VMEM((length + 8, lanes), F32),
+        pltpu.VMEM((length, lanes), BF16),
+        pltpu.VMEM((length, 2 * lanes), F32),
+        pltpu.VMEM((length, lanes), F32),
+    ]
+
+
+def rec_fwd(bx_own, bx_oth, by_own, by_oth, mask, prm, gates):
+    half, width = bx_own.shape
+    length, lanes, heads = 2 * half, gates.shape[2], gates.shape[1]
+    piece, whole, mask_spec, prm_spec, gate_spec = rec_specs(half, lanes, length)
+    return pl.pallas_call(
+        rec_fwd_kernel,
+        grid=(heads,),
+        in_specs=[piece] * 4 + [mask_spec, prm_spec, gate_spec],
+        out_specs=[piece, piece, whole],
+        out_shape=[
+            jax.ShapeDtypeStruct((half, width), BF16),
+            jax.ShapeDtypeStruct((half, width), BF16),
+            jax.ShapeDtypeStruct((length, width), F32),
+        ],
+        scratch_shapes=rec_scratch(length, lanes) + [pltpu.VMEM((length, lanes), BF16)],
+        compiler_params=pltpu.CompilerParams(vmem_limit_bytes=40 << 20),
+        cost_estimate=pl.CostEstimate(
+            flops=4 * length * width * lanes + 100 * length * width,
+            bytes_accessed=16 * length * width,
+            transcendentals=6 * length * width,
+        ),
+        name="rec_fwd",
+    )(bx_own, bx_oth, by_own, by_oth, mask, prm, gates)
+
+
+def rec_bwd(bx_own, bx_oth, by_own, by_oth, states, up_own, up_oth, mask, prm, gates, count):
+    half, width = bx_own.shape
+    length, lanes, heads = 2 * half, gates.shape[2], gates.shape[1]
+    piece, whole, mask_spec, prm_spec, gate_spec = rec_specs(half, lanes, length)
+    return pl.pallas_call(
+        functools.partial(rec_bwd_kernel, count, stage_bits(count)),
+        grid=(heads,),
+        in_specs=[piece] * 4 + [whole, piece, piece, mask_spec, prm_spec, gate_spec],
+        out_specs=[piece] * 4 + [pl.BlockSpec((count, 1, 2 * lanes // count, lanes), lambda h: (0, h, 0, 0)), prm_spec],
+        out_shape=[jax.ShapeDtypeStruct((half, width), BF16)] * 4
+        + [
+            jax.ShapeDtypeStruct((count, heads, 2 * lanes // count, lanes), BF16),
+            jax.ShapeDtypeStruct((8, width), F32),
+        ],
+        scratch_shapes=rec_scratch(length, lanes)
+        + [
+            pltpu.VMEM((length, lanes), F32),
+            pltpu.VMEM((length, lanes), BF16),
+            pltpu.VMEM((length, lanes), BF16),
+            pltpu.VMEM((2 * lanes, lanes), BF16),
+            pltpu.VMEM((length, 2 * lanes), BF16),
+            pltpu.VMEM((length + 8, lanes), F32),
+        ],
+        compiler_params=pltpu.CompilerParams(vmem_limit_bytes=48 << 20),
+        cost_estimate=pl.CostEstimate(
+            flops=12 * length * width * lanes + 250 * length * width,
+            bytes_accessed=24 * length * width,
+            transcendentals=8 * length * width,
+        ),
+        name="rec_bwd",
+    )(bx_own, bx_oth, by_own, by_oth, states, up_own, up_oth, mask, prm, gates)
+
+
+def stage_bits(count):
+    bits = count.bit_length() - 1
+    return [1 << bit for bit in ([0, 1] + list(reversed(range(2, bits))))[:bits]]
+
+
+def block_at(place, bits):
+    return sum(bit for step, bit in enumerate(bits) if (place >> (len(bits) - 1 - step)) & 1)
+
+
+def block_from(me, place, bits):
+    relative = block_at(place, bits)
+    block = 0
+    for bit in bits:
+        mine = lax.rem(me // bit, 2)
+        block = block + bit * (1 - mine if relative & bit else mine)
+    return block
+
+
+def arrange_kernel(count, bits, steps, first, second, keep, send):
+    me = lax.axis_index("dp")
+    cols = first.shape[1] // count
+
+    def move(piece):
+        for place in range(count):
+            source = pl.ds(pl.multiple_of(block_from(me, place, bits) * cols, cols), cols)
+            into, spot = (keep, place) if place < count // 2 else (send, place - count // 2)
+            into[:, spot * cols : (spot + 1) * cols] = piece[:, source]
+
+    @pl.when(pl.program_id(0) < steps)
+    def _():
+        move(first)
+
+    @pl.when(pl.program_id(0) >= steps)
+    def _():
+        move(second)
+
+
+def arrange(first, second, count):
+    half, width = first.shape
+    steps = 2
+    block = half // steps
+    shape = jax.ShapeDtypeStruct((2 * half, width // 2), first.dtype)
+    return pl.pallas_call(
+        functools.partial(arrange_kernel, count, stage_bits(count), steps),
+        grid=(2 * steps,),
+        in_specs=[
+            pl.BlockSpec((block, width), lambda i: (jnp.minimum(i, steps - 1), 0)),
+            pl.BlockSpec((block, width), lambda i: (jnp.maximum(i - steps, 0), 0)),
+        ],
+        out_specs=[pl.BlockSpec((block, width // 2), lambda i: (i, 0))] * 2,
+        out_shape=[shape, shape],
+        cost_estimate=pl.CostEstimate(flops=0, bytes_accessed=8 * half * width, transcendentals=0),
+        name="arrange",
+    )(first, second)
+
+
+def swap(value):
+    return lax.ppermute(value, "tp", [(0, 1), (1, 0)])
+
+
+def flip(value, bit):
+    count = lax.axis_size("dp")
+    return lax.ppermute(value, "dp", [(source, source ^ bit) for source in range(count)])
+
+
+class Reduction:
+    def __init__(self, keep, sent, bits):
+        self.keep, self.bits = keep, list(bits)
+        self.pass_on(sent)
+
+    def pass_on(self, sent):
+        self.sent = sent
+        self.received = flip(sent, self.bits.pop(0))
+
+    def step(self):
+        middle = self.keep.shape[0] // 2
+        keep, received = self.keep, self.received
+        self.keep = (keep[:middle].astype(F32) + received[:middle].astype(F32)).astype(BF16)
+        self.pass_on((keep[middle:].astype(F32) + received[middle:].astype(F32)).astype(BF16))
+        return self.sent
+
+    def total(self):
+        return self.keep.astype(F32) + self.received.astype(F32)
+
+
+def after(value, *others):
+    return lax.optimization_barrier((value, *others))[0]
+
+
+def sum_everywhere(value):
+    value = value + swap(value)
+    for bit in stage_bits(lax.axis_size("dp")):
+        value = value + flip(value, bit)
+    return value
+
+
+def norm_back(values, gain, grad):
+    scale = lax.rsqrt(jnp.mean(values * values, axis=-1, keepdims=True) + EPS)
+    lifted = gain * grad
+    pull = jnp.mean(values * lifted, axis=-1, keepdims=True)
+    grad_values = scale * lifted - values * (scale * scale * scale * pull)
+    return grad_values, grad * values * scale
+
+
+def weight_grad(parts, right, bits):
+    keep, send = parts
+    sent = matmul_left(send, right).astype(BF16)
+    kept = matmul_left(after(keep, sent), right).astype(BF16)
+    return Reduction(kept, sent, bits)
+
+
+def local_channels(
+    layer_in, cotangent, resets, norm_gains, w_x, w_y, conv_w, lru_bias, a_param, gate_blocks, w_out, w_gate, w_up, w_down,
+):
+    place = lax.axis_index("tp")
+    me = lax.axis_index("dp")
+    count = lax.axis_size("dp")
+    bits = stage_bits(count)
+    width = w_x.shape[1]
+    full_width = conv_w.shape[1]
+    heads = gate_blocks.shape[1] // 2
+    model = norm_gains.shape[1]
+
+    own_in, own_cot = layer_in[0], cotangent[0]
+    oth_in = swap(own_in)
+    oth_resets = swap(resets[0])
+    oth_cot = swap(own_cot)
+    normed_own = rms_scale(own_in.astype(F32), norm_gains[0]).astype(BF16)
+    bx_own = matmul(normed_own, w_x).astype(BF16)
+    by_own = matmul(normed_own, w_y)
+
+    first_place = place == 0
+    in_time = jnp.where(first_place, resets[0], oth_resets), jnp.where(first_place, oth_resets, resets[0])
+    keep = 1.0 - jnp.concatenate(in_time).astype(F32)
+    keep_1 = jnp.concatenate([jnp.ones((1,), F32), keep[:-1]])
+    keep_2 = jnp.concatenate([jnp.ones((1,), F32), keep_1[:-1]])
+    valid = [keep, keep, keep * keep_1, keep * keep_1 * keep_2]
+    mask = jnp.pad(jnp.stack(valid, axis=1), ((0, 8), (0, 4)))
+    table = jnp.concatenate([conv_w, lru_bias, -8.0 * jax.nn.softplus(a_param)[None]], axis=0)
+    prm = lax.dynamic_slice(table, (0, place * width), (8, width))
+    gates = lax.dynamic_slice_in_dim(gate_blocks, place * heads, heads, axis=1)
+
+    normed_oth = rms_scale(oth_in.astype(F32), norm_gains[0]).astype(BF16)
+    bx_oth = matmul(normed_oth, w_x).astype(BF16)
+    by_oth = matmul(normed_oth, w_y)
+    gated_own, gated_oth, states = rec_fwd(bx_own, bx_oth, by_own, by_oth, mask, prm, gates)
+
+    part_oth = matmul(gated_oth, w_out).astype(BF16)
+    swap_own = swap(part_oth)
+    part_own = matmul(after(gated_own, part_oth), w_out).astype(BF16)
+    swap_oth = swap(part_own)
+    cot_cols = arrange(after(own_cot, part_own), oth_cot, count)
+
+    def feed_in(tokens, part, other):
+        middle = tokens.astype(F32) + (part.astype(F32) + other.astype(F32))
+        normed = rms_scale(middle, norm_gains[1]).astype(BF16)
+        gate_val = matmul(normed, w_gate)
+        up_val = matmul(normed, w_up)
+        hidden_val, pull = jax.vjp(gelu_product, gate_val, up_val)
+        return middle, normed, hidden_val.astype(BF16), pull
+
+    def feed_back(cot, pull):
+        grad_gate, grad_up = pull(matmul_right(cot, w_down))
+        grad_gate, grad_up = grad_gate.astype(BF16), grad_up.astype(BF16)
+        back = (matmul_right(grad_gate, w_gate) + matmul_right(grad_up, w_up)).astype(BF16)
+        return grad_gate, grad_up, back
+
+    def norm_two_back(middle, back, other, cot):
+        grad, gain_rows = norm_back(middle, norm_gains[1], back.astype(F32) + other.astype(F32))
+        grad = cot.astype(F32) + grad
+        return grad, grad.astype(BF16), gain_rows
+
+    middle_own, normed_two_own, hidden_own, pull_own = feed_in(own_in, part_own, swap_own)
+    gg_own, gu_own, back_own = feed_back(own_cot, pull_own)
+    back_own_swapped = swap(back_own)
+    middle_oth, normed_two_oth, hidden_oth, pull_oth = feed_in(after(oth_in, back_own), part_oth, swap_oth)
+    hidden = jnp.concatenate([hidden_own, hidden_oth], axis=0)
+    down = weight_grad(cot_cols, hidden, bits)
+    gg_oth, gu_oth, back_oth = feed_back(after(oth_cot, down.keep), pull_oth)
+    back_oth_swapped = swap(back_oth)
+    normed_two_own_late = after(normed_two_own, back_oth, down.step())
+    normed_two_cols = arrange(normed_two_own_late, normed_two_oth, count)
+    gate = weight_grad(normed_two_cols, jnp.concatenate([gg_own, gg_oth], axis=0), bits)
+    keep_cols, send_cols = normed_two_cols
+    up = weight_grad((keep_cols, after(send_cols, gate.keep)), jnp.concatenate([gu_own, gu_oth], axis=0), bits)
+    hidden_late = after(hidden_oth, up.keep, gate.step())
+    out_send = matmul(hidden_late, w_down).astype(BF16)
+    out_swapped = swap(out_send)
+
+    grad_own, rec_own, gain_rows = norm_two_back(after(middle_own, out_send, up.step()), back_own, back_oth_swapped, own_cot)
+    gain_two = jnp.sum(gain_rows, axis=0)
+    _, rec_oth, _ = norm_two_back(middle_oth, back_oth, back_own_swapped, oth_cot)
+    up_own = matmul_right(rec_own, w_out)
+    up_oth = matmul_right(rec_oth, w_out)
+    gx_own, gx_oth, gy_own, gy_oth, gate_grad, sums = rec_bwd(
+        bx_own, bx_oth, by_own, by_oth, states, up_own, up_oth, mask, prm, gates, count
+    )
+
+    def rec_back(piece_x, piece_y):
+        return (matmul_right(piece_x, w_x) + matmul_right(piece_y, w_y)).astype(BF16)
+
+    rec_cols = arrange(after(rec_own, gx_oth, down.step()), rec_oth, count)
+    out = weight_grad(rec_cols, jnp.concatenate([gated_own, gated_oth], axis=0), bits)
+    half_gates = count // 2
+    blocks = Reduction(gate_grad[:half_gates], gate_grad[half_gates:], bits)
+    normed_cols = arrange(after(normed_own, out.keep), normed_oth, count)
+    keep_cols, send_cols = normed_cols
+    in_x = weight_grad(normed_cols, jnp.concatenate([gx_own, gx_oth], axis=0), bits)
+    in_y = weight_grad((keep_cols, after(send_cols, in_x.keep)), jnp.concatenate([gy_own, gy_oth], axis=0), bits)
+    rec_send = rec_back(after(gx_oth, in_y.keep, out.step(), gate.step()), gy_oth)
+    rec_swapped = swap(rec_send)
+    sums = sums.at[7].multiply(-8.0 * lax.dynamic_slice(jax.nn.sigmoid(a_param), (place * width,), (width,)))
+    wide = lax.dynamic_update_slice(jnp.zeros((8, full_width), F32), sums, (0, place * width))
+    rec_keep = rec_back(after(gx_own, rec_send, in_x.step(), in_y.step(), blocks.step()), gy_own)
+    out_keep = matmul(after(hidden_own, rec_keep, up.step()), w_down).astype(BF16)
+    layer_out = (middle_own + out_keep.astype(F32) + out_swapped.astype(F32)).astype(BF16)
+    grad_normed = rec_keep.astype(F32) + after(rec_swapped, out_keep).astype(F32)
+    grad_inputs, gain_rows = norm_back(own_in.astype(F32), norm_gains[0], grad_normed)
+    input_grad = grad_own + grad_inputs
+    gain_one = jnp.sum(gain_rows, axis=0)
+    packed = jnp.concatenate([wide.reshape(-1), gain_one, gain_two]).reshape(-1, 128)
+    packed = sum_everywhere(packed).reshape(-1)
+    for task in (down, blocks, out, gate, up, in_x, in_y) * 3:
+        if task.bits:
+            task.step()
+
+    small = packed[: 8 * full_width].reshape(8, full_width)
+    small = lax.dynamic_slice(small, (0, me * (full_width // count)), (8, full_width // count))
+    gains = packed[8 * full_width :].reshape(2, model)
+    gains = lax.dynamic_slice(gains, (0, me * (model // count)), (2, model // count))
+    mine = blocks.total()[0].astype(BF16)
+    others = swap(mine)
+    mine = jnp.concatenate([jnp.where(first_place, mine, others), jnp.where(first_place, others, mine)], axis=0)
+    mine = mine.astype(F32).reshape(2 * heads, 2, -1, mine.shape[-1])
+    return (
+        layer_out[None],
+        input_grad[None],
+        gains,
+        in_x.total(),
+        in_y.total(),
+        small[0:4],
+        small[4:7],
+        small[7],
+        jnp.swapaxes(mine, 0, 1),
+        out.total().T,
+        gate.total(),
+        up.total(),
+        down.total().T,
+    )
 
 
 def from_behind(value, axis, steps):
@@ -289,8 +828,16 @@
 
 
 def solution(mesh):
+    rows, cols = mesh.shape["dp"], mesh.shape["tp"]
+    by_channels = cols == 2 and rows >= 4 and rows & (rows - 1) == 0
+
+    def step(*args):
+        heads, model = args[9].shape[1], args[3].shape[1]
+        fits = by_channels and heads % cols == 0 and model % (128 * rows) == 0
+        return (local_channels if fits else local)(*args)
+
     return jax.shard_map(
-        local,
+        step,
         mesh=mesh,
         in_specs=(
             P("dp", "tp", None),

time: 2950 us -> 1060 us (0.36)
  local copies, waits for them, and re-layouts: 973 us -> 15.9 us
  waiting for transfers between devices: 1250 us -> 474 us
  other arithmetic: 314 us -> 105 us
  Pallas kernels: 0 us -> 110 us
  blocking collectives: 38.8 us -> 0 us
  starting transfers between devices: 14.7 us -> 48.7 us
    reduce_scatter x9 -> x0, waiting for transfers between devices: 671 us -> none  [the longest x1 136 us: local(): lax.psum_scatter(w_up_grad.astype(jnp.bfloat16), 'dp', scatter_dimension=...]
    ppermute x5 -> x43, waiting for transfers between devices: 2.76 us -> 474 us  [the longest x32 378 us: flip(): lax.ppermute(value, 'dp', [(source, source ^ bit) for source in range(cou...]
    slice x134 -> x7, local copies, waits for them, and re-layouts: 470 us -> 2.84 us  [the longest x1 0.81 us: feed_in(): normed = rms_scale(middle, norm_gains[1]).astype(BF16)]
    unnamed x27 -> x0, waiting for transfers between devices: 355 us -> none
    pad x64 -> x1, local copies, waits for them, and re-layouts: 284 us -> 0.04 us  [local_channels(): mask = jnp.pad(jnp.stack(valid, axis=1), ((0, 8), (0, 4)))]
    all_gather x5 -> x0, waiting for transfers between devices: 203 us -> none  [the longest x1 124 us: local(): lax.all_gather(w_x, 'tp', axis=1, tiled=True)]
    add x55 -> x9, other arithmetic: 125 us -> 7.32 us  [the longest x4 7.25 us: total(): return self.keep.astype(F32) + self.received.astype(F32)]
    pallas_call x0 -> x6, Pallas kernels: none -> 110 us  [the longest x1 57.2 us: rec_bwd(): pl.pallas_call(functools.partial(rec_bwd_kernel, count, stage_bits(count)...]
  transfers between devices with their start and end apart: 26 -> 43, of which waited for: 17 -> 24; matrix products, arithmetic and copies ran while one was open for 34% -> 32% of each run, Pallas kernels for 0% -> 8%
where the time goes in v1:
time: 1060 us; the launch traced here: 1050 us
  waiting for transfers between devices  474 us (45%)
  matrix products  299 us (28%)
  Pallas kernels  110 us (10%)
  other arithmetic  105 us (10%)
  starting transfers between devices  48.7 us (5%)
  local copies, waits for them, and re-layouts  15.9 us (2%)
    ppermute x32, waiting for transfers between devices, flip(): lax.ppermute(value, 'dp', [(source, source ^ bit) for source in range(cou...  378 us
    dot_general x12, matrix products, matmul_right(): lax.dot_general(first_mat, second_mat, (((1,), (1,)), ((), ())), preferre...  114 us
    ppermute x11, waiting for transfers between devices, swap(): return lax.ppermute(value, 'tp', [(0, 1), (1, 0)])  95.9 us
    dot_general x12, matrix products, matmul(): return jnp.dot(first_mat, second_mat, preferred_element_type=jnp.float32)  94.4 us
    dot_general x12, matrix products, matmul_left(): lax.dot_general(first_mat, second_mat, (((0,), (0,)), ((), ())), preferre...  90.2 us
    pallas_call x1, Pallas kernels, rec_bwd(): pl.pallas_call(functools.partial(rec_bwd_kernel, count, stage_bits(count)...  57.2 us
    convert_element_type x14, other arithmetic, step(): (keep[:middle].astype(F32) + received[:middle].astype(F32)).astype(BF16)  46.3 us
    ppermute x32, starting transfers between devices, flip(): lax.ppermute(value, 'dp', [(source, source ^ bit) for source in range(cou...  34.5 us
  transfers between devices with their start and end apart: 43, of which 24 were waited for; matrix products, arithmetic and copies ran while one was open for 32% of the time, Pallas kernels for 8%

profile of v1, /device:TPU:0, one launch (start us, length us, event | category | flops | bytes accessed | tf_op | source)
XLA Modules:
  0.0 1054.2 jit_solution(3885738288327259273)
XLA Ops:
  10.0 39.6 %collective-permute-done.1 = s32[512]{0:T(512)S(1)} collective-permute-done((s32[512]{0:T(512)}, s32[512]{0:T(512)S(1)}, u32[]{:S(2)}, u32[]{:S(2)}) %collective-permute-start.1) | collective-permute-done | bytes 2080 | tf_op jit(solution)/shard_map/ppermute | solution.py:354
  67.7 30.7 %rec_fwd.1 = (bf16[512,1280]{1,0:T(8,128)(2,1)S(1)}, bf16[512,1280]{1,0:T(8,128)(2,1)S(1)}, f32[1024,1280]{1,0:T(8,128)}) custom-call(bf16[512,1280]{1,0:T(8,128)(2,1)S(1)} %convolution_convert_fusion.17.bx_own, bf16[512,1280]{1,0:T(8,128)(2,1)S(1)} %convolution_convert_fusion.16.bx_oth, f32[512,1280]{1,0:T(8,128)S(1)} %fusion.57.by_own, ...), custom_call_target="tpu_custom_call" | custom-call | flops 1473249280 | bytes 20971520 | tf_op jit(solution)/shard_map/rec_fwd/pallas_call | solution.py:243
  103.7 11.5 %fusion.50 = f32[512,3072]{1,0:T(8,128)} fusion(bf16[3072,2048]{1,0:T(8,128)(2,1)} %param.29, bf16[1,512,2048]{2,1,0:T(8,128)(2,1)S(1)} %copy-done.27), kind=kOutput, calls=%fused_computation.194 | convolution fusion | flops 6442450944 | bytes 20971520 | tf_op jit(solution)/shard_map/dot_general | solution.py:582
  115.2 35.0 %collective-permute-done.2 = bf16[512,2048]{1,0:T(8,128)(2,1)S(1)} collective-permute-done((bf16[512,2048]{1,0:T(8,128)(2,1)S(1)}, bf16[512,2048]{1,0:T(8,128)(2,1)S(1)}, u32[]{:S(2)}, u32[]{:S(2)}) %collective-permute-start.2) | collective-permute-done | bytes 2097184 | tf_op jit(solution)/shard_map/ppermute | solution.py:354
  157.4 12.2 %fusion.59 = f32[512,3072]{1,0:T(8,128)} fusion(bf16[512,2048]{1,0:T(8,128)(2,1)S(1)} %multiply_convert_fusion.5.first, bf16[2048,3072]{1,0:T(8,128)(2,1)} %param.27), kind=kOutput, calls=%fused_computation.201 | convolution fusion | flops 6442450944 | bytes 20971520 | tf_op jit(solution)/shard_map/dot_general | solution.py:572
  169.6 19.5 %multiply_convert_fusion.3 = (bf16[512,3072]{1,0:T(8,128)(2,1)}, bf16[512,3072]{1,0:T(8,128)(2,1)S(1)}, bf16[512,3072]{1,0:T(8,128)(2,1)}) fusion(f32[512,3072]{1,0:T(8,128)} %fusion.59, f32[512,3072]{1,0:T(8,128)} %fusion.50, bf16[512,2048]{1,0:T(8,128)(2,1)S(1)} %multiply_convert_fusion.5.first, bf16[2048,3072]{1,0:T(8,128)(2,1)} %param.28), kind=kOutput, calls=%fused_computation.36 | convolution fusion | flops 6483345408 | bytes 36700160 | tf_op jit(solution)/shard_map/dot_general | solution.py:572
  189.1 12.2 %fusion.60 = f32[512,2048]{1,0:T(8,128)} fusion(bf16[512,3072]{1,0:T(8,128)(2,1)S(1)} %get-tuple-element.159, bf16[2048,3072]{1,0:T(8,128)(2,1)} %param.27), kind=kOutput, calls=%fused_computation.202 | convolution fusion | flops 6442450944 | bytes 19922944 | tf_op jit(solution)/shard_map/dot_general | solution.py:582
  201.3 13.6 %add_convert_fusion.11 = bf16[512,2048]{1,0:T(8,128)(2,1)} fusion(f32[512,2048]{1,0:T(8,128)} %fusion.60, bf16[512,3072]{1,0:T(8,128)(2,1)} %get-tuple-element.160, bf16[2048,3072]{1,0:T(8,128)(2,1)} %param.28), kind=kOutput, calls=%fused_computation.75 | convolution fusion | flops 6444548096 | bytes 22020096 | tf_op jit(solution)/shard_map/dot_general | solution.py:582
  214.9 5.6 arrange.4
  220.6 17.9 %collective-permute-done.3 = bf16[512,2048]{1,0:T(8,128)(2,1)} collective-permute-done((bf16[512,2048]{1,0:T(8,128)(2,1)}, bf16[512,2048]{1,0:T(8,128)(2,1)}, u32[]{:S(2)}, u32[]{:S(2)}) %collective-permute-start.3) | collective-permute-done | bytes 2097184 | tf_op jit(solution)/shard_map/ppermute | solution.py:354
  245.7 12.3 %fusion.61 = f32[512,3072]{1,0:T(8,128)} fusion(bf16[512,2048]{1,0:T(8,128)(2,1)S(1)} %multiply_convert_fusion.4.second, bf16[2048,3072]{1,0:T(8,128)(2,1)} %param.27), kind=kOutput, calls=%fused_computation.203 | convolution fusion | flops 6442450944 | bytes 20971520 | tf_op jit(solution)/shard_map/dot_general | solution.py:572
  258.0 11.4 %multiply_convert_fusion.1 = (bf16[512,3072]{1,0:T(8,128)(2,1)}, f32[512,3072]{1,0:T(8,128)}) fusion(f32[512,3072]{1,0:T(8,128)} %fusion.61, bf16[512,2048]{1,0:T(8,128)(2,1)S(1)} %multiply_convert_fusion.4.second, bf16[2048,3072]{1,0:T(8,128)(2,1)S(1)} %bitcast.133), kind=kOutput, calls=%fused_computation.34 | convolution fusion | flops 6458179584 | bytes 30408704 | tf_op jit(solution)/shard_map/dot_general | solution.py:572
  269.5 11.7 %convolution_convert_fusion.5 = bf16[1024,3072]{1,0:T(8,128)(2,1)} fusion(bf16[1024,1024]{1,0:T(8,128)(2,1)S(1)} %copy-done.73, bf16[512,3072]{1,0:T(8,128)(2,1)} %get-tuple-element.79, bf16[512,3072]{1,0:T(8,128)(2,1)} %get-tuple-element.98), kind=kOutput, calls=%fused_computation.44 | convolution fusion | flops 6458179584 | bytes 14680064 | tf_op jit(solution)/shard_map/dot_general | solution.py:576
  281.2 9.0 convolution_convert_fusion.4
  290.2 18.1 %multiply_convert_fusion = (bf16[512,3072]{1,0:T(8,128)(2,1)S(1)}, bf16[512,3072]{1,0:T(8,128)(2,1)}) fusion(f32[512,3072]{1,0:T(8,128)} %fusion.61, f32[512,3072]{1,0:T(8,128)} %get-tuple-element.195, bf16[512,2048]{1,0:T(8,128)(2,1)} %collective-permute-done.4.second, bf16[3072,2048]{1,0:T(8,128)(2,1)} %param.29), kind=kOutput, calls=%fused_computation.33 | convolution fusion | flops 6480199680 | bytes 33554432 | tf_op jit(solution)/shard_map/dot_general | solution.py:582
  308.3 13.2 %fusion.62 = f32[512,2048]{1,0:T(8,128)} fusion(bf16[512,3072]{1,0:T(8,128)(2,1)} %get-tuple-element.157, bf16[2048,3072]{1,0:T(8,128)(2,1)} %param.27), kind=kOutput, calls=%fused_computation.204 | convolution fusion | flops 6442450944 | bytes 19922944 | tf_op jit(solution)/shard_map/dot_general | solution.py:582
  321.5 13.5 %add_convert_fusion.10 = bf16[512,2048]{1,0:T(8,128)(2,1)} fusion(f32[512,2048]{1,0:T(8,128)} %fusion.62, bf16[512,3072]{1,0:T(8,128)(2,1)S(1)} %get-tuple-element.156, bf16[2048,3072]{1,0:T(8,128)(2,1)} %param.28), kind=kOutput, calls=%fused_computation.71 | convolution fusion | flops 6444548096 | bytes 22020096 | tf_op jit(solution)/shard_map/dot_general | solution.py:582
  335.0 7.5 add_convert_fusion.2
  344.0 5.4 arrange.5
  349.4 11.9 %convolution_convert_fusion.3 = bf16[1024,3072]{1,0:T(8,128)(2,1)} fusion(bf16[1024,1024]{1,0:T(8,128)(2,1)} %get-tuple-element.77, bf16[512,3072]{1,0:T(8,128)(2,1)} %get-tuple-element.157, bf16[512,3072]{1,0:T(8,128)(2,1)} %copy-done.82), kind=kOutput, calls=%fused_computation.42 | convolution fusion | flops 6458179584 | bytes 14680064 | tf_op jit(solution)/shard_map/dot_general | solution.py:576
  361.6 8.8 convolution_convert_fusion.2
  370.4 8.9 convolution_convert_fusion.1
  379.5 33.8 %collective-permute-done.10 = bf16[512,3072]{1,0:T(8,128)(2,1)} collective-permute-done((bf16[512,3072]{1,0:T(8,128)(2,1)}, bf16[512,3072]{1,0:T(8,128)(2,1)}, u32[]{:S(2)}, u32[]{:S(2)}) %collective-permute-start.10) | collective-permute-done | bytes 3145760 | tf_op jit(solution)/shard_map/ppermute | solution.py:359
  423.0 66.0 %collective-permute-done.41 = bf16[256,3072]{1,0:T(8,128)(2,1)} collective-permute-done((bf16[256,3072]{1,0:T(8,128)(2,1)}, bf16[256,3072]{1,0:T(8,128)(2,1)}, u32[]{:S(2)}, u32[]{:S(2)}) %collective-permute-start.41) | collective-permute-done | bytes 1572896 | tf_op jit(solution)/shard_map/ppermute | solution.py:359
  491.0 11.5 %convolution_convert_fusion = bf16[1024,3072]{1,0:T(8,128)(2,1)} fusion(bf16[1024,1024]{1,0:T(8,128)(2,1)S(1)} %copy-done.69, bf16[512,3072]{1,0:T(8,128)(2,1)} %copy-done.80, bf16[512,3072]{1,0:T(8,128)(2,1)} %get-tuple-element.160), kind=kOutput, calls=%fused_computation.39 | convolution fusion | flops 6458179584 | bytes 14680064 | tf_op jit(solution)/shard_map/dot_general | solution.py:576
  502.5 6.4 collective-permute-done.42
  512.0 7.7 add_convert_fusion.1
  521.1 8.3 add_convert_fusion
  529.4 8.1 convolution_convert_fusion.13
  539.1 6.3 multiply_reduce_fusion
  545.5 9.2 add_convert_fusion.9
  563.6 57.2 %rec_bwd.1 = (bf16[512,1280]{1,0:T(8,128)(2,1)S(1)}, bf16[512,1280]{1,0:T(8,128)(2,1)S(1)}, bf16[512,1280]{1,0:T(8,128)(2,1)S(1)}, bf16[512,1280]{1,0:T(8,128)(2...) custom-call(bf16[512,1280]{1,0:T(8,128)(2,1)} %copy-done.7, bf16[512,1280]{1,0:T(8,128)(2,1)} %copy-done.8, ...), custom_call_target="tpu_custom_call" | custom-call | flops 4354211840 | bytes 31457280 | tf_op jit(solution)/shard_map/rec_bwd/pallas_call | solution.py:268
  628.4 7.0 convolution_convert_fusion.11
  639.7 5.5 arrange.7
  714.6 7.3 add_convert_fusion.8
  726.4 6.4 add_convert_fusion.7
  732.8 29.7 %collective-permute-done.16 = bf16[512,3072]{1,0:T(8,128)(2,1)S(1)} collective-permute-done((bf16[512,3072]{1,0:T(8,128)(2,1)}, bf16[512,3072]{1,0:T(8,128)(2,1)S(1)}, u32[]{:S(2)}, u32[]{:S(2)}) %collective-permute-start.16) | collective-permute-done | bytes 3145760 | tf_op jit(solution)/shard_map/ppermute | solution.py:359
  764.2 11.4 %convolution_convert_fusion.12 = bf16[512,2048]{1,0:T(8,128)(2,1)S(1)} fusion(bf16[512,3072]{1,0:T(8,128)(2,1)} %get-tuple-element.98, bf16[3072,2048]{1,0:T(8,128)(2,1)} %param.29), kind=kOutput, calls=%fused_computation.92 | convolution fusion | flops 6443499520 | bytes 17825792 | tf_op jit(solution)/shard_map/dot_general | solution.py:572
  780.0 10.7 %collective-permute-done.24 = bf16[512,1280]{1,0:T(8,128)(2,1)} collective-permute-done((bf16[512,1280]{1,0:T(8,128)(2,1)}, bf16[512,1280]{1,0:T(8,128)(2,1)}, u32[]{:S(2)}, u32[]{:S(2)}) %collective-permute-start.24) | collective-permute-done | bytes 1310752 | tf_op jit(solution)/shard_map/ppermute | solution.py:359
  794.1 24.5 %collective-permute-done.27 = bf16[512,1280]{1,0:T(8,128)(2,1)S(1)} collective-permute-done((bf16[512,1280]{1,0:T(8,128)(2,1)}, bf16[512,1280]{1,0:T(8,128)(2,1)S(1)}, u32[]{:S(2)}, u32[]{:S(2)}) %collective-permute-start.27) | collective-permute-done | bytes 1310752 | tf_op jit(solution)/shard_map/ppermute | solution.py:359
  820.8 21.0 %collective-permute-done.34 = bf16[512,1280]{1,0:T(8,128)(2,1)S(1)} collective-permute-done((bf16[512,1280]{1,0:T(8,128)(2,1)}, bf16[512,1280]{1,0:T(8,128)(2,1)S(1)}, u32[]{:S(2)}, u32[]{:S(2)}) %collective-permute-start.34) | collective-permute-done | bytes 1310752 | tf_op jit(solution)/shard_map/ppermute | solution.py:359
  845.9 103.5 %collective-permute-done.25 = bf16[256,1280]{1,0:T(8,128)(2,1)S(1)} collective-permute-done((bf16[256,1280]{1,0:T(8,128)(2,1)S(1)}, bf16[256,1280]{1,0:T(8,128)(2,1)S(1)}, u32[]{:S(2)}, u32[]{:S(2)}) %collective-permute-start.25) | collective-permute-done | bytes 655392 | tf_op jit(solution)/shard_map/ppermute | solution.py:359
  949.5 28.0 %collective-permute-done.28 = bf16[256,1280]{1,0:T(8,128)(2,1)S(1)} collective-permute-done((bf16[256,1280]{1,0:T(8,128)(2,1)S(1)}, bf16[256,1280]{1,0:T(8,128)(2,1)S(1)}, u32[]{:S(2)}, u32[]{:S(2)}) %collective-permute-start.28) | collective-permute-done | bytes 655392 | tf_op jit(solution)/shard_map/ppermute | solution.py:359
  978.3 13.2 %collective-permute-done.35 = bf16[256,1280]{1,0:T(8,128)(2,1)S(1)} collective-permute-done((bf16[256,1280]{1,0:T(8,128)(2,1)S(1)}, bf16[256,1280]{1,0:T(8,128)(2,1)S(1)}, u32[]{:S(2)}, u32[]{:S(2)}) %collective-permute-start.35) | collective-permute-done | bytes 655392 | tf_op jit(solution)/shard_map/ppermute | solution.py:359
  999.5 6.1 collective-permute-done.29
  1016.7 8.0 fusion.23
  1025.5 6.1 collective-permute-done.38
  1034.4 7.3 collective-permute-done.22
  (380 shorter events, 212.0 us)
Async XLA Ops:
  0.7 49.5 %collective-permute-start = (bf16[512,2048]{1,0:T(8,128)(2,1)}, bf16[512,2048]{1,0:T(8,128)(2,1)}, u32[]{:S(2)}, u32[]{:S(2)}) collective-permute-start(bf16[512,2048]{1,0:T(8,128)(2,1)} %bitcast.111), channel_id=1, source_target_pairs={{0,1},{1,0},{2,3},{3,2},{4,5},{5,4},{6,7},{7,6},{8,9},{9,8},{10,11... | collective-permute-start | bytes 6291464 | tf_op jit(solution)/shard_map/ppermute | solution.py:354
  3.7 46.0 %collective-permute-start.1 = (s32[512]{0:T(512)}, s32[512]{0:T(512)S(1)}, u32[]{:S(2)}, u32[]{:S(2)}) collective-permute-start(s32[512]{0:T(512)} %bitcast.129), channel_id=1, source_target_pairs={{0,1},{1,0},{2,3},{3,2},{4,5},{5,4},{6,7},{7,6},{8,9},{9,8},{10,11... | collective-permute-start | bytes 6152 | tf_op jit(solution)/shard_map/ppermute | solution.py:354
  8.9 232.9 %copy-start.54 = (f32[1,2048]{1,0:T(1,128)}, f32[1,2048]{1,0:T(1,128)S(1)}, u32[]{:S(2)}) copy-start(f32[1,2048]{1,0:T(1,128)S(1)} %get-tuple-element.185) | copy-start | bytes 24580
  101.6 48.6 %collective-permute-start.2 = (bf16[512,2048]{1,0:T(8,128)(2,1)S(1)}, bf16[512,2048]{1,0:T(8,128)(2,1)S(1)}, u32[]{:S(2)}, u32[]{:S(2)}) collective-permute-start(bf16[512,2048]{1,0:T(8,128)(2,1)S(1)} %convolution_convert_fusion.15), channel_id=1, source_target_pairs={{0,1},{1,0},{2,3},{3,2},{4,5},{5,4},{6,7},{7,6},{8,9},{9,8},{10,11... | collective-permute-start | bytes 6291464 | tf_op jit(solution)/shard_map/ppermute | solution.py:354
  103.4 111.5 %collective-permute-start.4 = (bf16[512,2048]{1,0:T(8,128)(2,1)S(1)}, bf16[512,2048]{1,0:T(8,128)(2,1)}, u32[]{:S(2)}, u32[]{:S(2)}) collective-permute-start(bf16[512,2048]{1,0:T(8,128)(2,1)S(1)} %bitcast.113), channel_id=1, source_target_pairs={{0,1},{1,0},{2,3},{3,2},{4,5},{5,4},{6,7},{7,6},{8,9},{9,8},{10,11... | collective-permute-start | bytes 6291464 | tf_op jit(solution)/shard_map/ppermute | solution.py:354
  154.9 83.5 %collective-permute-start.3 = (bf16[512,2048]{1,0:T(8,128)(2,1)}, bf16[512,2048]{1,0:T(8,128)(2,1)}, u32[]{:S(2)}, u32[]{:S(2)}) collective-permute-start(bf16[512,2048]{1,0:T(8,128)(2,1)} %get-tuple-element.193), channel_id=1, source_target_pairs={{0,1},{1,0},{2,3},{3,2},{4,5},{5,4},{6,7},{7,6},{8,9},{9,8},{10,11... | collective-permute-start | bytes 6291464 | tf_op jit(solution)/shard_map/ppermute | solution.py:354
  281.2 53.9 %collective-permute-start.5 = (bf16[1024,3072]{1,0:T(8,128)(2,1)}, bf16[1024,3072]{1,0:T(8,128)(2,1)}, u32[]{:S(2)}, u32[]{:S(2)}) collective-permute-start(bf16[1024,3072]{1,0:T(8,128)(2,1)} %convolution_convert_fusion.5), channel_id=1, source_target_pairs={{0,2},{2,0},{4,6},{6,4},{8,10},{10,8},{12,14},{14,12},{16,18},{18,... | collective-permute-start | bytes 18874376 | tf_op jit(solution)/shard_map/ppermute | solution.py:359
  342.5 70.8 %collective-permute-start.10 = (bf16[512,3072]{1,0:T(8,128)(2,1)}, bf16[512,3072]{1,0:T(8,128)(2,1)}, u32[]{:S(2)}, u32[]{:S(2)}) collective-permute-start(bf16[512,3072]{1,0:T(8,128)(2,1)} %get-tuple-element.155), channel_id=1, source_target_pairs={{0,4},{2,6},{4,0},{6,2},{8,12},{10,14},{12,8},{14,10},{16,20},{18,... | collective-permute-start | bytes 9437192 | tf_op jit(solution)/shard_map/ppermute | solution.py:359
  361.3 150.7 %collective-permute-start.6 = (bf16[1024,3072]{1,0:T(8,128)(2,1)}, bf16[1024,3072]{1,0:T(8,128)(2,1)}, u32[]{:S(2)}, u32[]{:S(2)}) collective-permute-start(bf16[1024,3072]{1,0:T(8,128)(2,1)} %convolution_convert_fusion.3), channel_id=1, source_target_pairs={{0,2},{2,0},{4,6},{6,4},{8,10},{10,8},{12,14},{14,12},{16,18},{18,... | collective-permute-start | bytes 18874376 | tf_op jit(solution)/shard_map/ppermute | solution.py:359
  379.2 141.9 %collective-permute-start.7 = (bf16[1024,3072]{1,0:T(8,128)(2,1)}, bf16[1024,3072]{1,0:T(8,128)(2,1)}, u32[]{:S(2)}, u32[]{:S(2)}) collective-permute-start(bf16[1024,3072]{1,0:T(8,128)(2,1)} %convolution_convert_fusion.1), channel_id=1, source_target_pairs={{0,2},{2,0},{4,6},{6,4},{8,10},{10,8},{12,14},{14,12},{16,18},{18,... | collective-permute-start | bytes 18874376 | tf_op jit(solution)/shard_map/ppermute | solution.py:359
  418.1 70.9 %collective-permute-start.41 = (bf16[256,3072]{1,0:T(8,128)(2,1)}, bf16[256,3072]{1,0:T(8,128)(2,1)}, u32[]{:S(2)}, u32[]{:S(2)}) collective-permute-start(bf16[256,3072]{1,0:T(8,128)(2,1)} %get-tuple-element.162), channel_id=1, source_target_pairs={{0,16},{2,18},{4,20},{6,22},{8,24},{10,26},{12,28},{14,30},{16,0},... | collective-permute-start | bytes 4718600 | tf_op jit(solution)/shard_map/ppermute | solution.py:359
  420.9 81.6 %copy-start.52 = (bf16[1024,1280]{1,0:T(8,128)(2,1)}, bf16[1024,1280]{1,0:T(8,128)(2,1)S(1)}, u32[]{:S(2)}) copy-start(bf16[1024,1280]{1,0:T(8,128)(2,1)S(1)} %constant_dynamic-update-slice_fusion) | copy-start | bytes 7864324
  420.9 117.0 %collective-permute-start.9 = (bf16[512,2048]{1,0:T(8,128)(2,1)}, bf16[512,2048]{1,0:T(8,128)(2,1)}, u32[]{:S(2)}, u32[]{:S(2)}) collective-permute-start(bf16[512,2048]{1,0:T(8,128)(2,1)} %add_convert_fusion.11), channel_id=1, source_target_pairs={{0,1},{1,0},{2,3},{3,2},{4,5},{5,4},{6,7},{7,6},{8,9},{9,8},{10,11... | collective-permute-start | bytes 6291464 | tf_op jit(solution)/shard_map/ppermute | solution.py:354
  422.5 115.4 %collective-permute-start.8 = (bf16[512,2048]{1,0:T(8,128)(2,1)}, bf16[512,2048]{1,0:T(8,128)(2,1)}, u32[]{:S(2)}, u32[]{:S(2)}) collective-permute-start(bf16[512,2048]{1,0:T(8,128)(2,1)} %add_convert_fusion.10), channel_id=1, source_target_pairs={{0,1},{1,0},{2,3},{3,2},{4,5},{5,4},{6,7},{7,6},{8,9},{9,8},{10,11... | collective-permute-start | bytes 6291464 | tf_op jit(solution)/shard_map/ppermute | solution.py:354
  490.4 18.6 %collective-permute-start.42 = (bf16[128,3072]{1,0:T(8,128)(2,1)S(1)}, bf16[128,3072]{1,0:T(8,128)(2,1)S(1)}, u32[]{:S(2)}, u32[]{:S(2)}) collective-permute-start(bf16[128,3072]{1,0:T(8,128)(2,1)S(1)} %add_convert_fusion.24), channel_id=1, source_target_pairs={{0,8},{2,10},{4,12},{6,14},{8,0},{10,2},{12,4},{14,6},{16,24},{18,... | collective-permute-start | bytes 2359304 | tf_op jit(solution)/shard_map/ppermute | solution.py:359
  519.7 186.1 %collective-permute-start.12 = (bf16[512,3072]{1,0:T(8,128)(2,1)}, bf16[512,3072]{1,0:T(8,128)(2,1)}, u32[]{:S(2)}, u32[]{:S(2)}) collective-permute-start(bf16[512,3072]{1,0:T(8,128)(2,1)} %get-tuple-element.153), channel_id=1, source_target_pairs={{0,4},{2,6},{4,0},{6,2},{8,12},{10,14},{12,8},{14,10},{16,20},{18,... | collective-permute-start | bytes 9437192 | tf_op jit(solution)/shard_map/ppermute | solution.py:359
  635.4 65.6 %collective-permute-start.11 = (bf16[1024,1280]{1,0:T(8,128)(2,1)}, bf16[1024,1280]{1,0:T(8,128)(2,1)}, u32[]{:S(2)}, u32[]{:S(2)}) collective-permute-start(bf16[1024,1280]{1,0:T(8,128)(2,1)} %convolution_convert_fusion.11), channel_id=1, source_target_pairs={{0,2},{2,0},{4,6},{6,4},{8,10},{10,8},{12,14},{14,12},{16,18},{18,... | collective-permute-start | bytes 7864328 | tf_op jit(solution)/shard_map/ppermute | solution.py:359
  651.6 39.6 %collective-permute-start.13 = (bf16[1024,1280]{1,0:T(8,128)(2,1)}, bf16[1024,1280]{1,0:T(8,128)(2,1)}, u32[]{:S(2)}, u32[]{:S(2)}) collective-permute-start(bf16[1024,1280]{1,0:T(8,128)(2,1)} %convolution_convert_fusion.9), channel_id=1, source_target_pairs={{0,2},{2,0},{4,6},{6,4},{8,10},{10,8},{12,14},{14,12},{16,18},{18,... | collective-permute-start | bytes 7864328 | tf_op jit(solution)/shard_map/ppermute | solution.py:359
  652.1 5.8 collective-permute-start.15
  658.2 10.2 collective-permute-start.30
  663.5 33.3 %collective-permute-start.14 = (bf16[1024,1280]{1,0:T(8,128)(2,1)}, bf16[1024,1280]{1,0:T(8,128)(2,1)}, u32[]{:S(2)}, u32[]{:S(2)}) collective-permute-start(bf16[1024,1280]{1,0:T(8,128)(2,1)} %convolution_convert_fusion.7), channel_id=1, source_target_pairs={{0,2},{2,0},{4,6},{6,4},{8,10},{10,8},{12,14},{14,12},{16,18},{18,... | collective-permute-start | bytes 7864328 | tf_op jit(solution)/shard_map/ppermute | solution.py:359
  668.4 11.0 %collective-permute-start.31 = (bf16[2,5,32,256]{3,2,1,0:T(8,128)(2,1)S(1)}, bf16[2,5,32,256]{3,2,1,0:T(8,128)(2,1)S(1)}, u32[]{:S(2)}, u32[]{:S(2)}) collective-permute-start(bf16[2,5,32,256]{3,2,1,0:T(8,128)(2,1)S(1)} %get-tuple-element.182), channel_id=1, source_target_pairs={{0,16},{2,18},{4,20},{6,22},{8,24},{10,26},{12,28},{14,30},{16,0},... | collective-permute-start | bytes 491528 | tf_op jit(solution)/shard_map/ppermute | solution.py:359
  679.5 4.5 collective-permute-start.32
  684.0 5.0 collective-permute-start.33
  689.0 86.7 %collective-permute-start.17 = (bf16[512,2048]{1,0:T(8,128)(2,1)}, bf16[512,2048]{1,0:T(8,128)(2,1)S(1)}, u32[]{:S(2)}, u32[]{:S(2)}) collective-permute-start(bf16[512,2048]{1,0:T(8,128)(2,1)} %convolution_convert_fusion.13), channel_id=1, source_target_pairs={{0,1},{1,0},{2,3},{3,2},{4,5},{5,4},{6,7},{7,6},{8,9},{9,8},{10,11... | collective-permute-start | bytes 6291464 | tf_op jit(solution)/shard_map/ppermute | solution.py:354
  691.2 71.2 %collective-permute-start.16 = (bf16[512,3072]{1,0:T(8,128)(2,1)}, bf16[512,3072]{1,0:T(8,128)(2,1)S(1)}, u32[]{:S(2)}, u32[]{:S(2)}) collective-permute-start(bf16[512,3072]{1,0:T(8,128)(2,1)} %get-tuple-element.151), channel_id=1, source_target_pairs={{0,4},{2,6},{4,0},{6,2},{8,12},{10,14},{12,8},{14,10},{16,20},{18,... | collective-permute-start | bytes 9437192 | tf_op jit(solution)/shard_map/ppermute | solution.py:359
  696.8 93.9 %collective-permute-start.24 = (bf16[512,1280]{1,0:T(8,128)(2,1)}, bf16[512,1280]{1,0:T(8,128)(2,1)}, u32[]{:S(2)}, u32[]{:S(2)}) collective-permute-start(bf16[512,1280]{1,0:T(8,128)(2,1)} %get-tuple-element.172), channel_id=1, source_target_pairs={{0,4},{2,6},{4,0},{6,2},{8,12},{10,14},{12,8},{14,10},{16,20},{18,... | collective-permute-start | bytes 3932168 | tf_op jit(solution)/shard_map/ppermute | solution.py:359
  701.0 117.7 %collective-permute-start.27 = (bf16[512,1280]{1,0:T(8,128)(2,1)}, bf16[512,1280]{1,0:T(8,128)(2,1)S(1)}, u32[]{:S(2)}, u32[]{:S(2)}) collective-permute-start(bf16[512,1280]{1,0:T(8,128)(2,1)} %get-tuple-element.170), channel_id=1, source_target_pairs={{0,4},{2,6},{4,0},{6,2},{8,12},{10,14},{12,8},{14,10},{16,20},{18,... | collective-permute-start | bytes 3932168 | tf_op jit(solution)/shard_map/ppermute | solution.py:359
  705.8 136.0 %collective-permute-start.34 = (bf16[512,1280]{1,0:T(8,128)(2,1)}, bf16[512,1280]{1,0:T(8,128)(2,1)S(1)}, u32[]{:S(2)}, u32[]{:S(2)}) collective-permute-start(bf16[512,1280]{1,0:T(8,128)(2,1)} %get-tuple-element.168), channel_id=1, source_target_pairs={{0,4},{2,6},{4,0},{6,2},{8,12},{10,14},{12,8},{14,10},{16,20},{18,... | collective-permute-start | bytes 3932168 | tf_op jit(solution)/shard_map/ppermute | solution.py:359
  709.8 283.9 %copy-start.40 = (bf16[256,3072]{1,0:T(8,128)(2,1)}, bf16[256,3072]{1,0:T(8,128)(2,1)S(1)}, u32[]{:S(2)}) copy-start(bf16[256,3072]{1,0:T(8,128)(2,1)S(1)} %get-tuple-element.165) | copy-start | bytes 4718596
  732.8 273.7 %copy-start.38 = (bf16[512,2048]{1,0:T(8,128)(2,1)}, bf16[512,2048]{1,0:T(8,128)(2,1)S(1)}, u32[]{:S(2)}) copy-start(bf16[512,2048]{1,0:T(8,128)(2,1)S(1)} %add_convert_fusion.7) | copy-start | bytes 6291460
  762.5 244.0 %collective-permute-start.18 = (bf16[512,2048]{1,0:T(8,128)(2,1)}, bf16[512,2048]{1,0:T(8,128)(2,1)S(1)}, u32[]{:S(2)}, u32[]{:S(2)}) collective-permute-start(bf16[512,2048]{1,0:T(8,128)(2,1)} %add_convert_fusion.8), channel_id=1, source_target_pairs={{0,1},{1,0},{2,3},{3,2},{4,5},{5,4},{6,7},{7,6},{8,9},{9,8},{10,11... | collective-permute-start | bytes 6291464 | tf_op jit(solution)/shard_map/ppermute | solution.py:354
  764.2 231.0 %copy-start.42 = (bf16[256,3072]{1,0:T(8,128)(2,1)}, bf16[256,3072]{1,0:T(8,128)(2,1)S(1)}, u32[]{:S(2)}) copy-start(bf16[256,3072]{1,0:T(8,128)(2,1)S(1)} %get-tuple-element.163) | copy-start | bytes 4718596
  775.7 215.9 %collective-permute-start.37 = (bf16[256,3072]{1,0:T(8,128)(2,1)S(1)}, bf16[256,3072]{1,0:T(8,128)(2,1)S(1)}, u32[]{:S(2)}, u32[]{:S(2)}) collective-permute-start(bf16[256,3072]{1,0:T(8,128)(2,1)S(1)} %get-tuple-element.166), channel_id=1, source_target_pairs={{0,16},{2,18},{4,20},{6,22},{8,24},{10,26},{12,28},{14,30},{16,0},... | collective-permute-start | bytes 4718600 | tf_op jit(solution)/shard_map/ppermute | solution.py:359
  790.7 204.1 %collective-permute-start.39 = (bf16[256,3072]{1,0:T(8,128)(2,1)S(1)}, bf16[256,3072]{1,0:T(8,128)(2,1)S(1)}, u32[]{:S(2)}, u32[]{:S(2)}) collective-permute-start(bf16[256,3072]{1,0:T(8,128)(2,1)S(1)} %get-tuple-element.164), channel_id=1, source_target_pairs={{0,16},{2,18},{4,20},{6,22},{8,24},{10,26},{12,28},{14,30},{16,0},... | collective-permute-start | bytes 4718600 | tf_op jit(solution)/shard_map/ppermute | solution.py:359
  818.7 130.7 %collective-permute-start.25 = (bf16[256,1280]{1,0:T(8,128)(2,1)S(1)}, bf16[256,1280]{1,0:T(8,128)(2,1)S(1)}, u32[]{:S(2)}, u32[]{:S(2)}) collective-permute-start(bf16[256,1280]{1,0:T(8,128)(2,1)S(1)} %get-tuple-element.178), channel_id=1, source_target_pairs={{0,16},{2,18},{4,20},{6,22},{8,24},{10,26},{12,28},{14,30},{16,0},... | collective-permute-start | bytes 1966088 | tf_op jit(solution)/shard_map/ppermute | solution.py:359
  841.8 135.7 %collective-permute-start.28 = (bf16[256,1280]{1,0:T(8,128)(2,1)S(1)}, bf16[256,1280]{1,0:T(8,128)(2,1)S(1)}, u32[]{:S(2)}, u32[]{:S(2)}) collective-permute-start(bf16[256,1280]{1,0:T(8,128)(2,1)S(1)} %get-tuple-element.176), channel_id=1, source_target_pairs={{0,16},{2,18},{4,20},{6,22},{8,24},{10,26},{12,28},{14,30},{16,0},... | collective-permute-start | bytes 1966088 | tf_op jit(solution)/shard_map/ppermute | solution.py:359
  949.4 42.1 %collective-permute-start.35 = (bf16[256,1280]{1,0:T(8,128)(2,1)S(1)}, bf16[256,1280]{1,0:T(8,128)(2,1)S(1)}, u32[]{:S(2)}, u32[]{:S(2)}) collective-permute-start(bf16[256,1280]{1,0:T(8,128)(2,1)S(1)} %get-tuple-element.174), channel_id=1, source_target_pairs={{0,16},{2,18},{4,20},{6,22},{8,24},{10,26},{12,28},{14,30},{16,0},... | collective-permute-start | bytes 1966088 | tf_op jit(solution)/shard_map/ppermute | solution.py:359
  977.5 21.1 %collective-permute-start.26 = (bf16[128,1280]{1,0:T(8,128)(2,1)S(1)}, bf16[128,1280]{1,0:T(8,128)(2,1)S(1)}, u32[]{:S(2)}, u32[]{:S(2)}) collective-permute-start(bf16[128,1280]{1,0:T(8,128)(2,1)S(1)} %add_convert_fusion.41), channel_id=1, source_target_pairs={{0,8},{2,10},{4,12},{6,14},{8,0},{10,2},{12,4},{14,6},{16,24},{18,... | collective-permute-start | bytes 983048 | tf_op jit(solution)/shard_map/ppermute | solution.py:359
  991.5 14.0 %collective-permute-start.29 = (bf16[128,1280]{1,0:T(8,128)(2,1)S(1)}, bf16[128,1280]{1,0:T(8,128)(2,1)S(1)}, u32[]{:S(2)}, u32[]{:S(2)}) collective-permute-start(bf16[128,1280]{1,0:T(8,128)(2,1)S(1)} %add_convert_fusion.39), channel_id=1, source_target_pairs={{0,8},{2,10},{4,12},{6,14},{8,0},{10,2},{12,4},{14,6},{16,24},{18,... | collective-permute-start | bytes 983048 | tf_op jit(solution)/shard_map/ppermute | solution.py:359
  991.6 20.9 %collective-permute-start.36 = (bf16[128,1280]{1,0:T(8,128)(2,1)S(1)}, bf16[128,1280]{1,0:T(8,128)(2,1)S(1)}, u32[]{:S(2)}, u32[]{:S(2)}) collective-permute-start(bf16[128,1280]{1,0:T(8,128)(2,1)S(1)} %add_convert_fusion.36), channel_id=1, source_target_pairs={{0,8},{2,10},{4,12},{6,14},{8,0},{10,2},{12,4},{14,6},{16,24},{18,... | collective-permute-start | bytes 983048 | tf_op jit(solution)/shard_map/ppermute | solution.py:359
  994.8 36.8 %collective-permute-start.38 = (bf16[128,3072]{1,0:T(8,128)(2,1)}, bf16[128,3072]{1,0:T(8,128)(2,1)}, u32[]{:S(2)}, u32[]{:S(2)}) collective-permute-start(bf16[128,3072]{1,0:T(8,128)(2,1)} %add_convert_fusion.28), channel_id=1, source_target_pairs={{0,8},{2,10},{4,12},{6,14},{8,0},{10,2},{12,4},{14,6},{16,24},{18,... | collective-permute-start | bytes 2359304 | tf_op jit(solution)/shard_map/ppermute | solution.py:359
  998.5 50.0 %collective-permute-start.40 = (bf16[128,3072]{1,0:T(8,128)(2,1)}, bf16[128,3072]{1,0:T(8,128)(2,1)}, u32[]{:S(2)}, u32[]{:S(2)}) collective-permute-start(bf16[128,3072]{1,0:T(8,128)(2,1)} %add_convert_fusion.26), channel_id=1, source_target_pairs={{0,8},{2,10},{4,12},{6,14},{8,0},{10,2},{12,4},{14,6},{16,24},{18,... | collective-permute-start | bytes 2359304 | tf_op jit(solution)/shard_map/ppermute | solution.py:359
  1008.3 5.5 collective-permute-start.19
  1013.8 1.4 collective-permute-start.20
  1015.2 9.5 collective-permute-start.21
  1024.7 17.0 %collective-permute-start.22 = (f32[192,128]{1,0:T(8,128)S(1)}, f32[192,128]{1,0:T(8,128)S(1)}, u32[]{:S(2)}, u32[]{:S(2)}) collective-permute-start(f32[192,128]{1,0:T(8,128)S(1)} %add.344), channel_id=1, source_target_pairs={{0,16},{2,18},{4,20},{6,22},{8,24},{10,26},{12,28},{14,30},{16,0},... | collective-permute-start | bytes 294920 | tf_op jit(solution)/shard_map/ppermute | solution.py:359
  1041.7 9.4 collective-permute-start.23
  (96 other events, 1281.1 us)

commit v2 on v1

--- a/solution.py
+++ b/solution.py
@@ -312,14 +312,19 @@
     return block
 
 
-def arrange_kernel(count, bits, steps, first, second, keep, send):
+def arrange_kernel(count, bits, steps, first, second, *parts):
     me = lax.axis_index("dp")
     cols = first.shape[1] // count
 
     def move(piece):
         for place in range(count):
             source = pl.ds(pl.multiple_of(block_from(me, place, bits) * cols, cols), cols)
-            into, spot = (keep, place) if place < count // 2 else (send, place - count // 2)
+            if place < count // 4:
+                into, spot = parts[0], place
+            elif place < count // 2:
+                into, spot = parts[1], place - count // 4
+            else:
+                into, spot = parts[2], place - count // 2
             into[:, spot * cols : (spot + 1) * cols] = piece[:, source]
 
     @pl.when(pl.program_id(0) < steps)
@@ -335,7 +340,7 @@
     half, width = first.shape
     steps = 2
     block = half // steps
-    shape = jax.ShapeDtypeStruct((2 * half, width // 2), first.dtype)
+    widths = width // 4, width // 4, width // 2
     return pl.pallas_call(
         functools.partial(arrange_kernel, count, stage_bits(count), steps),
         grid=(2 * steps,),
@@ -343,8 +348,8 @@
             pl.BlockSpec((block, width), lambda i: (jnp.minimum(i, steps - 1), 0)),
             pl.BlockSpec((block, width), lambda i: (jnp.maximum(i - steps, 0), 0)),
         ],
-        out_specs=[pl.BlockSpec((block, width // 2), lambda i: (i, 0))] * 2,
-        out_shape=[shape, shape],
+        out_specs=[pl.BlockSpec((block, cols), lambda i: (i, 0)) for cols in widths],
+        out_shape=[jax.ShapeDtypeStruct((2 * half, cols), first.dtype) for cols in widths],
         cost_estimate=pl.CostEstimate(flops=0, bytes_accessed=8 * half * width, transcendentals=0),
         name="arrange",
     )(first, second)
@@ -360,49 +365,45 @@
 
 
 class Reduction:
-    def __init__(self, keep, sent, bits):
-        self.keep, self.bits = keep, list(bits)
-        self.pass_on(sent)
-
-    def pass_on(self, sent):
-        self.sent = sent
+    def __init__(self, parts, right, bits):
+        self.keep_cols, self.next_cols, self.first_cols = parts
+        self.right, self.bits = right, list(bits)
+
+    def send(self, *others):
+        sent = matmul_left(after(self.first_cols, *others), self.right).astype(BF16)
         self.received = flip(sent, self.bits.pop(0))
-
-    def step(self):
-        middle = self.keep.shape[0] // 2
-        keep, received = self.keep, self.received
-        self.keep = (keep[:middle].astype(F32) + received[:middle].astype(F32)).astype(BF16)
-        self.pass_on((keep[middle:].astype(F32) + received[middle:].astype(F32)).astype(BF16))
-        return self.sent
-
-    def total(self):
-        return self.keep.astype(F32) + self.received.astype(F32)
+        return sent
+
+    def send_next(self, *others):
+        received = self.received
+        middle = received.shape[0] // 2
+        left, received = lax.optimization_barrier((self.next_cols, received, *others))[:2]
+        sent = (matmul_left(left, self.right) + received[middle:].astype(F32)).astype(BF16)
+        self.received = flip(sent, self.bits.pop(0))
+        self.keep = (matmul_left(after(self.keep_cols, sent), self.right) + received[:middle].astype(F32)).astype(BF16)
+        return self.keep
+
+    def step(self, *others):
+        received = after(self.received, *others)
+        middle = received.shape[0] // 2
+        sent = (self.keep[middle:].astype(F32) + received[middle:].astype(F32)).astype(BF16)
+        self.keep = (self.keep[:middle].astype(F32) + received[:middle].astype(F32)).astype(BF16)
+        self.received = flip(sent, self.bits.pop(0))
+        return sent
+
+    def total(self, *others):
+        return self.keep.astype(F32) + after(self.received, *others).astype(F32)
 
 
 def after(value, *others):
     return lax.optimization_barrier((value, *others))[0]
-
-
-def sum_everywhere(value):
-    value = value + swap(value)
-    for bit in stage_bits(lax.axis_size("dp")):
-        value = value + flip(value, bit)
-    return value
 
 
 def norm_back(values, gain, grad):
     scale = lax.rsqrt(jnp.mean(values * values, axis=-1, keepdims=True) + EPS)
     lifted = gain * grad
     pull = jnp.mean(values * lifted, axis=-1, keepdims=True)
-    grad_values = scale * lifted - values * (scale * scale * scale * pull)
-    return grad_values, grad * values * scale
-
-
-def weight_grad(parts, right, bits):
-    keep, send = parts
-    sent = matmul_left(send, right).astype(BF16)
-    kept = matmul_left(after(keep, sent), right).astype(BF16)
-    return Reduction(kept, sent, bits)
+    return scale * lifted - values * (scale * scale * scale * pull)
 
 
 def local_channels(
@@ -436,112 +437,160 @@
     prm = lax.dynamic_slice(table, (0, place * width), (8, width))
     gates = lax.dynamic_slice_in_dim(gate_blocks, place * heads, heads, axis=1)
 
-    normed_oth = rms_scale(oth_in.astype(F32), norm_gains[0]).astype(BF16)
+    gh_own = matmul_right(after(own_cot, bx_own, by_own), w_down)
+    normed_oth = rms_scale(after(oth_in, gh_own).astype(F32), norm_gains[0]).astype(BF16)
     bx_oth = matmul(normed_oth, w_x).astype(BF16)
     by_oth = matmul(normed_oth, w_y)
     gated_own, gated_oth, states = rec_fwd(bx_own, bx_oth, by_own, by_oth, mask, prm, gates)
 
+    gated = jnp.concatenate([gated_own, gated_oth], axis=0)
     part_oth = matmul(gated_oth, w_out).astype(BF16)
     swap_own = swap(part_oth)
     part_own = matmul(after(gated_own, part_oth), w_out).astype(BF16)
     swap_oth = swap(part_own)
-    cot_cols = arrange(after(own_cot, part_own), oth_cot, count)
+    gh_oth = matmul_right(after(oth_cot, part_own), w_down)
+    cot_cols = arrange(after(own_cot, gh_oth), oth_cot, count)
 
     def feed_in(tokens, part, other):
         middle = tokens.astype(F32) + (part.astype(F32) + other.astype(F32))
         normed = rms_scale(middle, norm_gains[1]).astype(BF16)
         gate_val = matmul(normed, w_gate)
         up_val = matmul(normed, w_up)
-        hidden_val, pull = jax.vjp(gelu_product, gate_val, up_val)
-        return middle, normed, hidden_val.astype(BF16), pull
-
-    def feed_back(cot, pull):
-        grad_gate, grad_up = pull(matmul_right(cot, w_down))
-        grad_gate, grad_up = grad_gate.astype(BF16), grad_up.astype(BF16)
-        back = (matmul_right(grad_gate, w_gate) + matmul_right(grad_up, w_up)).astype(BF16)
-        return grad_gate, grad_up, back
+        hidden = (jax.nn.gelu(gate_val, approximate=True) * up_val).astype(BF16)
+        return middle, normed, gate_val, up_val, hidden
+
+    def feed_grads(gate_val, up_val, grad_hidden):
+        _, pull = jax.vjp(gelu_product, gate_val, up_val)
+        grad_gate, grad_up = pull(grad_hidden)
+        return grad_gate.astype(BF16), grad_up.astype(BF16)
+
+    def feed_back(grad_gate, grad_up):
+        return (matmul_right(grad_gate, w_gate) + matmul_right(grad_up, w_up)).astype(BF16)
 
     def norm_two_back(middle, back, other, cot):
-        grad, gain_rows = norm_back(middle, norm_gains[1], back.astype(F32) + other.astype(F32))
-        grad = cot.astype(F32) + grad
-        return grad, grad.astype(BF16), gain_rows
-
-    middle_own, normed_two_own, hidden_own, pull_own = feed_in(own_in, part_own, swap_own)
-    gg_own, gu_own, back_own = feed_back(own_cot, pull_own)
+        grad = cot.astype(F32) + norm_back(middle, norm_gains[1], back.astype(F32) + other.astype(F32))
+        return grad, grad.astype(BF16)
+
+    middle_own, normed_two_own, gate_own, up_own, hidden_own = feed_in(own_in, part_own, after(swap_own, *cot_cols))
+    gg_own, gu_own = feed_grads(gate_own, up_own, after(gh_own, hidden_own))
+    middle_oth, normed_two_oth, gate_oth, up_oth, hidden_oth = feed_in(oth_in, part_oth, after(swap_oth, gg_own, gu_own))
+    down = Reduction(cot_cols, jnp.concatenate([hidden_own, hidden_oth], axis=0), bits)
+    done = down.send()
+    gg_oth, gu_oth = feed_grads(gate_oth, up_oth, after(gh_oth, done))
+    normed_two_cols = arrange(after(normed_two_own, gg_oth, gu_oth), normed_two_oth, count)
+    done = down.send_next(*normed_two_cols)
+    back_own = feed_back(after(gg_own, done), gu_own)
     back_own_swapped = swap(back_own)
-    middle_oth, normed_two_oth, hidden_oth, pull_oth = feed_in(after(oth_in, back_own), part_oth, swap_oth)
-    hidden = jnp.concatenate([hidden_own, hidden_oth], axis=0)
-    down = weight_grad(cot_cols, hidden, bits)
-    gg_oth, gu_oth, back_oth = feed_back(after(oth_cot, down.keep), pull_oth)
+    gate = Reduction(normed_two_cols, jnp.concatenate([gg_own, gg_oth], axis=0), bits)
+    up = Reduction(normed_two_cols, jnp.concatenate([gu_own, gu_oth], axis=0), bits)
+    done = gate.send(back_own)
+    done = up.send(done)
+    done = gate.send_next(done)
+    back_oth = feed_back(after(gg_oth, done), gu_oth)
     back_oth_swapped = swap(back_oth)
-    normed_two_own_late = after(normed_two_own, back_oth, down.step())
-    normed_two_cols = arrange(normed_two_own_late, normed_two_oth, count)
-    gate = weight_grad(normed_two_cols, jnp.concatenate([gg_own, gg_oth], axis=0), bits)
-    keep_cols, send_cols = normed_two_cols
-    up = weight_grad((keep_cols, after(send_cols, gate.keep)), jnp.concatenate([gu_own, gu_oth], axis=0), bits)
-    hidden_late = after(hidden_oth, up.keep, gate.step())
-    out_send = matmul(hidden_late, w_down).astype(BF16)
+    done = up.send_next(back_oth)
+    done = down.step(done)
+    out_send = matmul(after(hidden_oth, done), w_down).astype(BF16)
     out_swapped = swap(out_send)
-
-    grad_own, rec_own, gain_rows = norm_two_back(after(middle_own, out_send, up.step()), back_own, back_oth_swapped, own_cot)
-    gain_two = jnp.sum(gain_rows, axis=0)
-    _, rec_oth, _ = norm_two_back(middle_oth, back_oth, back_own_swapped, oth_cot)
-    up_own = matmul_right(rec_own, w_out)
-    up_oth = matmul_right(rec_oth, w_out)
+    out_keep = matmul(after(hidden_own, out_send), w_down).astype(BF16)
+
+    grad_own, rec_own = norm_two_back(middle_own, back_own, after(back_oth_swapped, out_keep), own_cot)
+    _, rec_oth = norm_two_back(middle_oth, back_oth, after(back_own_swapped, out_keep), oth_cot)
+    into_own = matmul_right(rec_own, w_out)
+    into_oth = matmul_right(rec_oth, w_out)
     gx_own, gx_oth, gy_own, gy_oth, gate_grad, sums = rec_bwd(
-        bx_own, bx_oth, by_own, by_oth, states, up_own, up_oth, mask, prm, gates, count
-    )
+        bx_own, bx_oth, by_own, by_oth, states, into_own, into_oth, mask, prm, gates, count
+    )
+    done = gate.step(gx_own, down.step(gx_own))
+    rec_cols = arrange(after(rec_own, done), rec_oth, count)
+    normed_cols = arrange(after(normed_own, *rec_cols), normed_oth, count)
+    in_x = Reduction(normed_cols, jnp.concatenate([gx_own, gx_oth], axis=0), bits)
+    in_y = Reduction(normed_cols, jnp.concatenate([gy_own, gy_oth], axis=0), bits)
+    out = Reduction(rec_cols, gated, bits)
+    done = in_x.send(*normed_cols)
+    done = in_y.send(done)
+    done = out.send(done)
+    done = in_x.send_next(done)
+    done = in_y.send_next(done)
+    done = out.send_next(done)
 
     def rec_back(piece_x, piece_y):
         return (matmul_right(piece_x, w_x) + matmul_right(piece_y, w_y)).astype(BF16)
 
-    rec_cols = arrange(after(rec_own, gx_oth, down.step()), rec_oth, count)
-    out = weight_grad(rec_cols, jnp.concatenate([gated_own, gated_oth], axis=0), bits)
-    half_gates = count // 2
-    blocks = Reduction(gate_grad[:half_gates], gate_grad[half_gates:], bits)
-    normed_cols = arrange(after(normed_own, out.keep), normed_oth, count)
-    keep_cols, send_cols = normed_cols
-    in_x = weight_grad(normed_cols, jnp.concatenate([gx_own, gx_oth], axis=0), bits)
-    in_y = weight_grad((keep_cols, after(send_cols, in_x.keep)), jnp.concatenate([gy_own, gy_oth], axis=0), bits)
-    rec_send = rec_back(after(gx_oth, in_y.keep, out.step(), gate.step()), gy_oth)
+    rec_send = rec_back(after(gx_oth, done), gy_oth)
     rec_swapped = swap(rec_send)
-    sums = sums.at[7].multiply(-8.0 * lax.dynamic_slice(jax.nn.sigmoid(a_param), (place * width,), (width,)))
-    wide = lax.dynamic_update_slice(jnp.zeros((8, full_width), F32), sums, (0, place * width))
-    rec_keep = rec_back(after(gx_own, rec_send, in_x.step(), in_y.step(), blocks.step()), gy_own)
-    out_keep = matmul(after(hidden_own, rec_keep, up.step()), w_down).astype(BF16)
-    layer_out = (middle_own + out_keep.astype(F32) + out_swapped.astype(F32)).astype(BF16)
-    grad_normed = rec_keep.astype(F32) + after(rec_swapped, out_keep).astype(F32)
-    grad_inputs, gain_rows = norm_back(own_in.astype(F32), norm_gains[0], grad_normed)
-    input_grad = grad_own + grad_inputs
-    gain_one = jnp.sum(gain_rows, axis=0)
-    packed = jnp.concatenate([wide.reshape(-1), gain_one, gain_two]).reshape(-1, 128)
-    packed = sum_everywhere(packed).reshape(-1)
-    for task in (down, blocks, out, gate, up, in_x, in_y) * 3:
-        if task.bits:
-            task.step()
-
-    small = packed[: 8 * full_width].reshape(8, full_width)
-    small = lax.dynamic_slice(small, (0, me * (full_width // count)), (8, full_width // count))
-    gains = packed[8 * full_width :].reshape(2, model)
-    gains = lax.dynamic_slice(gains, (0, me * (model // count)), (2, model // count))
-    mine = blocks.total()[0].astype(BF16)
-    others = swap(mine)
-    mine = jnp.concatenate([jnp.where(first_place, mine, others), jnp.where(first_place, others, mine)], axis=0)
-    mine = mine.astype(F32).reshape(2 * heads, 2, -1, mine.shape[-1])
+    layer_out = (middle_own + out_keep.astype(F32) + after(out_swapped, rec_send).astype(F32)).astype(BF16)
+    lanes = gate_grad.shape[-1]
+    blocks = gate_grad.reshape(-1, lanes)
+    row = jnp.arange(8)[:, None] == 7
+    slopes = -8.0 * lax.dynamic_slice(jax.nn.sigmoid(a_param), (place * width,), (width,))
+    sums = jnp.where(row, sums * slopes, sums).astype(BF16).reshape(-1, lanes)
+    done = rec_send
+    for bit in bits:
+        middle = blocks.shape[0] // 2
+        message = jnp.concatenate([blocks[middle:], sums], axis=0)
+        received = after(flip(message, bit), done).astype(F32)
+        blocks = (blocks[:middle].astype(F32) + received[:middle]).astype(BF16)
+        sums = (sums.astype(F32) + received[middle:]).astype(BF16)
+        if bit == bits[0]:
+            rec_keep = rec_back(after(gx_own, blocks), gy_own)
+            done = rec_keep
+    message = jnp.concatenate([blocks, sums], axis=0)
+    others = swap(message)
+    low, high = jnp.where(first_place, message, others), jnp.where(first_place, others, message)
+    n_blocks = blocks.shape[0]
+    block_sums = jnp.stack([low[:n_blocks], high[:n_blocks]]).astype(F32).reshape(2 * heads, 2, -1, lanes)
+    small = jnp.concatenate([low[n_blocks:].reshape(8, width), high[n_blocks:].reshape(8, width)], axis=1)
+    small = lax.dynamic_slice(small, (0, me * (full_width // count)), (8, full_width // count)).astype(F32)
+
+    grad_normed = rec_keep.astype(F32) + rec_swapped.astype(F32)
+    input_grad = grad_own + norm_back(own_in.astype(F32), norm_gains[0], grad_normed)
+    done = up.step(input_grad)
+    down_grad = down.total(done)
+    done = gate.step(down_grad)
+    done = in_x.step(done)
+    done = in_y.step(done)
+    gate_grad = gate.total(done)
+    done = up.step(gate_grad)
+    done = out.step(done)
+    done = in_x.step(done)
+    done = in_y.step(done)
+    up_grad = up.total(done)
+    done = out.step(up_grad)
+    x_grad = in_x.total(done)
+    y_grad = in_y.total(done)
+    out_grad = out.total()
+
+    block = model // count
+
+    def gain_grad(gain, *pairs):
+        weights = sum(
+            jnp.sum(lax.dynamic_slice_in_dim(weight, me * block, block, axis=0).astype(F32) * grad, axis=1)
+            for weight, grad in pairs
+        )
+        return weights / lax.dynamic_slice_in_dim(gain, me * block, block, axis=0)
+
+    gains = jnp.stack(
+        [
+            gain_grad(norm_gains[0], (w_x, x_grad), (w_y, y_grad)),
+            gain_grad(norm_gains[1], (w_gate, gate_grad), (w_up, up_grad)),
+        ]
+    )
+    gains = gains + swap(gains)
     return (
         layer_out[None],
         input_grad[None],
         gains,
-        in_x.total(),
-        in_y.total(),
+        x_grad,
+        y_grad,
         small[0:4],
         small[4:7],
         small[7],
-        jnp.swapaxes(mine, 0, 1),
-        out.total().T,
-        gate.total(),
-        up.total(),
-        down.total().T,
+        jnp.swapaxes(block_sums, 0, 1),
+        out_grad.T,
+        gate_grad,
+        up_grad,
+        down_grad.T,
     )
 
 
@@ -829,7 +878,7 @@
 
 def solution(mesh):
     rows, cols = mesh.shape["dp"], mesh.shape["tp"]
-    by_channels = cols == 2 and rows >= 4 and rows & (rows - 1) == 0
+    by_channels = cols == 2 and rows >= 16 and rows & (rows - 1) == 0
 
     def step(*args):
         heads, model = args[9].shape[1], args[3].shape[1]

time: 1060 us -> 861 us (0.81)
  waiting for transfers between devices: 474 us -> 263 us
  matrix products: 299 us -> 315 us
  starting transfers between devices: 48.7 us -> 35.9 us
    ppermute x32 -> x28, waiting for transfers between devices: 378 us -> 185 us  [flip(): lax.ppermute(value, 'dp', [(source, source ^ bit) for source in range(cou...]
    dot_general x12 -> x18, matrix products: 90.2 us -> 115 us  [matmul_left(): lax.dot_general(first_mat, second_mat, (((0,), (0,)), ((), ())), preferre...]
    ppermute x11, waiting for transfers between devices: 95.9 us -> 78.2 us  [swap(): return lax.ppermute(value, 'tp', [(0, 1), (1, 0)])]
    ppermute x32 -> x28, starting transfers between devices: 34.5 us -> 22.7 us  [flip(): lax.ppermute(value, 'dp', [(source, source ^ bit) for source in range(cou...]
    convert_element_type x24 -> x31, other arithmetic: 62.7 us -> 58.3 us  [the longest x6 18.3 us: step(): (self.keep[:middle].astype(F32) + received[:middle].astype(F32)).astype(B...]
  transfers between devices with their start and end apart: 43 -> 39, of which waited for: 24 -> 13; matrix products, arithmetic and copies ran while one was open for 32% -> 41% of each run, Pallas kernels for 8% -> 13%
where the time goes in v2:
time: 861 us; the launch traced here: 855 us
  matrix products  315 us (37%)
  waiting for transfers between devices  263 us (31%)
  other arithmetic  110 us (13%)
  Pallas kernels  110 us (13%)
  starting transfers between devices  35.9 us (4%)
  local copies, waits for them, and re-layouts  19 us (2%)
    ppermute x28, waiting for transfers between devices, flip(): lax.ppermute(value, 'dp', [(source, source ^ bit) for source in range(cou...  185 us
    dot_general x18, matrix products, matmul_left(): lax.dot_general(first_mat, second_mat, (((0,), (0,)), ((), ())), preferre...  115 us
    dot_general x12, matrix products, matmul_right(): lax.dot_general(first_mat, second_mat, (((1,), (1,)), ((), ())), preferre...  104 us
    dot_general x12, matrix products, matmul(): return jnp.dot(first_mat, second_mat, preferred_element_type=jnp.float32)  95.6 us
    ppermute x11, waiting for transfers between devices, swap(): return lax.ppermute(value, 'tp', [(0, 1), (1, 0)])  78.2 us
    pallas_call x1, Pallas kernels, rec_bwd(): pl.pallas_call(functools.partial(rec_bwd_kernel, count, stage_bits(count)...  57.2 us
    pallas_call x1, Pallas kernels, rec_fwd(): pl.pallas_call(rec_fwd_kernel, grid=(heads,), in_specs=[piece] * 4 + [mas...  30.5 us
    ppermute x28, starting transfers between devices, flip(): lax.ppermute(value, 'dp', [(source, source ^ bit) for source in range(cou...  22.7 us
  transfers between devices with their start and end apart: 39, of which 13 were waited for; matrix products, arithmetic and copies ran while one was open for 41% of the time, Pallas kernels for 13%

profile of v2, /device:TPU:0, one launch (start us, length us, event | category | flops | bytes accessed | tf_op | source)
XLA Modules:
  0.0 855.2 jit_solution(16039102527849737202)
XLA Ops:
  11.5 7.6 fusion.72.by_own
  23.3 12.3 %fusion.73 = f32[512,3072]{1,0:T(8,128)} fusion(bf16[512,2048]{1,0:T(8,128)(2,1)} %bitcast.133, bf16[3072,2048]{1,0:T(8,128)(2,1)} %param.27), kind=kOutput, calls=%fused_computation.219 | convolution fusion | flops 6442450944 | bytes 20971520 | tf_op jit(solution)/shard_map/dot_general | solution.py:631
  37.4 15.1 %collective-permute-done = bf16[512,2048]{1,0:T(8,128)(2,1)} collective-permute-done((bf16[512,2048]{1,0:T(8,128)(2,1)}, bf16[512,2048]{1,0:T(8,128)(2,1)}, u32[]{:S(2)}, u32[]{:S(2)}) %collective-permute-start) | collective-permute-done | bytes 2097184 | tf_op jit(solution)/shard_map/ppermute | solution.py:359
  57.0 6.1 fusion.74.by_oth
  66.6 30.5 %rec_fwd.1 = (bf16[512,1280]{1,0:T(8,128)(2,1)S(1)}, bf16[512,1280]{1,0:T(8,128)(2,1)S(1)}, f32[1024,1280]{1,0:T(8,128)}) custom-call(bf16[512,1280]{1,0:T(8,128)(2,1)S(1)} %copy-done.7, bf16[512,1280]{1,0:T(8,128)(2,1)S(1)} %convolution_convert_fusion.10.bx_oth, f32[512,1280]{1,0:T(8,128)S(1)} %copy-done.3, f32[512,1280]{1,0:T(8,128)S(1)} %fusion.74.by_oth, ...), custom_call_target="tpu_custom_call" | custom-call | flops 1473249280 | bytes 20971520 | tf_op jit(solution)/shard_map/rec_fwd/pallas_call | solution.py:243
  97.2 7.5 convolution_convert_fusion.9
  110.9 10.6 %fusion.75 = f32[512,3072]{1,0:T(8,128)} fusion(bf16[512,2048]{1,0:T(8,128)(2,1)} %collective-permute-done.3.second, bf16[3072,2048]{1,0:T(8,128)(2,1)S(1)} %bitcast.173), kind=kOutput, calls=%fused_computation.221 | convolution fusion | flops 6442450944 | bytes 20971520 | tf_op jit(solution)/shard_map/dot_general | solution.py:631
  121.5 5.5 arrange.4
  127.1 26.5 %collective-permute-done.2 = bf16[512,2048]{1,0:T(8,128)(2,1)} collective-permute-done((bf16[512,2048]{1,0:T(8,128)(2,1)}, bf16[512,2048]{1,0:T(8,128)(2,1)}, u32[]{:S(2)}, u32[]{:S(2)}) %collective-permute-start.2) | collective-permute-done | bytes 2097184 | tf_op jit(solution)/shard_map/ppermute | solution.py:359
  160.6 10.1 %fusion.76 = f32[512,3072]{1,0:T(8,128)S(1)} fusion(bf16[512,2048]{1,0:T(8,128)(2,1)S(1)} %multiply_convert_fusion.5.first, bf16[2048,3072]{1,0:T(8,128)(2,1)} %param.25), kind=kOutput, calls=%fused_computation.222 | convolution fusion | flops 6442450944 | bytes 20971520 | tf_op jit(solution)/shard_map/dot_general | solution.py:621
  170.7 12.7 %multiply_convert_fusion.3 = (bf16[512,3072]{1,0:T(8,128)(2,1)}, f32[512,3072]{1,0:T(8,128)}) fusion(f32[512,3072]{1,0:T(8,128)S(1)} %fusion.76, bf16[512,2048]{1,0:T(8,128)(2,1)S(1)} %multiply_convert_fusion.5.first, bf16[2048,3072]{1,0:T(8,128)(2,1)} %param.26), kind=kOutput, calls=%fused_computation.35 | convolution fusion | flops 6458179584 | bytes 30408704 | tf_op jit(solution)/shard_map/dot_general | solution.py:621
  183.5 9.0 %multiply_convert_fusion.2 = (bf16[512,3072]{1,0:T(8,128)(2,1)}, bf16[512,3072]{1,0:T(8,128)(2,1)}) fusion(f32[512,3072]{1,0:T(8,128)S(1)} %bitcast.137, f32[512,3072]{1,0:T(8,128)S(1)} %fusion.76, f32[512,3072]{1,0:T(8,128)} %get-tuple-element.266), kind=kLoop, calls=%fused_computation.34 | loop fusion | flops 37748736 | bytes 25165824 | tf_op jit(solution)/shard_map/convert_element_type | solution.py:465
  203.8 6.8 fusion.77
  210.6 11.7 %multiply_convert_fusion.1 = (bf16[512,3072]{1,0:T(8,128)(2,1)}, f32[512,3072]{1,0:T(8,128)S(1)}) fusion(f32[512,3072]{1,0:T(8,128)S(1)} %fusion.77, bf16[512,2048]{1,0:T(8,128)(2,1)S(1)} %multiply_convert_fusion.4.second, bf16[2048,3072]{1,0:T(8,128)(2,1)} %param.26), kind=kOutput, calls=%fused_computation.33 | convolution fusion | flops 6458179584 | bytes 30408704 | tf_op jit(solution)/shard_map/dot_general | solution.py:621
  222.3 11.9 %convolution_convert_fusion.2 = bf16[1024,3072]{1,0:T(8,128)(2,1)} fusion(bf16[1024,1024]{1,0:T(8,128)(2,1)S(1)} %copy-done.91, bf16[512,3072]{1,0:T(8,128)(2,1)} %get-tuple-element.131, bf16[512,3072]{1,0:T(8,128)(2,1)} %get-tuple-element.132), kind=kOutput, calls=%fused_computation.40 | convolution fusion | flops 6458179584 | bytes 14680064 | tf_op jit(solution)/shard_map/dot_general | solution.py:625
  234.2 6.4 multiply_convert_fusion
  246.1 9.0 %add_convert_fusion.5 = bf16[512,3072]{1,0:T(8,128)(2,1)} fusion(bf16[1024,512]{1,0:T(8,128)(2,1)S(1)} %copy-done.98, bf16[1024,3072]{1,0:T(8,128)(2,1)} %collective-permute-done.5, bf16[512,3072]{1,0:T(8,128)(2,1)} %get-tuple-element.131, bf16[512,3072]{1,0:T(8,128)(2,1)} %get-tuple-element.132), kind=kOutput, calls=%fused_computation.31 | convolution fusion | flops 3238526976 | bytes 13631488 | tf_op jit(solution)/shard_map/dot_general | solution.py:625
  255.1 6.5 add_convert_fusion.4
  261.7 8.7 %fusion.78 = f32[512,2048]{1,0:T(8,128)} fusion(bf16[512,3072]{1,0:T(8,128)(2,1)S(1)} %copy-done.52, bf16[2048,3072]{1,0:T(8,128)(2,1)S(1)} %bitcast.155), kind=kOutput, calls=%fused_computation.224 | convolution fusion | flops 6442450944 | bytes 19922944 | tf_op jit(solution)/shard_map/dot_general | solution.py:631
  270.4 10.4 %add_convert_fusion.11 = bf16[512,2048]{1,0:T(8,128)(2,1)S(1)} fusion(f32[512,2048]{1,0:T(8,128)} %fusion.78, bf16[512,3072]{1,0:T(8,128)(2,1)S(1)} %copy-done.50, bf16[2048,3072]{1,0:T(8,128)(2,1)} %param.26), kind=kOutput, calls=%fused_computation.63 | convolution fusion | flops 6444548096 | bytes 22020096 | tf_op jit(solution)/shard_map/dot_general | solution.py:631
  280.8 12.6 %convolution_convert_fusion.1 = bf16[1024,3072]{1,0:T(8,128)(2,1)} fusion(bf16[1024,1024]{1,0:T(8,128)(2,1)} %get-tuple-element.122, bf16[512,3072]{1,0:T(8,128)(2,1)} %get-tuple-element.126, bf16[512,3072]{1,0:T(8,128)(2,1)} %get-tuple-element.120), kind=kOutput, calls=%fused_computation.39 | convolution fusion | flops 6458179584 | bytes 14680064 | tf_op jit(solution)/shard_map/dot_general | solution.py:625
  293.9 8.9 %convolution_convert_fusion = bf16[1024,3072]{1,0:T(8,128)(2,1)} fusion(bf16[1024,1024]{1,0:T(8,128)(2,1)S(1)} %copy-done.93, bf16[512,3072]{1,0:T(8,128)(2,1)S(1)} %copy-done.54, bf16[512,3072]{1,0:T(8,128)(2,1)S(1)} %copy-done.50), kind=kOutput, calls=%fused_computation.38 | convolution fusion | flops 6458179584 | bytes 14680064 | tf_op jit(solution)/shard_map/dot_general | solution.py:625
  317.8 11.0 %fusion.79 = f32[512,2048]{1,0:T(8,128)} fusion(bf16[512,3072]{1,0:T(8,128)(2,1)S(1)} %copy-done.56, bf16[2048,3072]{1,0:T(8,128)(2,1)} %param.25), kind=kOutput, calls=%fused_computation.225 | convolution fusion | flops 6442450944 | bytes 19922944 | tf_op jit(solution)/shard_map/dot_general | solution.py:631
  328.8 13.8 %add_convert_fusion.10 = bf16[512,2048]{1,0:T(8,128)(2,1)} fusion(f32[512,2048]{1,0:T(8,128)} %fusion.79, bf16[512,3072]{1,0:T(8,128)(2,1)} %get-tuple-element.237, bf16[2048,3072]{1,0:T(8,128)(2,1)} %param.26), kind=kOutput, calls=%fused_computation.62 | convolution fusion | flops 6444548096 | bytes 22020096 | tf_op jit(solution)/shard_map/dot_general | solution.py:631
  344.0 9.5 %add_convert_fusion.1 = bf16[512,3072]{1,0:T(8,128)(2,1)} fusion(bf16[1024,512]{1,0:T(8,128)(2,1)} %get-tuple-element.127, bf16[1024,3072]{1,0:T(8,128)(2,1)} %collective-permute-done.7, bf16[512,3072]{1,0:T(8,128)(2,1)} %get-tuple-element.237, bf16[512,3072]{1,0:T(8,128)(2,1)} %get-tuple-element.239), kind=kOutput, calls=%fused_computation.27 | convolution fusion | flops 3238526976 | bytes 13631488 | tf_op jit(solution)/shard_map/dot_general | solution.py:625
  353.6 6.6 add_convert_fusion
  360.1 15.9 %collective-permute-done.6 = bf16[512,3072]{1,0:T(8,128)(2,1)} collective-permute-done((bf16[512,3072]{1,0:T(8,128)(2,1)}, bf16[512,3072]{1,0:T(8,128)(2,1)}, u32[]{:S(2)}, u32[]{:S(2)}) %collective-permute-start.6) | collective-permute-done | bytes 3145760 | tf_op jit(solution)/shard_map/ppermute | solution.py:364
  384.3 10.7 %convolution_convert_fusion.7 = bf16[512,2048]{1,0:T(8,128)(2,1)} fusion(bf16[512,3072]{1,0:T(8,128)(2,1)S(1)} %copy-done.102, bf16[3072,2048]{1,0:T(8,128)(2,1)} %param.27), kind=kOutput, calls=%fused_computation.82 | convolution fusion | flops 6443499520 | bytes 17825792 | tf_op jit(solution)/shard_map/dot_general | solution.py:621
  395.7 11.4 %convolution_convert_fusion.6 = bf16[512,2048]{1,0:T(8,128)(2,1)} fusion(bf16[512,3072]{1,0:T(8,128)(2,1)S(1)} %copy-done.100, bf16[3072,2048]{1,0:T(8,128)(2,1)} %param.27), kind=kOutput, calls=%fused_computation.81 | convolution fusion | flops 6443499520 | bytes 17825792 | tf_op jit(solution)/shard_map/dot_general | solution.py:621
  407.2 6.6 multiply_reduce_fusion
  413.9 10.0 %add_convert_fusion.9 = (bf16[512,2048]{1,0:T(8,128)(2,1)S(1)}, bf16[512,2048]{1,0:T(8,128)(2,1)S(1)}) fusion(bf16[512,2048]{1,0:T(8,128)(2,1)} %collective-permute-done.3.second, bf16[512,2048]{1,0:T(8,128)(2,1)S(1)} %collective-permute-done.11, bf16[512,2048]{1,0:T(8,128)(2,1)S(1)} %copy-done.40, f32[512]{0:T(512)S(1)} %fusion.53, f32[512]{0:T(512)S(1)} %copy-done.89, ...), kind=kLoop, calls=%fused_computation.56 | loop fusion | flops 31457280 | bytes 29376512 | tf_op jit(solution)/shard_map/convert_element_type | solution.py:472
  423.9 8.4 fusion.80.up_own
  432.3 7.0 fusion.81.up_oth
  439.4 57.2 %rec_bwd.1 = (bf16[512,1280]{1,0:T(8,128)(2,1)S(1)}, bf16[512,1280]{1,0:T(8,128)(2,1)S(1)}, bf16[512,1280]{1,0:T(8,128)(2,1)S(1)}, bf16[512,1280]{1,0:T(8,128)(2...) custom-call(bf16[512,1280]{1,0:T(8,128)(2,1)} %convolution_convert_fusion.11.bx_own, ...), custom_call_target="tpu_custom_call" | custom-call | flops 4354211840 | bytes 31457280 | tf_op jit(solution)/shard_map/rec_bwd/pallas_call | solution.py:268
  511.4 5.5 arrange.7
  516.9 6.8 convolution_convert_fusion.5
  576.9 7.1 fusion.83
  584.0 34.4 %collective-permute-done.18 = bf16[512,2048]{1,0:T(8,128)(2,1)} collective-permute-done((bf16[512,2048]{1,0:T(8,128)(2,1)}, bf16[512,2048]{1,0:T(8,128)(2,1)}, u32[]{:S(2)}, u32[]{:S(2)}) %collective-permute-start.18) | collective-permute-done | bytes 2097184 | tf_op jit(solution)/shard_map/ppermute | solution.py:359
  618.9 7.1 fusion.20
  626.1 10.1 %fusion.22 = (f32[512,2048]{1,0:T(8,128)}, bf16[1,512,2048]{2,1,0:T(8,128)(2,1)}) fusion(bf16[512,2048]{1,0:T(8,128)(2,1)} %collective-permute-done.18, bf16[512,2048]{1,0:T(8,128)(2,1)S(1)} %get-tuple-element.270, f32[512]{0:T(512)S(1)} %fusion.54, f32[2048]{0:T(1024)S(1)} %bitcast.151, f32[512]{0:T(512)S(1)} %copy-done.81, ...), kind=kLoop, calls=%fused_computation.51 | loop fusion | flops 28311552 | bytes 27287552 | tf_op jit(solution)/shard_map/add | solution.py:547
  636.2 6.3 collective-permute-done.22
  650.5 82.9 %collective-permute-done.34 = bf16[680,256]{1,0:T(8,128)(2,1)S(1)} collective-permute-done((bf16[680,256]{1,0:T(8,128)(2,1)S(1)}, bf16[680,256]{1,0:T(8,128)(2,1)S(1)}, u32[]{:S(2)}, u32[]{:S(2)}) %collective-permute-start.34) | collective-permute-done | bytes 348192 | tf_op jit(solution)/shard_map/ppermute | solution.py:364
  736.7 7.8 collective-permute-done.35
  749.0 21.4 %collective-permute-done.36 = bf16[200,256]{1,0:T(8,128)(2,1)S(1)} collective-permute-done((bf16[200,256]{1,0:T(8,128)(2,1)S(1)}, bf16[200,256]{1,0:T(8,128)(2,1)S(1)}, u32[]{:S(2)}, u32[]{:S(2)}) %collective-permute-start.36) | collective-permute-done | bytes 102432 | tf_op jit(solution)/shard_map/ppermute | solution.py:364
  790.0 17.2 %collective-permute-done.31 = bf16[256,1280]{1,0:T(8,128)(2,1)} collective-permute-done((bf16[256,1280]{1,0:T(8,128)(2,1)}, bf16[256,1280]{1,0:T(8,128)(2,1)}, u32[]{:S(2)}, u32[]{:S(2)}) %collective-permute-start.31) | collective-permute-done | bytes 655392 | tf_op jit(solution)/shard_map/ppermute | solution.py:364
  808.4 11.5 %collective-permute-done.30 = bf16[128,3072]{1,0:T(8,128)(2,1)S(1)} collective-permute-done((bf16[128,3072]{1,0:T(8,128)(2,1)S(1)}, bf16[128,3072]{1,0:T(8,128)(2,1)S(1)}, u32[]{:S(2)}, u32[]{:S(2)}) %collective-permute-start.30) | collective-permute-done | bytes 786464 | tf_op jit(solution)/shard_map/ppermute | solution.py:364
  822.8 12.4 %collective-permute-done.29 = bf16[256,1280]{1,0:T(8,128)(2,1)S(1)} collective-permute-done((bf16[256,1280]{1,0:T(8,128)(2,1)S(1)}, bf16[256,1280]{1,0:T(8,128)(2,1)S(1)}, u32[]{:S(2)}, u32[]{:S(2)}) %collective-permute-start.29) | collective-permute-done | bytes 655392 | tf_op jit(solution)/shard_map/ppermute | solution.py:364
  835.3 9.7 %collective-permute-done.32 = bf16[128,1280]{1,0:T(8,128)(2,1)S(1)} collective-permute-done((bf16[128,1280]{1,0:T(8,128)(2,1)S(1)}, bf16[128,1280]{1,0:T(8,128)(2,1)S(1)}, u32[]{:S(2)}, u32[]{:S(2)}) %collective-permute-start.32) | collective-permute-done | bytes 327712 | tf_op jit(solution)/shard_map/ppermute | solution.py:364
  (439 shorter events, 197.8 us)
Async XLA Ops:
  0.7 36.2 %collective-permute-start.1 = (s32[512]{0:T(512)}, s32[512]{0:T(512)S(1)}, u32[]{:S(2)}, u32[]{:S(2)}) collective-permute-start(s32[512]{0:T(512)} %bitcast.169), channel_id=1, source_target_pairs={{0,1},{1,0},{2,3},{3,2},{4,5},{5,4},{6,7},{7,6},{8,9},{9,8},{10,11... | collective-permute-start | bytes 6152 | tf_op jit(solution)/shard_map/ppermute | solution.py:359
  3.7 48.9 %collective-permute-start = (bf16[512,2048]{1,0:T(8,128)(2,1)}, bf16[512,2048]{1,0:T(8,128)(2,1)}, u32[]{:S(2)}, u32[]{:S(2)}) collective-permute-start(bf16[512,2048]{1,0:T(8,128)(2,1)} %bitcast.131), channel_id=1, source_target_pairs={{0,1},{1,0},{2,3},{3,2},{4,5},{5,4},{6,7},{7,6},{8,9},{9,8},{10,11... | collective-permute-start | bytes 6291464 | tf_op jit(solution)/shard_map/ppermute | solution.py:359
  3.7 107.1 %collective-permute-start.3 = (bf16[512,2048]{1,0:T(8,128)(2,1)}, bf16[512,2048]{1,0:T(8,128)(2,1)}, u32[]{:S(2)}, u32[]{:S(2)}) collective-permute-start(bf16[512,2048]{1,0:T(8,128)(2,1)} %bitcast.132), channel_id=1, source_target_pairs={{0,1},{1,0},{2,3},{3,2},{4,5},{5,4},{6,7},{7,6},{8,9},{9,8},{10,11... | collective-permute-start | bytes 6291464 | tf_op jit(solution)/shard_map/ppermute | solution.py:359
  8.6 46.0 %copy-start.72 = (f32[1,2048]{1,0:T(1,128)}, f32[1,2048]{1,0:T(1,128)S(1)}, u32[]{:S(2)}) copy-start(f32[1,2048]{1,0:T(1,128)S(1)} %get-tuple-element.260) | copy-start | bytes 24580
  8.6 190.7 %copy-start.70 = (f32[1,2048]{1,0:T(1,128)}, f32[1,2048]{1,0:T(1,128)S(1)}, u32[]{:S(2)}) copy-start(f32[1,2048]{1,0:T(1,128)S(1)} %get-tuple-element.259) | copy-start | bytes 24580
  104.7 48.9 %collective-permute-start.2 = (bf16[512,2048]{1,0:T(8,128)(2,1)}, bf16[512,2048]{1,0:T(8,128)(2,1)}, u32[]{:S(2)}, u32[]{:S(2)}) collective-permute-start(bf16[512,2048]{1,0:T(8,128)(2,1)} %convolution_convert_fusion.9), channel_id=1, source_target_pairs={{0,1},{1,0},{2,3},{3,2},{4,5},{5,4},{6,7},{7,6},{8,9},{9,8},{10,11... | collective-permute-start | bytes 6291464 | tf_op jit(solution)/shard_map/ppermute | solution.py:359
  108.9 85.7 %collective-permute-start.4 = (bf16[512,2048]{1,0:T(8,128)(2,1)}, bf16[512,2048]{1,0:T(8,128)(2,1)}, u32[]{:S(2)}, u32[]{:S(2)}) collective-permute-start(bf16[512,2048]{1,0:T(8,128)(2,1)} %convolution_convert_fusion.8), channel_id=1, source_target_pairs={{0,1},{1,0},{2,3},{3,2},{4,5},{5,4},{6,7},{7,6},{8,9},{9,8},{10,11... | collective-permute-start | bytes 6291464 | tf_op jit(solution)/shard_map/ppermute | solution.py:359
  234.2 11.8 %collective-permute-start.5 = (bf16[1024,3072]{1,0:T(8,128)(2,1)}, bf16[1024,3072]{1,0:T(8,128)(2,1)}, u32[]{:S(2)}, u32[]{:S(2)}) collective-permute-start(bf16[1024,3072]{1,0:T(8,128)(2,1)} %convolution_convert_fusion.2), channel_id=1, source_target_pairs={{0,2},{2,0},{4,6},{6,4},{8,10},{10,8},{12,14},{14,12},{16,18},{18,... | collective-permute-start | bytes 18874376 | tf_op jit(solution)/shard_map/ppermute | solution.py:364
  280.8 133.1 %copy-start.23 = (bf16[512,2048]{1,0:T(8,128)(2,1)}, bf16[512,2048]{1,0:T(8,128)(2,1)S(1)}, u32[]{:S(2)}) copy-start(bf16[512,2048]{1,0:T(8,128)(2,1)S(1)} %add_convert_fusion.11) | copy-start | bytes 6291460
  293.4 14.4 %collective-permute-start.8 = (bf16[1024,3072]{1,0:T(8,128)(2,1)}, bf16[1024,3072]{1,0:T(8,128)(2,1)S(1)}, u32[]{:S(2)}, u32[]{:S(2)}) collective-permute-start(bf16[1024,3072]{1,0:T(8,128)(2,1)} %convolution_convert_fusion.1), channel_id=1, source_target_pairs={{0,2},{2,0},{4,6},{6,4},{8,10},{10,8},{12,14},{14,12},{16,18},{18,... | collective-permute-start | bytes 18874376 | tf_op jit(solution)/shard_map/ppermute | solution.py:364
  302.8 41.2 %collective-permute-start.7 = (bf16[1024,3072]{1,0:T(8,128)(2,1)}, bf16[1024,3072]{1,0:T(8,128)(2,1)}, u32[]{:S(2)}, u32[]{:S(2)}) collective-permute-start(bf16[1024,3072]{1,0:T(8,128)(2,1)} %convolution_convert_fusion), channel_id=1, source_target_pairs={{0,2},{2,0},{4,6},{6,4},{8,10},{10,8},{12,14},{14,12},{16,18},{18,... | collective-permute-start | bytes 18874376 | tf_op jit(solution)/shard_map/ppermute | solution.py:364
  305.7 70.4 %collective-permute-start.6 = (bf16[512,3072]{1,0:T(8,128)(2,1)}, bf16[512,3072]{1,0:T(8,128)(2,1)}, u32[]{:S(2)}, u32[]{:S(2)}) collective-permute-start(bf16[512,3072]{1,0:T(8,128)(2,1)} %add_convert_fusion.5), channel_id=1, source_target_pairs={{0,4},{2,6},{4,0},{6,2},{8,12},{10,14},{12,8},{14,10},{16,20},{18,... | collective-permute-start | bytes 9437192 | tf_op jit(solution)/shard_map/ppermute | solution.py:364
  307.2 99.9 %collective-permute-start.11 = (bf16[512,2048]{1,0:T(8,128)(2,1)S(1)}, bf16[512,2048]{1,0:T(8,128)(2,1)S(1)}, u32[]{:S(2)}, u32[]{:S(2)}) collective-permute-start(bf16[512,2048]{1,0:T(8,128)(2,1)S(1)} %add_convert_fusion.11), channel_id=1, source_target_pairs={{0,1},{1,0},{2,3},{3,2},{4,5},{5,4},{6,7},{7,6},{8,9},{9,8},{10,11... | collective-permute-start | bytes 6291464 | tf_op jit(solution)/shard_map/ppermute | solution.py:359
  342.6 64.5 %collective-permute-start.10 = (bf16[512,2048]{1,0:T(8,128)(2,1)}, bf16[512,2048]{1,0:T(8,128)(2,1)S(1)}, u32[]{:S(2)}, u32[]{:S(2)}) collective-permute-start(bf16[512,2048]{1,0:T(8,128)(2,1)} %add_convert_fusion.10), channel_id=1, source_target_pairs={{0,1},{1,0},{2,3},{3,2},{4,5},{5,4},{6,7},{7,6},{8,9},{9,8},{10,11... | collective-permute-start | bytes 6291464 | tf_op jit(solution)/shard_map/ppermute | solution.py:359
  380.2 117.7 %copy-start.43 = (bf16[256,3072]{1,0:T(8,128)(2,1)}, bf16[256,3072]{1,0:T(8,128)(2,1)S(1)}, u32[]{:S(2)}) copy-start(bf16[256,3072]{1,0:T(8,128)(2,1)S(1)} %get-tuple-element.247) | copy-start | bytes 4718596
  380.2 116.3 %collective-permute-start.13 = (bf16[256,3072]{1,0:T(8,128)(2,1)}, bf16[256,3072]{1,0:T(8,128)(2,1)S(1)}, u32[]{:S(2)}, u32[]{:S(2)}) collective-permute-start(bf16[256,3072]{1,0:T(8,128)(2,1)} %get-tuple-element.248), channel_id=1, source_target_pairs={{0,16},{2,18},{4,20},{6,22},{8,24},{10,26},{12,28},{14,30},{16,0},... | collective-permute-start | bytes 4718600 | tf_op jit(solution)/shard_map/ppermute | solution.py:364
  382.8 118.4 %collective-permute-start.12 = (bf16[512,3072]{1,0:T(8,128)(2,1)}, bf16[512,3072]{1,0:T(8,128)(2,1)}, u32[]{:S(2)}, u32[]{:S(2)}) collective-permute-start(bf16[512,3072]{1,0:T(8,128)(2,1)} %add_convert_fusion.3), channel_id=1, source_target_pairs={{0,4},{2,6},{4,0},{6,2},{8,12},{10,14},{12,8},{14,10},{16,20},{18,... | collective-permute-start | bytes 9437192 | tf_op jit(solution)/shard_map/ppermute | solution.py:364
  395.1 180.8 %collective-permute-start.9 = (bf16[512,2048]{1,0:T(8,128)(2,1)}, bf16[512,2048]{1,0:T(8,128)(2,1)}, u32[]{:S(2)}, u32[]{:S(2)}) collective-permute-start(bf16[512,2048]{1,0:T(8,128)(2,1)} %convolution_convert_fusion.7), channel_id=1, source_target_pairs={{0,1},{1,0},{2,3},{3,2},{4,5},{5,4},{6,7},{7,6},{8,9},{9,8},{10,11... | collective-permute-start | bytes 6291464 | tf_op jit(solution)/shard_map/ppermute | solution.py:359
  523.7 14.1 %collective-permute-start.16 = (bf16[1024,1280]{1,0:T(8,128)(2,1)}, bf16[1024,1280]{1,0:T(8,128)(2,1)}, u32[]{:S(2)}, u32[]{:S(2)}) collective-permute-start(bf16[1024,1280]{1,0:T(8,128)(2,1)} %convolution_convert_fusion.5), channel_id=1, source_target_pairs={{0,2},{2,0},{4,6},{6,4},{8,10},{10,8},{12,14},{14,12},{16,18},{18,... | collective-permute-start | bytes 7864328 | tf_op jit(solution)/shard_map/ppermute | solution.py:364
  530.0 15.9 %collective-permute-start.15 = (bf16[1024,1280]{1,0:T(8,128)(2,1)}, bf16[1024,1280]{1,0:T(8,128)(2,1)}, u32[]{:S(2)}, u32[]{:S(2)}) collective-permute-start(bf16[1024,1280]{1,0:T(8,128)(2,1)} %convolution_convert_fusion.4), channel_id=1, source_target_pairs={{0,2},{2,0},{4,6},{6,4},{8,10},{10,8},{12,14},{14,12},{16,18},{18,... | collective-permute-start | bytes 7864328 | tf_op jit(solution)/shard_map/ppermute | solution.py:364
  534.6 19.5 %collective-permute-start.14 = (bf16[1024,1280]{1,0:T(8,128)(2,1)}, bf16[1024,1280]{1,0:T(8,128)(2,1)}, u32[]{:S(2)}, u32[]{:S(2)}) collective-permute-start(bf16[1024,1280]{1,0:T(8,128)(2,1)} %convolution_convert_fusion.3), channel_id=1, source_target_pairs={{0,2},{2,0},{4,6},{6,4},{8,10},{10,8},{12,14},{14,12},{16,18},{18,... | collective-permute-start | bytes 7864328 | tf_op jit(solution)/shard_map/ppermute | solution.py:364
  537.7 35.6 %collective-permute-start.17 = (bf16[1320,256]{1,0:T(8,128)(2,1)}, bf16[1320,256]{1,0:T(8,128)(2,1)}, u32[]{:S(2)}, u32[]{:S(2)}) collective-permute-start(bf16[1320,256]{1,0:T(8,128)(2,1)} %pad_maximum_fusion.18), channel_id=1, source_target_pairs={{0,2},{2,0},{4,6},{6,4},{8,10},{10,8},{12,14},{14,12},{16,18},{18,... | collective-permute-start | bytes 2027528 | tf_op jit(solution)/shard_map/ppermute | solution.py:364
  570.0 48.3 %collective-permute-start.18 = (bf16[512,2048]{1,0:T(8,128)(2,1)}, bf16[512,2048]{1,0:T(8,128)(2,1)}, u32[]{:S(2)}, u32[]{:S(2)}) collective-permute-start(bf16[512,2048]{1,0:T(8,128)(2,1)} %add_convert_fusion.8), channel_id=1, source_target_pairs={{0,1},{1,0},{2,3},{3,2},{4,5},{5,4},{6,7},{7,6},{8,9},{9,8},{10,11... | collective-permute-start | bytes 6291464 | tf_op jit(solution)/shard_map/ppermute | solution.py:359
  571.3 71.2 %collective-permute-start.22 = (bf16[512,3072]{1,0:T(8,128)(2,1)}, bf16[512,3072]{1,0:T(8,128)(2,1)S(1)}, u32[]{:S(2)}, u32[]{:S(2)}) collective-permute-start(bf16[512,3072]{1,0:T(8,128)(2,1)} %add_convert_fusion.1), channel_id=1, source_target_pairs={{0,4},{2,6},{4,0},{6,2},{8,12},{10,14},{12,8},{14,10},{16,20},{18,... | collective-permute-start | bytes 9437192 | tf_op jit(solution)/shard_map/ppermute | solution.py:364
  571.8 74.0 %collective-permute-start.21 = (bf16[128,3072]{1,0:T(8,128)(2,1)}, bf16[128,3072]{1,0:T(8,128)(2,1)}, u32[]{:S(2)}, u32[]{:S(2)}) collective-permute-start(bf16[128,3072]{1,0:T(8,128)(2,1)} %add_convert_fusion.26), channel_id=1, source_target_pairs={{0,8},{2,10},{4,12},{6,14},{8,0},{10,2},{12,4},{14,6},{16,24},{18,... | collective-permute-start | bytes 2359304 | tf_op jit(solution)/shard_map/ppermute | solution.py:364
  573.4 76.7 %collective-permute-start.20 = (bf16[256,3072]{1,0:T(8,128)(2,1)}, bf16[256,3072]{1,0:T(8,128)(2,1)S(1)}, u32[]{:S(2)}, u32[]{:S(2)}) collective-permute-start(bf16[256,3072]{1,0:T(8,128)(2,1)} %get-tuple-element.244), channel_id=1, source_target_pairs={{0,16},{2,18},{4,20},{6,22},{8,24},{10,26},{12,28},{14,30},{16,0},... | collective-permute-start | bytes 4718600 | tf_op jit(solution)/shard_map/ppermute | solution.py:364
  575.9 159.2 %collective-permute-start.19 = (bf16[512,1280]{1,0:T(8,128)(2,1)S(1)}, bf16[512,1280]{1,0:T(8,128)(2,1)}, u32[]{:S(2)}, u32[]{:S(2)}) collective-permute-start(bf16[512,1280]{1,0:T(8,128)(2,1)S(1)} %copy-done.67), channel_id=1, source_target_pairs={{0,4},{2,6},{4,0},{6,2},{8,12},{10,14},{12,8},{14,10},{16,20},{18,... | collective-permute-start | bytes 3932168 | tf_op jit(solution)/shard_map/ppermute | solution.py:364
  584.0 42.0 %copy-start.26 = (bf16[512,2048]{1,0:T(8,128)(2,1)S(1)}, bf16[512,2048]{1,0:T(8,128)(2,1)}, u32[]{:S(2)}) copy-start(bf16[512,2048]{1,0:T(8,128)(2,1)} %copy-done.25) | copy-start | bytes 6291460
  584.0 42.0 %copy-start.62 = (bf16[512,2048]{1,0:T(8,128)(2,1)S(1)}, bf16[512,2048]{1,0:T(8,128)(2,1)}, u32[]{:S(2)}) copy-start(bf16[512,2048]{1,0:T(8,128)(2,1)} %convolution_convert_fusion.6) | copy-start | bytes 6291460
  584.0 42.0 %copy-start.81 = (f32[512]{0:T(512)S(1)}, f32[512]{0:T(512)}, u32[]{:S(2)}) copy-start(f32[512]{0:T(512)} %copy-done.80) | copy-start | bytes 6148
  618.4 128.8 %collective-permute-start.27 = (bf16[512,1280]{1,0:T(8,128)(2,1)S(1)}, bf16[512,1280]{1,0:T(8,128)(2,1)}, u32[]{:S(2)}, u32[]{:S(2)}) collective-permute-start(bf16[512,1280]{1,0:T(8,128)(2,1)S(1)} %copy-done.66), channel_id=1, source_target_pairs={{0,4},{2,6},{4,0},{6,2},{8,12},{10,14},{12,8},{14,10},{16,20},{18,... | collective-permute-start | bytes 3932168 | tf_op jit(solution)/shard_map/ppermute | solution.py:364
  642.5 142.1 %collective-permute-start.24 = (bf16[512,1280]{1,0:T(8,128)(2,1)}, bf16[512,1280]{1,0:T(8,128)(2,1)}, u32[]{:S(2)}, u32[]{:S(2)}) collective-permute-start(bf16[512,1280]{1,0:T(8,128)(2,1)} %fusion.25), channel_id=1, source_target_pairs={{0,4},{2,6},{4,0},{6,2},{8,12},{10,14},{12,8},{14,10},{16,20},{18,... | collective-permute-start | bytes 3932168 | tf_op jit(solution)/shard_map/ppermute | solution.py:364
  645.9 87.6 %collective-permute-start.34 = (bf16[680,256]{1,0:T(8,128)(2,1)S(1)}, bf16[680,256]{1,0:T(8,128)(2,1)S(1)}, u32[]{:S(2)}, u32[]{:S(2)}) collective-permute-start(bf16[680,256]{1,0:T(8,128)(2,1)S(1)} %pad_maximum_fusion.19), channel_id=1, source_target_pairs={{0,4},{2,6},{4,0},{6,2},{8,12},{10,14},{12,8},{14,10},{16,20},{18,... | collective-permute-start | bytes 1044488 | tf_op jit(solution)/shard_map/ppermute | solution.py:364
  647.4 86.6 %copy-start.41 = (bf16[256,3072]{1,0:T(8,128)(2,1)S(1)}, bf16[256,3072]{1,0:T(8,128)(2,1)}, u32[]{:S(2)}) copy-start(bf16[256,3072]{1,0:T(8,128)(2,1)} %get-tuple-element.243) | copy-start | bytes 4718596
  650.1 94.5 %copy-start.63 = (bf16[256,3072]{1,0:T(8,128)(2,1)}, bf16[256,3072]{1,0:T(8,128)(2,1)S(1)}, u32[]{:S(2)}) copy-start(bf16[256,3072]{1,0:T(8,128)(2,1)S(1)} %collective-permute-done.20) | copy-start | bytes 4718596
  650.1 130.4 %collective-permute-start.25 = (bf16[256,3072]{1,0:T(8,128)(2,1)}, bf16[256,3072]{1,0:T(8,128)(2,1)}, u32[]{:S(2)}, u32[]{:S(2)}) collective-permute-start(bf16[256,3072]{1,0:T(8,128)(2,1)} %get-tuple-element.242), channel_id=1, source_target_pairs={{0,16},{2,18},{4,20},{6,22},{8,24},{10,26},{12,28},{14,30},{16,0},... | collective-permute-start | bytes 4718600 | tf_op jit(solution)/shard_map/ppermute | solution.py:364
  733.6 10.9 %collective-permute-start.35 = (bf16[360,256]{1,0:T(8,128)(2,1)S(1)}, bf16[360,256]{1,0:T(8,128)(2,1)S(1)}, u32[]{:S(2)}, u32[]{:S(2)}) collective-permute-start(bf16[360,256]{1,0:T(8,128)(2,1)S(1)} %pad_maximum_fusion.20), channel_id=1, source_target_pairs={{0,16},{2,18},{4,20},{6,22},{8,24},{10,26},{12,28},{14,30},{16,0},... | collective-permute-start | bytes 552968 | tf_op jit(solution)/shard_map/ppermute | solution.py:364
  735.1 42.2 %collective-permute-start.26 = (bf16[128,3072]{1,0:T(8,128)(2,1)}, bf16[128,3072]{1,0:T(8,128)(2,1)}, u32[]{:S(2)}, u32[]{:S(2)}) collective-permute-start(bf16[128,3072]{1,0:T(8,128)(2,1)} %add_convert_fusion.24), channel_id=1, source_target_pairs={{0,8},{2,10},{4,12},{6,14},{8,0},{10,2},{12,4},{14,6},{16,24},{18,... | collective-permute-start | bytes 2359304 | tf_op jit(solution)/shard_map/ppermute | solution.py:364
  744.6 25.8 %collective-permute-start.36 = (bf16[200,256]{1,0:T(8,128)(2,1)S(1)}, bf16[200,256]{1,0:T(8,128)(2,1)S(1)}, u32[]{:S(2)}, u32[]{:S(2)}) collective-permute-start(bf16[200,256]{1,0:T(8,128)(2,1)S(1)} %pad_maximum_fusion.22), channel_id=1, source_target_pairs={{0,8},{2,10},{4,12},{6,14},{8,0},{10,2},{12,4},{14,6},{16,24},{18,... | collective-permute-start | bytes 307208 | tf_op jit(solution)/shard_map/ppermute | solution.py:364
  747.2 39.8 %collective-permute-start.23 = (bf16[256,1280]{1,0:T(8,128)(2,1)}, bf16[256,1280]{1,0:T(8,128)(2,1)}, u32[]{:S(2)}, u32[]{:S(2)}) collective-permute-start(bf16[256,1280]{1,0:T(8,128)(2,1)} %get-tuple-element.252), channel_id=1, source_target_pairs={{0,16},{2,18},{4,20},{6,22},{8,24},{10,26},{12,28},{14,30},{16,0},... | collective-permute-start | bytes 1966088 | tf_op jit(solution)/shard_map/ppermute | solution.py:364
  770.5 6.6 collective-permute-start.37
  777.1 30.1 %collective-permute-start.31 = (bf16[256,1280]{1,0:T(8,128)(2,1)}, bf16[256,1280]{1,0:T(8,128)(2,1)}, u32[]{:S(2)}, u32[]{:S(2)}) collective-permute-start(bf16[256,1280]{1,0:T(8,128)(2,1)} %get-tuple-element.254), channel_id=1, source_target_pairs={{0,16},{2,18},{4,20},{6,22},{8,24},{10,26},{12,28},{14,30},{16,0},... | collective-permute-start | bytes 1966088 | tf_op jit(solution)/shard_map/ppermute | solution.py:364
  782.2 37.7 %collective-permute-start.30 = (bf16[128,3072]{1,0:T(8,128)(2,1)S(1)}, bf16[128,3072]{1,0:T(8,128)(2,1)S(1)}, u32[]{:S(2)}, u32[]{:S(2)}) collective-permute-start(bf16[128,3072]{1,0:T(8,128)(2,1)S(1)} %add_convert_fusion.22), channel_id=1, source_target_pairs={{0,8},{2,10},{4,12},{6,14},{8,0},{10,2},{12,4},{14,6},{16,24},{18,... | collective-permute-start | bytes 2359304 | tf_op jit(solution)/shard_map/ppermute | solution.py:364
  786.2 48.9 %collective-permute-start.29 = (bf16[256,1280]{1,0:T(8,128)(2,1)S(1)}, bf16[256,1280]{1,0:T(8,128)(2,1)S(1)}, u32[]{:S(2)}, u32[]{:S(2)}) collective-permute-start(bf16[256,1280]{1,0:T(8,128)(2,1)S(1)} %get-tuple-element.250), channel_id=1, source_target_pairs={{0,16},{2,18},{4,20},{6,22},{8,24},{10,26},{12,28},{14,30},{16,0},... | collective-permute-start | bytes 1966088 | tf_op jit(solution)/shard_map/ppermute | solution.py:364
  788.0 59.3 %collective-permute-start.28 = (bf16[128,1280]{1,0:T(8,128)(2,1)S(1)}, bf16[128,1280]{1,0:T(8,128)(2,1)S(1)}, u32[]{:S(2)}, u32[]{:S(2)}) collective-permute-start(bf16[128,1280]{1,0:T(8,128)(2,1)S(1)} %add_convert_fusion.37), channel_id=1, source_target_pairs={{0,8},{2,10},{4,12},{6,14},{8,0},{10,2},{12,4},{14,6},{16,24},{18,... | collective-permute-start | bytes 983048 | tf_op jit(solution)/shard_map/ppermute | solution.py:364
  808.3 36.8 %collective-permute-start.32 = (bf16[128,1280]{1,0:T(8,128)(2,1)S(1)}, bf16[128,1280]{1,0:T(8,128)(2,1)S(1)}, u32[]{:S(2)}, u32[]{:S(2)}) collective-permute-start(bf16[128,1280]{1,0:T(8,128)(2,1)S(1)} %add_convert_fusion.36), channel_id=1, source_target_pairs={{0,8},{2,10},{4,12},{6,14},{8,0},{10,2},{12,4},{14,6},{16,24},{18,... | collective-permute-start | bytes 983048 | tf_op jit(solution)/shard_map/ppermute | solution.py:364
  835.2 18.6 %collective-permute-start.38 = (bf16[128,1280]{1,0:T(8,128)(2,1)S(1)}, bf16[128,1280]{1,0:T(8,128)(2,1)S(1)}, u32[]{:S(2)}, u32[]{:S(2)}) collective-permute-start(bf16[128,1280]{1,0:T(8,128)(2,1)S(1)} %add_convert_fusion.35), channel_id=1, source_target_pairs={{0,8},{2,10},{4,12},{6,14},{8,0},{10,2},{12,4},{14,6},{16,24},{18,... | collective-permute-start | bytes 983048 | tf_op jit(solution)/shard_map/ppermute | solution.py:364
  849.4 3.9 collective-permute-start.33
  (117 other events, 1382.3 us)

commit v3 on v2

--- a/solution.py
+++ b/solution.py
@@ -11,6 +11,7 @@
 F32, BF16 = jnp.float32, jnp.bfloat16
 STEP = 64
 GELU_A, GELU_B = 0.7978845608028654, 0.044715
+MESH = pl.DeviceIdType.MESH
 
 
 def one_minus_exp(value, exp_neg):
@@ -120,7 +121,7 @@
 
 
 def rec_bwd_kernel(
-    count, bits, bx_own, bx_oth, by_own, by_oth, state_ref, up_own, up_oth, mask_ref, prm_ref, gate_ref,
+    count, bx_own, bx_oth, by_own, by_oth, state_ref, up_own, up_oth, mask_ref, prm_ref, gate_ref,
     gx_own, gx_oth, gy_own, gy_oth, gw_ref, sum_ref, xs, cs, pre, ys, up_ref, gx_ref, gy_ref, gw, dg, gc,
 ):
     place = lax.axis_index("tp")
@@ -187,12 +188,10 @@
     gw[0:lanes, :] = matmul_left(cs[...], dg[:, 0:lanes]).astype(BF16)
     gw[lanes:, :] = matmul_left(cs[...], dg[:, lanes:]).astype(BF16)
     rows_each = lanes // count
-    me = lax.axis_index("dp")
-    for spot in range(count):
-        block = block_from(me, spot, bits)
+    for block in range(count):
         for gate in (0, 1):
-            source = pl.ds(pl.multiple_of(gate * lanes + block * rows_each, rows_each), rows_each)
-            gw_ref[spot, 0, gate * rows_each : (gate + 1) * rows_each, :] = gw[source, :]
+            source = gate * lanes + block * rows_each
+            gw_ref[block, 0, gate * rows_each : (gate + 1) * rows_each, :] = gw[source : source + rows_each, :]
     taps = [prm_ref[k : k + 1, :] for k in range(4)]
 
     def conv_step(index, sums):
@@ -266,7 +265,7 @@
     length, lanes, heads = 2 * half, gates.shape[2], gates.shape[1]
     piece, whole, mask_spec, prm_spec, gate_spec = rec_specs(half, lanes, length)
     return pl.pallas_call(
-        functools.partial(rec_bwd_kernel, count, stage_bits(count)),
+        functools.partial(rec_bwd_kernel, count),
         grid=(heads,),
         in_specs=[piece] * 4 + [whole, piece, piece, mask_spec, prm_spec, gate_spec],
         out_specs=[piece] * 4 + [pl.BlockSpec((count, 1, 2 * lanes // count, lanes), lambda h: (0, h, 0, 0)), prm_spec],
@@ -294,9 +293,9 @@
     )(bx_own, bx_oth, by_own, by_oth, states, up_own, up_oth, mask, prm, gates)
 
 
-def stage_bits(count):
-    bits = count.bit_length() - 1
-    return [1 << bit for bit in ([0, 1] + list(reversed(range(2, bits))))[:bits]]
+def stage_bits(count, crossed=False):
+    bits = [1 << bit for bit in range(count.bit_length() - 1)]
+    return [bits[0], bits[2], bits[1]] + bits[3:] if crossed else bits
 
 
 def block_at(place, bits):
@@ -312,20 +311,14 @@
     return block
 
 
-def arrange_kernel(count, bits, steps, first, second, *parts):
+def arrange_kernel(count, bits, steps, first, second, out):
     me = lax.axis_index("dp")
     cols = first.shape[1] // count
 
     def move(piece):
         for place in range(count):
             source = pl.ds(pl.multiple_of(block_from(me, place, bits) * cols, cols), cols)
-            if place < count // 4:
-                into, spot = parts[0], place
-            elif place < count // 2:
-                into, spot = parts[1], place - count // 4
-            else:
-                into, spot = parts[2], place - count // 2
-            into[:, spot * cols : (spot + 1) * cols] = piece[:, source]
+            out[:, place * cols : (place + 1) * cols] = piece[:, source]
 
     @pl.when(pl.program_id(0) < steps)
     def _():
@@ -336,23 +329,132 @@
         move(second)
 
 
-def arrange(first, second, count):
+def arrange(first, second, bits):
     half, width = first.shape
     steps = 2
     block = half // steps
-    widths = width // 4, width // 4, width // 2
     return pl.pallas_call(
-        functools.partial(arrange_kernel, count, stage_bits(count), steps),
+        functools.partial(arrange_kernel, 1 << len(bits), bits, steps),
         grid=(2 * steps,),
         in_specs=[
             pl.BlockSpec((block, width), lambda i: (jnp.minimum(i, steps - 1), 0)),
             pl.BlockSpec((block, width), lambda i: (jnp.maximum(i - steps, 0), 0)),
         ],
-        out_specs=[pl.BlockSpec((block, cols), lambda i: (i, 0)) for cols in widths],
-        out_shape=[jax.ShapeDtypeStruct((2 * half, cols), first.dtype) for cols in widths],
-        cost_estimate=pl.CostEstimate(flops=0, bytes_accessed=8 * half * width, transcendentals=0),
+        out_specs=pl.BlockSpec((block, width), lambda i: (i, 0)),
+        out_shape=jax.ShapeDtypeStruct((2 * half, width), first.dtype),
+        cost_estimate=pl.CostEstimate(flops=0, bytes_accessed=12 * half * width, transcendentals=0),
         name="arrange",
     )(first, second)
+
+
+def tile_cols(step):
+    return lax.rem((step + 1) // 2, 2)
+
+
+def weight_grad_kernel(left_own, left_oth, right_own, right_oth, sent_next, kept, staged, landed, send_sem, recv_sem):
+    step = pl.program_id(0)
+    me = lax.axis_index("dp")
+    partner = {"dp": me + 1 - 2 * lax.rem(me, 2)}
+
+    @pl.when(step == 0)
+    def _():
+        barrier = pltpu.get_barrier_semaphore()
+        pl.semaphore_signal(barrier, inc=1, device_id=partner, device_id_type=MESH)
+        pl.semaphore_wait(barrier, 1)
+
+    def copy(tile):
+        return pltpu.make_async_remote_copy(
+            src_ref=staged.at[tile],
+            dst_ref=landed.at[tile],
+            send_sem=send_sem.at[tile],
+            recv_sem=recv_sem.at[tile],
+            device_id=partner,
+            device_id_type=MESH,
+        )
+
+    total = matmul_left(left_own[...], right_own[...]) + matmul_left(left_oth[...], right_oth[...])
+
+    @pl.when(step < 4)
+    def _():
+        staged[step] = total.astype(BF16)
+        copy(step).start()
+
+    @pl.when(step >= 4)
+    def _():
+        copy(step - 4).wait_recv()
+        value = (total + landed[step - 4].astype(F32)).astype(BF16)
+
+        @pl.when(step < 6)
+        def _():
+            sent_next[...] = value
+
+        @pl.when(step >= 6)
+        def _():
+            kept[...] = value
+
+    @pl.when(step == 7)
+    def _():
+        for tile in range(4):
+            copy(tile).wait_send()
+
+
+def weight_grad(left, right_own, right_oth, ident):
+    half, cols = right_own.shape
+    rows = left.shape[1] // 4
+    wide = cols // 2
+    out = pltpu.HBM((rows, cols), BF16)
+    return pl.pallas_call(
+        weight_grad_kernel,
+        grid=(8,),
+        in_specs=[
+            pl.BlockSpec((half, rows), lambda i: (0, 3 - i // 2)),
+            pl.BlockSpec((half, rows), lambda i: (1, 3 - i // 2)),
+            pl.BlockSpec((half, wide), lambda i: (0, tile_cols(i))),
+            pl.BlockSpec((half, wide), lambda i: (0, tile_cols(i))),
+        ],
+        out_specs=[
+            pl.BlockSpec((rows, wide), lambda i: (0, jnp.where(i < 5, 0, 1))),
+            pl.BlockSpec((rows, wide), lambda i: (0, jnp.where(i < 7, 1, 0))),
+        ],
+        out_shape=[out, out],
+        scratch_shapes=[
+            pltpu.VMEM((4, rows, wide), BF16),
+            pltpu.VMEM((4, rows, wide), BF16),
+            pltpu.SemaphoreType.DMA((4,)),
+            pltpu.SemaphoreType.DMA((4,)),
+        ],
+        compiler_params=pltpu.CompilerParams(
+            collective_id=ident, has_side_effects=True, vmem_limit_bytes=48 << 20
+        ),
+        cost_estimate=pl.CostEstimate(
+            flops=16 * half * rows * cols, bytes_accessed=16 * half * cols, transcendentals=0
+        ),
+        name="weight_grad",
+    )(left, left, right_own, right_oth)
+
+
+def two_back_kernel(first, first_w, second, second_w, out):
+    out[...] = (matmul_right(first[...], first_w[...]) + matmul_right(second[...], second_w[...])).astype(BF16)
+
+
+def two_back(first, first_w, second, second_w):
+    rows, depth = first.shape
+    cols = first_w.shape[0]
+    step = 512
+    left = pl.BlockSpec((rows, depth), lambda n: (0, 0))
+    right = pl.BlockSpec((step, depth), lambda n: (n, 0))
+    return pl.pallas_call(
+        two_back_kernel,
+        grid=(cols // step,),
+        in_specs=[left, right, left, right],
+        out_specs=pl.BlockSpec((rows, step), lambda n: (0, n)),
+        out_shape=jax.ShapeDtypeStruct((rows, cols), BF16),
+        compiler_params=pltpu.CompilerParams(vmem_limit_bytes=48 << 20),
+        cost_estimate=pl.CostEstimate(
+            flops=4 * rows * depth * cols, bytes_accessed=4 * depth * (rows + cols), transcendentals=0
+        ),
+        name="two_back",
+    )(first, first_w, second, second_w)
 
 
 def swap(value):
@@ -365,33 +467,26 @@
 
 
 class Reduction:
-    def __init__(self, parts, right, bits):
-        self.keep_cols, self.next_cols, self.first_cols = parts
-        self.right, self.bits = right, list(bits)
-
-    def send(self, *others):
-        sent = matmul_left(after(self.first_cols, *others), self.right).astype(BF16)
+    def __init__(self, left, right, bits, ident):
+        self.bits = list(bits[1:])
+        sent, self.keep = weight_grad(left, *right, ident)
+        self.pass_on(sent)
+
+    def pass_on(self, sent):
         self.received = flip(sent, self.bits.pop(0))
-        return sent
-
-    def send_next(self, *others):
-        received = self.received
-        middle = received.shape[0] // 2
-        left, received = lax.optimization_barrier((self.next_cols, received, *others))[:2]
-        sent = (matmul_left(left, self.right) + received[middle:].astype(F32)).astype(BF16)
-        self.received = flip(sent, self.bits.pop(0))
-        self.keep = (matmul_left(after(self.keep_cols, sent), self.right) + received[:middle].astype(F32)).astype(BF16)
-        return self.keep
 
     def step(self, *others):
         received = after(self.received, *others)
         middle = received.shape[0] // 2
         sent = (self.keep[middle:].astype(F32) + received[middle:].astype(F32)).astype(BF16)
-        self.keep = (self.keep[:middle].astype(F32) + received[:middle].astype(F32)).astype(BF16)
-        self.received = flip(sent, self.bits.pop(0))
+        keep = (self.keep[:middle].astype(F32) + received[:middle].astype(F32)).astype(BF16)
+        sent, self.keep = lax.optimization_barrier((sent, keep))
+        self.pass_on(sent)
         return sent
 
     def total(self, *others):
+        while self.bits:
+            self.step(*others)
         return self.keep.astype(F32) + after(self.received, *others).astype(F32)
 
 
@@ -412,7 +507,7 @@
     place = lax.axis_index("tp")
     me = lax.axis_index("dp")
     count = lax.axis_size("dp")
-    bits = stage_bits(count)
+    bits, crossed = stage_bits(count), stage_bits(count, True)
     width = w_x.shape[1]
     full_width = conv_w.shape[1]
     heads = gate_blocks.shape[1] // 2
@@ -443,13 +538,13 @@
     by_oth = matmul(normed_oth, w_y)
     gated_own, gated_oth, states = rec_fwd(bx_own, bx_oth, by_own, by_oth, mask, prm, gates)
 
-    gated = jnp.concatenate([gated_own, gated_oth], axis=0)
     part_oth = matmul(gated_oth, w_out).astype(BF16)
     swap_own = swap(part_oth)
     part_own = matmul(after(gated_own, part_oth), w_out).astype(BF16)
     swap_oth = swap(part_own)
     gh_oth = matmul_right(after(oth_cot, part_own), w_down)
-    cot_cols = arrange(after(own_cot, gh_oth), oth_cot, count)
+    cot_cols = arrange(after(own_cot, gh_oth), oth_cot, crossed)
+    normed_cols = arrange(after(normed_own, cot_cols), normed_oth, bits)
 
     def feed_in(tokens, part, other):
         middle = tokens.astype(F32) + (part.astype(F32) + other.astype(F32))
@@ -464,102 +559,77 @@
         grad_gate, grad_up = pull(grad_hidden)
         return grad_gate.astype(BF16), grad_up.astype(BF16)
 
-    def feed_back(grad_gate, grad_up):
-        return (matmul_right(grad_gate, w_gate) + matmul_right(grad_up, w_up)).astype(BF16)
-
-    def norm_two_back(middle, back, other, cot):
-        grad = cot.astype(F32) + norm_back(middle, norm_gains[1], back.astype(F32) + other.astype(F32))
+    def norm_two_back(middle, back, cot):
+        grad = cot.astype(F32) + norm_back(middle, norm_gains[1], back)
         return grad, grad.astype(BF16)
 
-    middle_own, normed_two_own, gate_own, up_own, hidden_own = feed_in(own_in, part_own, after(swap_own, *cot_cols))
+    middle_own, normed_two_own, gate_own, up_own, hidden_own = feed_in(own_in, part_own, after(swap_own, normed_cols))
     gg_own, gu_own = feed_grads(gate_own, up_own, after(gh_own, hidden_own))
-    middle_oth, normed_two_oth, gate_oth, up_oth, hidden_oth = feed_in(oth_in, part_oth, after(swap_oth, gg_own, gu_own))
-    down = Reduction(cot_cols, jnp.concatenate([hidden_own, hidden_oth], axis=0), bits)
-    done = down.send()
-    gg_oth, gu_oth = feed_grads(gate_oth, up_oth, after(gh_oth, done))
-    normed_two_cols = arrange(after(normed_two_own, gg_oth, gu_oth), normed_two_oth, count)
-    done = down.send_next(*normed_two_cols)
-    back_own = feed_back(after(gg_own, done), gu_own)
+    back_own = two_back(gg_own, w_gate, gu_own, w_up)
     back_own_swapped = swap(back_own)
-    gate = Reduction(normed_two_cols, jnp.concatenate([gg_own, gg_oth], axis=0), bits)
-    up = Reduction(normed_two_cols, jnp.concatenate([gu_own, gu_oth], axis=0), bits)
-    done = gate.send(back_own)
-    done = up.send(done)
-    done = gate.send_next(done)
-    back_oth = feed_back(after(gg_oth, done), gu_oth)
+    middle_oth, normed_two_oth, gate_oth, up_oth, hidden_oth = feed_in(oth_in, part_oth, after(swap_oth, back_own))
+    down = Reduction(after(cot_cols, hidden_oth), (hidden_own, hidden_oth), crossed, 1)
+    gg_oth, gu_oth = feed_grads(gate_oth, up_oth, after(gh_oth, down.keep))
+    normed_two_cols = arrange(after(normed_two_own, gg_oth, gu_oth), normed_two_oth, bits)
+    gate = Reduction(normed_two_cols, (gg_own, gg_oth), bits, 1)
+    back_oth = two_back(after(gg_oth, gate.keep), w_gate, gu_oth, w_up)
     back_oth_swapped = swap(back_oth)
-    done = up.send_next(back_oth)
-    done = down.step(done)
-    out_send = matmul(after(hidden_oth, done), w_down).astype(BF16)
+    oth_sum = (back_oth.astype(F32) + back_own_swapped.astype(F32)).astype(BF16)
+    up = Reduction(after(normed_two_cols, oth_sum), (gu_own, gu_oth), bits, 1)
+    done = down.step(up.keep)
+    _, rec_oth = norm_two_back(middle_oth, after(oth_sum, done).astype(F32), oth_cot)
+    into_oth = matmul_right(rec_oth, w_out)
+    out_send = matmul(after(hidden_oth, into_oth), w_down).astype(BF16)
     out_swapped = swap(out_send)
-    out_keep = matmul(after(hidden_own, out_send), w_down).astype(BF16)
-
-    grad_own, rec_own = norm_two_back(middle_own, back_own, after(back_oth_swapped, out_keep), own_cot)
-    _, rec_oth = norm_two_back(middle_oth, back_oth, after(back_own_swapped, out_keep), oth_cot)
+    done = gate.step(out_send)
+    own_sum = back_own.astype(F32) + after(back_oth_swapped, done).astype(F32)
+    grad_own, rec_own = norm_two_back(middle_own, own_sum, own_cot)
     into_own = matmul_right(rec_own, w_out)
-    into_oth = matmul_right(rec_oth, w_out)
-    gx_own, gx_oth, gy_own, gy_oth, gate_grad, sums = rec_bwd(
-        bx_own, bx_oth, by_own, by_oth, states, into_own, into_oth, mask, prm, gates, count
-    )
-    done = gate.step(gx_own, down.step(gx_own))
-    rec_cols = arrange(after(rec_own, done), rec_oth, count)
-    normed_cols = arrange(after(normed_own, *rec_cols), normed_oth, count)
-    in_x = Reduction(normed_cols, jnp.concatenate([gx_own, gx_oth], axis=0), bits)
-    in_y = Reduction(normed_cols, jnp.concatenate([gy_own, gy_oth], axis=0), bits)
-    out = Reduction(rec_cols, gated, bits)
-    done = in_x.send(*normed_cols)
-    done = in_y.send(done)
-    done = out.send(done)
-    done = in_x.send_next(done)
-    done = in_y.send_next(done)
-    done = out.send_next(done)
-
-    def rec_back(piece_x, piece_y):
-        return (matmul_right(piece_x, w_x) + matmul_right(piece_y, w_y)).astype(BF16)
-
-    rec_send = rec_back(after(gx_oth, done), gy_oth)
-    rec_swapped = swap(rec_send)
-    layer_out = (middle_own + out_keep.astype(F32) + after(out_swapped, rec_send).astype(F32)).astype(BF16)
-    lanes = gate_grad.shape[-1]
-    blocks = gate_grad.reshape(-1, lanes)
+    rec_cols = arrange(after(rec_own, into_own), rec_oth, crossed)
+    gx_own, gx_oth, gy_own, gy_oth, gate_sums, sums = rec_bwd(
+        bx_own, bx_oth, by_own, by_oth, states, after(into_own, rec_cols), into_oth, mask, prm, gates, count
+    )
+
+    lanes = gate_sums.shape[-1]
     row = jnp.arange(8)[:, None] == 7
     slopes = -8.0 * lax.dynamic_slice(jax.nn.sigmoid(a_param), (place * width,), (width,))
-    sums = jnp.where(row, sums * slopes, sums).astype(BF16).reshape(-1, lanes)
-    done = rec_send
-    for bit in bits:
-        middle = blocks.shape[0] // 2
-        message = jnp.concatenate([blocks[middle:], sums], axis=0)
-        received = after(flip(message, bit), done).astype(F32)
-        blocks = (blocks[:middle].astype(F32) + received[:middle]).astype(BF16)
-        sums = (sums.astype(F32) + received[middle:]).astype(BF16)
-        if bit == bits[0]:
-            rec_keep = rec_back(after(gx_own, blocks), gy_own)
-            done = rec_keep
-    message = jnp.concatenate([blocks, sums], axis=0)
-    others = swap(message)
-    low, high = jnp.where(first_place, message, others), jnp.where(first_place, others, message)
-    n_blocks = blocks.shape[0]
-    block_sums = jnp.stack([low[:n_blocks], high[:n_blocks]]).astype(F32).reshape(2 * heads, 2, -1, lanes)
-    small = jnp.concatenate([low[n_blocks:].reshape(8, width), high[n_blocks:].reshape(8, width)], axis=1)
-    small = lax.dynamic_slice(small, (0, me * (full_width // count)), (8, full_width // count)).astype(F32)
-
-    grad_normed = rec_keep.astype(F32) + rec_swapped.astype(F32)
+    each = full_width // count
+    sums = jnp.swapaxes(jnp.where(row, sums * slopes, sums).reshape(8, count // 2, each), 0, 1)
+    sums = jnp.pad(jnp.concatenate([sums, sums], axis=0), ((0, 0), (0, 0), (0, lanes - each))).astype(BF16)
+    blocks = jnp.concatenate([gate_sums.reshape(count, -1, lanes), sums], axis=1)
+    blocks = lax.psum_scatter(blocks.reshape(-1, lanes), "dp", scatter_dimension=0, tiled=True)
+
+    done = up.step(gx_own)
+    done = down.step(done)
+    done = gate.step(done)
+    in_x = Reduction(after(normed_cols, done), (gx_own, gx_oth), bits, 2)
+    out = Reduction(after(rec_cols, in_x.keep), (gated_own, gated_oth), crossed, 2)
+    done = up.step(out.keep)
+    in_y = Reduction(after(normed_cols, done), (gy_own, gy_oth), bits, 2)
+    rec_send = two_back(after(gx_oth, in_y.keep), w_x, gy_oth, w_y)
+    rec_swapped = swap(rec_send)
+    down_grad = down.total(rec_send)
+    gate_grad = gate.total(rec_send)
+    done = in_x.step(down_grad, gate_grad)
+    rec_keep = two_back(after(gx_own, done), w_x, gy_own, w_y)
+    done = out.step(rec_keep)
+    out_keep = matmul(after(hidden_own, done), w_down).astype(BF16)
+    layer_out = (middle_own + out_keep.astype(F32) + after(out_swapped, out_keep).astype(F32)).astype(BF16)
+    up_grad = up.total(layer_out)
+    done = in_x.step(layer_out, up_grad)
+    done = in_y.step(done)
+    grad_normed = rec_keep.astype(F32) + after(rec_swapped, done).astype(F32)
     input_grad = grad_own + norm_back(own_in.astype(F32), norm_gains[0], grad_normed)
-    done = up.step(input_grad)
-    down_grad = down.total(done)
-    done = gate.step(down_grad)
-    done = in_x.step(done)
+    done = out.step(input_grad)
     done = in_y.step(done)
-    gate_grad = gate.total(done)
-    done = up.step(gate_grad)
-    done = out.step(done)
-    done = in_x.step(done)
-    done = in_y.step(done)
-    up_grad = up.total(done)
-    done = out.step(up_grad)
     x_grad = in_x.total(done)
-    y_grad = in_y.total(done)
-    out_grad = out.total()
+    others = swap(after(blocks, x_grad))
+    out_grad = out.total(others)
+    y_grad = in_y.total(out_grad)
+
+    low, high = jnp.where(first_place, blocks, others), jnp.where(first_place, others, blocks)
+    block_sums = jnp.stack([low[:-8], high[:-8]]).astype(F32).reshape(2 * heads, 2, -1, lanes)
+    small = jnp.where(me < count // 2, low[-8:], high[-8:])[:, :each].astype(F32)
 
     block = model // count
 

time: 861 us -> 716 us (0.83)
  matrix products: 315 us -> 131 us
  Pallas kernels: 110 us -> 270 us
  waiting for transfers between devices: 263 us -> 115 us
  other arithmetic: 110 us -> 125 us
  between operations: 2.48 us -> 15.4 us
    pallas_call x5 -> x15, Pallas kernels: 79.1 us -> 239 us  [the longest x6 107 us: weight_grad(): pl.pallas_call(weight_grad_kernel, grid=(8,), in_specs=[pl.BlockSpec((hal...]
    dot_general x18 -> x0, matrix products: 115 us -> none  [matmul_left(): lax.dot_general(first_mat, second_mat, (((0,), (0,)), ((), ())), preferre...]
    ppermute x28 -> x18, waiting for transfers between devices: 185 us -> 77.9 us  [flip(): lax.ppermute(value, 'dp', [(source, source ^ bit) for source in range(cou...]
    dot_general x12 -> x4, matrix products: 104 us -> 34.3 us  [matmul_right(): lax.dot_general(first_mat, second_mat, (((1,), (1,)), ((), ())), preferre...]
    ppermute x11, waiting for transfers between devices: 78.2 us -> 37.1 us  [swap(): return lax.ppermute(value, 'tp', [(0, 1), (1, 0)])]
    convert_element_type x6 -> x12, other arithmetic: 18.3 us -> 27.4 us  [step(): (self.keep[:middle].astype(F32) + received[:middle].astype(F32)).astype(B...]
    ppermute x28 -> x18, starting transfers between devices: 22.7 us -> 19.6 us  [flip(): lax.ppermute(value, 'dp', [(source, source ^ bit) for source in range(cou...]
  transfers between devices with their start and end apart: 39 -> 30, of which waited for: 13 -> 8; matrix products, arithmetic and copies ran while one was open for 41% -> 37% of each run, Pallas kernels for 13% -> 38%
where the time goes in v3:
time: 716 us; the launch traced here: 710 us
  Pallas kernels  270 us (38%)
  matrix products  131 us (18%)
  other arithmetic  125 us (17%)
  waiting for transfers between devices  115 us (16%)
  starting transfers between devices  32.5 us (5%)
  local copies, waits for them, and re-layouts  21 us (3%)
  between operations  15.4 us (2%)
    pallas_call x6, Pallas kernels, weight_grad(): pl.pallas_call(weight_grad_kernel, grid=(8,), in_specs=[pl.BlockSpec((hal...  107 us
    dot_general x12, matrix products, matmul(): return jnp.dot(first_mat, second_mat, preferred_element_type=jnp.float32)  97.2 us
    ppermute x18, waiting for transfers between devices, flip(): lax.ppermute(value, 'dp', [(source, source ^ bit) for source in range(cou...  77.9 us
    pallas_call x1, Pallas kernels, rec_bwd(): pl.pallas_call(functools.partial(rec_bwd_kernel, count), grid=(heads,), i...  57.1 us
    pallas_call x4, Pallas kernels, two_back(): pl.pallas_call(two_back_kernel, grid=(cols // step,), in_specs=[left, rig...  53.3 us
    ppermute x11, waiting for transfers between devices, swap(): return lax.ppermute(value, 'tp', [(0, 1), (1, 0)])  37.1 us
    dot_general x4, matrix products, matmul_right(): lax.dot_general(first_mat, second_mat, (((1,), (1,)), ((), ())), preferre...  34.3 us
    pallas_call x1, Pallas kernels, rec_fwd(): pl.pallas_call(rec_fwd_kernel, grid=(heads,), in_specs=[piece] * 4 + [mas...  30.5 us
  transfers between devices with their start and end apart: 30, of which 8 were waited for; matrix products, arithmetic and copies ran while one was open for 37% of the time, Pallas kernels for 38%

profile of v3, /device:TPU:0, one launch (start us, length us, event | category | flops | bytes accessed | tf_op | source)
XLA Modules:
  0.0 710.2 jit_solution(7322396829760385035)
XLA Ops:
  17.5 7.6 %fusion.50.by_own = f32[512,1280]{1,0:T(8,128)} fusion(bf16[512,2048]{1,0:T(8,128)(2,1)S(1)} %fusion.19.first, bf16[2048,1280]{1,0:T(8,128)(2,1)} %second_w.7), kind=kOutput, calls=%fused_computation.154 | convolution fusion | flops 2684354560 | bytes 9961472 | tf_op jit(solution)/shard_map/dot_general | solution.py:691
  31.3 12.5 %fusion.51 = f32[512,3072]{1,0:T(8,128)} fusion(bf16[512,2048]{1,0:T(8,128)(2,1)} %bitcast.89, bf16[3072,2048]{1,0:T(8,128)(2,1)} %param.27), kind=kOutput, calls=%fused_computation.155 | convolution fusion | flops 6442450944 | bytes 20971520 | tf_op jit(solution)/shard_map/dot_general | solution.py:701
  44.8 14.3 %collective-permute-done = bf16[512,2048]{1,0:T(8,128)(2,1)} collective-permute-done((bf16[512,2048]{1,0:T(8,128)(2,1)}, bf16[512,2048]{1,0:T(8,128)(2,1)}, u32[]{:S(2)}, u32[]{:S(2)}) %collective-permute-start) | collective-permute-done | bytes 2097184 | tf_op jit(solution)/shard_map/ppermute | solution.py:461
  63.5 6.2 fusion.52.by_oth
  73.2 30.5 %rec_fwd.1 = (bf16[512,1280]{1,0:T(8,128)(2,1)S(1)}, bf16[512,1280]{1,0:T(8,128)(2,1)S(1)}, f32[1024,1280]{1,0:T(8,128)}) custom-call(bf16[512,1280]{1,0:T(8,128)(2,1)S(1)} %copy-done.11, bf16[512,1280]{1,0:T(8,128)(2,1)S(1)} %convolution_convert_fusion.4.bx_oth, f32[512,1280]{1,0:T(8,128)S(1)} %copy-done.7, f32[512,1280]{1,0:T(8,128)S(1)} %fusion.52.by_oth, ...), custom_call_target="tpu_custom_call" | custom-call | flops 1473249280 | bytes 20971520 | tf_op jit(solution)/shard_map/rec_fwd/pallas_call | solution.py:242
  103.7 4.1 convolution_convert_fusion.3
  107.8 4.1 convolution_convert_fusion.2
  114.0 10.3 %fusion.53 = f32[512,3072]{1,0:T(8,128)} fusion(bf16[512,2048]{1,0:T(8,128)(2,1)} %collective-permute-done.3.second, bf16[3072,2048]{1,0:T(8,128)(2,1)S(1)} %bitcast.125), kind=kOutput, calls=%fused_computation.157 | convolution fusion | flops 6442450944 | bytes 20971520 | tf_op jit(solution)/shard_map/dot_general | solution.py:701
  124.2 5.4 arrange.4.left_own.left_oth
  129.6 5.5 arrange.5.left_own.left_oth
  135.1 21.5 %collective-permute-done.2 = bf16[512,2048]{1,0:T(8,128)(2,1)} collective-permute-done((bf16[512,2048]{1,0:T(8,128)(2,1)}, bf16[512,2048]{1,0:T(8,128)(2,1)}, u32[]{:S(2)}, u32[]{:S(2)}) %collective-permute-start.2) | collective-permute-done | bytes 2097184 | tf_op jit(solution)/shard_map/ppermute | solution.py:461
  163.7 12.1 %fusion.54 = f32[512,3072]{1,0:T(8,128)} fusion(bf16[512,2048]{1,0:T(8,128)(2,1)S(1)} %multiply_convert_fusion.5.first, bf16[2048,3072]{1,0:T(8,128)(2,1)} %first_w.5), kind=kOutput, calls=%fused_computation.158 | convolution fusion | flops 6442450944 | bytes 20971520 | tf_op jit(solution)/shard_map/dot_general | solution.py:691
  175.8 15.2 %multiply_convert_fusion.3 = (bf16[512,3072]{1,0:T(8,128)(2,1)S(1)}, f32[512,3072]{1,0:T(8,128)}) fusion(f32[512,3072]{1,0:T(8,128)} %fusion.54, bf16[512,2048]{1,0:T(8,128)(2,1)S(1)} %multiply_convert_fusion.5.first, bf16[2048,3072]{1,0:T(8,128)(2,1)} %second_w.5), kind=kOutput, calls=%fused_computation.26 | convolution fusion | flops 6458179584 | bytes 30408704 | tf_op jit(solution)/shard_map/dot_general | solution.py:691
  191.1 10.3 %multiply_convert_fusion.2 = (bf16[512,3072]{1,0:T(8,128)(2,1)}, bf16[512,3072]{1,0:T(8,128)(2,1)S(1)}) fusion(f32[512,3072]{1,0:T(8,128)S(1)} %bitcast.92, f32[512,3072]{1,0:T(8,128)} %fusion.54, f32[512,3072]{1,0:T(8,128)} %get-tuple-element.280), kind=kLoop, calls=%fused_computation.25 | loop fusion | flops 37748736 | bytes 25165824 | tf_op jit(solution)/shard_map/convert_element_type | solution.py:560
  201.4 18.8 %two_back.4 = bf16[512,2048]{1,0:T(8,128)(2,1)S(1)} custom-call(bf16[512,3072]{1,0:T(8,128)(2,1)S(1)} %get-tuple-element.248.first.right_own, bf16[2048,3072]{1,0:T(8,128)(2,1)} %first_w.5, bf16[512,3072]{1,0:T(8,128)(2,1)} %get-tuple-element.247.second.right_own, bf16[2048,3072]{1,0:T(8,128)(2,1)} %second_w.5), custom_call_target="tpu_custom_call" | custom-call | flops 12884901888 | bytes 31457280 | tf_op jit(solution)/shard_map/two_back/pallas_call | solution.py:446
  224.2 4.4 multiply_convert_fusion.4.second
  228.6 10.1 %fusion.55 = f32[512,3072]{1,0:T(8,128)S(1)} fusion(bf16[512,2048]{1,0:T(8,128)(2,1)S(1)} %multiply_convert_fusion.4.second, bf16[2048,3072]{1,0:T(8,128)(2,1)} %first_w.5), kind=kOutput, calls=%fused_computation.159 | convolution fusion | flops 6442450944 | bytes 20971520 | tf_op jit(solution)/shard_map/dot_general | solution.py:691
  241.3 13.1 %multiply_convert_fusion.1 = (bf16[512,3072]{1,0:T(8,128)(2,1)}, f32[512,3072]{1,0:T(8,128)}) fusion(f32[512,3072]{1,0:T(8,128)S(1)} %fusion.55, bf16[512,2048]{1,0:T(8,128)(2,1)S(1)} %multiply_convert_fusion.4.second, bf16[2048,3072]{1,0:T(8,128)(2,1)} %second_w.5), kind=kOutput, calls=%fused_computation.24 | convolution fusion | flops 6458179584 | bytes 30408704 | tf_op jit(solution)/shard_map/dot_general | solution.py:691
  254.4 22.4 %weight_grad.6 = (bf16[512,3072]{1,0:T(8,128)(2,1)}, bf16[512,3072]{1,0:T(8,128)(2,1)}) custom-call(bf16[1024,2048]{1,0:T(8,128)(2,1)} %arrange.4.left_own.left_oth, bf16[1024,2048]{1,0:T(8,128)(2,1)} %arrange.4.left_own.left_oth, bf16[512,3072]{1,0:T(8,128)(2,1)S(1)} %get-tuple-element.169.right_own, bf16[512,3072]{1,0:T(8,128)(2,1)} %get-tuple-element.128.right_oth), custom_call_target="tpu_custom_call" | custom-call | flops 12884901888 | bytes 25165824 | tf_op jit(solution)/shard_map/weight_grad/pallas_call | solution.py:406
  276.9 10.7 %multiply_convert_fusion = (bf16[512,3072]{1,0:T(8,128)(2,1)}, bf16[512,3072]{1,0:T(8,128)(2,1)}) fusion(f32[512,3072]{1,0:T(8,128)S(1)} %bitcast.94, f32[512,3072]{1,0:T(8,128)} %copy-done.44, f32[512,3072]{1,0:T(8,128)} %get-tuple-element.282), kind=kLoop, calls=%fused_computation.23 | loop fusion | flops 37748736 | bytes 25165824 | tf_op jit(solution)/shard_map/convert_element_type | solution.py:560
  287.5 5.4 arrange.6.left_own.left_oth
  296.8 22.7 %weight_grad.7 = (bf16[512,3072]{1,0:T(8,128)(2,1)}, bf16[512,3072]{1,0:T(8,128)(2,1)}) custom-call(bf16[1024,2048]{1,0:T(8,128)(2,1)} %arrange.6.left_own.left_oth, bf16[1024,2048]{1,0:T(8,128)(2,1)} %arrange.6.left_own.left_oth, bf16[512,3072]{1,0:T(8,128)(2,1)S(1)} %copy-done.5, bf16[512,3072]{1,0:T(8,128)(2,1)} %get-tuple-element.120.right_oth.first), custom_call_target="tpu_custom_call" | custom-call | flops 12884901888 | bytes 25165824 | tf_op jit(solution)/shard_map/weight_grad/pallas_call | solution.py:406
  321.1 17.8 %two_back.5 = bf16[512,2048]{1,0:T(8,128)(2,1)S(1)} custom-call(bf16[512,3072]{1,0:T(8,128)(2,1)S(1)} %copy-done.6, bf16[2048,3072]{1,0:T(8,128)(2,1)} %first_w.5, bf16[512,3072]{1,0:T(8,128)(2,1)} %get-tuple-element.245.second.right_oth, bf16[2048,3072]{1,0:T(8,128)(2,1)} %second_w.5), custom_call_target="tpu_custom_call" | custom-call | flops 12884901888 | bytes 31457280 | tf_op jit(solution)/shard_map/two_back/pallas_call | solution.py:446
  343.0 22.4 %weight_grad.8 = (bf16[512,3072]{1,0:T(8,128)(2,1)}, bf16[512,3072]{1,0:T(8,128)(2,1)}) custom-call(bf16[1024,2048]{1,0:T(8,128)(2,1)} %arrange.6.left_own.left_oth, bf16[1024,2048]{1,0:T(8,128)(2,1)} %arrange.6.left_own.left_oth, bf16[512,3072]{1,0:T(8,128)(2,1)S(1)} %copy-done.3, bf16[512,3072]{1,0:T(8,128)(2,1)} %get-tuple-element.245.second.right_oth), custom_call_target="tpu_custom_call" | custom-call | flops 12884901888 | bytes 25165824 | tf_op jit(solution)/shard_map/weight_grad/pallas_call | solution.py:406
  366.0 5.7 add_convert_fusion.7
  373.2 4.1 multiply_reduce_fusion.1
  377.4 5.1 add_convert_fusion.1.second
  383.7 7.1 fusion.56.up_oth
  390.9 8.0 %convolution_convert_fusion.1 = bf16[512,2048]{1,0:T(8,128)(2,1)} fusion(bf16[512,3072]{1,0:T(8,128)(2,1)S(1)} %copy-done.69, bf16[3072,2048]{1,0:T(8,128)(2,1)S(1)} %bitcast.127), kind=kOutput, calls=%fused_computation.61 | convolution fusion | flops 6443499520 | bytes 17825792 | tf_op jit(solution)/shard_map/dot_general | solution.py:691
  403.0 4.9 multiply_reduce_fusion
  407.9 4.7 fusion.46.first
  414.0 4.4 fusion.57.up_own
  418.4 5.9 arrange.7.left_own.left_oth
  424.4 57.1 %rec_bwd.1 = (bf16[512,1280]{1,0:T(8,128)(2,1)S(1)}, bf16[512,1280]{1,0:T(8,128)(2,1)S(1)}, bf16[512,1280]{1,0:T(8,128)(2,1)S(1)}, bf16[512,1280]{1,0:T(8,128)(2...) custom-call(bf16[512,1280]{1,0:T(8,128)(2,1)} %convolution_convert_fusion.5.bx_own, ...), custom_call_target="tpu_custom_call" | custom-call | flops 4354211840 | bytes 31457280 | tf_op jit(solution)/shard_map/rec_bwd/pallas_call | solution.py:267
  488.7 4.1 add_convert_fusion.3
  503.1 13.1 %weight_grad.9 = (bf16[512,1280]{1,0:T(8,128)(2,1)}, bf16[512,1280]{1,0:T(8,128)(2,1)}) custom-call(bf16[1024,2048]{1,0:T(8,128)(2,1)} %arrange.5.left_own.left_oth, bf16[1024,2048]{1,0:T(8,128)(2,1)} %arrange.5.left_own.left_oth, bf16[512,1280]{1,0:T(8,128)(2,1)S(1)} %copy-done.16, bf16[512,1280]{1,0:T(8,128)(2,1)S(1)} %copy-done.20), custom_call_target="tpu_custom_call" | custom-call | flops 5368709120 | bytes 10485760 | tf_op jit(solution)/shard_map/weight_grad/pallas_call | solution.py:406
  516.9 13.1 %weight_grad.10 = (bf16[512,1280]{1,0:T(8,128)(2,1)}, bf16[512,1280]{1,0:T(8,128)(2,1)}) custom-call(bf16[1024,2048]{1,0:T(8,128)(2,1)} %arrange.7.left_own.left_oth, bf16[1024,2048]{1,0:T(8,128)(2,1)} %arrange.7.left_own.left_oth, bf16[512,1280]{1,0:T(8,128)(2,1)S(1)} %copy-done.24, bf16[512,1280]{1,0:T(8,128)(2,1)S(1)} %copy-done.26), custom_call_target="tpu_custom_call" | custom-call | flops 5368709120 | bytes 10485760 | tf_op jit(solution)/shard_map/weight_grad/pallas_call | solution.py:406
  530.0 34.4 %collective-permute-done.15 = bf16[256,3072]{1,0:T(8,128)(2,1)S(1)} collective-permute-done((bf16[256,3072]{1,0:T(8,128)(2,1)S(1)}, bf16[256,3072]{1,0:T(8,128)(2,1)S(1)}, u32[]{:S(2)}, u32[]{:S(2)}) %collective-permute-start.15) | collective-permute-done | bytes 1572896 | tf_op jit(solution)/shard_map/ppermute | solution.py:466
  565.9 12.9 %weight_grad.11 = (bf16[512,1280]{1,0:T(8,128)(2,1)}, bf16[512,1280]{1,0:T(8,128)(2,1)}) custom-call(bf16[1024,2048]{1,0:T(8,128)(2,1)} %arrange.5.left_own.left_oth, bf16[1024,2048]{1,0:T(8,128)(2,1)} %arrange.5.left_own.left_oth, bf16[512,1280]{1,0:T(8,128)(2,1)S(1)} %copy-done.18, bf16[512,1280]{1,0:T(8,128)(2,1)S(1)} %copy-done.22), custom_call_target="tpu_custom_call" | custom-call | flops 5368709120 | bytes 10485760 | tf_op jit(solution)/shard_map/weight_grad/pallas_call | solution.py:406
  578.7 8.2 %two_back.6 = bf16[512,2048]{1,0:T(8,128)(2,1)S(1)} custom-call(bf16[512,1280]{1,0:T(8,128)(2,1)S(1)} %copy-done.20, bf16[2048,1280]{1,0:T(8,128)(2,1)} %first_w.7, bf16[512,1280]{1,0:T(8,128)(2,1)S(1)} %copy-done.22, bf16[2048,1280]{1,0:T(8,128)(2,1)} %second_w.7), custom_call_target="tpu_custom_call" | custom-call | flops 5368709120 | bytes 13107200 | tf_op jit(solution)/shard_map/two_back/pallas_call | solution.py:446
  595.0 8.5 %two_back.7 = bf16[512,2048]{1,0:T(8,128)(2,1)S(1)} custom-call(bf16[512,1280]{1,0:T(8,128)(2,1)S(1)} %copy-done.16, bf16[2048,1280]{1,0:T(8,128)(2,1)} %first_w.7, bf16[512,1280]{1,0:T(8,128)(2,1)S(1)} %copy-done.18, bf16[2048,1280]{1,0:T(8,128)(2,1)} %second_w.7), custom_call_target="tpu_custom_call" | custom-call | flops 5368709120 | bytes 13107200 | tf_op jit(solution)/shard_map/two_back/pallas_call | solution.py:446
  603.5 8.3 %collective-permute-done.12 = bf16[512,1280]{1,0:T(8,128)(2,1)} collective-permute-done((bf16[512,1280]{1,0:T(8,128)(2,1)}, bf16[512,1280]{1,0:T(8,128)(2,1)}, u32[]{:S(2)}, u32[]{:S(2)}) %collective-permute-start.12) | collective-permute-done | bytes 1310752 | tf_op jit(solution)/shard_map/ppermute | solution.py:466
  614.5 9.9 %convolution_convert_fusion = bf16[512,2048]{1,0:T(8,128)(2,1)S(1)} fusion(bf16[512,3072]{1,0:T(8,128)(2,1)S(1)} %copy-done.28, bf16[3072,2048]{1,0:T(8,128)(2,1)} %param.27), kind=kOutput, calls=%fused_computation.60 | convolution fusion | flops 6443499520 | bytes 17825792 | tf_op jit(solution)/shard_map/dot_general | solution.py:691
  624.9 6.7 add_convert_fusion
  637.5 18.7 %collective-permute-done.19 = bf16[512,1280]{1,0:T(8,128)(2,1)S(1)} collective-permute-done((bf16[512,1280]{1,0:T(8,128)(2,1)S(1)}, bf16[512,1280]{1,0:T(8,128)(2,1)S(1)}, u32[]{:S(2)}, u32[]{:S(2)}) %collective-permute-start.19) | collective-permute-done | bytes 1310752 | tf_op jit(solution)/shard_map/ppermute | solution.py:466
  658.7 7.4 %fusion.22 = f32[512,2048]{1,0:T(8,128)} fusion(bf16[512,2048]{1,0:T(8,128)(2,1)S(1)} %collective-permute-done.18, bf16[512,2048]{1,0:T(8,128)(2,1)S(1)} %two_back.7, f32[512]{0:T(512)S(1)} %fusion.40, f32[2048]{0:T(1024)S(1)} %bitcast.110, f32[512]{0:T(512)S(1)} %copy-done.61, bf16[1,512,2048]{2,1,0:T(8,128)(2,1)S(1)} %copy-done.31, f32[512]{0:T(512)S(1)} %fusion.39, ...), kind=kLoop, calls=%fused_computation.39 | loop fusion | flops 23068672 | bytes 20996096 | tf_op jit(solution)/shard_map/add | solution.py:622
  680.6 12.2 %collective-permute-done.26 = bf16[128,1280]{1,0:T(8,128)(2,1)S(1)} collective-permute-done((bf16[128,1280]{1,0:T(8,128)(2,1)}, bf16[128,1280]{1,0:T(8,128)(2,1)S(1)}, u32[]{:S(2)}, u32[]{:S(2)}) %collective-permute-start.26) | collective-permute-done | bytes 327712 | tf_op jit(solution)/shard_map/ppermute | solution.py:466
  692.7 4.3 collective-permute-done.25
  (307 shorter events, 118.8 us)
Async XLA Ops:
  7.2 662.9 %reduce-scatter.2.cloned.1.call-start = ((), (), s32[]{:S(2)}) async-start(), calls=%async_computation.1 | async-start | bytes 1462272 | tf_op jit(solution)/shard_map/reduce_scatter | solution.py:600
  7.2 37.1 %collective-permute-start.1 = (s32[512]{0:T(512)}, s32[512]{0:T(512)S(1)}, u32[]{:S(2)}, u32[]{:S(2)}) collective-permute-start(s32[512]{0:T(512)} %bitcast.121), channel_id=1, source_target_pairs={{0,1},{1,0},{2,3},{3,2},{4,5},{5,4},{6,7},{7,6},{8,9},{9,8},{10,11... | collective-permute-start | bytes 6152 | tf_op jit(solution)/shard_map/ppermute | solution.py:461
  10.2 48.9 %collective-permute-start = (bf16[512,2048]{1,0:T(8,128)(2,1)}, bf16[512,2048]{1,0:T(8,128)(2,1)}, u32[]{:S(2)}, u32[]{:S(2)}) collective-permute-start(bf16[512,2048]{1,0:T(8,128)(2,1)} %bitcast.87), channel_id=1, source_target_pairs={{0,1},{1,0},{2,3},{3,2},{4,5},{5,4},{6,7},{7,6},{8,9},{9,8},{10,11... | collective-permute-start | bytes 6291464 | tf_op jit(solution)/shard_map/ppermute | solution.py:461
  10.3 103.6 %collective-permute-start.3 = (bf16[512,2048]{1,0:T(8,128)(2,1)}, bf16[512,2048]{1,0:T(8,128)(2,1)}, u32[]{:S(2)}, u32[]{:S(2)}) collective-permute-start(bf16[512,2048]{1,0:T(8,128)(2,1)} %bitcast.88), channel_id=1, source_target_pairs={{0,1},{1,0},{2,3},{3,2},{4,5},{5,4},{6,7},{7,6},{8,9},{9,8},{10,11... | collective-permute-start | bytes 6291464 | tf_op jit(solution)/shard_map/ppermute | solution.py:461
  15.2 46.0 %copy-start.51 = (f32[1,2048]{1,0:T(1,128)}, f32[1,2048]{1,0:T(1,128)S(1)}, u32[]{:S(2)}) copy-start(f32[1,2048]{1,0:T(1,128)S(1)} %get-tuple-element.276) | copy-start | bytes 24580
  31.3 41.4 %copy-start.13 = (f32[8,1280]{1,0:T(8,128)}, f32[8,1280]{1,0:T(8,128)S(1)}, u32[]{:S(2)}) copy-start(f32[8,1280]{1,0:T(8,128)S(1)} %fusion.27.prm_ref) | copy-start | bytes 122884
  44.8 27.9 %copy-start.9 = (f32[1032,8]{1,0:T(8,128)}, f32[1032,8]{1,0:T(8,128)S(1)}, u32[]{:S(2)}) copy-start(f32[1032,8]{1,0:T(8,128)S(1)} %pad.9.mask_ref) | copy-start | bytes 99076
  63.5 40.2 %slice-start.14 = ((s8[5242880]{0:T(1024)(128)(4,1)}), s8[4194304]{0:T(1024)(128)(4,1)S(1)}, s32[]{:S(2)}) async-start(s8[5242880]{0:T(1024)(128)(4,1)} %bitcast.128), calls=%async_computation.16 | async-start | bytes 8388608
  69.8 33.9 %slice-start.15 = ((s8[5242880]{0:T(1024)(128)(4,1)}), s8[1048576]{0:T(1024)(128)(4,1)S(1)}, s32[]{:S(2)}) async-start(s8[5242880]{0:T(1024)(128)(4,1)} %bitcast.128), calls=%async_computation.17 | async-start | bytes 2097152
  73.2 30.5 %copy-start.12 = (bf16[512,1280]{1,0:T(8,128)(2,1)}, bf16[512,1280]{1,0:T(8,128)(2,1)S(1)}, u32[]{:S(2)}) copy-start(bf16[512,1280]{1,0:T(8,128)(2,1)S(1)} %convolution_convert_fusion.4.bx_oth) | copy-start | bytes 3932164
  107.8 48.9 %collective-permute-start.2 = (bf16[512,2048]{1,0:T(8,128)(2,1)}, bf16[512,2048]{1,0:T(8,128)(2,1)}, u32[]{:S(2)}, u32[]{:S(2)}) collective-permute-start(bf16[512,2048]{1,0:T(8,128)(2,1)} %convolution_convert_fusion.3), channel_id=1, source_target_pairs={{0,1},{1,0},{2,3},{3,2},{4,5},{5,4},{6,7},{7,6},{8,9},{9,8},{10,11... | collective-permute-start | bytes 6291464 | tf_op jit(solution)/shard_map/ppermute | solution.py:461
  112.0 108.4 %collective-permute-start.4 = (bf16[512,2048]{1,0:T(8,128)(2,1)}, bf16[512,2048]{1,0:T(8,128)(2,1)}, u32[]{:S(2)}, u32[]{:S(2)}) collective-permute-start(bf16[512,2048]{1,0:T(8,128)(2,1)} %convolution_convert_fusion.2), channel_id=1, source_target_pairs={{0,1},{1,0},{2,3},{3,2},{4,5},{5,4},{6,7},{7,6},{8,9},{9,8},{10,11... | collective-permute-start | bytes 6291464 | tf_op jit(solution)/shard_map/ppermute | solution.py:461
  129.6 27.0 %copy-start.29 = (bf16[1,512,2048]{2,1,0:T(8,128)(2,1)S(1)}, bf16[1,512,2048]{2,1,0:T(8,128)(2,1)}, u32[]{:S(2)}) copy-start(bf16[1,512,2048]{2,1,0:T(8,128)(2,1)} %param.14) | copy-start | bytes 6291460
  163.7 27.4 %slice-start = ((s8[6291456]{0:T(1024)(128)(4,1)}), s8[4194304]{0:T(1024)(128)(4,1)S(1)}, s32[]{:S(2)}) async-start(s8[6291456]{0:T(1024)(128)(4,1)} %bitcast.91), calls=%async_computation.2 | async-start | bytes 8388608
  191.1 63.3 %copy-start.27 = (bf16[512,3072]{1,0:T(8,128)(2,1)}, bf16[512,3072]{1,0:T(8,128)(2,1)S(1)}, u32[]{:S(2)}) copy-start(bf16[512,3072]{1,0:T(8,128)(2,1)S(1)} %get-tuple-element.169.right_own) | copy-start | bytes 9437188
  220.2 120.3 %collective-permute-start.7 = (bf16[512,2048]{1,0:T(8,128)(2,1)S(1)}, bf16[512,2048]{1,0:T(8,128)(2,1)}, u32[]{:S(2)}, u32[]{:S(2)}) collective-permute-start(bf16[512,2048]{1,0:T(8,128)(2,1)S(1)} %two_back.4), channel_id=1, source_target_pairs={{0,1},{1,0},{2,3},{3,2},{4,5},{5,4},{6,7},{7,6},{8,9},{9,8},{10,11... | collective-permute-start | bytes 6291464 | tf_op jit(solution)/shard_map/ppermute | solution.py:461
  292.9 73.1 %collective-permute-start.8 = (bf16[512,3072]{1,0:T(8,128)(2,1)}, bf16[512,3072]{1,0:T(8,128)(2,1)}, u32[]{:S(2)}, u32[]{:S(2)}) collective-permute-start(bf16[512,3072]{1,0:T(8,128)(2,1)} %get-tuple-element.122), channel_id=1, source_target_pairs={{0,8},{2,10},{4,12},{6,14},{8,0},{10,2},{12,4},{14,6},{16,24},{18,... | collective-permute-start | bytes 9437192 | tf_op jit(solution)/shard_map/ppermute | solution.py:466
  296.8 24.3 %copy-start.6 = (bf16[512,3072]{1,0:T(8,128)(2,1)S(1)}, bf16[512,3072]{1,0:T(8,128)(2,1)}, u32[]{:S(2)}) copy-start(bf16[512,3072]{1,0:T(8,128)(2,1)} %get-tuple-element.120.right_oth.first) | copy-start | bytes 9437188
  319.5 80.2 %collective-permute-start.6 = (bf16[512,3072]{1,0:T(8,128)(2,1)}, bf16[512,3072]{1,0:T(8,128)(2,1)S(1)}, u32[]{:S(2)}, u32[]{:S(2)}) collective-permute-start(bf16[512,3072]{1,0:T(8,128)(2,1)} %get-tuple-element.121), channel_id=1, source_target_pairs={{0,4},{2,6},{4,0},{6,2},{8,12},{10,14},{12,8},{14,10},{16,20},{18,... | collective-permute-start | bytes 9437192 | tf_op jit(solution)/shard_map/ppermute | solution.py:466
  339.0 64.0 %collective-permute-start.5 = (bf16[512,2048]{1,0:T(8,128)(2,1)S(1)}, bf16[512,2048]{1,0:T(8,128)(2,1)S(1)}, u32[]{:S(2)}, u32[]{:S(2)}) collective-permute-start(bf16[512,2048]{1,0:T(8,128)(2,1)S(1)} %two_back.5), channel_id=1, source_target_pairs={{0,1},{1,0},{2,3},{3,2},{4,5},{5,4},{6,7},{7,6},{8,9},{9,8},{10,11... | collective-permute-start | bytes 6291464 | tf_op jit(solution)/shard_map/ppermute | solution.py:461
  365.4 123.2 %collective-permute-start.11 = (bf16[512,3072]{1,0:T(8,128)(2,1)}, bf16[512,3072]{1,0:T(8,128)(2,1)}, u32[]{:S(2)}, u32[]{:S(2)}) collective-permute-start(bf16[512,3072]{1,0:T(8,128)(2,1)} %get-tuple-element.135), channel_id=1, source_target_pairs={{0,4},{2,6},{4,0},{6,2},{8,12},{10,14},{12,8},{14,10},{16,20},{18,... | collective-permute-start | bytes 9437192 | tf_op jit(solution)/shard_map/ppermute | solution.py:466
  371.7 122.5 %collective-permute-start.10 = (bf16[256,3072]{1,0:T(8,128)(2,1)}, bf16[256,3072]{1,0:T(8,128)(2,1)}, u32[]{:S(2)}, u32[]{:S(2)}) collective-permute-start(bf16[256,3072]{1,0:T(8,128)(2,1)} %get-tuple-element.126), channel_id=1, source_target_pairs={{0,4},{2,6},{4,0},{6,2},{8,12},{10,14},{12,8},{14,10},{16,20},{18,... | collective-permute-start | bytes 4718600 | tf_op jit(solution)/shard_map/ppermute | solution.py:466
  398.9 225.5 %collective-permute-start.17 = (bf16[512,2048]{1,0:T(8,128)(2,1)}, bf16[512,2048]{1,0:T(8,128)(2,1)}, u32[]{:S(2)}, u32[]{:S(2)}) collective-permute-start(bf16[512,2048]{1,0:T(8,128)(2,1)} %convolution_convert_fusion.1), channel_id=1, source_target_pairs={{0,1},{1,0},{2,3},{3,2},{4,5},{5,4},{6,7},{7,6},{8,9},{9,8},{10,11... | collective-permute-start | bytes 6291464 | tf_op jit(solution)/shard_map/ppermute | solution.py:461
  402.6 97.1 %collective-permute-start.9 = (bf16[256,3072]{1,0:T(8,128)(2,1)}, bf16[256,3072]{1,0:T(8,128)(2,1)}, u32[]{:S(2)}, u32[]{:S(2)}) collective-permute-start(bf16[256,3072]{1,0:T(8,128)(2,1)} %get-tuple-element.130), channel_id=1, source_target_pairs={{0,8},{2,10},{4,12},{6,14},{8,0},{10,2},{12,4},{14,6},{16,24},{18,... | collective-permute-start | bytes 4718600 | tf_op jit(solution)/shard_map/ppermute | solution.py:466
  424.3 61.6 %copy-start.57 = (f32[1280]{0:T(1024)S(1)}, f32[1280]{0:T(1024)}, u32[]{:S(2)}) copy-start(f32[1280]{0:T(1024)} %fusion.32) | copy-start | bytes 15364
  424.4 61.6 %copy-start.67 = (pred[8]{0:T(512)(128)(4,1)S(1)}, pred[8]{0:T(512)(128)(4,1)}, u32[]{:S(2)}) copy-start(pred[8]{0:T(512)(128)(4,1)} %iota_compare_fusion.1) | copy-start | bytes 28
  492.8 71.6 %collective-permute-start.15 = (bf16[256,3072]{1,0:T(8,128)(2,1)S(1)}, bf16[256,3072]{1,0:T(8,128)(2,1)S(1)}, u32[]{:S(2)}, u32[]{:S(2)}) collective-permute-start(bf16[256,3072]{1,0:T(8,128)(2,1)S(1)} %get-tuple-element.140), channel_id=1, source_target_pairs={{0,8},{2,10},{4,12},{6,14},{8,0},{10,2},{12,4},{14,6},{16,24},{18,... | collective-permute-start | bytes 4718600 | tf_op jit(solution)/shard_map/ppermute | solution.py:466
  497.1 134.5 %collective-permute-start.14 = (bf16[128,3072]{1,0:T(8,128)(2,1)}, bf16[128,3072]{1,0:T(8,128)(2,1)}, u32[]{:S(2)}, u32[]{:S(2)}) collective-permute-start(bf16[128,3072]{1,0:T(8,128)(2,1)} %get-tuple-element.142), channel_id=1, source_target_pairs={{0,16},{2,18},{4,20},{6,22},{8,24},{10,26},{12,28},{14,30},{16,0},... | collective-permute-start | bytes 2359304 | tf_op jit(solution)/shard_map/ppermute | solution.py:466
  502.6 84.4 %collective-permute-start.16 = (bf16[128,3072]{1,0:T(8,128)(2,1)}, bf16[128,3072]{1,0:T(8,128)(2,1)}, u32[]{:S(2)}, u32[]{:S(2)}) collective-permute-start(bf16[128,3072]{1,0:T(8,128)(2,1)} %get-tuple-element.144), channel_id=1, source_target_pairs={{0,16},{2,18},{4,20},{6,22},{8,24},{10,26},{12,28},{14,30},{16,0},... | collective-permute-start | bytes 2359304 | tf_op jit(solution)/shard_map/ppermute | solution.py:466
  516.3 76.3 %collective-permute-start.13 = (bf16[512,1280]{1,0:T(8,128)(2,1)}, bf16[512,1280]{1,0:T(8,128)(2,1)}, u32[]{:S(2)}, u32[]{:S(2)}) collective-permute-start(bf16[512,1280]{1,0:T(8,128)(2,1)} %get-tuple-element.151), channel_id=1, source_target_pairs={{0,4},{2,6},{4,0},{6,2},{8,12},{10,14},{12,8},{14,10},{16,20},{18,... | collective-permute-start | bytes 3932168 | tf_op jit(solution)/shard_map/ppermute | solution.py:466
  529.9 35.9 %copy-start.18 = (bf16[512,1280]{1,0:T(8,128)(2,1)S(1)}, bf16[512,1280]{1,0:T(8,128)(2,1)}, u32[]{:S(2)}) copy-start(bf16[512,1280]{1,0:T(8,128)(2,1)} %copy-done.17) | copy-start | bytes 3932164
  529.9 35.9 %copy-start.22 = (bf16[512,1280]{1,0:T(8,128)(2,1)S(1)}, bf16[512,1280]{1,0:T(8,128)(2,1)}, u32[]{:S(2)}) copy-start(bf16[512,1280]{1,0:T(8,128)(2,1)} %copy-done.21) | copy-start | bytes 3932164
  564.4 47.3 %collective-permute-start.12 = (bf16[512,1280]{1,0:T(8,128)(2,1)}, bf16[512,1280]{1,0:T(8,128)(2,1)}, u32[]{:S(2)}, u32[]{:S(2)}) collective-permute-start(bf16[512,1280]{1,0:T(8,128)(2,1)} %get-tuple-element.150), channel_id=1, source_target_pairs={{0,8},{2,10},{4,12},{6,14},{8,0},{10,2},{12,4},{14,6},{16,24},{18,... | collective-permute-start | bytes 3932168 | tf_op jit(solution)/shard_map/ppermute | solution.py:466
  587.0 46.2 %collective-permute-start.21 = (bf16[128,3072]{1,0:T(8,128)(2,1)}, bf16[128,3072]{1,0:T(8,128)(2,1)S(1)}, u32[]{:S(2)}, u32[]{:S(2)}) collective-permute-start(bf16[128,3072]{1,0:T(8,128)(2,1)} %get-tuple-element.155), channel_id=1, source_target_pairs={{0,16},{2,18},{4,20},{6,22},{8,24},{10,26},{12,28},{14,30},{16,0},... | collective-permute-start | bytes 2359304 | tf_op jit(solution)/shard_map/ppermute | solution.py:466
  595.0 40.8 %collective-permute-start.20 = (bf16[256,1280]{1,0:T(8,128)(2,1)}, bf16[256,1280]{1,0:T(8,128)(2,1)}, u32[]{:S(2)}, u32[]{:S(2)}) collective-permute-start(bf16[256,1280]{1,0:T(8,128)(2,1)} %get-tuple-element.165), channel_id=1, source_target_pairs={{0,8},{2,10},{4,12},{6,14},{8,0},{10,2},{12,4},{14,6},{16,24},{18,... | collective-permute-start | bytes 1966088 | tf_op jit(solution)/shard_map/ppermute | solution.py:466
  611.7 44.9 %collective-permute-start.18 = (bf16[512,2048]{1,0:T(8,128)(2,1)S(1)}, bf16[512,2048]{1,0:T(8,128)(2,1)S(1)}, u32[]{:S(2)}, u32[]{:S(2)}) collective-permute-start(bf16[512,2048]{1,0:T(8,128)(2,1)S(1)} %two_back.6), channel_id=1, source_target_pairs={{0,1},{1,0},{2,3},{3,2},{4,5},{5,4},{6,7},{7,6},{8,9},{9,8},{10,11... | collective-permute-start | bytes 6291464 | tf_op jit(solution)/shard_map/ppermute | solution.py:461
  624.4 31.8 %collective-permute-start.19 = (bf16[512,1280]{1,0:T(8,128)(2,1)S(1)}, bf16[512,1280]{1,0:T(8,128)(2,1)S(1)}, u32[]{:S(2)}, u32[]{:S(2)}) collective-permute-start(bf16[512,1280]{1,0:T(8,128)(2,1)S(1)} %copy-done.68), channel_id=1, source_target_pairs={{0,4},{2,6},{4,0},{6,2},{8,12},{10,14},{12,8},{14,10},{16,20},{18,... | collective-permute-start | bytes 3932168 | tf_op jit(solution)/shard_map/ppermute | solution.py:466
  631.6 24.6 %copy-start.46 = (bf16[512,1280]{1,0:T(8,128)(2,1)S(1)}, bf16[512,1280]{1,0:T(8,128)(2,1)}, u32[]{:S(2)}) copy-start(bf16[512,1280]{1,0:T(8,128)(2,1)} %get-tuple-element.159) | copy-start | bytes 3932164
  631.6 34.5 %collective-permute-start.24 = (bf16[256,1280]{1,0:T(8,128)(2,1)S(1)}, bf16[256,1280]{1,0:T(8,128)(2,1)S(1)}, u32[]{:S(2)}, u32[]{:S(2)}) collective-permute-start(bf16[256,1280]{1,0:T(8,128)(2,1)S(1)} %get-tuple-element.168), channel_id=1, source_target_pairs={{0,4},{2,6},{4,0},{6,2},{8,12},{10,14},{12,8},{14,10},{16,20},{18,... | collective-permute-start | bytes 1966088 | tf_op jit(solution)/shard_map/ppermute | solution.py:466
  637.0 31.1 %collective-permute-start.22 = (bf16[128,1280]{1,0:T(8,128)(2,1)S(1)}, bf16[128,1280]{1,0:T(8,128)(2,1)S(1)}, u32[]{:S(2)}, u32[]{:S(2)}) collective-permute-start(bf16[128,1280]{1,0:T(8,128)(2,1)S(1)} %get-tuple-element.176), channel_id=1, source_target_pairs={{0,16},{2,18},{4,20},{6,22},{8,24},{10,26},{12,28},{14,30},{16,0},... | collective-permute-start | bytes 983048 | tf_op jit(solution)/shard_map/ppermute | solution.py:466
  656.5 10.7 %collective-permute-start.23 = (bf16[256,1280]{1,0:T(8,128)(2,1)S(1)}, bf16[256,1280]{1,0:T(8,128)(2,1)S(1)}, u32[]{:S(2)}, u32[]{:S(2)}) collective-permute-start(bf16[256,1280]{1,0:T(8,128)(2,1)S(1)} %get-tuple-element.178), channel_id=1, source_target_pairs={{0,8},{2,10},{4,12},{6,14},{8,0},{10,2},{12,4},{14,6},{16,24},{18,... | collective-permute-start | bytes 1966088 | tf_op jit(solution)/shard_map/ppermute | solution.py:466
  670.1 6.8 collective-permute-start.27
  672.3 24.7 %copy-start.50 = (bf16[128,1280]{1,0:T(8,128)(2,1)S(1)}, bf16[128,1280]{1,0:T(8,128)(2,1)}, u32[]{:S(2)}) copy-start(bf16[128,1280]{1,0:T(8,128)(2,1)} %get-tuple-element.188) | copy-start | bytes 983044
  673.9 26.3 %copy-start.49 = (bf16[128,1280]{1,0:T(8,128)(2,1)S(1)}, bf16[128,1280]{1,0:T(8,128)(2,1)}, u32[]{:S(2)}) copy-start(bf16[128,1280]{1,0:T(8,128)(2,1)} %get-tuple-element.189) | copy-start | bytes 983044
  674.0 18.8 %collective-permute-start.26 = (bf16[128,1280]{1,0:T(8,128)(2,1)}, bf16[128,1280]{1,0:T(8,128)(2,1)S(1)}, u32[]{:S(2)}, u32[]{:S(2)}) collective-permute-start(bf16[128,1280]{1,0:T(8,128)(2,1)} %get-tuple-element.184), channel_id=1, source_target_pairs={{0,16},{2,18},{4,20},{6,22},{8,24},{10,26},{12,28},{14,30},{16,0},... | collective-permute-start | bytes 983048 | tf_op jit(solution)/shard_map/ppermute | solution.py:466
  675.7 21.2 %collective-permute-start.25 = (bf16[128,1280]{1,0:T(8,128)(2,1)}, bf16[128,1280]{1,0:T(8,128)(2,1)S(1)}, u32[]{:S(2)}, u32[]{:S(2)}) collective-permute-start(bf16[128,1280]{1,0:T(8,128)(2,1)} %get-tuple-element.186), channel_id=1, source_target_pairs={{0,16},{2,18},{4,20},{6,22},{8,24},{10,26},{12,28},{14,30},{16,0},... | collective-permute-start | bytes 983048 | tf_op jit(solution)/shard_map/ppermute | solution.py:466
  676.9 26.3 %copy-start.1 = (bf16[2,10,256,256]{3,2,1,0:T(8,128)(2,1)S(1)}, bf16[2,10,256,256]{3,2,1,0:T(8,128)(2,1)}, u32[]{:S(2)}) copy-start(bf16[2,10,256,256]{3,2,1,0:T(8,128)(2,1)} %param.23) | copy-start | bytes 7864324
  699.0 3.6 collective-permute-start.28
  (70 other events, 535.6 us)
Sparse Core Ops, SparseCore 0:
  488.8 96.9 reduce-scatter.1

commit v4 on v0

--- a/solution.py
+++ b/solution.py
@@ -1,9 +1,775 @@
+import functools
+
 import jax
 import jax.numpy as jnp
 from jax import lax
+from jax.experimental import pallas as pl
+from jax.experimental.pallas import tpu as pltpu
 from jax.sharding import PartitionSpec as P
 
 EPS = 1e-06
+F32, BF16 = jnp.float32, jnp.bfloat16
+GELU_A, GELU_B = 0.7978845608028654, 0.044715
+MESH = pl.DeviceIdType.MESH
+
+
+AT_ONCE = 8
+SEGMENTS = 8
+
+
+def in_steps(own, other, into, first):
+    steps = own.shape[0] // SEGMENTS
+    for piece, spot in ((own, 0), (other, SEGMENTS)):
+        rows = piece[...].astype(F32).reshape(SEGMENTS, steps, piece.shape[1])
+        into[first : first + steps, spot : spot + SEGMENTS, :] = jnp.swapaxes(rows, 0, 1)
+
+
+def in_rows(source, own, other):
+    steps, _, lanes = source.shape
+    for piece, spot in ((own, 0), (other, SEGMENTS)):
+        rows = jnp.swapaxes(source[:, spot : spot + SEGMENTS, :], 0, 1)
+        piece[...] = rows.reshape(SEGMENTS * steps, lanes).astype(piece.dtype)
+
+
+def from_segment(value, place, later):
+    segment = lax.broadcasted_iota(jnp.int32, value.shape, 1)
+    if later:
+        return jnp.where(segment == 2 * SEGMENTS - 1 - SEGMENTS * place, 0.0, pltpu.roll(value, 2 * SEGMENTS - 1, 1))
+    return jnp.where(segment == SEGMENTS * place, 0.0, pltpu.roll(value, 1, 1))
+
+
+def entering(added, factor, place, later):
+    def turned(value):
+        return jnp.where(place == 1, pltpu.roll(value, SEGMENTS, 0), value)
+
+    added, factor = turned(added), turned(factor)
+    state = jnp.zeros_like(added[0:1])
+    rows = [None] * (2 * SEGMENTS)
+    for index in reversed(range(2 * SEGMENTS)) if later else range(2 * SEGMENTS):
+        rows[index] = state
+        state = added[index : index + 1] + factor[index : index + 1] * state
+    return turned(jnp.concatenate(rows, axis=0))
+
+
+def wide_mask(mask_ref, index, first, count):
+    mask = mask_ref[index, pl.ds(first, count)]
+    return jnp.concatenate([mask, mask], axis=2)
+
+
+def decay_terms(rate_gate, prm_ref):
+    log_decay = prm_ref[7:8, :] * rate_gate
+    decay = jnp.exp(log_decay)
+    squared = decay * decay
+    gap = jnp.maximum(-jnp.tanh(log_decay) * (1.0 + squared), 1e-37)
+    return decay, squared, gap, lax.rsqrt(gap)
+
+
+def rec_fwd_kernel(
+    bx_own, bx_oth, by_own, by_oth, mask_ref, prm_ref, gate_ref,
+    gated_own, gated_oth, state_ref, in_ref, rate_ref, conv_ref, xs, ys, pre, factor,
+):
+    place = lax.axis_index("tp")
+    steps, both, lanes = state_ref.shape
+    in_steps(bx_own, bx_oth, xs, 3)
+    xs[0:3] = from_segment(xs[steps : steps + 3], place, False)
+    in_steps(by_own, by_oth, ys, 0)
+    taps = [prm_ref[k : k + 1, :] for k in range(4)]
+
+    def conv_step(index, _):
+        at = index * AT_ONCE
+        total = taps[0] * xs[pl.ds(at + 3, AT_ONCE)] + prm_ref[4:5, :]
+        for k in (1, 2, 3):
+            total = total + taps[k] * (wide_mask(mask_ref, k - 1, at, AT_ONCE) * xs[pl.ds(at + 3 - k, AT_ONCE)])
+        conv_ref[pl.ds(at, AT_ONCE)] = total.astype(BF16)
+        return 0
+
+    lax.fori_loop(0, steps // AT_ONCE, conv_step, 0)
+
+    def gate_step(index, _):
+        conv = conv_ref[pl.ds(index * 16, 16)].reshape(16 * both, lanes)
+        rows = pl.ds(pl.multiple_of(index * 16 * both, 16 * both), 16 * both)
+        pre[rows, 0:lanes] = jnp.dot(conv, gate_ref[0, 0], preferred_element_type=F32)
+        pre[rows, lanes:] = jnp.dot(conv, gate_ref[1, 0], preferred_element_type=F32)
+        return 0
+
+    lax.fori_loop(0, steps // 16, gate_step, 0)
+
+    def scan_step(index, carried):
+        state, product = carried
+        at = index * AT_ONCE
+        block = pl.ds(at, AT_ONCE)
+        rows = pl.ds(pl.multiple_of(at * both, AT_ONCE * both), AT_ONCE * both)
+        shape = (AT_ONCE, both, lanes)
+        in_gate = jax.nn.sigmoid(pre[rows, 0:lanes] + prm_ref[5:6, :]).reshape(shape)
+        rate_gate = (1.0 / (1.0 + jnp.exp(-(pre[rows, lanes:] + prm_ref[6:7, :])))).reshape(shape)
+        in_ref[block] = in_gate
+        rate_ref[block] = rate_gate
+        keep = wide_mask(mask_ref, 0, at, AT_ONCE)
+        decay, _, gap, inverse = decay_terms(rate_gate, prm_ref)
+        scaling = (1.0 - keep) + keep * (gap * inverse)
+        pushed = conv_ref[block].astype(F32) * in_gate * scaling
+        coef = decay * keep
+        for one in range(AT_ONCE):
+            state = coef[one] * state + pushed[one]
+            product = coef[one] * product
+            state_ref[at + one] = state
+            factor[at + one] = product
+        return state, product
+
+    zero = jnp.zeros((both, lanes), F32)
+    state, product = lax.fori_loop(0, steps // AT_ONCE, scan_step, (zero, zero + 1.0))
+    enters = entering(state, product, place, False)
+
+    def gated_step(index, _):
+        block = pl.ds(index * AT_ONCE, AT_ONCE)
+        state = state_ref[block] + factor[block] * enters
+        state_ref[block] = state
+        y = ys[block]
+        tanh = jnp.tanh(GELU_A * y * (1.0 + GELU_B * (y * y)))
+        ys[block] = state * (0.5 * y * (1.0 + tanh))
+        return 0
+
+    lax.fori_loop(0, steps // AT_ONCE, gated_step, 0)
+    in_rows(ys, gated_own, gated_oth)
+
+
+def fold(value):
+    return jnp.sum(value, axis=0)
+
+
+def rec_bwd_kernel(
+    count, bx_own, bx_oth, by_own, by_oth, state_ref, in_ref, rate_ref, conv_ref, up_own, up_oth, mask_ref, prm_ref, gate_ref,
+    gx_own, gx_oth, gy_own, gy_oth, gw_ref, sum_ref, xs, ys, us, gs, factor, to_log, to_in, to_rate, to_conv, gc, dg, gw,
+):
+    place = lax.axis_index("tp")
+    steps, both, lanes = state_ref.shape
+    length = steps * both
+    in_steps(bx_own, bx_oth, xs, 3)
+    xs[0:3] = from_segment(xs[steps : steps + 3], place, False)
+    in_steps(by_own, by_oth, ys, 0)
+    in_steps(up_own, up_oth, us, 0)
+
+    def scan_step(index, carried):
+        sent, product = carried
+        at = steps - AT_ONCE - index * AT_ONCE
+        block = pl.ds(at, AT_ONCE)
+        in_gate, rate_gate = in_ref[block], rate_ref[block]
+        keep = wide_mask(mask_ref, 0, at, AT_ONCE)
+        decay, squared, gap, inverse = decay_terms(rate_gate, prm_ref)
+        scaling = (1.0 - keep) + keep * (gap * inverse)
+        y = ys[block]
+        y2 = y * y
+        tanh = jnp.tanh(GELU_A * y * (1.0 + GELU_B * y2))
+        lift = 0.5 + 0.5 * tanh
+        slope = lift + y * (1.0 - tanh * tanh) * (0.5 * GELU_A + (1.5 * GELU_A * GELU_B) * y2)
+        up = us[block]
+        state = state_ref[block]
+        ys[block] = up * state * slope
+        direct = up * (y * lift)
+        coef = decay * keep
+        entered = conv_ref[block].astype(F32) * in_gate
+        pushed = entered * scaling
+        to_log[block] = ((state - pushed) - entered * (keep * squared * inverse)) * rate_gate
+        to_in[block] = pushed * (1.0 - in_gate)
+        to_rate[block] = (1.0 - rate_gate) * prm_ref[7:8, :]
+        to_conv[block] = in_gate * scaling
+        for one in reversed(range(AT_ONCE)):
+            grad = direct[one] + sent
+            gs[at + one] = grad
+            factor[at + one] = product
+            sent = coef[one] * grad
+            product = coef[one] * product
+        return sent, product
+
+    zero = jnp.zeros((both, lanes), F32)
+    sent, product = lax.fori_loop(0, steps // AT_ONCE, scan_step, (zero, zero + 1.0))
+    enters = entering(sent, product, place, True)
+
+    def grad_step(index, sum_log):
+        at = index * AT_ONCE
+        block = pl.ds(at, AT_ONCE)
+        rows = pl.ds(pl.multiple_of(at * both, AT_ONCE * both), AT_ONCE * both)
+        grad = gs[block] + factor[block] * enters
+        through = grad * to_log[block]
+        dg[rows, 0:lanes] = (grad * to_in[block]).astype(BF16).reshape(AT_ONCE * both, lanes)
+        dg[rows, lanes:] = (through * to_rate[block]).astype(BF16).reshape(AT_ONCE * both, lanes)
+        gc[block] = grad * to_conv[block]
+        return sum_log + fold(through)
+
+    sum_log = lax.fori_loop(0, steps // AT_ONCE, grad_step, zero)
+
+    def back_step(index, _):
+        rows = pl.ds(pl.multiple_of(index * 16 * both, 16 * both), 16 * both)
+        more = matmul_right(dg[rows, 0:lanes], gate_ref[0, 0]) + matmul_right(dg[rows, lanes:], gate_ref[1, 0])
+        gc[pl.ds(index * 16, 16)] += more.reshape(16, both, lanes)
+        return 0
+
+    lax.fori_loop(0, steps // 16, back_step, 0)
+    conv = conv_ref[...].reshape(length, lanes)
+    gw[0:lanes, :] = matmul_left(conv, dg[:, 0:lanes]).astype(BF16)
+    gw[lanes:, :] = matmul_left(conv, dg[:, lanes:]).astype(BF16)
+    gate_sums = jnp.dot(jnp.ones((8, length), BF16), dg[...], preferred_element_type=F32)
+    rows_each = lanes // count
+    for block in range(count):
+        for gate in (0, 1):
+            source = gate * lanes + block * rows_each
+            gw_ref[block, 0, gate * rows_each : (gate + 1) * rows_each, :] = gw[source : source + rows_each, :]
+    gc[steps : steps + 3] = from_segment(gc[0:3], place, True)
+    taps = [prm_ref[k : k + 1, :] for k in range(4)]
+
+    def conv_step(index, sums):
+        at = index * AT_ONCE
+        here = gc[pl.ds(at, AT_ONCE)]
+        total = taps[0] * here
+        sums = [sums[0] + fold(here), sums[1] + fold(here * xs[pl.ds(at + 3, AT_ONCE)])] + list(sums[2:])
+        for k in (1, 2, 3):
+            total = total + taps[k] * (gc[pl.ds(at + k, AT_ONCE)] * wide_mask(mask_ref, k - 1, at + k, AT_ONCE))
+            masked = here * wide_mask(mask_ref, k - 1, at, AT_ONCE)
+            sums[k + 1] = sums[k + 1] + fold(masked * xs[pl.ds(at + 3 - k, AT_ONCE)])
+        us[pl.ds(at, AT_ONCE)] = total
+        return tuple(sums)
+
+    sums = lax.fori_loop(0, steps // AT_ONCE, conv_step, (zero,) * 5)
+    for index, value in ((0, sums[1]), (1, sums[2]), (2, sums[3]), (3, sums[4]), (4, sums[0]), (7, sum_log)):
+        sum_ref[index : index + 1, :] = jnp.sum(value, axis=0, keepdims=True)
+    sum_ref[5:6, :] = gate_sums[0:1, 0:lanes]
+    sum_ref[6:7, :] = gate_sums[0:1, lanes:]
+    in_rows(us, gx_own, gx_oth)
+    in_rows(ys, gy_own, gy_oth)
+
+
+def rec_specs(half, lanes):
+    steps = half // SEGMENTS
+    piece = pl.BlockSpec((half, lanes), lambda h: (0, h))
+    stepped = pl.BlockSpec((steps, 2 * SEGMENTS, lanes), lambda h: (0, 0, h))
+    mask = pl.BlockSpec((3, steps + 3, 2 * SEGMENTS, 128), lambda h: (0, 0, 0, 0))
+    prm = pl.BlockSpec((8, lanes), lambda h: (0, h))
+    gate = pl.BlockSpec((2, 1, lanes, lanes), lambda h: (0, h, 0, 0))
+    return piece, stepped, mask, prm, gate
+
+
+def rec_fwd(bx_own, bx_oth, by_own, by_oth, mask, prm, gates):
+    half, width = bx_own.shape
+    length, lanes, heads = 2 * half, gates.shape[2], gates.shape[1]
+    steps, both = half // SEGMENTS, 2 * SEGMENTS
+    piece, stepped, mask_spec, prm_spec, gate_spec = rec_specs(half, lanes)
+    out = jax.ShapeDtypeStruct((half, width), BF16)
+    kept = jax.ShapeDtypeStruct((steps, both, width), F32)
+    return pl.pallas_call(
+        rec_fwd_kernel,
+        grid=(heads,),
+        in_specs=[piece] * 4 + [mask_spec, prm_spec, gate_spec],
+        out_specs=[piece] * 2 + [stepped] * 4,
+        out_shape=[out, out, kept, kept, kept, jax.ShapeDtypeStruct((steps, both, width), BF16)],
+        scratch_shapes=[
+            pltpu.VMEM((steps + 3, both, lanes), F32),
+            pltpu.VMEM((steps, both, lanes), F32),
+            pltpu.VMEM((length, 2 * lanes), F32),
+            pltpu.VMEM((steps, both, lanes), F32),
+        ],
+        compiler_params=pltpu.CompilerParams(vmem_limit_bytes=40 << 20),
+        cost_estimate=pl.CostEstimate(
+            flops=4 * length * width * lanes + 100 * length * width,
+            bytes_accessed=26 * length * width,
+            transcendentals=6 * length * width,
+        ),
+        name="rec_fwd",
+    )(bx_own, bx_oth, by_own, by_oth, mask, prm, gates)
+
+
+def rec_bwd(bx_own, bx_oth, by_own, by_oth, kept, up_own, up_oth, mask, prm, gates, count):
+    half, width = bx_own.shape
+    length, lanes, heads = 2 * half, gates.shape[2], gates.shape[1]
+    steps, both = half // SEGMENTS, 2 * SEGMENTS
+    piece, stepped, mask_spec, prm_spec, gate_spec = rec_specs(half, lanes)
+    block = pltpu.VMEM((steps, both, lanes), F32)
+    padded = pltpu.VMEM((steps + 3, both, lanes), F32)
+    return pl.pallas_call(
+        functools.partial(rec_bwd_kernel, count),
+        grid=(heads,),
+        in_specs=[piece] * 4 + [stepped] * 4 + [piece] * 2 + [mask_spec, prm_spec, gate_spec],
+        out_specs=[piece] * 4 + [pl.BlockSpec((count, 1, 2 * lanes // count, lanes), lambda h: (0, h, 0, 0)), prm_spec],
+        out_shape=[jax.ShapeDtypeStruct((half, width), BF16)] * 4
+        + [
+            jax.ShapeDtypeStruct((count, heads, 2 * lanes // count, lanes), BF16),
+            jax.ShapeDtypeStruct((8, width), F32),
+        ],
+        scratch_shapes=[padded]
+        + [block] * 8
+        + [padded, pltpu.VMEM((length, 2 * lanes), BF16), pltpu.VMEM((2 * lanes, lanes), BF16)],
+        compiler_params=pltpu.CompilerParams(vmem_limit_bytes=52 << 20),
+        cost_estimate=pl.CostEstimate(
+            flops=8 * length * width * lanes + 150 * length * width,
+            bytes_accessed=34 * length * width,
+            transcendentals=4 * length * width,
+        ),
+        name="rec_bwd",
+    )(bx_own, bx_oth, by_own, by_oth, *kept, up_own, up_oth, mask, prm, gates)
+
+
+def stage_bits(count, crossed=False):
+    bits = [1 << bit for bit in range(count.bit_length() - 1)]
+    return [bits[0], bits[2], bits[1]] + bits[3:] if crossed else bits
+
+
+def block_at(place, bits):
+    return sum(bit for step, bit in enumerate(bits) if (place >> (len(bits) - 1 - step)) & 1)
+
+
+def block_from(me, place, bits):
+    relative = block_at(place, bits)
+    block = 0
+    for bit in bits:
+        mine = lax.rem(me // bit, 2)
+        block = block + bit * (1 - mine if relative & bit else mine)
+    return block
+
+
+def arrange_kernel(bits, first, second, first_out, second_out):
+    @pl.when(pl.program_id(0) == 0)
+    def _():
+        arranged(first, first_out, bits)
+
+    @pl.when(pl.program_id(0) == 1)
+    def _():
+        arranged(second, second_out, bits)
+
+
+def arrange(first, second, bits):
+    whole = pl.BlockSpec(first.shape, lambda i: (0, 0))
+    shape = jax.ShapeDtypeStruct(first.shape, first.dtype)
+    return pl.pallas_call(
+        functools.partial(arrange_kernel, bits),
+        grid=(2,),
+        in_specs=[whole, whole],
+        out_specs=[whole, whole],
+        out_shape=[shape, shape],
+        compiler_params=pltpu.CompilerParams(vmem_limit_bytes=24 << 20),
+        cost_estimate=pl.CostEstimate(flops=0, bytes_accessed=12 * first.size, transcendentals=0),
+        name="arrange",
+    )(first, second)
+
+
+def weight_grad_kernel(splits, own_a, own_b, oth_a, oth_b, right_own, right_oth, sent_next, kept, staged, landed, send_sem, recv_sem):
+    step = pl.program_id(0)
+    half = 2 * splits
+    me = lax.axis_index("dp")
+    partner = {"dp": me + 1 - 2 * lax.rem(me, 2)}
+
+    @pl.when(step == 0)
+    def _():
+        barrier = pltpu.get_barrier_semaphore()
+        pl.semaphore_signal(barrier, inc=1, device_id=partner, device_id_type=MESH)
+        pl.semaphore_wait(barrier, 1)
+
+    def copy(tile):
+        return pltpu.make_async_remote_copy(
+            src_ref=staged.at[tile],
+            dst_ref=landed.at[tile],
+            send_sem=send_sem.at[tile],
+            recv_sem=recv_sem.at[tile],
+            device_id=partner,
+            device_id_type=MESH,
+        )
+
+    left_own = jnp.concatenate([own_a[...], own_b[...]], axis=1)
+    left_oth = jnp.concatenate([oth_a[...], oth_b[...]], axis=1)
+    total = matmul_left(left_own, right_own[...]) + matmul_left(left_oth, right_oth[...])
+
+    @pl.when(step < half)
+    def _():
+        staged[step] = total.astype(BF16)
+        copy(step).start()
+
+    @pl.when(step >= half)
+    def _():
+        copy(step - half).wait_recv()
+        value = (total + landed[step - half].astype(F32)).astype(BF16)
+
+        @pl.when(step < half + splits)
+        def _():
+            sent_next[...] = value
+
+        @pl.when(step >= half + splits)
+        def _():
+            kept[...] = value
+
+    @pl.when(step == 2 * half - 1)
+    def _():
+        for tile in range(half):
+            copy(tile).wait_send()
+
+
+def weight_grad(left_own, left_oth, right_own, right_oth, crossed, cost):
+    half, cols = right_own.shape
+    rows = left_own.shape[1] // 4
+    splits = 2 if cols > 2048 else 1
+    wide = cols // splits
+    out = pltpu.HBM((rows, cols), BF16)
+
+    def tile(i):
+        return lax.rem((i + 1) // 2, 2) if splits == 2 else 0
+
+    def columns(part):
+        def index(i):
+            quarter = 3 - i // splits
+            return 0, (quarter // 2 * 4 + part * 2 + lax.rem(quarter, 2) if crossed else quarter * 2 + part)
+
+        return pl.BlockSpec((half, rows // 2), index)
+
+    last = 4 * splits - 1
+    return pl.pallas_call(
+        functools.partial(weight_grad_kernel, splits),
+        grid=(4 * splits,),
+        in_specs=[
+            columns(0),
+            columns(1),
+            columns(0),
+            columns(1),
+            pl.BlockSpec((half, wide), lambda i: (0, tile(i))),
+            pl.BlockSpec((half, wide), lambda i: (0, tile(i))),
+        ],
+        out_specs=[
+            pl.BlockSpec((rows, wide), lambda i: (0, jnp.where(i < last - 2, 0, 1) if splits == 2 else 0)),
+            pl.BlockSpec((rows, wide), lambda i: (0, jnp.where(i < last, 1, 0) if splits == 2 else 0)),
+        ],
+        out_shape=[out, out],
+        scratch_shapes=[
+            pltpu.VMEM((2 * splits, rows, wide), BF16),
+            pltpu.VMEM((2 * splits, rows, wide), BF16),
+            pltpu.SemaphoreType.DMA((2 * splits,)),
+            pltpu.SemaphoreType.DMA((2 * splits,)),
+        ],
+        compiler_params=pltpu.CompilerParams(
+            collective_id=2 * splits + crossed, has_side_effects=True, vmem_limit_bytes=48 << 20
+        ),
+        cost_estimate=pl.CostEstimate(
+            flops=int(cost * 16 * half * rows * cols), bytes_accessed=int(cost * 16 * half * cols), transcendentals=0
+        ),
+        name="weight_grad",
+    )(left_own, left_own, left_oth, left_oth, right_own, right_oth)
+
+
+ROWS = 64
+
+
+def arranged(source, into, bits):
+    me = lax.axis_index("dp")
+    count = 1 << len(bits)
+    cols = source.shape[1] // count
+    for place in range(count):
+        block = pl.ds(pl.multiple_of(block_from(me, place, bits) * cols, cols), cols)
+        into[:, place * cols : (place + 1) * cols] = source[:, block]
+
+
+def feed_kernel(bits, sub, tokens, part, other, gain, grad_hidden, w_gate, w_up, middle, cols, hidden, grad_gate, grad_up, normed):
+    @pl.when(pl.program_id(0) == 0)
+    def _():
+        def rows_step(index, _):
+            rows = pl.ds(pl.multiple_of(index * ROWS, ROWS), ROWS)
+            total = tokens[rows, :].astype(F32) + (part[rows, :].astype(F32) + other[rows, :].astype(F32))
+            middle[rows, :] = total
+            scale = lax.rsqrt(jnp.mean(total * total, axis=-1, keepdims=True) + EPS)
+            normed[rows, :] = (total * scale * gain[...]).astype(BF16)
+            return 0
+
+        lax.fori_loop(0, tokens.shape[0] // ROWS, rows_step, 0)
+        arranged(normed, cols, bits)
+
+    for start in range(0, w_gate.shape[1], sub):
+        part_cols = slice(start, start + sub)
+        gate = jnp.dot(normed[...], w_gate[:, part_cols], preferred_element_type=F32)
+        up = jnp.dot(normed[...], w_up[:, part_cols], preferred_element_type=F32)
+        squared = gate * gate
+        tanh = jnp.tanh(GELU_A * gate * (1.0 + GELU_B * squared))
+        lift = 0.5 + 0.5 * tanh
+        slope = lift + gate * (1.0 - tanh * tanh) * (0.5 * GELU_A + (1.5 * GELU_A * GELU_B) * squared)
+        gelu = gate * lift
+        back = grad_hidden[:, part_cols].astype(F32)
+        hidden[:, part_cols] = (gelu * up).astype(BF16)
+        grad_gate[:, part_cols] = (back * up * slope).astype(BF16)
+        grad_up[:, part_cols] = (back * gelu).astype(BF16)
+
+
+def feed(tokens, part, other, gain, grad_hidden, w_gate, w_up, bits, wide=512, sub=256):
+    rows, model = tokens.shape
+    cols = w_gate.shape[1]
+    whole = pl.BlockSpec((rows, model), lambda n: (0, 0))
+    piece = pl.BlockSpec((rows, wide), lambda n: (0, n))
+    weight = pl.BlockSpec((model, wide), lambda n: (0, n))
+    out = jax.ShapeDtypeStruct((rows, cols), BF16)
+    return pl.pallas_call(
+        functools.partial(feed_kernel, bits, sub),
+        grid=(cols // wide,),
+        in_specs=[whole] * 3 + [pl.BlockSpec((1, model), lambda n: (0, 0)), piece, weight, weight],
+        out_specs=[whole, whole, piece, piece, piece],
+        out_shape=[jax.ShapeDtypeStruct((rows, model), F32), jax.ShapeDtypeStruct((rows, model), BF16), out, out, out],
+        scratch_shapes=[pltpu.VMEM((rows, model), BF16)],
+        compiler_params=pltpu.CompilerParams(vmem_limit_bytes=56 << 20),
+        cost_estimate=pl.CostEstimate(
+            flops=4 * rows * model * cols, bytes_accessed=4 * model * cols + 12 * rows * cols, transcendentals=rows * cols
+        ),
+        name="feed",
+    )(tokens, part, other, gain, grad_hidden, w_gate, w_up)
+
+
+def pull_kernel(bits, middle, back, other, cot, gain, weight, grad, cols, into, rec):
+    @pl.when(pl.program_id(0) == 0)
+    def _():
+        def rows_step(index, _):
+            rows = pl.ds(pl.multiple_of(index * ROWS, ROWS), ROWS)
+            values = middle[rows, :]
+            scale = lax.rsqrt(jnp.mean(values * values, axis=-1, keepdims=True) + EPS)
+            lifted = gain[...] * (back[rows, :].astype(F32) + other[rows, :].astype(F32))
+            pulled = jnp.mean(values * lifted, axis=-1, keepdims=True)
+            total = cot[rows, :].astype(F32) + (scale * lifted - values * (scale * scale * scale * pulled))
+            grad[rows, :] = total
+            rec[rows, :] = total.astype(BF16)
+            return 0
+
+        lax.fori_loop(0, middle.shape[0] // ROWS, rows_step, 0)
+        arranged(rec, cols, bits)
+
+    into[...] = matmul_right(rec[...], weight[...])
+
+
+def pull(middle, back, other, cot, gain, weight, bits, wide=640):
+    rows, model = middle.shape
+    cols = weight.shape[0]
+    wide = wide if cols % wide == 0 else cols
+    whole = pl.BlockSpec((rows, model), lambda n: (0, 0))
+    return pl.pallas_call(
+        functools.partial(pull_kernel, bits),
+        grid=(cols // wide,),
+        in_specs=[whole] * 4 + [pl.BlockSpec((1, model), lambda n: (0, 0)), pl.BlockSpec((wide, model), lambda n: (n, 0))],
+        out_specs=[whole, whole, pl.BlockSpec((rows, wide), lambda n: (0, n))],
+        out_shape=[
+            jax.ShapeDtypeStruct((rows, model), F32),
+            jax.ShapeDtypeStruct((rows, model), BF16),
+            jax.ShapeDtypeStruct((rows, cols), F32),
+        ],
+        scratch_shapes=[pltpu.VMEM((rows, model), BF16)],
+        compiler_params=pltpu.CompilerParams(vmem_limit_bytes=56 << 20),
+        cost_estimate=pl.CostEstimate(
+            flops=2 * rows * model * cols, bytes_accessed=16 * rows * model + 4 * rows * cols, transcendentals=0
+        ),
+        name="pull",
+    )(middle, back, other, cot, gain, weight)
+
+
+def two_back_kernel(first, first_w, second, second_w, out):
+    out[...] = (matmul_right(first[...], first_w[...]) + matmul_right(second[...], second_w[...])).astype(BF16)
+
+
+def two_back(first, first_w, second, second_w, cost=1.0):
+    rows, depth = first.shape
+    cols = first_w.shape[0]
+    step = 512
+    left = pl.BlockSpec((rows, depth), lambda n: (0, 0))
+    right = pl.BlockSpec((step, depth), lambda n: (n, 0))
+    return pl.pallas_call(
+        two_back_kernel,
+        grid=(cols // step,),
+        in_specs=[left, right, left, right],
+        out_specs=pl.BlockSpec((rows, step), lambda n: (0, n)),
+        out_shape=jax.ShapeDtypeStruct((rows, cols), BF16),
+        compiler_params=pltpu.CompilerParams(vmem_limit_bytes=48 << 20),
+        cost_estimate=pl.CostEstimate(
+            flops=int(cost * 4 * rows * depth * cols), bytes_accessed=int(cost * 4 * depth * (rows + cols)), transcendentals=0
+        ),
+        name="two_back",
+    )(first, first_w, second, second_w)
+
+
+def swap(value):
+    return lax.ppermute(value, "tp", [(0, 1), (1, 0)])
+
+
+def flip(value, bit):
+    count = lax.axis_size("dp")
+    return lax.ppermute(value, "dp", [(source, source ^ bit) for source in range(count)])
+
+
+class Reduction:
+    def __init__(self, left, right, count, crossed=False, cost=1.0):
+        self.bits = stage_bits(count, crossed)[1:]
+        sent, self.keep = weight_grad(*left, *right, crossed, cost)
+        self.pass_on(sent)
+
+    def pass_on(self, sent):
+        self.received = flip(sent, self.bits.pop(0))
+
+    def step(self, *others):
+        received = after(self.received, *others)
+        middle = received.shape[0] // 2
+        sent = (self.keep[middle:].astype(F32) + received[middle:].astype(F32)).astype(BF16)
+        keep = (self.keep[:middle].astype(F32) + received[:middle].astype(F32)).astype(BF16)
+        sent, self.keep = lax.optimization_barrier((sent, keep))
+        self.pass_on(sent)
+        return sent
+
+    def total(self, *others):
+        while self.bits:
+            self.step(*others)
+        return self.keep.astype(F32) + after(self.received, *others).astype(F32)
+
+
+def after(value, *others):
+    return lax.optimization_barrier((value, *others))[0]
+
+
+def norm_back(values, gain, grad):
+    scale = lax.rsqrt(jnp.mean(values * values, axis=-1, keepdims=True) + EPS)
+    lifted = gain * grad
+    pull = jnp.mean(values * lifted, axis=-1, keepdims=True)
+    return scale * lifted - values * (scale * scale * scale * pull)
+
+
+def local_channels(
+    layer_in, cotangent, resets, norm_gains, w_x, w_y, conv_w, lru_bias, a_param, gate_blocks, w_out, w_gate, w_up, w_down,
+):
+    place = lax.axis_index("tp")
+    me = lax.axis_index("dp")
+    count = lax.axis_size("dp")
+    bits = stage_bits(count)
+    width = w_x.shape[1]
+    full_width = conv_w.shape[1]
+    heads = gate_blocks.shape[1] // 2
+    model = norm_gains.shape[1]
+
+    own_in, own_cot = layer_in[0], cotangent[0]
+    oth_in = swap(own_in)
+    oth_resets = swap(resets[0])
+    oth_cot = swap(own_cot)
+    normed_own = rms_scale(own_in.astype(F32), norm_gains[0]).astype(BF16)
+    bx_own = matmul(normed_own, w_x).astype(BF16)
+    by_own = matmul(normed_own, w_y)
+
+    first_place = place == 0
+    in_time = jnp.where(first_place, resets[0], oth_resets), jnp.where(first_place, oth_resets, resets[0])
+    keep = 1.0 - jnp.concatenate(in_time).astype(F32)
+    keep_1 = jnp.concatenate([jnp.ones((1,), F32), keep[:-1]])
+    keep_2 = jnp.concatenate([jnp.ones((1,), F32), keep_1[:-1]])
+    valid = jnp.stack([keep, keep * keep_1, keep * keep_1 * keep_2]).reshape(3, 2, SEGMENTS, -1)
+    valid = jnp.where(first_place, valid, valid[:, ::-1]).reshape(3, 2 * SEGMENTS, -1)
+    later = jnp.concatenate([valid[:, 1:, :3], valid[:, :1, :3]], axis=1)
+    mask = jnp.swapaxes(jnp.concatenate([valid, later], axis=2), 1, 2)
+    mask = jnp.broadcast_to(mask[..., None], mask.shape + (128,))
+    table = jnp.concatenate([conv_w, lru_bias, -8.0 * jax.nn.softplus(a_param)[None]], axis=0)
+    prm = lax.dynamic_slice(table, (0, place * width), (8, width))
+    gates = lax.dynamic_slice_in_dim(gate_blocks, place * heads, heads, axis=1)
+
+    gh_own = matmul_right(after(own_cot, bx_own, by_own), w_down)
+    normed_oth = rms_scale(after(oth_in, gh_own).astype(F32), norm_gains[0]).astype(BF16)
+    bx_oth = matmul(normed_oth, w_x).astype(BF16)
+    by_oth = matmul(normed_oth, w_y)
+    gated_own, gated_oth, *kept = rec_fwd(bx_own, bx_oth, by_own, by_oth, mask, prm, gates)
+
+    part_oth = matmul(gated_oth, w_out).astype(BF16)
+    swap_own = swap(part_oth)
+    part_own = matmul(after(gated_own, part_oth), w_out).astype(BF16)
+    swap_oth = swap(part_own)
+    gh_oth = matmul_right(after(oth_cot, part_own), w_down)
+    cot_cols = arrange(after(own_cot, gh_oth), oth_cot, bits)
+    normed_cols = arrange(after(normed_own, cot_cols[0]), normed_oth, bits)
+    gains = norm_gains[1:2]
+
+    middle_own, two_own, hidden_own, gg_own, gu_own = feed(
+        own_in, part_own, after(swap_own, normed_cols[0]), gains, gh_own, w_gate, w_up, bits
+    )
+    back_own = two_back(gg_own, w_gate, gu_own, w_up)
+    back_own_swapped = swap(back_own)
+    middle_oth, two_oth, hidden_oth, gg_oth, gu_oth = feed(
+        oth_in, part_oth, after(swap_oth, back_own), gains, gh_oth, w_gate, w_up, bits
+    )
+    down = Reduction((after(cot_cols[0], hidden_oth), cot_cols[1]), (hidden_own, hidden_oth), count)
+    gate = Reduction((after(two_own, down.keep), two_oth), (gg_own, gg_oth), count, True)
+    back_oth = two_back(after(gg_oth, gate.keep), w_gate, gu_oth, w_up)
+    back_oth_swapped = swap(back_oth)
+    _, rec_oth, into_oth = pull(middle_oth, back_oth, back_own_swapped, oth_cot, gains, w_out, bits)
+    up = Reduction((after(two_own, into_oth), two_oth), (gu_own, gu_oth), count)
+    done = down.step(up.keep)
+    done = gate.step(done)
+    grad_own, rec_own, into_own = pull(middle_own, back_own, after(back_oth_swapped, done), own_cot, gains, w_out, bits)
+    out = Reduction((rec_own, rec_oth), (gated_own, gated_oth), count)
+    done = down.step(out.keep)
+    gx_own, gx_oth, gy_own, gy_oth, gate_sums, sums = rec_bwd(
+        bx_own, bx_oth, by_own, by_oth, kept, after(into_own, done), into_oth, mask, prm, gates, count
+    )
+
+    lanes = gate_sums.shape[-1]
+    row = jnp.arange(8)[:, None] == 7
+    slopes = -8.0 * lax.dynamic_slice(jax.nn.sigmoid(a_param), (place * width,), (width,))
+    each = full_width // count
+    sums = jnp.swapaxes(jnp.where(row, sums * slopes, sums).reshape(8, count // 2, each), 0, 1)
+    sums = jnp.pad(jnp.concatenate([sums, sums], axis=0), ((0, 0), (0, 0), (0, lanes - each))).astype(BF16)
+    blocks = jnp.concatenate([gate_sums.reshape(count, -1, lanes), sums], axis=1)
+    blocks = lax.psum_scatter(blocks.reshape(-1, lanes), "dp", scatter_dimension=0, tiled=True)
+
+    small_cost = 0.1
+    done = up.step(gx_own)
+    in_x = Reduction((after(normed_cols[0], done), normed_cols[1]), (gx_own, gx_oth), count, cost=small_cost)
+    done = gate.step(in_x.keep)
+    in_y = Reduction((after(normed_cols[0], done), normed_cols[1]), (gy_own, gy_oth), count, cost=small_cost)
+    out_send = matmul(after(hidden_oth, in_y.keep), w_down).astype(BF16)
+    out_swapped = swap(out_send)
+    rec_send = two_back(after(gx_oth, out_send), w_x, gy_oth, w_y, small_cost)
+    rec_swapped = swap(rec_send)
+    down_grad = down.total(rec_send).T
+    done = out.step(down_grad)
+    rec_keep = two_back(after(gx_own, done), w_x, gy_own, w_y, small_cost)
+    done = up.step(rec_keep)
+    gate_grad = gate.total(done)
+    done = in_x.step(gate_grad)
+    done = out.step(done)
+    out_keep = matmul(after(hidden_own, done), w_down).astype(BF16)
+    done = in_y.step(out_keep)
+    layer_out = (middle_own + out_keep.astype(F32) + after(out_swapped, done).astype(F32)).astype(BF16)
+    done = in_x.step(layer_out)
+    up_grad = up.total(done)
+    grad_normed = rec_keep.astype(F32) + after(rec_swapped, up_grad).astype(F32)
+    input_grad = grad_own + norm_back(own_in.astype(F32), norm_gains[0], grad_normed)
+    out_grad = out.total(input_grad).T
+    done = in_y.step(out_grad)
+    others = swap(after(blocks, done))
+    x_grad = in_x.total(others)
+    y_grad = in_y.total(x_grad)
+
+    low, high = jnp.where(first_place, blocks, others), jnp.where(first_place, others, blocks)
+    block_sums = jnp.stack([low[:-8], high[:-8]]).astype(F32).reshape(2 * heads, 2, -1, lanes)
+    small = jnp.where(me < count // 2, low[-8:], high[-8:])[:, :each].astype(F32)
+
+    block = model // count
+
+    def gain_grad(gain, *pairs):
+        weights = sum(
+            jnp.sum(lax.dynamic_slice_in_dim(weight, me * block, block, axis=0).astype(F32) * grad, axis=1)
+            for weight, grad in pairs
+        )
+        return weights / lax.dynamic_slice_in_dim(gain, me * block, block, axis=0)
+
+    gains = jnp.stack(
+        [
+            gain_grad(norm_gains[0], (w_x, x_grad), (w_y, y_grad)),
+            gain_grad(norm_gains[1], (w_gate, gate_grad), (w_up, up_grad)),
+        ]
+    )
+    gains = gains + swap(gains)
+    return (
+        layer_out[None],
+        input_grad[None],
+        gains,
+        x_grad,
+        y_grad,
+        small[0:4],
+        small[4:7],
+        small[7],
+        jnp.swapaxes(block_sums, 0, 1),
+        out_grad,
+        gate_grad,
+        up_grad,
+        down_grad,
+    )
 
 
 def from_behind(value, axis, steps):
@@ -289,8 +1055,16 @@
 
 
 def solution(mesh):
+    rows, cols = mesh.shape["dp"], mesh.shape["tp"]
+    by_channels = cols == 2 and rows >= 16 and rows & (rows - 1) == 0
+
+    def step(*args):
+        heads, model = args[9].shape[1], args[3].shape[1]
+        fits = by_channels and heads % cols == 0 and model % (128 * rows) == 0
+        return (local_channels if fits else local)(*args)
+
     return jax.shard_map(
-        local,
+        step,
         mesh=mesh,
         in_specs=(
             P("dp", "tp", None),

time: 2950 us -> 630 us (0.21)
  waiting for transfers between devices: 1250 us -> 122 us
  local copies, waits for them, and re-layouts: 973 us -> 22.9 us
  Pallas kernels: 0 us -> 298 us
  other arithmetic: 314 us -> 59.3 us
  matrix products: 315 us -> 70.8 us
  blocking collectives: 38.8 us -> 0 us
    reduce_scatter x9 -> x1, waiting for transfers between devices: 671 us -> 0.01 us  [local_channels(): lax.psum_scatter(blocks.reshape(-1, lanes), 'dp', scatter_dimension=0, ti...]
    slice x134 -> x8, local copies, waits for them, and re-layouts: 470 us -> 2.37 us  [the longest x1 0.61 us: local_channels(): gains = norm_gains[1:2]]
    unnamed x27 -> x1, waiting for transfers between devices: 355 us -> 0.02 us
    pallas_call x0 -> x18, Pallas kernels: none -> 298 us  [the longest x6 102 us: weight_grad(): pl.pallas_call(functools.partial(weight_grad_kernel, splits), grid=(4 * s...]
    pad x64 -> x0, local copies, waits for them, and re-layouts: 284 us -> none  [the longest x32 143 us: local(): lax.associative_scan(combine_state, (decay_rate, pushed), axis=0)]
    all_gather x5 -> x0, waiting for transfers between devices: 203 us -> none  [the longest x1 124 us: local(): lax.all_gather(w_x, 'tp', axis=1, tiled=True)]
    add x55 -> x2, other arithmetic: 125 us -> 3.84 us  [the longest x1 3.27 us: local_channels(): grad_own + norm_back(own_in.astype(F32), norm_gains[0], grad_normed)]
    ppermute x5 -> x29, waiting for transfers between devices: 2.76 us -> 122 us  [the longest x18 79.1 us: flip(): lax.ppermute(value, 'dp', [(source, source ^ bit) for source in range(cou...]
  transfers between devices with their start and end apart: 26 -> 30, of which waited for: 17 -> 11; matrix products, arithmetic and copies ran while one was open for 34% -> 22% of each run, Pallas kernels for 0% -> 48%
where the time goes in v4:
time: 630 us; the launch traced here: 624 us
  Pallas kernels  298 us (47%)
  waiting for transfers between devices  122 us (19%)
  matrix products  70.8 us (11%)
  other arithmetic  59.3 us (9%)
  starting transfers between devices  36.6 us (6%)
  local copies, waits for them, and re-layouts  22.9 us (4%)
  between operations  15.2 us (2%)
    pallas_call x6, Pallas kernels, weight_grad(): pl.pallas_call(functools.partial(weight_grad_kernel, splits), grid=(4 * s...  102 us
    ppermute x18, waiting for transfers between devices, flip(): lax.ppermute(value, 'dp', [(source, source ^ bit) for source in range(cou...  79.1 us
    pallas_call x2, Pallas kernels, feed(): pl.pallas_call(functools.partial(feed_kernel, bits, sub), grid=(cols // w...  54.8 us
    pallas_call x4, Pallas kernels, two_back(): pl.pallas_call(two_back_kernel, grid=(cols // step,), in_specs=[left, rig...  52.2 us
    dot_general x8, matrix products, matmul(): return jnp.dot(first_mat, second_mat, preferred_element_type=jnp.float32)  49.9 us
    ppermute x11, waiting for transfers between devices, swap(): return lax.ppermute(value, 'tp', [(0, 1), (1, 0)])  42.5 us
    pallas_call x1, Pallas kernels, rec_bwd(): pl.pallas_call(functools.partial(rec_bwd_kernel, count), grid=(heads,), i...  33.6 us
    pallas_call x2, Pallas kernels, pull(): pl.pallas_call(functools.partial(pull_kernel, bits), grid=(cols // wide,)...  27.9 us
  transfers between devices with their start and end apart: 30, of which 11 were waited for; matrix products, arithmetic and copies ran while one was open for 22% of the time, Pallas kernels for 48%

profile of v4, /device:TPU:0, one launch (start us, length us, event | category | flops | bytes accessed | tf_op | source)
XLA Modules:
  0.0 624.3 jit_solution(15775136630657719792)
XLA Ops:
  7.3 3.0 collective-permute-start
  16.2 7.5 %convolution_convert_fusion.5.bx_own = bf16[512,1280]{1,0:T(8,128)(2,1)} fusion(bf16[512,2048]{1,0:T(8,128)(2,1)S(1)} %fusion.5.first, bf16[2048,1280]{1,0:T(8,128)(2,1)} %first_w.7), kind=kOutput, calls=%fused_computation.28 | convolution fusion | flops 2685009920 | bytes 8650752 | tf_op jit(solution)/shard_map/dot_general | solution.py:799
  23.7 4.5 fusion.33.by_own
  28.3 8.8 %fusion.34.grad_hidden = f32[512,3072]{1,0:T(8,128)} fusion(bf16[512,2048]{1,0:T(8,128)(2,1)S(1)} %bitcast.60, bf16[3072,2048]{1,0:T(8,128)(2,1)S(1)} %bitcast.87), kind=kOutput, calls=%fused_computation.114 | convolution fusion | flops 6442450944 | bytes 20971520 | tf_op jit(solution)/shard_map/dot_general | solution.py:809
  39.6 17.4 %collective-permute-done.1 = s32[512]{0:T(512)S(1)} collective-permute-done((s32[512]{0:T(512)}, s32[512]{0:T(512)S(1)}, u32[]{:S(2)}, u32[]{:S(2)}) %collective-permute-start.1) | collective-permute-done | bytes 2080 | tf_op jit(solution)/shard_map/ppermute | solution.py:585
  62.3 5.5 convolution_convert_fusion.4.bx_oth
  67.9 4.4 fusion.35.by_oth
  72.8 23.4 %rec_fwd.1 = (bf16[512,1280]{1,0:T(8,128)(2,1)S(1)}, bf16[512,1280]{1,0:T(8,128)(2,1)S(1)}, f32[64,16,1280]{2,1,0:T(8,128)}, f32[64,16,1280]{2,1,0:T(8,128)}, f3...) custom-call(bf16[512,1280]{1,0:T(8,128)(2,1)S(1)} %copy-done.18, ...), custom_call_target="tpu_custom_call" | custom-call | flops 1473249280 | bytes 34078720 | tf_op jit(solution)/shard_map/rec_fwd/pallas_call | solution.py:258
  96.2 3.2 convolution_convert_fusion.3.part
  101.6 4.3 convolution_convert_fusion.2.part
  105.9 12.1 %fusion.36.grad_hidden = f32[512,3072]{1,0:T(8,128)} fusion(bf16[512,2048]{1,0:T(8,128)(2,1)} %collective-permute-done.3.second.cot, bf16[3072,2048]{1,0:T(8,128)(2,1)} %param.27), kind=kOutput, calls=%fused_computation.116 | convolution fusion | flops 6442450944 | bytes 20971520 | tf_op jit(solution)/shard_map/dot_general | solution.py:809
  118.0 2.9 arrange.2
  123.8 24.3 %collective-permute-done.2.other = bf16[512,2048]{1,0:T(8,128)(2,1)S(1)} collective-permute-done((bf16[512,2048]{1,0:T(8,128)(2,1)S(1)}, bf16[512,2048]{1,0:T(8,128)(2,1)S(1)}, u32[]{:S(2)}, u32[]{:S(2)}) %collective-permute-start.2) | collective-permute-done | bytes 2097184 | tf_op jit(solution)/shard_map/ppermute | solution.py:585
  149.5 27.2 %feed.2 = (f32[512,2048]{1,0:T(8,128)}, bf16[512,2048]{1,0:T(8,128)(2,1)}, bf16[512,3072]{1,0:T(8,128)(2,1)}, bf16[512,3072]{1,0:T(8,128)(2,1)}, bf16[512,3072]{1,0:T(8,128)(2,1)}) custom-call(bf16[512,2048]{1,0:T(8,128)(2,1)} %bitcast.63, bf16[512,2048]{1,0:T(8,128)(2,1)} %convolution_convert_fusion.2.part, bf16[512,2048]{1,0:T(8,128)(2,1)} %copy-done.61, ...), custom_call_target="tpu_custom_call" | custom-call | flops 12884901888 | bytes 44040192 | tf_op jit(solution)/shard_map/feed/pallas_call | solution.py:501
  178.6 17.7 %two_back.4.back = bf16[512,2048]{1,0:T(8,128)(2,1)S(1)} custom-call(bf16[512,3072]{1,0:T(8,128)(2,1)S(1)} %copy-done.27, bf16[2048,3072]{1,0:T(8,128)(2,1)} %first_w.5, bf16[512,3072]{1,0:T(8,128)(2,1)} %get-tuple-element.135.second.right_own, bf16[2048,3072]{1,0:T(8,128)(2,1)} %second_w.5), custom_call_target="tpu_custom_call" | custom-call | flops 12884901888 | bytes 31457280 | tf_op jit(solution)/shard_map/two_back/pallas_call | solution.py:570
  198.4 27.6 %feed.3 = (f32[512,2048]{1,0:T(8,128)}, bf16[512,2048]{1,0:T(8,128)(2,1)}, bf16[512,3072]{1,0:T(8,128)(2,1)}, bf16[512,3072]{1,0:T(8,128)(2,1)}, bf16[512,3072]{1,0:T(8,128)(2,1)}) custom-call(bf16[512,2048]{1,0:T(8,128)(2,1)} %collective-permute-done.tokens, bf16[512,2048]{1,0:T(8,128)(2,1)} %copy-done.60, bf16[512,2048]{1,0:T(8,128)(2,1)} %collective-permute-done.4.other, ...), custom_call_target="tpu_custom_call" | custom-call | flops 12884901888 | bytes 44040192 | tf_op jit(solution)/shard_map/feed/pallas_call | solution.py:501
  227.6 23.0 %weight_grad.6 = (bf16[512,3072]{1,0:T(8,128)(2,1)}, bf16[512,3072]{1,0:T(8,128)(2,1)}) custom-call(bf16[512,2048]{1,0:T(8,128)(2,1)S(1)} %get-tuple-element.140.own_a.own_b, bf16[512,2048]{1,0:T(8,128)(2,1)S(1)} %get-tuple-element.140.own_a.own_b, bf16[512,2048]{1,0:T(8,128)(2,1)S(1)} %copy-done.21, bf16[512,2048]{1,0:T(8,128)(2,1)S(1)} %copy-done.21, ...), custom_call_target="tpu_custom_call" | custom-call | flops 12884901888 | bytes 25165824 | tf_op jit(solution)/shard_map/weight_grad/pallas_call | solution.py:421
  253.9 23.2 %weight_grad.7 = (bf16[512,3072]{1,0:T(8,128)(2,1)}, bf16[512,3072]{1,0:T(8,128)(2,1)}) custom-call(bf16[512,2048]{1,0:T(8,128)(2,1)S(1)} %copy-done.29, bf16[512,2048]{1,0:T(8,128)(2,1)S(1)} %copy-done.29, bf16[512,2048]{1,0:T(8,128)(2,1)S(1)} %copy-done.31, bf16[512,2048]{1,0:T(8,128)(2,1)S(1)} %copy-done.31, ...), custom_call_target="tpu_custom_call" | custom-call | flops 12884901888 | bytes 25165824 | tf_op jit(solution)/shard_map/weight_grad/pallas_call | solution.py:421
  278.6 17.7 %two_back.5.back = bf16[512,2048]{1,0:T(8,128)(2,1)S(1)} custom-call(bf16[512,3072]{1,0:T(8,128)(2,1)S(1)} %copy-done.28, bf16[2048,3072]{1,0:T(8,128)(2,1)} %first_w.5, bf16[512,3072]{1,0:T(8,128)(2,1)} %get-tuple-element.147.second.right_oth, bf16[2048,3072]{1,0:T(8,128)(2,1)} %second_w.5), custom_call_target="tpu_custom_call" | custom-call | flops 12884901888 | bytes 31457280 | tf_op jit(solution)/shard_map/two_back/pallas_call | solution.py:570
  297.6 14.0 %pull.2 = (f32[512,2048]{1,0:T(8,128)}, bf16[512,2048]{1,0:T(8,128)(2,1)}, f32[512,1280]{1,0:T(8,128)}) custom-call(f32[512,2048]{1,0:T(8,128)} %get-tuple-element.150.middle, bf16[512,2048]{1,0:T(8,128)(2,1)} %copy-done.17, bf16[512,2048]{1,0:T(8,128)(2,1)} %collective-permute-done.8.other, bf16[512,2048]{1,0:T(8,128)(2,1)} %collective-permute-done.3.second.cot, ...), custom_call_target="tpu_custom_call" | custom-call | flops 2684354560 | bytes 19398656 | tf_op jit(solution)/shard_map/pull/pallas_call | solution.py:541
  313.2 22.9 %weight_grad.8 = (bf16[512,3072]{1,0:T(8,128)(2,1)}, bf16[512,3072]{1,0:T(8,128)(2,1)}) custom-call(bf16[512,2048]{1,0:T(8,128)(2,1)S(1)} %copy-done.30, bf16[512,2048]{1,0:T(8,128)(2,1)S(1)} %copy-done.30, bf16[512,2048]{1,0:T(8,128)(2,1)S(1)} %copy-done.32, bf16[512,2048]{1,0:T(8,128)(2,1)S(1)} %copy-done.32, ...), custom_call_target="tpu_custom_call" | custom-call | flops 12884901888 | bytes 25165824 | tf_op jit(solution)/shard_map/weight_grad/pallas_call | solution.py:421
  336.9 4.9 add_convert_fusion.5
  342.1 6.3 %collective-permute-done.6 = bf16[512,3072]{1,0:T(8,128)(2,1)} collective-permute-done((bf16[512,3072]{1,0:T(8,128)(2,1)}, bf16[512,3072]{1,0:T(8,128)(2,1)}, u32[]{:S(2)}, u32[]{:S(2)}) %collective-permute-start.6) | collective-permute-done | bytes 3145760 | tf_op jit(solution)/shard_map/ppermute | solution.py:590
  348.4 4.7 add_convert_fusion.3
  353.5 13.9 %pull.3 = (f32[512,2048]{1,0:T(8,128)}, bf16[512,2048]{1,0:T(8,128)(2,1)}, f32[512,1280]{1,0:T(8,128)}) custom-call(f32[512,2048]{1,0:T(8,128)} %get-tuple-element.132.middle, bf16[512,2048]{1,0:T(8,128)(2,1)} %copy-done.16, bf16[512,2048]{1,0:T(8,128)(2,1)} %collective-permute-done.5.other, bf16[512,2048]{1,0:T(8,128)(2,1)} %bitcast.59, ...), custom_call_target="tpu_custom_call" | custom-call | flops 2684354560 | bytes 19398656 | tf_op jit(solution)/shard_map/pull/pallas_call | solution.py:541
  369.0 10.7 %weight_grad.9 = (bf16[512,1280]{1,0:T(8,128)(2,1)}, bf16[512,1280]{1,0:T(8,128)(2,1)}) custom-call(bf16[512,2048]{1,0:T(8,128)(2,1)S(1)} %copy-done.22, bf16[512,2048]{1,0:T(8,128)(2,1)S(1)} %copy-done.22, bf16[512,2048]{1,0:T(8,128)(2,1)} %get-tuple-element.160.oth_a.oth_b, bf16[512,2048]{1,0:T(8,128)(2,1)} %get-tuple-element.160.oth_a.oth_b, ...), custom_call_target="tpu_custom_call" | custom-call | flops 5368709120 | bytes 10485760 | tf_op jit(solution)/shard_map/weight_grad/pallas_call | solution.py:421
  381.5 2.8 add_convert_fusion.11
  384.3 2.6 collective-permute-start.11
  386.9 33.6 %rec_bwd.1 = (bf16[512,1280]{1,0:T(8,128)(2,1)S(1)}, bf16[512,1280]{1,0:T(8,128)(2,1)}, bf16[512,1280]{1,0:T(8,128)(2,1)}, bf16[512,1280]{1,0:T(8,128)(2,1)}, bf...) custom-call(bf16[512,1280]{1,0:T(8,128)(2,1)} %convolution_convert_fusion.5.bx_own, bf16[512,1280]{1,0:T(8,128)(2,1)} %copy-done.19, ...), custom_call_target="tpu_custom_call" | custom-call | flops 2880962560 | bytes 44564480 | tf_op jit(solution)/shard_map/rec_bwd/pallas_call | solution.py:287
  424.4 5.3 add_convert_fusion.1
  431.1 10.6 %weight_grad.10 = (bf16[512,1280]{1,0:T(8,128)(2,1)}, bf16[512,1280]{1,0:T(8,128)(2,1)}) custom-call(bf16[512,2048]{1,0:T(8,128)(2,1)S(1)} %get-tuple-element.184.own_a.own_b, bf16[512,2048]{1,0:T(8,128)(2,1)S(1)} %get-tuple-element.184.own_a.own_b, bf16[512,2048]{1,0:T(8,128)(2,1)} %copy-done.2, bf16[512,2048]{1,0:T(8,128)(2,1)} %copy-done.2, ...), custom_call_target="tpu_custom_call" | custom-call | flops 536870912 | bytes 1048576 | tf_op jit(solution)/shard_map/weight_grad/pallas_call | solution.py:421
  441.8 3.0 add_convert_fusion.9
  444.8 11.2 %weight_grad.11 = (bf16[512,1280]{1,0:T(8,128)(2,1)}, bf16[512,1280]{1,0:T(8,128)(2,1)}) custom-call(bf16[512,2048]{1,0:T(8,128)(2,1)S(1)} %get-tuple-element.184.own_a.own_b, bf16[512,2048]{1,0:T(8,128)(2,1)S(1)} %get-tuple-element.184.own_a.own_b, bf16[512,2048]{1,0:T(8,128)(2,1)} %copy-done.2, bf16[512,2048]{1,0:T(8,128)(2,1)} %copy-done.2, ...), custom_call_target="tpu_custom_call" | custom-call | flops 536870912 | bytes 1048576 | tf_op jit(solution)/shard_map/weight_grad/pallas_call | solution.py:421
  456.0 10.6 %convolution_convert_fusion.1 = bf16[512,2048]{1,0:T(8,128)(2,1)} fusion(bf16[512,3072]{1,0:T(8,128)(2,1)S(1)} %copy-done.63, bf16[3072,2048]{1,0:T(8,128)(2,1)} %param.27), kind=kOutput, calls=%fused_computation.24 | convolution fusion | flops 6443499520 | bytes 17825792 | tf_op jit(solution)/shard_map/dot_general | solution.py:799
  468.9 8.6 %two_back.6 = bf16[512,2048]{1,0:T(8,128)(2,1)S(1)} custom-call(bf16[512,1280]{1,0:T(8,128)(2,1)S(1)} %copy-done.12, bf16[2048,1280]{1,0:T(8,128)(2,1)} %first_w.7, bf16[512,1280]{1,0:T(8,128)(2,1)S(1)} %copy-done.13, bf16[2048,1280]{1,0:T(8,128)(2,1)} %second_w.7), custom_call_target="tpu_custom_call" | custom-call | flops 536870912 | bytes 1310720 | tf_op jit(solution)/shard_map/two_back/pallas_call | solution.py:570
  484.5 8.2 %two_back.7 = bf16[512,2048]{1,0:T(8,128)(2,1)S(1)} custom-call(bf16[512,1280]{1,0:T(8,128)(2,1)S(1)} %copy-done.10, bf16[2048,1280]{1,0:T(8,128)(2,1)} %first_w.7, bf16[512,1280]{1,0:T(8,128)(2,1)S(1)} %copy-done.11, bf16[2048,1280]{1,0:T(8,128)(2,1)} %second_w.7), custom_call_target="tpu_custom_call" | custom-call | flops 536870912 | bytes 1310720 | tf_op jit(solution)/shard_map/two_back/pallas_call | solution.py:570
  496.0 11.3 %collective-permute-done.16 = bf16[128,3072]{1,0:T(8,128)(2,1)} collective-permute-done((bf16[128,3072]{1,0:T(8,128)(2,1)}, bf16[128,3072]{1,0:T(8,128)(2,1)}, u32[]{:S(2)}, u32[]{:S(2)}) %collective-permute-start.16) | collective-permute-done | bytes 786464 | tf_op jit(solution)/shard_map/ppermute | solution.py:590
  507.3 2.8 multiply_reduce_fusion.1
  510.1 3.0 collective-permute-done.15
  515.0 18.0 %collective-permute-done.14 = bf16[256,1280]{1,0:T(8,128)(2,1)S(1)} collective-permute-done((bf16[256,1280]{1,0:T(8,128)(2,1)S(1)}, bf16[256,1280]{1,0:T(8,128)(2,1)S(1)}, u32[]{:S(2)}, u32[]{:S(2)}) %collective-permute-start.14) | collective-permute-done | bytes 655392 | tf_op jit(solution)/shard_map/ppermute | solution.py:590
  533.3 10.0 %convolution_convert_fusion = bf16[512,2048]{1,0:T(8,128)(2,1)S(1)} fusion(bf16[512,3072]{1,0:T(8,128)(2,1)S(1)} %copy-done.62, bf16[3072,2048]{1,0:T(8,128)(2,1)} %param.27), kind=kOutput, calls=%fused_computation.23 | convolution fusion | flops 6443499520 | bytes 17825792 | tf_op jit(solution)/shard_map/dot_general | solution.py:799
  543.3 3.3 collective-permute-start.25
  549.5 15.3 %collective-permute-done.22 = bf16[256,1280]{1,0:T(8,128)(2,1)S(1)} collective-permute-done((bf16[256,1280]{1,0:T(8,128)(2,1)S(1)}, bf16[256,1280]{1,0:T(8,128)(2,1)S(1)}, u32[]{:S(2)}, u32[]{:S(2)}) %collective-permute-start.22) | collective-permute-done | bytes 655392 | tf_op jit(solution)/shard_map/ppermute | solution.py:590
  565.7 2.7 multiply_reduce_fusion
  570.7 3.3 fusion.8
  581.2 2.9 collective-permute-start.27
  585.4 18.0 %collective-permute-done.23 = bf16[128,1280]{1,0:T(8,128)(2,1)} collective-permute-done((bf16[128,1280]{1,0:T(8,128)(2,1)}, bf16[128,1280]{1,0:T(8,128)(2,1)}, u32[]{:S(2)}, u32[]{:S(2)}) %collective-permute-start.23) | collective-permute-done | bytes 327712 | tf_op jit(solution)/shard_map/ppermute | solution.py:590
  605.5 4.9 collective-permute-done.27
  (264 shorter events, 81.8 us)
Async XLA Ops:
  7.2 30.6 %copy-start = (bf16[2,10,256,256]{3,2,1,0:T(8,128)(2,1)S(1)}, bf16[2,10,256,256]{3,2,1,0:T(8,128)(2,1)}, u32[]{:S(2)}) copy-start(bf16[2,10,256,256]{3,2,1,0:T(8,128)(2,1)} %param.23) | copy-start | bytes 7864324
  7.2 569.9 %reduce-scatter.2.cloned.1.call-start = ((), (), s32[]{:S(2)}) async-start(), calls=%async_computation.1 | async-start | bytes 1462272 | tf_op jit(solution)/shard_map/reduce_scatter | solution.py:707
  7.3 50.6 %collective-permute-start = (bf16[512,2048]{1,0:T(8,128)(2,1)}, bf16[512,2048]{1,0:T(8,128)(2,1)}, u32[]{:S(2)}, u32[]{:S(2)}) collective-permute-start(bf16[512,2048]{1,0:T(8,128)(2,1)} %bitcast.62), channel_id=1, source_target_pairs={{0,1},{1,0},{2,3},{3,2},{4,5},{5,4},{6,7},{7,6},{8,9},{9,8},{10,11... | collective-permute-start | bytes 6291464 | tf_op jit(solution)/shard_map/ppermute | solution.py:585
  10.3 46.8 %collective-permute-start.1 = (s32[512]{0:T(512)}, s32[512]{0:T(512)S(1)}, u32[]{:S(2)}, u32[]{:S(2)}) collective-permute-start(s32[512]{0:T(512)} %bitcast.83), channel_id=1, source_target_pairs={{0,1},{1,0},{2,3},{3,2},{4,5},{5,4},{6,7},{7,6},{8,9},{9,8},{10,11... | collective-permute-start | bytes 6152 | tf_op jit(solution)/shard_map/ppermute | solution.py:585
  10.3 95.6 %collective-permute-start.3 = (bf16[512,2048]{1,0:T(8,128)(2,1)}, bf16[512,2048]{1,0:T(8,128)(2,1)}, u32[]{:S(2)}, u32[]{:S(2)}) collective-permute-start(bf16[512,2048]{1,0:T(8,128)(2,1)} %bitcast.58), channel_id=1, source_target_pairs={{0,1},{1,0},{2,3},{3,2},{4,5},{5,4},{6,7},{7,6},{8,9},{9,8},{10,11... | collective-permute-start | bytes 6291464 | tf_op jit(solution)/shard_map/ppermute | solution.py:585
  15.0 45.0 %copy-start.46 = (f32[1,2048]{1,0:T(1,128)}, f32[1,2048]{1,0:T(1,128)S(1)}, u32[]{:S(2)}) copy-start(f32[1,2048]{1,0:T(1,128)S(1)} %get-tuple-element.318) | copy-start | bytes 24580
  37.1 20.0 %copy-start.58 = (s32[1,512]{1,0:T(1,128)S(1)}, s32[1,512]{1,0:T(1,128)}, u32[]{:S(2)}) copy-start(s32[1,512]{1,0:T(1,128)} %param.16) | copy-start | bytes 6148
  62.3 33.9 %slice-start.4 = ((s8[5242880]{0:T(1024)(128)(4,1)}), s8[4194304]{0:T(1024)(128)(4,1)S(1)}, s32[]{:S(2)}) async-start(s8[5242880]{0:T(1024)(128)(4,1)} %bitcast.68), calls=%async_computation.6 | async-start | bytes 8388608
  67.9 28.3 %slice-start.5 = ((s8[5242880]{0:T(1024)(128)(4,1)}), s8[1048576]{0:T(1024)(128)(4,1)S(1)}, s32[]{:S(2)}) async-start(s8[5242880]{0:T(1024)(128)(4,1)} %bitcast.68), calls=%async_computation.7 | async-start | bytes 2097152
  72.8 23.4 %copy-start.7 = (f32[3,67,16,128]{3,2,1,0:T(8,128)}, f32[3,67,16,128]{3,2,1,0:T(8,128)S(1)}, u32[]{:S(2)}) copy-start(f32[3,67,16,128]{3,2,1,0:T(8,128)S(1)} %broadcast_in_dim.11.mask_ref) | copy-start | bytes 4939780
  99.4 48.7 %collective-permute-start.2 = (bf16[512,2048]{1,0:T(8,128)(2,1)S(1)}, bf16[512,2048]{1,0:T(8,128)(2,1)S(1)}, u32[]{:S(2)}, u32[]{:S(2)}) collective-permute-start(bf16[512,2048]{1,0:T(8,128)(2,1)S(1)} %convolution_convert_fusion.3.part), channel_id=1, source_target_pairs={{0,1},{1,0},{2,3},{3,2},{4,5},{5,4},{6,7},{7,6},{8,9},{9,8},{10,11... | collective-permute-start | bytes 6291464 | tf_op jit(solution)/shard_map/ppermute | solution.py:585
  105.9 92.5 %collective-permute-start.4 = (bf16[512,2048]{1,0:T(8,128)(2,1)}, bf16[512,2048]{1,0:T(8,128)(2,1)}, u32[]{:S(2)}, u32[]{:S(2)}) collective-permute-start(bf16[512,2048]{1,0:T(8,128)(2,1)} %convolution_convert_fusion.2.part), channel_id=1, source_target_pairs={{0,1},{1,0},{2,3},{3,2},{4,5},{5,4},{6,7},{7,6},{8,9},{9,8},{10,11... | collective-permute-start | bytes 6291464 | tf_op jit(solution)/shard_map/ppermute | solution.py:585
  196.3 29.7 %copy-start.16 = (bf16[512,2048]{1,0:T(8,128)(2,1)}, bf16[512,2048]{1,0:T(8,128)(2,1)S(1)}, u32[]{:S(2)}) copy-start(bf16[512,2048]{1,0:T(8,128)(2,1)S(1)} %two_back.4.back) | copy-start | bytes 6291460
  196.3 100.6 %collective-permute-start.8 = (bf16[512,2048]{1,0:T(8,128)(2,1)S(1)}, bf16[512,2048]{1,0:T(8,128)(2,1)}, u32[]{:S(2)}, u32[]{:S(2)}) collective-permute-start(bf16[512,2048]{1,0:T(8,128)(2,1)S(1)} %two_back.4.back), channel_id=1, source_target_pairs={{0,1},{1,0},{2,3},{3,2},{4,5},{5,4},{6,7},{7,6},{8,9},{9,8},{10,11... | collective-permute-start | bytes 6291464 | tf_op jit(solution)/shard_map/ppermute | solution.py:585
  227.6 24.7 %copy-start.29 = (bf16[512,2048]{1,0:T(8,128)(2,1)S(1)}, bf16[512,2048]{1,0:T(8,128)(2,1)}, u32[]{:S(2)}) copy-start(bf16[512,2048]{1,0:T(8,128)(2,1)} %get-tuple-element.152.own_a.own_b) | copy-start | bytes 6291460
  250.6 86.3 %collective-permute-start.7 = (bf16[512,3072]{1,0:T(8,128)(2,1)}, bf16[512,3072]{1,0:T(8,128)(2,1)}, u32[]{:S(2)}, u32[]{:S(2)}) collective-permute-start(bf16[512,3072]{1,0:T(8,128)(2,1)} %get-tuple-element.149), channel_id=1, source_target_pairs={{0,4},{2,6},{4,0},{6,2},{8,12},{10,14},{12,8},{14,10},{16,20},{18,... | collective-permute-start | bytes 9437192 | tf_op jit(solution)/shard_map/ppermute | solution.py:590
  253.9 24.8 %copy-start.28 = (bf16[512,3072]{1,0:T(8,128)(2,1)S(1)}, bf16[512,3072]{1,0:T(8,128)(2,1)}, u32[]{:S(2)}) copy-start(bf16[512,3072]{1,0:T(8,128)(2,1)} %get-tuple-element.146.right_oth.first) | copy-start | bytes 9437188
  277.1 71.3 %collective-permute-start.6 = (bf16[512,3072]{1,0:T(8,128)(2,1)}, bf16[512,3072]{1,0:T(8,128)(2,1)}, u32[]{:S(2)}, u32[]{:S(2)}) collective-permute-start(bf16[512,3072]{1,0:T(8,128)(2,1)} %get-tuple-element.148), channel_id=1, source_target_pairs={{0,8},{2,10},{4,12},{6,14},{8,0},{10,2},{12,4},{14,6},{16,24},{18,... | collective-permute-start | bytes 9437192 | tf_op jit(solution)/shard_map/ppermute | solution.py:590
  296.3 57.2 %collective-permute-start.5 = (bf16[512,2048]{1,0:T(8,128)(2,1)S(1)}, bf16[512,2048]{1,0:T(8,128)(2,1)}, u32[]{:S(2)}, u32[]{:S(2)}) collective-permute-start(bf16[512,2048]{1,0:T(8,128)(2,1)S(1)} %two_back.5.back), channel_id=1, source_target_pairs={{0,1},{1,0},{2,3},{3,2},{4,5},{5,4},{6,7},{7,6},{8,9},{9,8},{10,11... | collective-permute-start | bytes 6291464 | tf_op jit(solution)/shard_map/ppermute | solution.py:585
  297.6 14.0 %copy-start.30 = (bf16[512,2048]{1,0:T(8,128)(2,1)S(1)}, bf16[512,2048]{1,0:T(8,128)(2,1)}, u32[]{:S(2)}) copy-start(bf16[512,2048]{1,0:T(8,128)(2,1)} %get-tuple-element.152.own_a.own_b) | copy-start | bytes 6291460
  313.2 23.6 %copy-start.41 = (bf16[512,3072]{1,0:T(8,128)(2,1)S(1)}, bf16[512,3072]{1,0:T(8,128)(2,1)}, u32[]{:S(2)}) copy-start(bf16[512,3072]{1,0:T(8,128)(2,1)} %get-tuple-element.142) | copy-start | bytes 9437188
  336.2 88.2 %collective-permute-start.13 = (bf16[512,3072]{1,0:T(8,128)(2,1)}, bf16[512,3072]{1,0:T(8,128)(2,1)}, u32[]{:S(2)}, u32[]{:S(2)}) collective-permute-start(bf16[512,3072]{1,0:T(8,128)(2,1)} %get-tuple-element.175), channel_id=1, source_target_pairs={{0,4},{2,6},{4,0},{6,2},{8,12},{10,14},{12,8},{14,10},{16,20},{18,... | collective-permute-start | bytes 9437192 | tf_op jit(solution)/shard_map/ppermute | solution.py:590
  341.8 39.7 %collective-permute-start.10 = (bf16[256,3072]{1,0:T(8,128)(2,1)}, bf16[256,3072]{1,0:T(8,128)(2,1)}, u32[]{:S(2)}, u32[]{:S(2)}) collective-permute-start(bf16[256,3072]{1,0:T(8,128)(2,1)} %get-tuple-element.155), channel_id=1, source_target_pairs={{0,8},{2,10},{4,12},{6,14},{8,0},{10,2},{12,4},{14,6},{16,24},{18,... | collective-permute-start | bytes 4718600 | tf_op jit(solution)/shard_map/ppermute | solution.py:590
  353.1 88.6 %collective-permute-start.12 = (bf16[256,3072]{1,0:T(8,128)(2,1)}, bf16[256,3072]{1,0:T(8,128)(2,1)}, u32[]{:S(2)}, u32[]{:S(2)}) collective-permute-start(bf16[256,3072]{1,0:T(8,128)(2,1)} %get-tuple-element.157), channel_id=1, source_target_pairs={{0,4},{2,6},{4,0},{6,2},{8,12},{10,14},{12,8},{14,10},{16,20},{18,... | collective-permute-start | bytes 4718600 | tf_op jit(solution)/shard_map/ppermute | solution.py:590
  353.5 13.9 %copy-start.26 = (bf16[512,1280]{1,0:T(8,128)(2,1)S(1)}, bf16[512,1280]{1,0:T(8,128)(2,1)}, u32[]{:S(2)}) copy-start(bf16[512,1280]{1,0:T(8,128)(2,1)} %copy-done.25) | copy-start | bytes 3932164
  379.7 101.5 %collective-permute-start.9 = (bf16[512,1280]{1,0:T(8,128)(2,1)}, bf16[512,1280]{1,0:T(8,128)(2,1)}, u32[]{:S(2)}, u32[]{:S(2)}) collective-permute-start(bf16[512,1280]{1,0:T(8,128)(2,1)} %get-tuple-element.162), channel_id=1, source_target_pairs={{0,4},{2,6},{4,0},{6,2},{8,12},{10,14},{12,8},{14,10},{16,20},{18,... | collective-permute-start | bytes 3932168 | tf_op jit(solution)/shard_map/ppermute | solution.py:590
  384.3 93.3 %collective-permute-start.11 = (bf16[128,3072]{1,0:T(8,128)(2,1)}, bf16[128,3072]{1,0:T(8,128)(2,1)}, u32[]{:S(2)}, u32[]{:S(2)}) collective-permute-start(bf16[128,3072]{1,0:T(8,128)(2,1)} %get-tuple-element.166), channel_id=1, source_target_pairs={{0,16},{2,18},{4,20},{6,22},{8,24},{10,26},{12,28},{14,30},{16,0},... | collective-permute-start | bytes 2359304 | tf_op jit(solution)/shard_map/ppermute | solution.py:590
  386.9 34.7 %copy-start.52 = (f32[1280]{0:T(1024)S(1)}, f32[1280]{0:T(1024)}, u32[]{:S(2)}) copy-start(f32[1280]{0:T(1024)} %fusion.19) | copy-start | bytes 15364
  386.9 34.7 %copy-start.59 = (pred[8]{0:T(512)(128)(4,1)S(1)}, pred[8]{0:T(512)(128)(4,1)}, u32[]{:S(2)}) copy-start(pred[8]{0:T(512)(128)(4,1)} %iota_compare_fusion.1) | copy-start | bytes 28
  429.7 63.0 %collective-permute-start.17 = (bf16[256,3072]{1,0:T(8,128)(2,1)}, bf16[256,3072]{1,0:T(8,128)(2,1)}, u32[]{:S(2)}, u32[]{:S(2)}) collective-permute-start(bf16[256,3072]{1,0:T(8,128)(2,1)} %get-tuple-element.178), channel_id=1, source_target_pairs={{0,8},{2,10},{4,12},{6,14},{8,0},{10,2},{12,4},{14,6},{16,24},{18,... | collective-permute-start | bytes 4718600 | tf_op jit(solution)/shard_map/ppermute | solution.py:590
  466.6 80.3 %collective-permute-start.18 = (bf16[512,2048]{1,0:T(8,128)(2,1)}, bf16[512,2048]{1,0:T(8,128)(2,1)S(1)}, u32[]{:S(2)}, u32[]{:S(2)}) collective-permute-start(bf16[512,2048]{1,0:T(8,128)(2,1)} %convolution_convert_fusion.1), channel_id=1, source_target_pairs={{0,1},{1,0},{2,3},{3,2},{4,5},{5,4},{6,7},{7,6},{8,9},{9,8},{10,11... | collective-permute-start | bytes 6291464 | tf_op jit(solution)/shard_map/ppermute | solution.py:585
  467.2 40.1 %collective-permute-start.16 = (bf16[128,3072]{1,0:T(8,128)(2,1)}, bf16[128,3072]{1,0:T(8,128)(2,1)}, u32[]{:S(2)}, u32[]{:S(2)}) collective-permute-start(bf16[128,3072]{1,0:T(8,128)(2,1)} %get-tuple-element.183), channel_id=1, source_target_pairs={{0,16},{2,18},{4,20},{6,22},{8,24},{10,26},{12,28},{14,30},{16,0},... | collective-permute-start | bytes 2359304 | tf_op jit(solution)/shard_map/ppermute | solution.py:590
  477.6 90.9 %collective-permute-start.20 = (bf16[512,2048]{1,0:T(8,128)(2,1)S(1)}, bf16[512,2048]{1,0:T(8,128)(2,1)S(1)}, u32[]{:S(2)}, u32[]{:S(2)}) collective-permute-start(bf16[512,2048]{1,0:T(8,128)(2,1)S(1)} %two_back.6), channel_id=1, source_target_pairs={{0,1},{1,0},{2,3},{3,2},{4,5},{5,4},{6,7},{7,6},{8,9},{9,8},{10,11... | collective-permute-start | bytes 6291464 | tf_op jit(solution)/shard_map/ppermute | solution.py:585
  481.3 31.9 %collective-permute-start.15 = (bf16[512,1280]{1,0:T(8,128)(2,1)}, bf16[512,1280]{1,0:T(8,128)(2,1)S(1)}, u32[]{:S(2)}, u32[]{:S(2)}) collective-permute-start(bf16[512,1280]{1,0:T(8,128)(2,1)} %get-tuple-element.194), channel_id=1, source_target_pairs={{0,4},{2,6},{4,0},{6,2},{8,12},{10,14},{12,8},{14,10},{16,20},{18,... | collective-permute-start | bytes 3932168 | tf_op jit(solution)/shard_map/ppermute | solution.py:590
  492.7 14.6 %copy-start.45 = (bf16[256,1280]{1,0:T(8,128)(2,1)S(1)}, bf16[256,1280]{1,0:T(8,128)(2,1)}, u32[]{:S(2)}) copy-start(bf16[256,1280]{1,0:T(8,128)(2,1)} %get-tuple-element.193) | copy-start | bytes 1966084
  492.7 50.5 %collective-permute-start.19 = (bf16[512,1280]{1,0:T(8,128)(2,1)}, bf16[512,1280]{1,0:T(8,128)(2,1)S(1)}, u32[]{:S(2)}, u32[]{:S(2)}) collective-permute-start(bf16[512,1280]{1,0:T(8,128)(2,1)} %get-tuple-element.206), channel_id=1, source_target_pairs={{0,4},{2,6},{4,0},{6,2},{8,12},{10,14},{12,8},{14,10},{16,20},{18,... | collective-permute-start | bytes 3932168 | tf_op jit(solution)/shard_map/ppermute | solution.py:590
  496.0 18.7 %copy-start.44 = (bf16[512,1280]{1,0:T(8,128)(2,1)S(1)}, bf16[512,1280]{1,0:T(8,128)(2,1)}, u32[]{:S(2)}) copy-start(bf16[512,1280]{1,0:T(8,128)(2,1)} %get-tuple-element.181) | copy-start | bytes 3932164
  507.3 25.8 %collective-permute-start.14 = (bf16[256,1280]{1,0:T(8,128)(2,1)S(1)}, bf16[256,1280]{1,0:T(8,128)(2,1)S(1)}, u32[]{:S(2)}, u32[]{:S(2)}) collective-permute-start(bf16[256,1280]{1,0:T(8,128)(2,1)S(1)} %copy-done.45), channel_id=1, source_target_pairs={{0,8},{2,10},{4,12},{6,14},{8,0},{10,2},{12,4},{14,6},{16,24},{18,... | collective-permute-start | bytes 1966088 | tf_op jit(solution)/shard_map/ppermute | solution.py:590
  513.2 52.5 %collective-permute-start.21 = (bf16[128,3072]{1,0:T(8,128)(2,1)S(1)}, bf16[128,3072]{1,0:T(8,128)(2,1)S(1)}, u32[]{:S(2)}, u32[]{:S(2)}) collective-permute-start(bf16[128,3072]{1,0:T(8,128)(2,1)S(1)} %get-tuple-element.199), channel_id=1, source_target_pairs={{0,16},{2,18},{4,20},{6,22},{8,24},{10,26},{12,28},{14,30},{16,0},... | collective-permute-start | bytes 2359304 | tf_op jit(solution)/shard_map/ppermute | solution.py:590
  514.7 18.5 %copy-start.62 = (bf16[512,3072]{1,0:T(8,128)(2,1)S(1)}, bf16[512,3072]{1,0:T(8,128)(2,1)}, u32[]{:S(2)}) copy-start(bf16[512,3072]{1,0:T(8,128)(2,1)} %get-tuple-element.205.right_own) | copy-start | bytes 9437188
  533.1 31.7 %collective-permute-start.22 = (bf16[256,1280]{1,0:T(8,128)(2,1)S(1)}, bf16[256,1280]{1,0:T(8,128)(2,1)S(1)}, u32[]{:S(2)}, u32[]{:S(2)}) collective-permute-start(bf16[256,1280]{1,0:T(8,128)(2,1)S(1)} %get-tuple-element.202), channel_id=1, source_target_pairs={{0,8},{2,10},{4,12},{6,14},{8,0},{10,2},{12,4},{14,6},{16,24},{18,... | collective-permute-start | bytes 1966088 | tf_op jit(solution)/shard_map/ppermute | solution.py:590
  543.3 30.7 %collective-permute-start.25 = (bf16[128,1280]{1,0:T(8,128)(2,1)S(1)}, bf16[128,1280]{1,0:T(8,128)(2,1)S(1)}, u32[]{:S(2)}, u32[]{:S(2)}) collective-permute-start(bf16[128,1280]{1,0:T(8,128)(2,1)S(1)} %get-tuple-element.204), channel_id=1, source_target_pairs={{0,16},{2,18},{4,20},{6,22},{8,24},{10,26},{12,28},{14,30},{16,0},... | collective-permute-start | bytes 983048 | tf_op jit(solution)/shard_map/ppermute | solution.py:590
  546.9 29.3 %collective-permute-start.24 = (bf16[256,1280]{1,0:T(8,128)(2,1)S(1)}, bf16[256,1280]{1,0:T(8,128)(2,1)S(1)}, u32[]{:S(2)}, u32[]{:S(2)}) collective-permute-start(bf16[256,1280]{1,0:T(8,128)(2,1)S(1)} %get-tuple-element.208), channel_id=1, source_target_pairs={{0,8},{2,10},{4,12},{6,14},{8,0},{10,2},{12,4},{14,6},{16,24},{18,... | collective-permute-start | bytes 1966088 | tf_op jit(solution)/shard_map/ppermute | solution.py:590
  577.1 8.1 %collective-permute-start.26 = (bf16[168,256]{1,0:T(8,128)(2,1)}, bf16[168,256]{1,0:T(8,128)(2,1)S(1)}, u32[]{:S(2)}, u32[]{:S(2)}) collective-permute-start(bf16[168,256]{1,0:T(8,128)(2,1)} %reduce-scatter.2.cloned.1.call-done), channel_id=1, source_target_pairs={{0,1},{1,0},{2,3},{3,2},{4,5},{5,4},{6,7},{7,6},{8,9},{9,8},{10,11... | collective-permute-start | bytes 258056 | tf_op jit(solution)/shard_map/ppermute | solution.py:585
  581.2 22.2 %collective-permute-start.23 = (bf16[128,1280]{1,0:T(8,128)(2,1)}, bf16[128,1280]{1,0:T(8,128)(2,1)}, u32[]{:S(2)}, u32[]{:S(2)}) collective-permute-start(bf16[128,1280]{1,0:T(8,128)(2,1)} %get-tuple-element.214), channel_id=1, source_target_pairs={{0,16},{2,18},{4,20},{6,22},{8,24},{10,26},{12,28},{14,30},{16,0},... | collective-permute-start | bytes 983048 | tf_op jit(solution)/shard_map/ppermute | solution.py:590
  581.2 29.1 %collective-permute-start.27 = (bf16[128,1280]{1,0:T(8,128)(2,1)}, bf16[128,1280]{1,0:T(8,128)(2,1)}, u32[]{:S(2)}, u32[]{:S(2)}) collective-permute-start(bf16[128,1280]{1,0:T(8,128)(2,1)} %get-tuple-element.224), channel_id=1, source_target_pairs={{0,16},{2,18},{4,20},{6,22},{8,24},{10,26},{12,28},{14,30},{16,0},... | collective-permute-start | bytes 983048 | tf_op jit(solution)/shard_map/ppermute | solution.py:590
  585.3 32.0 %copy-start.1 = (bf16[2,10,256,256]{3,2,1,0:T(8,128)(2,1)S(1)}, bf16[2,10,256,256]{3,2,1,0:T(8,128)(2,1)}, u32[]{:S(2)}) copy-start(bf16[2,10,256,256]{3,2,1,0:T(8,128)(2,1)} %param.23) | copy-start | bytes 7864324
  613.1 3.6 collective-permute-start.28
  (55 other events, 300.1 us)
Sparse Core Ops, SparseCore 0:
  424.5 84.0 reduce-scatter.1

commit v5 on v4

--- a/solution.py
+++ b/solution.py
@@ -10,6 +10,13 @@
 EPS = 1e-06
 F32, BF16 = jnp.float32, jnp.bfloat16
 GELU_A, GELU_B = 0.7978845608028654, 0.044715
+ORDER = (
+    "DK", "GK", "B2", "UK", "OK", "P2", "D1", "G1", "P1", "OUT", "D2", "U1",
+    "RB", "G2", "X", "Dt", "O1", "RS", "U2", "Gt", "Y", "O2", "X1", "OS",
+    "RK", "IG", "Y1", "Ut", "Ot", "X2", "Y2", "LO", "Xt", "SW", "Yt",
+)
+CROSSED = "G"
+COSTS = {}
 MESH = pl.DeviceIdType.MESH
 
 
@@ -138,7 +145,7 @@
 
 
 def rec_bwd_kernel(
-    count, bx_own, bx_oth, by_own, by_oth, state_ref, in_ref, rate_ref, conv_ref, up_own, up_oth, mask_ref, prm_ref, gate_ref,
+    count, bits, bx_own, bx_oth, by_own, by_oth, state_ref, in_ref, rate_ref, conv_ref, up_own, up_oth, mask_ref, prm_ref, gate_ref,
     gx_own, gx_oth, gy_own, gy_oth, gw_ref, sum_ref, xs, ys, us, gs, factor, to_log, to_in, to_rate, to_conv, gc, dg, gw,
 ):
     place = lax.axis_index("tp")
@@ -210,10 +217,12 @@
     gw[lanes:, :] = matmul_left(conv, dg[:, lanes:]).astype(BF16)
     gate_sums = jnp.dot(jnp.ones((8, length), BF16), dg[...], preferred_element_type=F32)
     rows_each = lanes // count
-    for block in range(count):
+    me = lax.axis_index("dp")
+    for spot in range(count):
+        block = block_from(me, spot, bits)
         for gate in (0, 1):
-            source = gate * lanes + block * rows_each
-            gw_ref[block, 0, gate * rows_each : (gate + 1) * rows_each, :] = gw[source : source + rows_each, :]
+            source = pl.ds(pl.multiple_of(gate * lanes + block * rows_each, rows_each), rows_each)
+            gw_ref[spot, gate * rows_each : (gate + 1) * rows_each, :] = gw[source, :]
     gc[steps : steps + 3] = from_segment(gc[0:3], place, True)
     taps = [prm_ref[k : k + 1, :] for k in range(4)]
 
@@ -277,7 +286,7 @@
     )(bx_own, bx_oth, by_own, by_oth, mask, prm, gates)
 
 
-def rec_bwd(bx_own, bx_oth, by_own, by_oth, kept, up_own, up_oth, mask, prm, gates, count):
+def rec_bwd(bx_own, bx_oth, by_own, by_oth, kept, up_own, up_oth, mask, prm, gates, count, cost):
     half, width = bx_own.shape
     length, lanes, heads = 2 * half, gates.shape[2], gates.shape[1]
     steps, both = half // SEGMENTS, 2 * SEGMENTS
@@ -285,13 +294,13 @@
     block = pltpu.VMEM((steps, both, lanes), F32)
     padded = pltpu.VMEM((steps + 3, both, lanes), F32)
     return pl.pallas_call(
-        functools.partial(rec_bwd_kernel, count),
+        functools.partial(rec_bwd_kernel, count, stage_bits(count, "X" in CROSSED)),
         grid=(heads,),
         in_specs=[piece] * 4 + [stepped] * 4 + [piece] * 2 + [mask_spec, prm_spec, gate_spec],
-        out_specs=[piece] * 4 + [pl.BlockSpec((count, 1, 2 * lanes // count, lanes), lambda h: (0, h, 0, 0)), prm_spec],
+        out_specs=[piece] * 4 + [pl.BlockSpec((count, 2 * lanes // count, lanes), lambda h: (0, 0, h)), prm_spec],
         out_shape=[jax.ShapeDtypeStruct((half, width), BF16)] * 4
         + [
-            jax.ShapeDtypeStruct((count, heads, 2 * lanes // count, lanes), BF16),
+            jax.ShapeDtypeStruct((count, 2 * lanes // count, width), BF16),
             jax.ShapeDtypeStruct((8, width), F32),
         ],
         scratch_shapes=[padded]
@@ -299,9 +308,9 @@
         + [padded, pltpu.VMEM((length, 2 * lanes), BF16), pltpu.VMEM((2 * lanes, lanes), BF16)],
         compiler_params=pltpu.CompilerParams(vmem_limit_bytes=52 << 20),
         cost_estimate=pl.CostEstimate(
-            flops=8 * length * width * lanes + 150 * length * width,
-            bytes_accessed=34 * length * width,
-            transcendentals=4 * length * width,
+            flops=int(cost * (8 * length * width * lanes + 150 * length * width)),
+            bytes_accessed=int(cost * 34 * length * width),
+            transcendentals=int(cost * 4 * length * width),
         ),
         name="rec_bwd",
     )(bx_own, bx_oth, by_own, by_oth, *kept, up_own, up_oth, mask, prm, gates)
@@ -350,9 +359,9 @@
     )(first, second)
 
 
-def weight_grad_kernel(splits, own_a, own_b, oth_a, oth_b, right_own, right_oth, sent_next, kept, staged, landed, send_sem, recv_sem):
+def weight_grad_kernel(more, own_a, own_b, oth_a, oth_b, right_own, right_oth, *rest):
+    extra, (sent_next, kept, staged, landed, send_sem, recv_sem) = rest[:-6], rest[-6:]
     step = pl.program_id(0)
-    half = 2 * splits
     me = lax.axis_index("dp")
     partner = {"dp": me + 1 - 2 * lax.rem(me, 2)}
 
@@ -376,78 +385,79 @@
     left_oth = jnp.concatenate([oth_a[...], oth_b[...]], axis=1)
     total = matmul_left(left_own, right_own[...]) + matmul_left(left_oth, right_oth[...])
 
-    @pl.when(step < half)
+    def pieces():
+        if not more:
+            return [(slice(0, total.shape[0]), total)]
+        out = []
+        for block in range(total.shape[0] // 128):
+            first = block * (128 + more)
+            out.append((slice(first, first + 128), total[block * 128 : (block + 1) * 128]))
+            out.append((slice(first + 128, first + 128 + more), extra[0][block].astype(F32)))
+        return out
+
+    @pl.when(step < 2)
     def _():
-        staged[step] = total.astype(BF16)
+        for rows, value in pieces():
+            staged[step, rows, :] = value.astype(BF16)
         copy(step).start()
 
-    @pl.when(step >= half)
+    def finish(tile, into):
+        copy(tile).wait_recv()
+        for rows, value in pieces():
+            into[rows, :] = (value + landed[tile, rows, :].astype(F32)).astype(BF16)
+
+    @pl.when(step == 2)
     def _():
-        copy(step - half).wait_recv()
-        value = (total + landed[step - half].astype(F32)).astype(BF16)
-
-        @pl.when(step < half + splits)
-        def _():
-            sent_next[...] = value
-
-        @pl.when(step >= half + splits)
-        def _():
-            kept[...] = value
-
-    @pl.when(step == 2 * half - 1)
+        finish(0, sent_next)
+
+    @pl.when(step == 3)
     def _():
-        for tile in range(half):
+        finish(1, kept)
+        for tile in range(2):
             copy(tile).wait_send()
 
 
-def weight_grad(left_own, left_oth, right_own, right_oth, crossed, cost):
+def weight_grad(left_own, left_oth, right_own, right_oth, crossed, cost, extra=None):
     half, cols = right_own.shape
     rows = left_own.shape[1] // 4
-    splits = 2 if cols > 2048 else 1
-    wide = cols // splits
-    out = pltpu.HBM((rows, cols), BF16)
-
-    def tile(i):
-        return lax.rem((i + 1) // 2, 2) if splits == 2 else 0
+    more = 0 if extra is None else extra.shape[1]
+    height = rows + rows // 128 * more
+    out = pltpu.HBM((height, cols), BF16)
 
     def columns(part):
         def index(i):
-            quarter = 3 - i // splits
+            quarter = 3 - i
             return 0, (quarter // 2 * 4 + part * 2 + lax.rem(quarter, 2) if crossed else quarter * 2 + part)
 
         return pl.BlockSpec((half, rows // 2), index)
 
-    last = 4 * splits - 1
+    right = pl.BlockSpec((half, cols), lambda i: (0, 0))
+    whole = pl.BlockSpec((height, cols), lambda i: (0, 0))
+    specs = [columns(0), columns(1), columns(0), columns(1), right, right]
+    args = [left_own, left_own, left_oth, left_oth, right_own, right_oth]
+    if more:
+        specs.append(pl.BlockSpec((rows // 128, more, cols), lambda i: (3 - i, 0, 0)))
+        args.append(extra)
     return pl.pallas_call(
-        functools.partial(weight_grad_kernel, splits),
-        grid=(4 * splits,),
-        in_specs=[
-            columns(0),
-            columns(1),
-            columns(0),
-            columns(1),
-            pl.BlockSpec((half, wide), lambda i: (0, tile(i))),
-            pl.BlockSpec((half, wide), lambda i: (0, tile(i))),
-        ],
-        out_specs=[
-            pl.BlockSpec((rows, wide), lambda i: (0, jnp.where(i < last - 2, 0, 1) if splits == 2 else 0)),
-            pl.BlockSpec((rows, wide), lambda i: (0, jnp.where(i < last, 1, 0) if splits == 2 else 0)),
-        ],
+        functools.partial(weight_grad_kernel, more),
+        grid=(4,),
+        in_specs=specs,
+        out_specs=[whole, whole],
         out_shape=[out, out],
         scratch_shapes=[
-            pltpu.VMEM((2 * splits, rows, wide), BF16),
-            pltpu.VMEM((2 * splits, rows, wide), BF16),
-            pltpu.SemaphoreType.DMA((2 * splits,)),
-            pltpu.SemaphoreType.DMA((2 * splits,)),
+            pltpu.VMEM((2, height, cols), BF16),
+            pltpu.VMEM((2, height, cols), BF16),
+            pltpu.SemaphoreType.DMA((2,)),
+            pltpu.SemaphoreType.DMA((2,)),
         ],
         compiler_params=pltpu.CompilerParams(
-            collective_id=2 * splits + crossed, has_side_effects=True, vmem_limit_bytes=48 << 20
+            collective_id=4 * bool(more) + 2 * (cols > 2048) + crossed, has_side_effects=True, vmem_limit_bytes=60 << 20
         ),
         cost_estimate=pl.CostEstimate(
             flops=int(cost * 16 * half * rows * cols), bytes_accessed=int(cost * 16 * half * cols), transcendentals=0
         ),
         name="weight_grad",
-    )(left_own, left_own, left_oth, left_oth, right_own, right_oth)
+    )(*args)
 
 
 ROWS = 64
@@ -491,7 +501,7 @@
         grad_up[:, part_cols] = (back * gelu).astype(BF16)
 
 
-def feed(tokens, part, other, gain, grad_hidden, w_gate, w_up, bits, wide=512, sub=256):
+def feed(tokens, part, other, gain, grad_hidden, w_gate, w_up, bits, wide=768, sub=768):
     rows, model = tokens.shape
     cols = w_gate.shape[1]
     whole = pl.BlockSpec((rows, model), lambda n: (0, 0))
@@ -533,7 +543,7 @@
     into[...] = matmul_right(rec[...], weight[...])
 
 
-def pull(middle, back, other, cot, gain, weight, bits, wide=640):
+def pull(middle, back, other, cot, gain, weight, bits, cost, wide=640):
     rows, model = middle.shape
     cols = weight.shape[0]
     wide = wide if cols % wide == 0 else cols
@@ -551,7 +561,9 @@
         scratch_shapes=[pltpu.VMEM((rows, model), BF16)],
         compiler_params=pltpu.CompilerParams(vmem_limit_bytes=56 << 20),
         cost_estimate=pl.CostEstimate(
-            flops=2 * rows * model * cols, bytes_accessed=16 * rows * model + 4 * rows * cols, transcendentals=0
+            flops=int(cost * 2 * rows * model * cols),
+            bytes_accessed=int(cost * (16 * rows * model + 4 * rows * cols)),
+            transcendentals=0,
         ),
         name="pull",
     )(middle, back, other, cot, gain, weight)
@@ -590,27 +602,46 @@
     return lax.ppermute(value, "dp", [(source, source ^ bit) for source in range(count)])
 
 
+def halve_kernel(keep_low, keep_high, received_low, received_high, kept, sent):
+    kept[...] = (keep_low[...].astype(F32) + received_low[...].astype(F32)).astype(BF16)
+    sent[...] = (keep_high[...].astype(F32) + received_high[...].astype(F32)).astype(BF16)
+
+
+def halve(keep, received, cost):
+    rows, cols = keep.shape
+    block = rows // 4 if rows > 512 else rows // 2
+    steps = rows // 2 // block
+    low = pl.BlockSpec((block, cols), lambda i: (i, 0))
+    high = pl.BlockSpec((block, cols), lambda i: (i + steps, 0))
+    return pl.pallas_call(
+        halve_kernel,
+        grid=(steps,),
+        in_specs=[low, high, low, high],
+        out_specs=[low, low],
+        out_shape=[pltpu.HBM((rows // 2, cols), BF16)] * 2,
+        compiler_params=pltpu.CompilerParams(vmem_limit_bytes=32 << 20),
+        cost_estimate=pl.CostEstimate(flops=0, bytes_accessed=int(cost * 6 * rows * cols), transcendentals=0),
+        name="halve",
+    )(keep, keep, received, received)
+
+
 class Reduction:
-    def __init__(self, left, right, count, crossed=False, cost=1.0):
+    def __init__(self, left, right, count, crossed, cost, extra=None):
         self.bits = stage_bits(count, crossed)[1:]
-        sent, self.keep = weight_grad(*left, *right, crossed, cost)
+        sent, self.keep = weight_grad(*left, *right, crossed, cost, extra)
         self.pass_on(sent)
 
     def pass_on(self, sent):
         self.received = flip(sent, self.bits.pop(0))
 
-    def step(self, *others):
-        received = after(self.received, *others)
-        middle = received.shape[0] // 2
-        sent = (self.keep[middle:].astype(F32) + received[middle:].astype(F32)).astype(BF16)
-        keep = (self.keep[:middle].astype(F32) + received[:middle].astype(F32)).astype(BF16)
-        sent, self.keep = lax.optimization_barrier((sent, keep))
+    def step(self, cost, *others):
+        self.keep, sent = halve(self.keep, after(self.received, *others), cost)
         self.pass_on(sent)
         return sent
 
     def total(self, *others):
         while self.bits:
-            self.step(*others)
+            self.step(1.0, *others)
         return self.keep.astype(F32) + after(self.received, *others).astype(F32)
 
 
@@ -682,64 +713,114 @@
     middle_oth, two_oth, hidden_oth, gg_oth, gu_oth = feed(
         oth_in, part_oth, after(swap_oth, back_own), gains, gh_oth, w_gate, w_up, bits
     )
-    down = Reduction((after(cot_cols[0], hidden_oth), cot_cols[1]), (hidden_own, hidden_oth), count)
-    gate = Reduction((after(two_own, down.keep), two_oth), (gg_own, gg_oth), count, True)
-    back_oth = two_back(after(gg_oth, gate.keep), w_gate, gu_oth, w_up)
-    back_oth_swapped = swap(back_oth)
-    _, rec_oth, into_oth = pull(middle_oth, back_oth, back_own_swapped, oth_cot, gains, w_out, bits)
-    up = Reduction((after(two_own, into_oth), two_oth), (gu_own, gu_oth), count)
-    done = down.step(up.keep)
-    done = gate.step(done)
-    grad_own, rec_own, into_own = pull(middle_own, back_own, after(back_oth_swapped, done), own_cot, gains, w_out, bits)
-    out = Reduction((rec_own, rec_oth), (gated_own, gated_oth), count)
-    done = down.step(out.keep)
-    gx_own, gx_oth, gy_own, gy_oth, gate_sums, sums = rec_bwd(
-        bx_own, bx_oth, by_own, by_oth, kept, after(into_own, done), into_oth, mask, prm, gates, count
-    )
-
-    lanes = gate_sums.shape[-1]
-    row = jnp.arange(8)[:, None] == 7
-    slopes = -8.0 * lax.dynamic_slice(jax.nn.sigmoid(a_param), (place * width,), (width,))
+    sums_over = {}
+    at = {"done": hidden_oth}
+
+    def reduce_kernel(name, letter, left, right, extra=None):
+        left = (after(left[0], at["done"]), left[1])
+        sums_over[letter] = Reduction(left, right, count, letter in CROSSED, COSTS.get(name, 1.0), extra)
+        return sums_over[letter].keep
+
+    def back_other(cost):
+        at["back"] = two_back(after(gg_oth, at["done"]), w_gate, gu_oth, w_up, cost)
+        at["back_swapped"] = swap(at["back"])
+        return at["back"]
+
+    def pull_other(cost):
+        other = after(back_own_swapped, at["done"])
+        _, at["rec_oth"], at["into_oth"] = pull(middle_oth, at["back"], other, oth_cot, gains, w_out, bits, cost)
+        return at["into_oth"]
+
+    def pull_own(cost):
+        other = after(at["back_swapped"], at["done"])
+        at["grad_own"], at["rec_own"], at["into_own"] = pull(middle_own, back_own, other, own_cot, gains, w_out, bits, cost)
+        return at["into_own"]
+
+    def recurrence(cost):
+        into = after(at["into_own"], at["done"]), at["into_oth"]
+        *grads, gate_sums, sums = rec_bwd(bx_own, bx_oth, by_own, by_oth, kept, *into, mask, prm, gates, count, cost)
+        at["gx"], at["gy"] = grads[0:2], grads[2:4]
+        row = jnp.arange(8)[:, None] == 7
+        slopes = -8.0 * lax.dynamic_slice(jax.nn.sigmoid(a_param), (place * width,), (width,))
+        sums = jnp.swapaxes(jnp.where(row, sums * slopes, sums).reshape(8, count // 2, each), 0, 1)
+        order = [block_at(spot, stage_bits(count, "X" in CROSSED)) for spot in range(count)]
+        chosen = jnp.bitwise_xor(jnp.array(order), me)[:, None] % (count // 2) == jnp.arange(count // 2)[None, :]
+        sums = matmul(chosen.astype(BF16), sums.astype(BF16).reshape(count // 2, -1)).reshape(count, 8, each)
+        sums = jnp.pad(sums.astype(BF16), ((0, 0), (0, 8), (0, width - each)))
+        at["extra"] = jnp.concatenate([gate_sums, sums], axis=1)
+        return grads[0]
+
+    def rec_rows(index):
+        def run(cost):
+            name = ("rec_keep", "rec_send")[index]
+            at[name] = two_back(after(at["gx"][index], at["done"]), w_x, at["gy"][index], w_y, cost)
+            if index == 1:
+                at["rec_swapped"] = swap(at[name])
+            return at[name]
+
+        return run
+
+    def out_other(cost):
+        sent = matmul(after(hidden_oth, at["done"]), w_down).astype(BF16)
+        at["out_swapped"] = swap(sent)
+        return sent
+
+    def out_own(cost):
+        at["out_keep"] = matmul(after(hidden_own, at["done"]), w_down).astype(BF16)
+        return at["out_keep"]
+
+    def to_inputs(cost):
+        grad_normed = at["rec_keep"].astype(F32) + after(at["rec_swapped"], at["done"]).astype(F32)
+        at["input_grad"] = at["grad_own"] + norm_back(own_in.astype(F32), norm_gains[0], grad_normed)
+        return at["input_grad"]
+
+    def to_outputs(cost):
+        total = middle_own + at["out_keep"].astype(F32) + after(at["out_swapped"], at["done"]).astype(F32)
+        at["layer_out"] = total.astype(BF16)
+        return at["layer_out"]
+
+    def swap_blocks(cost):
+        at["mine"] = after(grads["X"][block:], at["done"]).astype(BF16)
+        at["others"] = swap(at["mine"])
+        return at["others"]
+
     each = full_width // count
-    sums = jnp.swapaxes(jnp.where(row, sums * slopes, sums).reshape(8, count // 2, each), 0, 1)
-    sums = jnp.pad(jnp.concatenate([sums, sums], axis=0), ((0, 0), (0, 0), (0, lanes - each))).astype(BF16)
-    blocks = jnp.concatenate([gate_sums.reshape(count, -1, lanes), sums], axis=1)
-    blocks = lax.psum_scatter(blocks.reshape(-1, lanes), "dp", scatter_dimension=0, tiled=True)
-
-    small_cost = 0.1
-    done = up.step(gx_own)
-    in_x = Reduction((after(normed_cols[0], done), normed_cols[1]), (gx_own, gx_oth), count, cost=small_cost)
-    done = gate.step(in_x.keep)
-    in_y = Reduction((after(normed_cols[0], done), normed_cols[1]), (gy_own, gy_oth), count, cost=small_cost)
-    out_send = matmul(after(hidden_oth, in_y.keep), w_down).astype(BF16)
-    out_swapped = swap(out_send)
-    rec_send = two_back(after(gx_oth, out_send), w_x, gy_oth, w_y, small_cost)
-    rec_swapped = swap(rec_send)
-    down_grad = down.total(rec_send).T
-    done = out.step(down_grad)
-    rec_keep = two_back(after(gx_own, done), w_x, gy_own, w_y, small_cost)
-    done = up.step(rec_keep)
-    gate_grad = gate.total(done)
-    done = in_x.step(gate_grad)
-    done = out.step(done)
-    out_keep = matmul(after(hidden_own, done), w_down).astype(BF16)
-    done = in_y.step(out_keep)
-    layer_out = (middle_own + out_keep.astype(F32) + after(out_swapped, done).astype(F32)).astype(BF16)
-    done = in_x.step(layer_out)
-    up_grad = up.total(done)
-    grad_normed = rec_keep.astype(F32) + after(rec_swapped, up_grad).astype(F32)
-    input_grad = grad_own + norm_back(own_in.astype(F32), norm_gains[0], grad_normed)
-    out_grad = out.total(input_grad).T
-    done = in_y.step(out_grad)
-    others = swap(after(blocks, done))
-    x_grad = in_x.total(others)
-    y_grad = in_y.total(x_grad)
-
-    low, high = jnp.where(first_place, blocks, others), jnp.where(first_place, others, blocks)
-    block_sums = jnp.stack([low[:-8], high[:-8]]).astype(F32).reshape(2 * heads, 2, -1, lanes)
-    small = jnp.where(me < count // 2, low[-8:], high[-8:])[:, :each].astype(F32)
-
     block = model // count
+    steps = {
+        "DK": lambda cost: reduce_kernel("DK", "D", cot_cols, (hidden_own, hidden_oth)),
+        "GK": lambda cost: reduce_kernel("GK", "G", (two_own, two_oth), (gg_own, gg_oth)),
+        "UK": lambda cost: reduce_kernel("UK", "U", (two_own, two_oth), (gu_own, gu_oth)),
+        "OUT": lambda cost: reduce_kernel("OUT", "O", (at["rec_own"], at["rec_oth"]), (gated_own, gated_oth)),
+        "X": lambda cost: reduce_kernel("X", "X", normed_cols, at["gx"], at["extra"]),
+        "Y": lambda cost: reduce_kernel("Y", "Y", normed_cols, at["gy"]),
+        "B2": back_other,
+        "P2": pull_other,
+        "P1": pull_own,
+        "RB": recurrence,
+        "RS": rec_rows(1),
+        "RK": rec_rows(0),
+        "OS": out_other,
+        "OK": out_own,
+        "IG": to_inputs,
+        "LO": to_outputs,
+        "SW": swap_blocks,
+    }
+    grads = {}
+    for name in ORDER:
+        if name in steps:
+            at["done"] = steps[name](COSTS.get(name, 1.0))
+        elif name[1] == "t":
+            total = sums_over[name[0]].total(at["done"])
+            at["done"] = grads[name[0]] = total.T if name[0] in "DO" else total
+        else:
+            at["done"] = sums_over[name[0]].step(COSTS.get(name, 1.0), at["done"])
+    mine, others, layer_out, input_grad = (at[name] for name in ("mine", "others", "layer_out", "input_grad"))
+    down_grad, gate_grad, up_grad, out_grad, x_grad, y_grad = (grads[letter] for letter in "DGUOXY")
+    x_grad = x_grad[:block]
+    low, high = jnp.where(first_place, mine, others), jnp.where(first_place, others, mine)
+    both = jnp.stack([low[:-16], high[:-16]]).astype(F32).reshape(2, 2, -1, heads, gates.shape[-1])
+    block_sums = jnp.transpose(both, (1, 0, 3, 2, 4)).reshape(2, 2 * heads, -1, gates.shape[-1])
+    small = jnp.where(me < count // 2, low[-16:-8], high[-16:-8])[:, :each].astype(F32)
 
     def gain_grad(gain, *pairs):
         weights = sum(
@@ -764,7 +845,7 @@
         small[0:4],
         small[4:7],
         small[7],
-        jnp.swapaxes(block_sums, 0, 1),
+        block_sums,
         out_grad,
         gate_grad,
         up_grad,

time: 630 us -> 598 us (0.949)
  waiting for transfers between devices: 122 us -> 91.1 us
  Pallas kernels: 298 us -> 322 us
  other arithmetic: 59.3 us -> 36.2 us
  between operations: 15.2 us -> 1.96 us
    ppermute x18, waiting for transfers between devices: 79.1 us -> 41.9 us  [flip(): lax.ppermute(value, 'dp', [(source, source ^ bit) for source in range(cou...]
    convert_element_type x14 -> x3, other arithmetic: 30.3 us -> 4.82 us  [the longest x1 4.74 us: to_outputs(): at['layer_out'] = total.astype(BF16)]
    pallas_call x7 -> x19, Pallas kernels: 135 us -> 161 us  [the longest x6 100 us: weight_grad(): pl.pallas_call(functools.partial(weight_grad_kernel, more), grid=(4,), in...]
    ppermute x11, waiting for transfers between devices: 42.5 us -> 49.2 us  [swap(): return lax.ppermute(value, 'tp', [(0, 1), (1, 0)])]
    unnamed x150 -> x144, local copies, waits for them, and re-layouts: 18.4 us -> 19.9 us
    dot_general x8 -> x9, matrix products: 49.9 us -> 50.7 us  [matmul(): return jnp.dot(first_mat, second_mat, preferred_element_type=jnp.float32)]
  transfers between devices with their start and end apart: 30 -> 29, of which waited for: 11 -> 10; matrix products, arithmetic and copies ran while one was open for 22% -> 20% of each run, Pallas kernels for 48% -> 54%
where the time goes in v5:
time: 598 us; the launch traced here: 592 us
  Pallas kernels  322 us (54%)
  waiting for transfers between devices  91.1 us (15%)
  matrix products  74.7 us (12%)
  starting transfers between devices  40.2 us (7%)
  other arithmetic  36.2 us (6%)
  local copies, waits for them, and re-layouts  26.6 us (4%)
    pallas_call x6, Pallas kernels, weight_grad(): pl.pallas_call(functools.partial(weight_grad_kernel, more), grid=(4,), in...  100 us
    pallas_call x4, Pallas kernels, two_back(): pl.pallas_call(two_back_kernel, grid=(cols // step,), in_specs=[left, rig...  54.7 us
    pallas_call x2, Pallas kernels, feed(): pl.pallas_call(functools.partial(feed_kernel, bits, sub), grid=(cols // w...  51.3 us
    dot_general x9, matrix products, matmul(): return jnp.dot(first_mat, second_mat, preferred_element_type=jnp.float32)  50.7 us
    ppermute x11, waiting for transfers between devices, swap(): return lax.ppermute(value, 'tp', [(0, 1), (1, 0)])  49.2 us
    ppermute x18, waiting for transfers between devices, flip(): lax.ppermute(value, 'dp', [(source, source ^ bit) for source in range(cou...  41.9 us
    pallas_call x1, Pallas kernels, rec_bwd(): pl.pallas_call(functools.partial(rec_bwd_kernel, count, stage_bits(count,...  33.7 us
    pallas_call x2, Pallas kernels, pull(): pl.pallas_call(functools.partial(pull_kernel, bits), grid=(cols // wide,)...  27.7 us
  transfers between devices with their start and end apart: 29, of which 10 were waited for; matrix products, arithmetic and copies ran while one was open for 20% of the time, Pallas kernels for 54%

profile of v5, /device:TPU:0, one launch (start us, length us, event | category | flops | bytes accessed | tf_op | source)
XLA Modules:
  0.0 592.5 jit_solution(7832485413269848862)
XLA Ops:
  0.7 3.0 collective-permute-start.1
  9.8 7.7 %fusion.39.by_own = f32[512,1280]{1,0:T(8,128)} fusion(bf16[512,2048]{1,0:T(8,128)(2,1)S(1)} %fusion.5.first, bf16[2048,1280]{1,0:T(8,128)(2,1)} %second_w.7), kind=kOutput, calls=%fused_computation.96 | convolution fusion | flops 2684354560 | bytes 9961472 | tf_op jit(solution)/shard_map/dot_general | solution.py:880
  17.6 4.0 convolution_convert_fusion.5.bx_own
  21.6 11.9 %fusion.40.grad_hidden = f32[512,3072]{1,0:T(8,128)} fusion(bf16[512,2048]{1,0:T(8,128)(2,1)S(1)} %bitcast.61, bf16[3072,2048]{1,0:T(8,128)(2,1)} %param.28), kind=kOutput, calls=%fused_computation.97 | convolution fusion | flops 6442450944 | bytes 20971520 | tf_op jit(solution)/shard_map/dot_general | solution.py:890
  35.6 16.9 %collective-permute-done.tokens = bf16[512,2048]{1,0:T(8,128)(2,1)} collective-permute-done((bf16[512,2048]{1,0:T(8,128)(2,1)}, bf16[512,2048]{1,0:T(8,128)(2,1)}, u32[]{:S(2)}, u32[]{:S(2)}) %collective-permute-start) | collective-permute-done | bytes 2097184 | tf_op jit(solution)/shard_map/ppermute | solution.py:597
  57.0 7.0 %fusion.41.by_oth = f32[512,1280]{1,0:T(8,128)} fusion(bf16[512,2048]{1,0:T(8,128)(2,1)S(1)} %fusion.2.second, bf16[2048,1280]{1,0:T(8,128)(2,1)} %second_w.7), kind=kOutput, calls=%fused_computation.98 | convolution fusion | flops 2684354560 | bytes 9961472 | tf_op jit(solution)/shard_map/dot_general | solution.py:880
  64.0 2.9 convolution_convert_fusion.4.bx_oth
  67.4 23.4 %rec_fwd.1 = (bf16[512,1280]{1,0:T(8,128)(2,1)S(1)}, bf16[512,1280]{1,0:T(8,128)(2,1)S(1)}, f32[64,16,1280]{2,1,0:T(8,128)}, f32[64,16,1280]{2,1,0:T(8,128)}, f3...) custom-call(bf16[512,1280]{1,0:T(8,128)(2,1)S(1)} %copy-done.22, ...), custom_call_target="tpu_custom_call" | custom-call | flops 1473249280 | bytes 34078720 | tf_op jit(solution)/shard_map/rec_fwd/pallas_call | solution.py:267
  90.9 3.1 convolution_convert_fusion.3.part
  94.1 3.2 convolution_convert_fusion.2.part
  99.5 12.1 %fusion.42.grad_hidden = f32[512,3072]{1,0:T(8,128)} fusion(bf16[512,2048]{1,0:T(8,128)(2,1)} %collective-permute-done.3.second.cot, bf16[3072,2048]{1,0:T(8,128)(2,1)} %param.28), kind=kOutput, calls=%fused_computation.99 | convolution fusion | flops 6442450944 | bytes 20971520 | tf_op jit(solution)/shard_map/dot_general | solution.py:890
  111.6 2.9 arrange.2
  119.9 22.9 %collective-permute-done.2.other = bf16[512,2048]{1,0:T(8,128)(2,1)} collective-permute-done((bf16[512,2048]{1,0:T(8,128)(2,1)S(1)}, bf16[512,2048]{1,0:T(8,128)(2,1)}, u32[]{:S(2)}, u32[]{:S(2)}) %collective-permute-start.2) | collective-permute-done | bytes 2097184 | tf_op jit(solution)/shard_map/ppermute | solution.py:597
  142.8 25.6 %feed.2 = (f32[512,2048]{1,0:T(8,128)}, bf16[512,2048]{1,0:T(8,128)(2,1)}, bf16[512,3072]{1,0:T(8,128)(2,1)}, bf16[512,3072]{1,0:T(8,128)(2,1)}, bf16[512,3072]{1,0:T(8,128)(2,1)}) custom-call(bf16[512,2048]{1,0:T(8,128)(2,1)} %bitcast.64, bf16[512,2048]{1,0:T(8,128)(2,1)} %copy-done.62, bf16[512,2048]{1,0:T(8,128)(2,1)} %collective-permute-done.2.other, ...), custom_call_target="tpu_custom_call" | custom-call | flops 12884901888 | bytes 44040192 | tf_op jit(solution)/shard_map/feed/pallas_call | solution.py:511
  170.3 18.7 %two_back.4.back = bf16[512,2048]{1,0:T(8,128)(2,1)} custom-call(bf16[512,3072]{1,0:T(8,128)(2,1)S(1)} %copy-done.37, bf16[2048,3072]{1,0:T(8,128)(2,1)} %first_w.5, bf16[512,3072]{1,0:T(8,128)(2,1)} %get-tuple-element.138.second.right_own, bf16[2048,3072]{1,0:T(8,128)(2,1)} %second_w.5), custom_call_target="tpu_custom_call" | custom-call | flops 12884901888 | bytes 31457280 | tf_op jit(solution)/shard_map/two_back/pallas_call | solution.py:582
  190.3 25.6 %feed.3 = (f32[512,2048]{1,0:T(8,128)}, bf16[512,2048]{1,0:T(8,128)(2,1)}, bf16[512,3072]{1,0:T(8,128)(2,1)}, bf16[512,3072]{1,0:T(8,128)(2,1)}, bf16[512,3072]{1,0:T(8,128)(2,1)}) custom-call(bf16[512,2048]{1,0:T(8,128)(2,1)} %collective-permute-done.tokens, bf16[512,2048]{1,0:T(8,128)(2,1)} %copy-done.60, bf16[512,2048]{1,0:T(8,128)(2,1)} %copy-done.61, ...), custom_call_target="tpu_custom_call" | custom-call | flops 12884901888 | bytes 44040192 | tf_op jit(solution)/shard_map/feed/pallas_call | solution.py:511
  216.0 21.6 %weight_grad.6 = (bf16[512,3072]{1,0:T(8,128)(2,1)}, bf16[512,3072]{1,0:T(8,128)(2,1)}) custom-call(bf16[512,2048]{1,0:T(8,128)(2,1)} %copy-done.28, bf16[512,2048]{1,0:T(8,128)(2,1)} %copy-done.28, bf16[512,2048]{1,0:T(8,128)(2,1)} %copy-done.29, bf16[512,2048]{1,0:T(8,128)(2,1)} %copy-done.29, bf16[512,3072]{1,0:T(8,128)(2,1)} %get-tuple-element.152.right_own, ...), custom_call_target="tpu_custom_call" | custom-call | flops 12884901888 | bytes 25165824 | tf_op jit(solution)/shard_map/weight_grad/pallas_call | solution.py:441
  237.6 22.8 %weight_grad.7 = (bf16[512,3072]{1,0:T(8,128)(2,1)}, bf16[512,3072]{1,0:T(8,128)(2,1)}) custom-call(bf16[512,2048]{1,0:T(8,128)(2,1)} %get-tuple-element.150.own_a.own_b, bf16[512,2048]{1,0:T(8,128)(2,1)} %get-tuple-element.150.own_a.own_b, bf16[512,2048]{1,0:T(8,128)(2,1)} %get-tuple-element.146.oth_a.oth_b, ...), custom_call_target="tpu_custom_call" | custom-call | flops 12884901888 | bytes 25165824 | tf_op jit(solution)/shard_map/weight_grad/pallas_call | solution.py:441
  262.6 18.4 %two_back.5.back = bf16[512,2048]{1,0:T(8,128)(2,1)} custom-call(bf16[512,3072]{1,0:T(8,128)(2,1)S(1)} %copy-done.38, bf16[2048,3072]{1,0:T(8,128)(2,1)} %first_w.5, bf16[512,3072]{1,0:T(8,128)(2,1)} %get-tuple-element.149.second.right_oth, bf16[2048,3072]{1,0:T(8,128)(2,1)} %second_w.5), custom_call_target="tpu_custom_call" | custom-call | flops 12884901888 | bytes 31457280 | tf_op jit(solution)/shard_map/two_back/pallas_call | solution.py:582
  283.9 21.6 %weight_grad.8 = (bf16[512,3072]{1,0:T(8,128)(2,1)}, bf16[512,3072]{1,0:T(8,128)(2,1)}) custom-call(bf16[512,2048]{1,0:T(8,128)(2,1)} %get-tuple-element.150.own_a.own_b, bf16[512,2048]{1,0:T(8,128)(2,1)} %get-tuple-element.150.own_a.own_b, bf16[512,2048]{1,0:T(8,128)(2,1)} %get-tuple-element.146.oth_a.oth_b, ...), custom_call_target="tpu_custom_call" | custom-call | flops 12884901888 | bytes 25165824 | tf_op jit(solution)/shard_map/weight_grad/pallas_call | solution.py:441
  306.2 11.8 %convolution_convert_fusion.1 = bf16[512,2048]{1,0:T(8,128)(2,1)} fusion(bf16[512,3072]{1,0:T(8,128)(2,1)} %get-tuple-element.152.right_own, bf16[3072,2048]{1,0:T(8,128)(2,1)} %param.28), kind=kOutput, calls=%fused_computation.20 | convolution fusion | flops 6443499520 | bytes 17825792 | tf_op jit(solution)/shard_map/dot_general | solution.py:880
  318.0 13.9 %pull.2 = (f32[512,2048]{1,0:T(8,128)}, bf16[512,2048]{1,0:T(8,128)(2,1)}, f32[512,1280]{1,0:T(8,128)}) custom-call(f32[512,2048]{1,0:T(8,128)} %get-tuple-element.155.middle, bf16[512,2048]{1,0:T(8,128)(2,1)} %two_back.5.back, bf16[512,2048]{1,0:T(8,128)(2,1)} %collective-permute-done.7.other, bf16[512,2048]{1,0:T(8,128)(2,1)} %collective-permute-done.3.second.cot, ...), custom_call_target="tpu_custom_call" | custom-call | flops 2684354560 | bytes 19398656 | tf_op jit(solution)/shard_map/pull/pallas_call | solution.py:551
  331.9 4.0 halve.12
  338.0 15.7 %collective-permute-done.5.received_low.received_high = bf16[512,3072]{1,0:T(8,128)(2,1)} collective-permute-done((bf16[512,3072]{1,0:T(8,128)(2,1)}, bf16[512,3072]{1,0:T(8,128)(2,1)}, u32[]{:S(2)}, u32[]{:S(2)}) %collective-permute-start.5) | collective-permute-done | bytes 3145760 | tf_op jit(solution)/shard_map/ppermute | solution.py:602
  355.7 3.9 halve.13
  360.0 13.8 %pull.3 = (f32[512,2048]{1,0:T(8,128)}, bf16[512,2048]{1,0:T(8,128)(2,1)}, f32[512,1280]{1,0:T(8,128)}) custom-call(f32[512,2048]{1,0:T(8,128)} %get-tuple-element.134.middle, bf16[512,2048]{1,0:T(8,128)(2,1)} %two_back.4.back, bf16[512,2048]{1,0:T(8,128)(2,1)} %collective-permute-done.9.other, bf16[512,2048]{1,0:T(8,128)(2,1)} %bitcast.60, ...), custom_call_target="tpu_custom_call" | custom-call | flops 2684354560 | bytes 19398656 | tf_op jit(solution)/shard_map/pull/pallas_call | solution.py:551
  373.7 11.0 %weight_grad.9 = (bf16[512,1280]{1,0:T(8,128)(2,1)}, bf16[512,1280]{1,0:T(8,128)(2,1)}) custom-call(bf16[512,2048]{1,0:T(8,128)(2,1)} %get-tuple-element.172.own_a.own_b, bf16[512,2048]{1,0:T(8,128)(2,1)} %get-tuple-element.172.own_a.own_b, bf16[512,2048]{1,0:T(8,128)(2,1)} %get-tuple-element.173.oth_a.oth_b, ...), custom_call_target="tpu_custom_call" | custom-call | flops 5368709120 | bytes 10485760 | tf_op jit(solution)/shard_map/weight_grad/pallas_call | solution.py:441
  387.9 2.9 halve.14
  390.8 2.6 collective-permute-start.14
  393.3 5.7 collective-permute-done.10.received_low.received_high
  403.5 33.7 %rec_bwd.1 = (bf16[512,1280]{1,0:T(8,128)(2,1)S(1)}, bf16[512,1280]{1,0:T(8,128)(2,1)}, bf16[512,1280]{1,0:T(8,128)(2,1)}, bf16[512,1280]{1,0:T(8,128)(2,1)}, bf...) custom-call(bf16[512,1280]{1,0:T(8,128)(2,1)} %convolution_convert_fusion.5.bx_own, bf16[512,1280]{1,0:T(8,128)(2,1)} %copy-done.23, ...), custom_call_target="tpu_custom_call" | custom-call | flops 2880962560 | bytes 44564480 | tf_op jit(solution)/shard_map/rec_bwd/pallas_call | solution.py:296
  439.0 2.8 halve.16
  441.8 2.6 collective-permute-start.16
  445.8 12.6 %weight_grad.10 = (bf16[704,1280]{1,0:T(8,128)(2,1)}, bf16[704,1280]{1,0:T(8,128)(2,1)}) custom-call(bf16[512,2048]{1,0:T(8,128)(2,1)} %copy-done.26, bf16[512,2048]{1,0:T(8,128)(2,1)} %copy-done.26, bf16[512,2048]{1,0:T(8,128)(2,1)} %copy-done.27, bf16[512,2048]{1,0:T(8,128)(2,1)} %copy-done.27, bf16[512,1280]{1,0:T(8,128)(2,1)} %copy-done.30, ...), custom_call_target="tpu_custom_call" | custom-call | flops 5368709120 | bytes 10485760 | tf_op jit(solution)/shard_map/weight_grad/pallas_call | solution.py:441
  459.9 2.7 add_bitcast_fusion
  465.7 3.0 copy.61
  471.4 9.3 %two_back.6 = bf16[512,2048]{1,0:T(8,128)(2,1)} custom-call(bf16[512,1280]{1,0:T(8,128)(2,1)S(1)} %copy-done.34, bf16[2048,1280]{1,0:T(8,128)(2,1)} %first_w.7, bf16[512,1280]{1,0:T(8,128)(2,1)S(1)} %copy-done.33, bf16[2048,1280]{1,0:T(8,128)(2,1)} %second_w.7), custom_call_target="tpu_custom_call" | custom-call | flops 5368709120 | bytes 13107200 | tf_op jit(solution)/shard_map/two_back/pallas_call | solution.py:582
  486.1 2.8 multiply_reduce_fusion.1
  488.9 10.8 %weight_grad.11 = (bf16[512,1280]{1,0:T(8,128)(2,1)}, bf16[512,1280]{1,0:T(8,128)(2,1)}) custom-call(bf16[512,2048]{1,0:T(8,128)(2,1)} %copy-done.26, bf16[512,2048]{1,0:T(8,128)(2,1)} %copy-done.26, bf16[512,2048]{1,0:T(8,128)(2,1)} %copy-done.27, bf16[512,2048]{1,0:T(8,128)(2,1)} %copy-done.27, bf16[512,1280]{1,0:T(8,128)(2,1)} %get-tuple-element.204.right_own.second, ...), custom_call_target="tpu_custom_call" | custom-call | flops 5368709120 | bytes 10485760 | tf_op jit(solution)/shard_map/weight_grad/pallas_call | solution.py:441
  505.8 10.8 %convolution_convert_fusion = bf16[512,2048]{1,0:T(8,128)(2,1)} fusion(bf16[512,3072]{1,0:T(8,128)(2,1)S(1)} %copy-done.64, bf16[3072,2048]{1,0:T(8,128)(2,1)} %param.28), kind=kOutput, calls=%fused_computation.19 | convolution fusion | flops 6443499520 | bytes 17825792 | tf_op jit(solution)/shard_map/dot_general | solution.py:880
  516.6 8.4 %two_back.7 = bf16[512,2048]{1,0:T(8,128)(2,1)S(1)} custom-call(bf16[512,1280]{1,0:T(8,128)(2,1)S(1)} %copy-done.31, bf16[2048,1280]{1,0:T(8,128)(2,1)} %first_w.7, bf16[512,1280]{1,0:T(8,128)(2,1)S(1)} %copy-done.32, bf16[2048,1280]{1,0:T(8,128)(2,1)} %second_w.7), custom_call_target="tpu_custom_call" | custom-call | flops 5368709120 | bytes 13107200 | tf_op jit(solution)/shard_map/two_back/pallas_call | solution.py:582
  525.0 3.0 collective-permute-done.20
  529.5 2.6 fusion.6
  532.2 5.0 fusion.8
  539.9 2.9 multiply_reduce_fusion
  550.0 18.4 %collective-permute-done.21.received_low.received_high = bf16[256,1280]{1,0:T(8,128)(2,1)S(1)} collective-permute-done((bf16[256,1280]{1,0:T(8,128)(2,1)}, bf16[256,1280]{1,0:T(8,128)(2,1)S(1)}, u32[]{:S(2)}, u32[]{:S(2)}) %collective-permute-start.21) | collective-permute-done | bytes 655392 | tf_op jit(solution)/shard_map/ppermute | solution.py:602
  569.4 5.0 collective-permute-done.18
  574.4 4.7 add_convert_fusion
  (264 shorter events, 88.7 us)
Async XLA Ops:
  0.6 32.9 %copy-start = (bf16[2,10,256,256]{3,2,1,0:T(8,128)(2,1)S(1)}, bf16[2,10,256,256]{3,2,1,0:T(8,128)(2,1)}, u32[]{:S(2)}) copy-start(bf16[2,10,256,256]{3,2,1,0:T(8,128)(2,1)} %param.24) | copy-start | bytes 7864324
  0.7 34.1 %collective-permute-start.1 = (s32[512]{0:T(512)}, s32[512]{0:T(512)S(1)}, u32[]{:S(2)}, u32[]{:S(2)}) collective-permute-start(s32[512]{0:T(512)} %bitcast.83), channel_id=1, source_target_pairs={{0,1},{1,0},{2,3},{3,2},{4,5},{5,4},{6,7},{7,6},{8,9},{9,8},{10,11... | collective-permute-start | bytes 6152 | tf_op jit(solution)/shard_map/ppermute | solution.py:597
  3.7 48.9 %collective-permute-start = (bf16[512,2048]{1,0:T(8,128)(2,1)}, bf16[512,2048]{1,0:T(8,128)(2,1)}, u32[]{:S(2)}, u32[]{:S(2)}) collective-permute-start(bf16[512,2048]{1,0:T(8,128)(2,1)} %bitcast.63), channel_id=1, source_target_pairs={{0,1},{1,0},{2,3},{3,2},{4,5},{5,4},{6,7},{7,6},{8,9},{9,8},{10,11... | collective-permute-start | bytes 6291464 | tf_op jit(solution)/shard_map/ppermute | solution.py:597
  3.8 95.7 %collective-permute-start.3 = (bf16[512,2048]{1,0:T(8,128)(2,1)}, bf16[512,2048]{1,0:T(8,128)(2,1)}, u32[]{:S(2)}, u32[]{:S(2)}) collective-permute-start(bf16[512,2048]{1,0:T(8,128)(2,1)} %bitcast.59), channel_id=1, source_target_pairs={{0,1},{1,0},{2,3},{3,2},{4,5},{5,4},{6,7},{7,6},{8,9},{9,8},{10,11... | collective-permute-start | bytes 6291464 | tf_op jit(solution)/shard_map/ppermute | solution.py:597
  9.2 45.4 %copy-start.49 = (f32[1,2048]{1,0:T(1,128)}, f32[1,2048]{1,0:T(1,128)S(1)}, u32[]{:S(2)}) copy-start(f32[1,2048]{1,0:T(1,128)S(1)} %get-tuple-element.311) | copy-start | bytes 24580
  33.6 33.8 %copy-start.24 = (f32[8,1280]{1,0:T(8,128)}, f32[8,1280]{1,0:T(8,128)S(1)}, u32[]{:S(2)}) copy-start(f32[8,1280]{1,0:T(8,128)S(1)} %fusion.13.prm_ref) | copy-start | bytes 122884
  57.0 33.9 %slice-start = ((s8[5242880]{0:T(1024)(128)(4,1)}), s8[4194304]{0:T(1024)(128)(4,1)S(1)}, s32[]{:S(2)}) async-start(s8[5242880]{0:T(1024)(128)(4,1)} %bitcast.65), calls=%async_computation | async-start | bytes 8388608
  64.0 26.9 %slice-start.1 = ((s8[5242880]{0:T(1024)(128)(4,1)}), s8[1048576]{0:T(1024)(128)(4,1)S(1)}, s32[]{:S(2)}) async-start(s8[5242880]{0:T(1024)(128)(4,1)} %bitcast.65), calls=%async_computation.1 | async-start | bytes 2097152
  66.9 23.9 %copy-start.23 = (bf16[512,1280]{1,0:T(8,128)(2,1)}, bf16[512,1280]{1,0:T(8,128)(2,1)S(1)}, u32[]{:S(2)}) copy-start(bf16[512,1280]{1,0:T(8,128)(2,1)S(1)} %convolution_convert_fusion.4.bx_oth) | copy-start | bytes 3932164
  67.4 23.4 %copy-start.10 = (f32[3,67,16,128]{3,2,1,0:T(8,128)}, f32[3,67,16,128]{3,2,1,0:T(8,128)S(1)}, u32[]{:S(2)}) copy-start(f32[3,67,16,128]{3,2,1,0:T(8,128)S(1)} %broadcast_in_dim.11.mask_ref) | copy-start | bytes 4939780
  94.0 48.7 %collective-permute-start.2 = (bf16[512,2048]{1,0:T(8,128)(2,1)S(1)}, bf16[512,2048]{1,0:T(8,128)(2,1)}, u32[]{:S(2)}, u32[]{:S(2)}) collective-permute-start(bf16[512,2048]{1,0:T(8,128)(2,1)S(1)} %convolution_convert_fusion.3.part), channel_id=1, source_target_pairs={{0,1},{1,0},{2,3},{3,2},{4,5},{5,4},{6,7},{7,6},{8,9},{9,8},{10,11... | collective-permute-start | bytes 6291464 | tf_op jit(solution)/shard_map/ppermute | solution.py:597
  97.4 14.2 %copy-start.62 = (bf16[512,2048]{1,0:T(8,128)(2,1)}, bf16[512,2048]{1,0:T(8,128)(2,1)S(1)}, u32[]{:S(2)}) copy-start(bf16[512,2048]{1,0:T(8,128)(2,1)S(1)} %convolution_convert_fusion.2.part) | copy-start | bytes 6291460
  97.4 14.1 %copy-start.6 = (bf16[1,512,2048]{2,1,0:T(8,128)(2,1)S(1)}, bf16[1,512,2048]{2,1,0:T(8,128)(2,1)}, u32[]{:S(2)}) copy-start(bf16[1,512,2048]{2,1,0:T(8,128)(2,1)} %param.16) | copy-start | bytes 6291460
  97.4 91.6 %collective-permute-start.4 = (bf16[512,2048]{1,0:T(8,128)(2,1)S(1)}, bf16[512,2048]{1,0:T(8,128)(2,1)S(1)}, u32[]{:S(2)}, u32[]{:S(2)}) collective-permute-start(bf16[512,2048]{1,0:T(8,128)(2,1)S(1)} %convolution_convert_fusion.2.part), channel_id=1, source_target_pairs={{0,1},{1,0},{2,3},{3,2},{4,5},{5,4},{6,7},{7,6},{8,9},{9,8},{10,11... | collective-permute-start | bytes 6291464 | tf_op jit(solution)/shard_map/ppermute | solution.py:597
  189.0 129.0 %collective-permute-start.7 = (bf16[512,2048]{1,0:T(8,128)(2,1)}, bf16[512,2048]{1,0:T(8,128)(2,1)}, u32[]{:S(2)}, u32[]{:S(2)}) collective-permute-start(bf16[512,2048]{1,0:T(8,128)(2,1)} %two_back.4.back), channel_id=1, source_target_pairs={{0,1},{1,0},{2,3},{3,2},{4,5},{5,4},{6,7},{7,6},{8,9},{9,8},{10,11... | collective-permute-start | bytes 6291464 | tf_op jit(solution)/shard_map/ppermute | solution.py:597
  237.6 25.0 %copy-start.38 = (bf16[512,3072]{1,0:T(8,128)(2,1)S(1)}, bf16[512,3072]{1,0:T(8,128)(2,1)}, u32[]{:S(2)}) copy-start(bf16[512,3072]{1,0:T(8,128)(2,1)} %get-tuple-element.148.right_oth.first) | copy-start | bytes 9437188
  260.3 71.6 %collective-permute-start.6 = (bf16[512,3072]{1,0:T(8,128)(2,1)}, bf16[512,3072]{1,0:T(8,128)(2,1)}, u32[]{:S(2)}, u32[]{:S(2)}) collective-permute-start(bf16[512,3072]{1,0:T(8,128)(2,1)} %get-tuple-element.154), channel_id=1, source_target_pairs={{0,4},{2,6},{4,0},{6,2},{8,12},{10,14},{12,8},{14,10},{16,20},{18,... | collective-permute-start | bytes 9437192 | tf_op jit(solution)/shard_map/ppermute | solution.py:602
  281.0 79.0 %collective-permute-start.9 = (bf16[512,2048]{1,0:T(8,128)(2,1)}, bf16[512,2048]{1,0:T(8,128)(2,1)}, u32[]{:S(2)}, u32[]{:S(2)}) collective-permute-start(bf16[512,2048]{1,0:T(8,128)(2,1)} %two_back.5.back), channel_id=1, source_target_pairs={{0,1},{1,0},{2,3},{3,2},{4,5},{5,4},{6,7},{7,6},{8,9},{9,8},{10,11... | collective-permute-start | bytes 6291464 | tf_op jit(solution)/shard_map/ppermute | solution.py:597
  282.4 71.4 %collective-permute-start.5 = (bf16[512,3072]{1,0:T(8,128)(2,1)}, bf16[512,3072]{1,0:T(8,128)(2,1)}, u32[]{:S(2)}, u32[]{:S(2)}) collective-permute-start(bf16[512,3072]{1,0:T(8,128)(2,1)} %get-tuple-element.153), channel_id=1, source_target_pairs={{0,8},{2,10},{4,12},{6,14},{8,0},{10,2},{12,4},{14,6},{16,24},{18,... | collective-permute-start | bytes 9437192 | tf_op jit(solution)/shard_map/ppermute | solution.py:602
  305.5 93.6 %collective-permute-start.10 = (bf16[512,3072]{1,0:T(8,128)(2,1)}, bf16[512,3072]{1,0:T(8,128)(2,1)S(1)}, u32[]{:S(2)}, u32[]{:S(2)}) collective-permute-start(bf16[512,3072]{1,0:T(8,128)(2,1)} %get-tuple-element.169), channel_id=1, source_target_pairs={{0,4},{2,6},{4,0},{6,2},{8,12},{10,14},{12,8},{14,10},{16,20},{18,... | collective-permute-start | bytes 9437192 | tf_op jit(solution)/shard_map/ppermute | solution.py:602
  318.0 13.9 %copy-start.4 = (bf16[512,3072]{1,0:T(8,128)(2,1)S(1)}, bf16[512,3072]{1,0:T(8,128)(2,1)}, u32[]{:S(2)}) copy-start(bf16[512,3072]{1,0:T(8,128)(2,1)} %get-tuple-element.144.keep_low.keep_high) | copy-start | bytes 9437188
  336.0 50.5 %collective-permute-start.11 = (bf16[256,3072]{1,0:T(8,128)(2,1)}, bf16[256,3072]{1,0:T(8,128)(2,1)}, u32[]{:S(2)}, u32[]{:S(2)}) collective-permute-start(bf16[256,3072]{1,0:T(8,128)(2,1)} %get-tuple-element.159), channel_id=1, source_target_pairs={{0,8},{2,10},{4,12},{6,14},{8,0},{10,2},{12,4},{14,6},{16,24},{18,... | collective-permute-start | bytes 4718600 | tf_op jit(solution)/shard_map/ppermute | solution.py:602
  359.6 79.4 %collective-permute-start.8 = (bf16[256,3072]{1,0:T(8,128)(2,1)}, bf16[256,3072]{1,0:T(8,128)(2,1)}, u32[]{:S(2)}, u32[]{:S(2)}) collective-permute-start(bf16[256,3072]{1,0:T(8,128)(2,1)} %get-tuple-element.162), channel_id=1, source_target_pairs={{0,4},{2,6},{4,0},{6,2},{8,12},{10,14},{12,8},{14,10},{16,20},{18,... | collective-permute-start | bytes 4718600 | tf_op jit(solution)/shard_map/ppermute | solution.py:602
  384.7 77.9 %collective-permute-start.13 = (bf16[512,1280]{1,0:T(8,128)(2,1)}, bf16[512,1280]{1,0:T(8,128)(2,1)}, u32[]{:S(2)}, u32[]{:S(2)}) collective-permute-start(bf16[512,1280]{1,0:T(8,128)(2,1)} %get-tuple-element.190), channel_id=1, source_target_pairs={{0,4},{2,6},{4,0},{6,2},{8,12},{10,14},{12,8},{14,10},{16,20},{18,... | collective-permute-start | bytes 3932168 | tf_op jit(solution)/shard_map/ppermute | solution.py:602
  390.8 12.7 %copy-start.25 = (f32[8,1280]{1,0:T(8,128)S(1)}, f32[8,1280]{1,0:T(8,128)}, u32[]{:S(2)}) copy-start(f32[8,1280]{1,0:T(8,128)} %copy-done.24) | copy-start | bytes 122884
  390.8 69.2 %collective-permute-start.14 = (bf16[128,3072]{1,0:T(8,128)(2,1)}, bf16[128,3072]{1,0:T(8,128)(2,1)}, u32[]{:S(2)}, u32[]{:S(2)}) collective-permute-start(bf16[128,3072]{1,0:T(8,128)(2,1)} %get-tuple-element.176), channel_id=1, source_target_pairs={{0,16},{2,18},{4,20},{6,22},{8,24},{10,26},{12,28},{14,30},{16,0},... | collective-permute-start | bytes 2359304 | tf_op jit(solution)/shard_map/ppermute | solution.py:602
  401.4 80.8 %collective-permute-start.17 = (bf16[256,3072]{1,0:T(8,128)(2,1)}, bf16[256,3072]{1,0:T(8,128)(2,1)S(1)}, u32[]{:S(2)}, u32[]{:S(2)}) collective-permute-start(bf16[256,3072]{1,0:T(8,128)(2,1)} %get-tuple-element.178), channel_id=1, source_target_pairs={{0,8},{2,10},{4,12},{6,14},{8,0},{10,2},{12,4},{14,6},{16,24},{18,... | collective-permute-start | bytes 4718600 | tf_op jit(solution)/shard_map/ppermute | solution.py:602
  403.5 35.5 %copy-start.12 = (bf16[256,3072]{1,0:T(8,128)(2,1)S(1)}, bf16[256,3072]{1,0:T(8,128)(2,1)}, u32[]{:S(2)}) copy-start(bf16[256,3072]{1,0:T(8,128)(2,1)} %get-tuple-element.161.keep_low.keep_high) | copy-start | bytes 4718596
  441.8 44.3 %collective-permute-start.16 = (bf16[128,3072]{1,0:T(8,128)(2,1)}, bf16[128,3072]{1,0:T(8,128)(2,1)}, u32[]{:S(2)}, u32[]{:S(2)}) collective-permute-start(bf16[128,3072]{1,0:T(8,128)(2,1)} %get-tuple-element.182), channel_id=1, source_target_pairs={{0,16},{2,18},{4,20},{6,22},{8,24},{10,26},{12,28},{14,30},{16,0},... | collective-permute-start | bytes 2359304 | tf_op jit(solution)/shard_map/ppermute | solution.py:602
  458.5 44.8 %collective-permute-start.12 = (bf16[704,1280]{1,0:T(8,128)(2,1)}, bf16[704,1280]{1,0:T(8,128)(2,1)S(1)}, u32[]{:S(2)}, u32[]{:S(2)}) collective-permute-start(bf16[704,1280]{1,0:T(8,128)(2,1)} %get-tuple-element.189), channel_id=1, source_target_pairs={{0,4},{2,6},{4,0},{6,2},{8,12},{10,14},{12,8},{14,10},{16,20},{18,... | collective-permute-start | bytes 5406728 | tf_op jit(solution)/shard_map/ppermute | solution.py:602
  465.1 34.6 %collective-permute-start.15 = (bf16[256,1280]{1,0:T(8,128)(2,1)}, bf16[256,1280]{1,0:T(8,128)(2,1)}, u32[]{:S(2)}, u32[]{:S(2)}) collective-permute-start(bf16[256,1280]{1,0:T(8,128)(2,1)} %get-tuple-element.195), channel_id=1, source_target_pairs={{0,8},{2,10},{4,12},{6,14},{8,0},{10,2},{12,4},{14,6},{16,24},{18,... | collective-permute-start | bytes 1966088 | tf_op jit(solution)/shard_map/ppermute | solution.py:602
  480.7 47.3 %collective-permute-start.20 = (bf16[512,2048]{1,0:T(8,128)(2,1)}, bf16[512,2048]{1,0:T(8,128)(2,1)}, u32[]{:S(2)}, u32[]{:S(2)}) collective-permute-start(bf16[512,2048]{1,0:T(8,128)(2,1)} %two_back.6), channel_id=1, source_target_pairs={{0,1},{1,0},{2,3},{3,2},{4,5},{5,4},{6,7},{7,6},{8,9},{9,8},{10,11... | collective-permute-start | bytes 6291464 | tf_op jit(solution)/shard_map/ppermute | solution.py:597
  483.7 56.2 %collective-permute-start.24 = (bf16[128,3072]{1,0:T(8,128)(2,1)}, bf16[128,3072]{1,0:T(8,128)(2,1)}, u32[]{:S(2)}, u32[]{:S(2)}) collective-permute-start(bf16[128,3072]{1,0:T(8,128)(2,1)} %get-tuple-element.201), channel_id=1, source_target_pairs={{0,16},{2,18},{4,20},{6,22},{8,24},{10,26},{12,28},{14,30},{16,0},... | collective-permute-start | bytes 2359304 | tf_op jit(solution)/shard_map/ppermute | solution.py:602
  488.9 12.3 %copy-start.20 = (bf16[256,1280]{1,0:T(8,128)(2,1)S(1)}, bf16[256,1280]{1,0:T(8,128)(2,1)}, u32[]{:S(2)}) copy-start(bf16[256,1280]{1,0:T(8,128)(2,1)} %get-tuple-element.194.keep_low.keep_high) | copy-start | bytes 1966084
  499.8 37.4 %collective-permute-start.19 = (bf16[512,1280]{1,0:T(8,128)(2,1)}, bf16[512,1280]{1,0:T(8,128)(2,1)S(1)}, u32[]{:S(2)}, u32[]{:S(2)}) collective-permute-start(bf16[512,1280]{1,0:T(8,128)(2,1)} %get-tuple-element.211), channel_id=1, source_target_pairs={{0,4},{2,6},{4,0},{6,2},{8,12},{10,14},{12,8},{14,10},{16,20},{18,... | collective-permute-start | bytes 3932168 | tf_op jit(solution)/shard_map/ppermute | solution.py:602
  503.2 39.6 %collective-permute-start.23 = (bf16[128,1280]{1,0:T(8,128)(2,1)}, bf16[128,1280]{1,0:T(8,128)(2,1)S(1)}, u32[]{:S(2)}, u32[]{:S(2)}) collective-permute-start(bf16[128,1280]{1,0:T(8,128)(2,1)} %get-tuple-element.207), channel_id=1, source_target_pairs={{0,16},{2,18},{4,20},{6,22},{8,24},{10,26},{12,28},{14,30},{16,0},... | collective-permute-start | bytes 983048 | tf_op jit(solution)/shard_map/ppermute | solution.py:602
  504.7 12.0 %copy-start.32 = (bf16[512,1280]{1,0:T(8,128)(2,1)S(1)}, bf16[512,1280]{1,0:T(8,128)(2,1)}, u32[]{:S(2)}) copy-start(bf16[512,1280]{1,0:T(8,128)(2,1)} %get-tuple-element.204.right_own.second) | copy-start | bytes 3932164
  504.7 43.0 %collective-permute-start.22 = (bf16[352,1280]{1,0:T(8,128)(2,1)}, bf16[352,1280]{1,0:T(8,128)(2,1)S(1)}, u32[]{:S(2)}, u32[]{:S(2)}) collective-permute-start(bf16[352,1280]{1,0:T(8,128)(2,1)} %get-tuple-element.209), channel_id=1, source_target_pairs={{0,8},{2,10},{4,12},{6,14},{8,0},{10,2},{12,4},{14,6},{16,24},{18,... | collective-permute-start | bytes 2703368 | tf_op jit(solution)/shard_map/ppermute | solution.py:602
  516.6 12.9 %copy-start.40 = (bf16[1,512,2048]{2,1,0:T(8,128)(2,1)S(1)}, bf16[1,512,2048]{2,1,0:T(8,128)(2,1)}, u32[]{:S(2)}) copy-start(bf16[1,512,2048]{2,1,0:T(8,128)(2,1)} %param.15) | copy-start | bytes 6291460
  516.6 12.9 %copy-start.50 = (f32[1,2048]{1,0:T(1,128)S(1)}, f32[1,2048]{1,0:T(1,128)}, u32[]{:S(2)}) copy-start(f32[1,2048]{1,0:T(1,128)} %copy-done.49) | copy-start | bytes 24580
  528.0 46.4 %collective-permute-start.18 = (bf16[512,2048]{1,0:T(8,128)(2,1)}, bf16[512,2048]{1,0:T(8,128)(2,1)}, u32[]{:S(2)}, u32[]{:S(2)}) collective-permute-start(bf16[512,2048]{1,0:T(8,128)(2,1)} %convolution_convert_fusion), channel_id=1, source_target_pairs={{0,1},{1,0},{2,3},{3,2},{4,5},{5,4},{6,7},{7,6},{8,9},{9,8},{10,11... | collective-permute-start | bytes 6291464 | tf_op jit(solution)/shard_map/ppermute | solution.py:597
  538.4 30.0 %collective-permute-start.21 = (bf16[256,1280]{1,0:T(8,128)(2,1)}, bf16[256,1280]{1,0:T(8,128)(2,1)S(1)}, u32[]{:S(2)}, u32[]{:S(2)}) collective-permute-start(bf16[256,1280]{1,0:T(8,128)(2,1)} %get-tuple-element.217), channel_id=1, source_target_pairs={{0,8},{2,10},{4,12},{6,14},{8,0},{10,2},{12,4},{14,6},{16,24},{18,... | collective-permute-start | bytes 1966088 | tf_op jit(solution)/shard_map/ppermute | solution.py:602
  543.7 24.7 %copy-start.21 = (bf16[256,1280]{1,0:T(8,128)(2,1)S(1)}, bf16[256,1280]{1,0:T(8,128)(2,1)}, u32[]{:S(2)}) copy-start(bf16[256,1280]{1,0:T(8,128)(2,1)} %get-tuple-element.216.keep_low.keep_high) | copy-start | bytes 1966084
  547.7 26.7 %copy-start.41 = (f32[512,2048]{1,0:T(8,128)S(1)}, f32[512,2048]{1,0:T(8,128)}, u32[]{:S(2)}) copy-start(f32[512,2048]{1,0:T(8,128)} %get-tuple-element.134.middle) | copy-start | bytes 12582916
  548.7 30.4 %collective-permute-start.25 = (bf16[176,1280]{1,0:T(8,128)(2,1)}, bf16[176,1280]{1,0:T(8,128)(2,1)S(1)}, u32[]{:S(2)}, u32[]{:S(2)}) collective-permute-start(bf16[176,1280]{1,0:T(8,128)(2,1)} %get-tuple-element.224), channel_id=1, source_target_pairs={{0,16},{2,18},{4,20},{6,22},{8,24},{10,26},{12,28},{14,30},{16,0},... | collective-permute-start | bytes 1351688 | tf_op jit(solution)/shard_map/ppermute | solution.py:602
  569.3 15.4 %collective-permute-start.26 = (bf16[128,1280]{1,0:T(8,128)(2,1)}, bf16[128,1280]{1,0:T(8,128)(2,1)}, u32[]{:S(2)}, u32[]{:S(2)}) collective-permute-start(bf16[128,1280]{1,0:T(8,128)(2,1)} %get-tuple-element.226), channel_id=1, source_target_pairs={{0,16},{2,18},{4,20},{6,22},{8,24},{10,26},{12,28},{14,30},{16,0},... | collective-permute-start | bytes 983048 | tf_op jit(solution)/shard_map/ppermute | solution.py:602
  579.3 4.9 collective-permute-start.27
  587.4 4.1 collective-permute-start.28
  (52 other events, 284.5 us)

commit v6 on v5

--- a/solution.py
+++ b/solution.py
@@ -11,12 +11,12 @@
 F32, BF16 = jnp.float32, jnp.bfloat16
 GELU_A, GELU_B = 0.7978845608028654, 0.044715
 ORDER = (
-    "DK", "GK", "B2", "UK", "OK", "P2", "D1", "G1", "P1", "OUT", "D2", "U1",
-    "RB", "G2", "X", "Dt", "O1", "RS", "U2", "Gt", "Y", "O2", "X1", "OS",
-    "RK", "IG", "Y1", "Ut", "Ot", "X2", "Y2", "LO", "Xt", "SW", "Yt",
+    "DK", "GK", "UK", "B2", "P2", "D1", "G1", "P1", "OUT", "D2", "U1", "RB",
+    "G2", "X", "Dt", "O1", "RS", "U2", "Gt", "Y", "O2", "X1", "OS", "RK",
+    "IG", "Y1", "Ut", "Ot", "X2", "Y2", "OK", "LO", "Xt", "SW", "Yt", "GN",
 )
 CROSSED = "G"
-COSTS = {}
+COSTS = {"B2": 0.6, "GK": 0.6, "P2": 6, "UK": 0.6}
 MESH = pl.DeviceIdType.MESH
 
 
@@ -786,6 +786,21 @@
 
     each = full_width // count
     block = model // count
+
+    def gain_grad(gain, *pairs):
+        weights = sum(
+            jnp.sum(lax.dynamic_slice_in_dim(weight, me * block, block, axis=0).astype(F32) * grad, axis=1)
+            for weight, grad in pairs
+        )
+        return weights / lax.dynamic_slice_in_dim(gain, me * block, block, axis=0)
+
+    def sum_gains(cost):
+        first = gain_grad(norm_gains[0], (w_x, grads["X"][:block]), (w_y, grads["Y"]))
+        second = gain_grad(norm_gains[1], (w_gate, grads["G"]), (w_up, grads["U"]))
+        gains = after(jnp.stack([first, second]), at["done"])
+        at["gains"] = gains + swap(gains)
+        return gains
+
     steps = {
         "DK": lambda cost: reduce_kernel("DK", "D", cot_cols, (hidden_own, hidden_oth)),
         "GK": lambda cost: reduce_kernel("GK", "G", (two_own, two_oth), (gg_own, gg_oth)),
@@ -804,6 +819,7 @@
         "IG": to_inputs,
         "LO": to_outputs,
         "SW": swap_blocks,
+        "GN": sum_gains,
     }
     grads = {}
     for name in ORDER:
@@ -822,24 +838,10 @@
     block_sums = jnp.transpose(both, (1, 0, 3, 2, 4)).reshape(2, 2 * heads, -1, gates.shape[-1])
     small = jnp.where(me < count // 2, low[-16:-8], high[-16:-8])[:, :each].astype(F32)
 
-    def gain_grad(gain, *pairs):
-        weights = sum(
-            jnp.sum(lax.dynamic_slice_in_dim(weight, me * block, block, axis=0).astype(F32) * grad, axis=1)
-            for weight, grad in pairs
-        )
-        return weights / lax.dynamic_slice_in_dim(gain, me * block, block, axis=0)
-
-    gains = jnp.stack(
-        [
-            gain_grad(norm_gains[0], (w_x, x_grad), (w_y, y_grad)),
-            gain_grad(norm_gains[1], (w_gate, gate_grad), (w_up, up_grad)),
-        ]
-    )
-    gains = gains + swap(gains)
     return (
         layer_out[None],
         input_grad[None],
-        gains,
+        at["gains"],
         x_grad,
         y_grad,
         small[0:4],

time: 598 us -> 588 us (0.983)
  starting transfers between devices: 40.2 us -> 33.4 us
    ppermute x18, waiting for transfers between devices: 41.9 us -> 28.1 us  [flip(): lax.ppermute(value, 'dp', [(source, source ^ bit) for source in range(cou...]
    ppermute x11, waiting for transfers between devices: 49.2 us -> 59.9 us  [swap(): return lax.ppermute(value, 'tp', [(0, 1), (1, 0)])]
    unnamed x144 -> x140, local copies, waits for them, and re-layouts: 19.9 us -> 21.3 us
  transfers between devices with their start and end apart: 29 -> 29, of which waited for: 10 -> 9; matrix products, arithmetic and copies ran while one was open for 20% -> 20% of each run, Pallas kernels for 54% -> 55%
where the time goes in v6:
time: 588 us; the launch traced here: 582 us
  Pallas kernels  322 us (55%)
  waiting for transfers between devices  88 us (15%)
  matrix products  73.4 us (12%)
  other arithmetic  35.5 us (6%)
  starting transfers between devices  33.4 us (6%)
  local copies, waits for them, and re-layouts  28 us (5%)
    pallas_call x6, Pallas kernels, weight_grad(): pl.pallas_call(functools.partial(weight_grad_kernel, more), grid=(4,), in...  99.8 us
    ppermute x11, waiting for transfers between devices, swap(): return lax.ppermute(value, 'tp', [(0, 1), (1, 0)])  59.9 us
    pallas_call x4, Pallas kernels, two_back(): pl.pallas_call(two_back_kernel, grid=(cols // step,), in_specs=[left, rig...  54.9 us
    pallas_call x2, Pallas kernels, feed(): pl.pallas_call(functools.partial(feed_kernel, bits, sub), grid=(cols // w...  51.3 us
    dot_general x9, matrix products, matmul(): return jnp.dot(first_mat, second_mat, preferred_element_type=jnp.float32)  49.5 us
    pallas_call x1, Pallas kernels, rec_bwd(): pl.pallas_call(functools.partial(rec_bwd_kernel, count, stage_bits(count,...  33.9 us
    ppermute x18, waiting for transfers between devices, flip(): lax.ppermute(value, 'dp', [(source, source ^ bit) for source in range(cou...  28.1 us
    pallas_call x2, Pallas kernels, pull(): pl.pallas_call(functools.partial(pull_kernel, bits), grid=(cols // wide,)...  27.8 us
  transfers between devices with their start and end apart: 29, of which 9 were waited for; matrix products, arithmetic and copies ran while one was open for 20% of the time, Pallas kernels for 55%

profile of v6, /device:TPU:0, one launch (start us, length us, event | category | flops | bytes accessed | tf_op | source)
XLA Modules:
  0.0 582.1 jit_solution(12167196494414168241)
XLA Ops:
  0.7 3.0 collective-permute-start.1
  10.4 7.7 %fusion.38.by_own = f32[512,1280]{1,0:T(8,128)} fusion(bf16[512,2048]{1,0:T(8,128)(2,1)S(1)} %fusion.5.first, bf16[2048,1280]{1,0:T(8,128)(2,1)} %second_w.7), kind=kOutput, calls=%fused_computation.95 | convolution fusion | flops 2684354560 | bytes 9961472 | tf_op jit(solution)/shard_map/dot_general | solution.py:882
  18.1 4.0 convolution_convert_fusion.5.bx_own
  22.0 11.9 %fusion.39.grad_hidden = f32[512,3072]{1,0:T(8,128)} fusion(bf16[512,2048]{1,0:T(8,128)(2,1)S(1)} %bitcast.61, bf16[3072,2048]{1,0:T(8,128)(2,1)} %param.28), kind=kOutput, calls=%fused_computation.96 | convolution fusion | flops 6442450944 | bytes 20971520 | tf_op jit(solution)/shard_map/dot_general | solution.py:892
  36.2 16.4 %collective-permute-done.tokens = bf16[512,2048]{1,0:T(8,128)(2,1)} collective-permute-done((bf16[512,2048]{1,0:T(8,128)(2,1)}, bf16[512,2048]{1,0:T(8,128)(2,1)}, u32[]{:S(2)}, u32[]{:S(2)}) %collective-permute-start) | collective-permute-done | bytes 2097184 | tf_op jit(solution)/shard_map/ppermute | solution.py:597
  57.0 7.0 %fusion.40.by_oth = f32[512,1280]{1,0:T(8,128)} fusion(bf16[512,2048]{1,0:T(8,128)(2,1)S(1)} %fusion.2.second, bf16[2048,1280]{1,0:T(8,128)(2,1)} %second_w.7), kind=kOutput, calls=%fused_computation.97 | convolution fusion | flops 2684354560 | bytes 9961472 | tf_op jit(solution)/shard_map/dot_general | solution.py:882
  64.0 2.9 convolution_convert_fusion.4.bx_oth
  67.4 23.3 %rec_fwd.1 = (bf16[512,1280]{1,0:T(8,128)(2,1)S(1)}, bf16[512,1280]{1,0:T(8,128)(2,1)S(1)}, f32[64,16,1280]{2,1,0:T(8,128)}, f32[64,16,1280]{2,1,0:T(8,128)}, f3...) custom-call(bf16[512,1280]{1,0:T(8,128)(2,1)S(1)} %copy-done.23, ...), custom_call_target="tpu_custom_call" | custom-call | flops 1473249280 | bytes 34078720 | tf_op jit(solution)/shard_map/rec_fwd/pallas_call | solution.py:267
  90.8 3.1 convolution_convert_fusion.3.part
  94.1 4.2 convolution_convert_fusion.2.part
  100.3 12.1 %fusion.41.grad_hidden = f32[512,3072]{1,0:T(8,128)} fusion(bf16[512,2048]{1,0:T(8,128)(2,1)} %collective-permute-done.3.second.cot, bf16[3072,2048]{1,0:T(8,128)(2,1)} %param.28), kind=kOutput, calls=%fused_computation.98 | convolution fusion | flops 6442450944 | bytes 20971520 | tf_op jit(solution)/shard_map/dot_general | solution.py:892
  112.3 2.9 arrange.2
  119.4 23.3 %collective-permute-done.2.other = bf16[512,2048]{1,0:T(8,128)(2,1)} collective-permute-done((bf16[512,2048]{1,0:T(8,128)(2,1)S(1)}, bf16[512,2048]{1,0:T(8,128)(2,1)}, u32[]{:S(2)}, u32[]{:S(2)}) %collective-permute-start.2) | collective-permute-done | bytes 2097184 | tf_op jit(solution)/shard_map/ppermute | solution.py:597
  142.7 25.6 %feed.2 = (f32[512,2048]{1,0:T(8,128)}, bf16[512,2048]{1,0:T(8,128)(2,1)}, bf16[512,3072]{1,0:T(8,128)(2,1)}, bf16[512,3072]{1,0:T(8,128)(2,1)}, bf16[512,3072]{1,0:T(8,128)(2,1)}) custom-call(bf16[512,2048]{1,0:T(8,128)(2,1)} %bitcast.64, bf16[512,2048]{1,0:T(8,128)(2,1)} %convolution_convert_fusion.2.part, bf16[512,2048]{1,0:T(8,128)(2,1)} %collective-permute-done.2.other, ...), custom_call_target="tpu_custom_call" | custom-call | flops 12884901888 | bytes 44040192 | tf_op jit(solution)/shard_map/feed/pallas_call | solution.py:511
  170.2 18.6 %two_back.4.back = bf16[512,2048]{1,0:T(8,128)(2,1)} custom-call(bf16[512,3072]{1,0:T(8,128)(2,1)S(1)} %copy-done.36, bf16[2048,3072]{1,0:T(8,128)(2,1)} %first_w.5, bf16[512,3072]{1,0:T(8,128)(2,1)} %get-tuple-element.139.second.right_own, bf16[2048,3072]{1,0:T(8,128)(2,1)} %second_w.5), custom_call_target="tpu_custom_call" | custom-call | flops 12884901888 | bytes 31457280 | tf_op jit(solution)/shard_map/two_back/pallas_call | solution.py:582
  190.3 25.6 %feed.3 = (f32[512,2048]{1,0:T(8,128)}, bf16[512,2048]{1,0:T(8,128)(2,1)}, bf16[512,3072]{1,0:T(8,128)(2,1)}, bf16[512,3072]{1,0:T(8,128)(2,1)}, bf16[512,3072]{1,0:T(8,128)(2,1)}) custom-call(bf16[512,2048]{1,0:T(8,128)(2,1)} %collective-permute-done.tokens, bf16[512,2048]{1,0:T(8,128)(2,1)} %copy-done.58, bf16[512,2048]{1,0:T(8,128)(2,1)} %copy-done.59, ...), custom_call_target="tpu_custom_call" | custom-call | flops 12884901888 | bytes 44040192 | tf_op jit(solution)/shard_map/feed/pallas_call | solution.py:511
  215.9 21.8 %weight_grad.6 = (bf16[512,3072]{1,0:T(8,128)(2,1)}, bf16[512,3072]{1,0:T(8,128)(2,1)}) custom-call(bf16[512,2048]{1,0:T(8,128)(2,1)} %copy-done.27, bf16[512,2048]{1,0:T(8,128)(2,1)} %copy-done.27, bf16[512,2048]{1,0:T(8,128)(2,1)} %copy-done.28, bf16[512,2048]{1,0:T(8,128)(2,1)} %copy-done.28, bf16[512,3072]{1,0:T(8,128)(2,1)} %get-tuple-element.227.right_own, ...), custom_call_target="tpu_custom_call" | custom-call | flops 12884901888 | bytes 25165824 | tf_op jit(solution)/shard_map/weight_grad/pallas_call | solution.py:441
  239.9 22.2 %weight_grad.7 = (bf16[512,3072]{1,0:T(8,128)(2,1)}, bf16[512,3072]{1,0:T(8,128)(2,1)}) custom-call(bf16[512,2048]{1,0:T(8,128)(2,1)} %get-tuple-element.152.own_a.own_b, bf16[512,2048]{1,0:T(8,128)(2,1)} %get-tuple-element.152.own_a.own_b, bf16[512,2048]{1,0:T(8,128)(2,1)} %get-tuple-element.146.oth_a.oth_b, ...), custom_call_target="tpu_custom_call" | custom-call | flops 7730940928 | bytes 15099494 | tf_op jit(solution)/shard_map/weight_grad/pallas_call | solution.py:441
  263.7 21.6 %weight_grad.8 = (bf16[512,3072]{1,0:T(8,128)(2,1)}, bf16[512,3072]{1,0:T(8,128)(2,1)}) custom-call(bf16[512,2048]{1,0:T(8,128)(2,1)} %get-tuple-element.152.own_a.own_b, bf16[512,2048]{1,0:T(8,128)(2,1)} %get-tuple-element.152.own_a.own_b, bf16[512,2048]{1,0:T(8,128)(2,1)} %get-tuple-element.146.oth_a.oth_b, ...), custom_call_target="tpu_custom_call" | custom-call | flops 7730940928 | bytes 15099494 | tf_op jit(solution)/shard_map/weight_grad/pallas_call | solution.py:441
  287.8 18.4 %two_back.5.back = bf16[512,2048]{1,0:T(8,128)(2,1)} custom-call(bf16[512,3072]{1,0:T(8,128)(2,1)S(1)} %copy-done.18, bf16[2048,3072]{1,0:T(8,128)(2,1)} %first_w.5, bf16[512,3072]{1,0:T(8,128)(2,1)} %get-tuple-element.153.right_oth.second, bf16[2048,3072]{1,0:T(8,128)(2,1)} %second_w.5), custom_call_target="tpu_custom_call" | custom-call | flops 7730940928 | bytes 18874368 | tf_op jit(solution)/shard_map/two_back/pallas_call | solution.py:582
  307.7 14.1 %pull.2 = (f32[512,2048]{1,0:T(8,128)}, bf16[512,2048]{1,0:T(8,128)(2,1)}, f32[512,1280]{1,0:T(8,128)}) custom-call(f32[512,2048]{1,0:T(8,128)} %get-tuple-element.151.middle, bf16[512,2048]{1,0:T(8,128)(2,1)} %two_back.5.back, bf16[512,2048]{1,0:T(8,128)(2,1)} %collective-permute-done.7.other, bf16[512,2048]{1,0:T(8,128)(2,1)} %collective-permute-done.3.second.cot, ...), custom_call_target="tpu_custom_call" | custom-call | flops 16106127360 | bytes 116391936 | tf_op jit(solution)/shard_map/pull/pallas_call | solution.py:551
  321.8 3.9 halve.12
  326.2 7.2 %collective-permute-done.5.received_low.received_high = bf16[512,3072]{1,0:T(8,128)(2,1)} collective-permute-done((bf16[512,3072]{1,0:T(8,128)(2,1)}, bf16[512,3072]{1,0:T(8,128)(2,1)}, u32[]{:S(2)}, u32[]{:S(2)}) %collective-permute-start.5) | collective-permute-done | bytes 3145760 | tf_op jit(solution)/shard_map/ppermute | solution.py:602
  335.3 3.9 halve.13
  339.6 14.7 %collective-permute-done.9.other = bf16[512,2048]{1,0:T(8,128)(2,1)} collective-permute-done((bf16[512,2048]{1,0:T(8,128)(2,1)}, bf16[512,2048]{1,0:T(8,128)(2,1)}, u32[]{:S(2)}, u32[]{:S(2)}) %collective-permute-start.9) | collective-permute-done | bytes 2097184 | tf_op jit(solution)/shard_map/ppermute | solution.py:597
  354.3 13.7 %pull.3 = (f32[512,2048]{1,0:T(8,128)}, bf16[512,2048]{1,0:T(8,128)(2,1)}, f32[512,1280]{1,0:T(8,128)}) custom-call(f32[512,2048]{1,0:T(8,128)} %get-tuple-element.135.middle, bf16[512,2048]{1,0:T(8,128)(2,1)} %two_back.4.back, bf16[512,2048]{1,0:T(8,128)(2,1)} %collective-permute-done.9.other, bf16[512,2048]{1,0:T(8,128)(2,1)} %bitcast.60, ...), custom_call_target="tpu_custom_call" | custom-call | flops 2684354560 | bytes 19398656 | tf_op jit(solution)/shard_map/pull/pallas_call | solution.py:551
  368.0 10.8 %weight_grad.9 = (bf16[512,1280]{1,0:T(8,128)(2,1)}, bf16[512,1280]{1,0:T(8,128)(2,1)}) custom-call(bf16[512,2048]{1,0:T(8,128)(2,1)} %get-tuple-element.172.own_a.own_b, bf16[512,2048]{1,0:T(8,128)(2,1)} %get-tuple-element.172.own_a.own_b, bf16[512,2048]{1,0:T(8,128)(2,1)} %get-tuple-element.173.oth_a.oth_b, ...), custom_call_target="tpu_custom_call" | custom-call | flops 5368709120 | bytes 10485760 | tf_op jit(solution)/shard_map/weight_grad/pallas_call | solution.py:441
  381.8 2.9 halve.14
  384.6 2.6 collective-permute-start.15
  390.0 33.9 %rec_bwd.1 = (bf16[512,1280]{1,0:T(8,128)(2,1)S(1)}, bf16[512,1280]{1,0:T(8,128)(2,1)}, bf16[512,1280]{1,0:T(8,128)(2,1)}, bf16[512,1280]{1,0:T(8,128)(2,1)}, bf...) custom-call(bf16[512,1280]{1,0:T(8,128)(2,1)} %convolution_convert_fusion.5.bx_own, bf16[512,1280]{1,0:T(8,128)(2,1)} %copy-done.24, ...), custom_call_target="tpu_custom_call" | custom-call | flops 2880962560 | bytes 44564480 | tf_op jit(solution)/shard_map/rec_bwd/pallas_call | solution.py:296
  425.7 2.9 halve.16
  430.4 12.5 %weight_grad.10 = (bf16[704,1280]{1,0:T(8,128)(2,1)}, bf16[704,1280]{1,0:T(8,128)(2,1)}) custom-call(bf16[512,2048]{1,0:T(8,128)(2,1)} %copy-done.25, bf16[512,2048]{1,0:T(8,128)(2,1)} %copy-done.25, bf16[512,2048]{1,0:T(8,128)(2,1)} %copy-done.26, bf16[512,2048]{1,0:T(8,128)(2,1)} %copy-done.26, bf16[512,1280]{1,0:T(8,128)(2,1)} %copy-done.29, ...), custom_call_target="tpu_custom_call" | custom-call | flops 5368709120 | bytes 10485760 | tf_op jit(solution)/shard_map/weight_grad/pallas_call | solution.py:441
  443.5 2.7 add_bitcast_fusion
  450.3 3.0 copy.61
  456.0 9.3 %two_back.6 = bf16[512,2048]{1,0:T(8,128)(2,1)} custom-call(bf16[512,1280]{1,0:T(8,128)(2,1)S(1)} %copy-done.33, bf16[2048,1280]{1,0:T(8,128)(2,1)} %first_w.7, bf16[512,1280]{1,0:T(8,128)(2,1)S(1)} %copy-done.32, bf16[2048,1280]{1,0:T(8,128)(2,1)} %second_w.7), custom_call_target="tpu_custom_call" | custom-call | flops 5368709120 | bytes 13107200 | tf_op jit(solution)/shard_map/two_back/pallas_call | solution.py:582
  468.2 2.6 collective-permute-start.23
  470.8 2.8 multiply_reduce_fusion.1
  473.6 10.9 %weight_grad.11 = (bf16[512,1280]{1,0:T(8,128)(2,1)}, bf16[512,1280]{1,0:T(8,128)(2,1)}) custom-call(bf16[512,2048]{1,0:T(8,128)(2,1)} %copy-done.25, bf16[512,2048]{1,0:T(8,128)(2,1)} %copy-done.25, bf16[512,2048]{1,0:T(8,128)(2,1)} %copy-done.26, bf16[512,2048]{1,0:T(8,128)(2,1)} %copy-done.26, bf16[512,1280]{1,0:T(8,128)(2,1)} %get-tuple-element.202.right_own.second, ...), custom_call_target="tpu_custom_call" | custom-call | flops 5368709120 | bytes 10485760 | tf_op jit(solution)/shard_map/weight_grad/pallas_call | solution.py:441
  490.6 10.6 %convolution_convert_fusion.1 = bf16[512,2048]{1,0:T(8,128)(2,1)} fusion(bf16[512,3072]{1,0:T(8,128)(2,1)S(1)} %copy-done.62, bf16[3072,2048]{1,0:T(8,128)(2,1)} %param.28), kind=kOutput, calls=%fused_computation.20 | convolution fusion | flops 6443499520 | bytes 17825792 | tf_op jit(solution)/shard_map/dot_general | solution.py:882
  501.2 8.6 %two_back.7 = bf16[512,2048]{1,0:T(8,128)(2,1)S(1)} custom-call(bf16[512,1280]{1,0:T(8,128)(2,1)S(1)} %copy-done.30, bf16[2048,1280]{1,0:T(8,128)(2,1)} %first_w.7, bf16[512,1280]{1,0:T(8,128)(2,1)S(1)} %copy-done.31, bf16[2048,1280]{1,0:T(8,128)(2,1)} %second_w.7), custom_call_target="tpu_custom_call" | custom-call | flops 5368709120 | bytes 13107200 | tf_op jit(solution)/shard_map/two_back/pallas_call | solution.py:582
  509.8 2.8 collective-permute-done.19
  514.1 2.6 fusion.6
  516.8 5.0 fusion.8
  523.5 2.9 multiply_reduce_fusion
  529.5 3.1 collective-permute-done.21.received_low.received_high
  535.7 17.8 %collective-permute-done.20.received_low.received_high = bf16[256,1280]{1,0:T(8,128)(2,1)S(1)} collective-permute-done((bf16[256,1280]{1,0:T(8,128)(2,1)}, bf16[256,1280]{1,0:T(8,128)(2,1)S(1)}, u32[]{:S(2)}, u32[]{:S(2)}) %collective-permute-start.20) | collective-permute-done | bytes 655392 | tf_op jit(solution)/shard_map/ppermute | solution.py:602
  555.4 9.9 %convolution_convert_fusion = bf16[512,2048]{1,0:T(8,128)(2,1)S(1)} fusion(bf16[512,3072]{1,0:T(8,128)(2,1)S(1)} %copy-done.61, bf16[3072,2048]{1,0:T(8,128)(2,1)} %param.28), kind=kOutput, calls=%fused_computation.19 | convolution fusion | flops 6443499520 | bytes 17825792 | tf_op jit(solution)/shard_map/dot_general | solution.py:882
  565.3 4.1 add_convert_fusion
  (260 shorter events, 82.9 us)
Async XLA Ops:
  0.6 33.5 %copy-start = (bf16[2,10,256,256]{3,2,1,0:T(8,128)(2,1)S(1)}, bf16[2,10,256,256]{3,2,1,0:T(8,128)(2,1)}, u32[]{:S(2)}) copy-start(bf16[2,10,256,256]{3,2,1,0:T(8,128)(2,1)} %param.24) | copy-start | bytes 7864324
  0.7 34.7 %collective-permute-start.1 = (s32[512]{0:T(512)}, s32[512]{0:T(512)S(1)}, u32[]{:S(2)}, u32[]{:S(2)}) collective-permute-start(s32[512]{0:T(512)} %bitcast.83), channel_id=1, source_target_pairs={{0,1},{1,0},{2,3},{3,2},{4,5},{5,4},{6,7},{7,6},{8,9},{9,8},{10,11... | collective-permute-start | bytes 6152 | tf_op jit(solution)/shard_map/ppermute | solution.py:597
  3.7 48.9 %collective-permute-start = (bf16[512,2048]{1,0:T(8,128)(2,1)}, bf16[512,2048]{1,0:T(8,128)(2,1)}, u32[]{:S(2)}, u32[]{:S(2)}) collective-permute-start(bf16[512,2048]{1,0:T(8,128)(2,1)} %bitcast.63), channel_id=1, source_target_pairs={{0,1},{1,0},{2,3},{3,2},{4,5},{5,4},{6,7},{7,6},{8,9},{9,8},{10,11... | collective-permute-start | bytes 6291464 | tf_op jit(solution)/shard_map/ppermute | solution.py:597
  3.8 96.5 %collective-permute-start.3 = (bf16[512,2048]{1,0:T(8,128)(2,1)}, bf16[512,2048]{1,0:T(8,128)(2,1)}, u32[]{:S(2)}, u32[]{:S(2)}) collective-permute-start(bf16[512,2048]{1,0:T(8,128)(2,1)} %bitcast.59), channel_id=1, source_target_pairs={{0,1},{1,0},{2,3},{3,2},{4,5},{5,4},{6,7},{7,6},{8,9},{9,8},{10,11... | collective-permute-start | bytes 6291464 | tf_op jit(solution)/shard_map/ppermute | solution.py:597
  9.2 45.4 %copy-start.47 = (f32[1,2048]{1,0:T(1,128)}, f32[1,2048]{1,0:T(1,128)S(1)}, u32[]{:S(2)}) copy-start(f32[1,2048]{1,0:T(1,128)S(1)} %get-tuple-element.313) | copy-start | bytes 24580
  22.0 11.9 %copy-start.51 = (f32[2560]{0:T(1024)S(1)}, f32[2560]{0:T(1024)}, u32[]{:S(2)}) copy-start(f32[2560]{0:T(1024)} %param.23) | copy-start | bytes 30724
  22.0 11.9 %copy-start.49 = (f32[4,2560]{1,0:T(4,128)S(1)}, f32[4,2560]{1,0:T(4,128)}, u32[]{:S(2)}) copy-start(f32[4,2560]{1,0:T(4,128)} %param.21) | copy-start | bytes 122884
  22.0 12.0 %copy-start.50 = (f32[3,2560]{1,0:T(4,128)S(1)}, f32[3,2560]{1,0:T(4,128)}, u32[]{:S(2)}) copy-start(f32[3,2560]{1,0:T(4,128)} %param.22) | copy-start | bytes 92164
  57.0 33.8 %slice-start = ((s8[5242880]{0:T(1024)(128)(4,1)}), s8[4194304]{0:T(1024)(128)(4,1)S(1)}, s32[]{:S(2)}) async-start(s8[5242880]{0:T(1024)(128)(4,1)} %bitcast.65), calls=%async_computation | async-start | bytes 8388608
  64.0 26.8 %slice-start.1 = ((s8[5242880]{0:T(1024)(128)(4,1)}), s8[1048576]{0:T(1024)(128)(4,1)S(1)}, s32[]{:S(2)}) async-start(s8[5242880]{0:T(1024)(128)(4,1)} %bitcast.65), calls=%async_computation.1 | async-start | bytes 2097152
  66.9 23.9 %copy-start.24 = (bf16[512,1280]{1,0:T(8,128)(2,1)}, bf16[512,1280]{1,0:T(8,128)(2,1)S(1)}, u32[]{:S(2)}) copy-start(bf16[512,1280]{1,0:T(8,128)(2,1)S(1)} %convolution_convert_fusion.4.bx_oth) | copy-start | bytes 3932164
  67.4 23.3 %copy-start.10 = (f32[3,67,16,128]{3,2,1,0:T(8,128)}, f32[3,67,16,128]{3,2,1,0:T(8,128)S(1)}, u32[]{:S(2)}) copy-start(f32[3,67,16,128]{3,2,1,0:T(8,128)S(1)} %broadcast_in_dim.11.mask_ref) | copy-start | bytes 4939780
  94.0 48.7 %collective-permute-start.2 = (bf16[512,2048]{1,0:T(8,128)(2,1)S(1)}, bf16[512,2048]{1,0:T(8,128)(2,1)}, u32[]{:S(2)}, u32[]{:S(2)}) collective-permute-start(bf16[512,2048]{1,0:T(8,128)(2,1)S(1)} %convolution_convert_fusion.3.part), channel_id=1, source_target_pairs={{0,1},{1,0},{2,3},{3,2},{4,5},{5,4},{6,7},{7,6},{8,9},{9,8},{10,11... | collective-permute-start | bytes 6291464 | tf_op jit(solution)/shard_map/ppermute | solution.py:597
  98.3 14.0 %copy-start.6 = (bf16[1,512,2048]{2,1,0:T(8,128)(2,1)S(1)}, bf16[1,512,2048]{2,1,0:T(8,128)(2,1)}, u32[]{:S(2)}) copy-start(bf16[1,512,2048]{2,1,0:T(8,128)(2,1)} %param.16) | copy-start | bytes 6291460
  98.3 90.6 %collective-permute-start.4 = (bf16[512,2048]{1,0:T(8,128)(2,1)}, bf16[512,2048]{1,0:T(8,128)(2,1)S(1)}, u32[]{:S(2)}, u32[]{:S(2)}) collective-permute-start(bf16[512,2048]{1,0:T(8,128)(2,1)} %convolution_convert_fusion.2.part), channel_id=1, source_target_pairs={{0,1},{1,0},{2,3},{3,2},{4,5},{5,4},{6,7},{7,6},{8,9},{9,8},{10,11... | collective-permute-start | bytes 6291464 | tf_op jit(solution)/shard_map/ppermute | solution.py:597
  115.2 27.5 %copy-start.28 = (bf16[512,2048]{1,0:T(8,128)(2,1)}, bf16[512,2048]{1,0:T(8,128)(2,1)S(1)}, u32[]{:S(2)}) copy-start(bf16[512,2048]{1,0:T(8,128)(2,1)S(1)} %get-tuple-element.143.oth_a.oth_b) | copy-start | bytes 6291460
  188.9 118.8 %collective-permute-start.7 = (bf16[512,2048]{1,0:T(8,128)(2,1)}, bf16[512,2048]{1,0:T(8,128)(2,1)}, u32[]{:S(2)}, u32[]{:S(2)}) collective-permute-start(bf16[512,2048]{1,0:T(8,128)(2,1)} %two_back.4.back), channel_id=1, source_target_pairs={{0,1},{1,0},{2,3},{3,2},{4,5},{5,4},{6,7},{7,6},{8,9},{9,8},{10,11... | collective-permute-start | bytes 6291464 | tf_op jit(solution)/shard_map/ppermute | solution.py:597
  237.7 84.1 %collective-permute-start.6 = (bf16[512,3072]{1,0:T(8,128)(2,1)}, bf16[512,3072]{1,0:T(8,128)(2,1)}, u32[]{:S(2)}, u32[]{:S(2)}) collective-permute-start(bf16[512,3072]{1,0:T(8,128)(2,1)} %get-tuple-element.150), channel_id=1, source_target_pairs={{0,4},{2,6},{4,0},{6,2},{8,12},{10,14},{12,8},{14,10},{16,20},{18,... | collective-permute-start | bytes 9437192 | tf_op jit(solution)/shard_map/ppermute | solution.py:602
  262.1 71.3 %collective-permute-start.5 = (bf16[512,3072]{1,0:T(8,128)(2,1)}, bf16[512,3072]{1,0:T(8,128)(2,1)}, u32[]{:S(2)}, u32[]{:S(2)}) collective-permute-start(bf16[512,3072]{1,0:T(8,128)(2,1)} %get-tuple-element.149), channel_id=1, source_target_pairs={{0,8},{2,10},{4,12},{6,14},{8,0},{10,2},{12,4},{14,6},{16,24},{18,... | collective-permute-start | bytes 9437192 | tf_op jit(solution)/shard_map/ppermute | solution.py:602
  285.3 101.9 %collective-permute-start.10 = (bf16[512,3072]{1,0:T(8,128)(2,1)}, bf16[512,3072]{1,0:T(8,128)(2,1)S(1)}, u32[]{:S(2)}, u32[]{:S(2)}) collective-permute-start(bf16[512,3072]{1,0:T(8,128)(2,1)} %get-tuple-element.169), channel_id=1, source_target_pairs={{0,4},{2,6},{4,0},{6,2},{8,12},{10,14},{12,8},{14,10},{16,20},{18,... | collective-permute-start | bytes 9437192 | tf_op jit(solution)/shard_map/ppermute | solution.py:602
  306.2 48.1 %collective-permute-start.9 = (bf16[512,2048]{1,0:T(8,128)(2,1)}, bf16[512,2048]{1,0:T(8,128)(2,1)}, u32[]{:S(2)}, u32[]{:S(2)}) collective-permute-start(bf16[512,2048]{1,0:T(8,128)(2,1)} %two_back.5.back), channel_id=1, source_target_pairs={{0,1},{1,0},{2,3},{3,2},{4,5},{5,4},{6,7},{7,6},{8,9},{9,8},{10,11... | collective-permute-start | bytes 6291464 | tf_op jit(solution)/shard_map/ppermute | solution.py:597
  307.7 14.1 %copy-start.4 = (bf16[512,3072]{1,0:T(8,128)(2,1)S(1)}, bf16[512,3072]{1,0:T(8,128)(2,1)}, u32[]{:S(2)}) copy-start(bf16[512,3072]{1,0:T(8,128)(2,1)} %get-tuple-element.144.keep_low.keep_high) | copy-start | bytes 9437188
  325.7 54.6 %collective-permute-start.11 = (bf16[256,3072]{1,0:T(8,128)(2,1)}, bf16[256,3072]{1,0:T(8,128)(2,1)}, u32[]{:S(2)}, u32[]{:S(2)}) collective-permute-start(bf16[256,3072]{1,0:T(8,128)(2,1)} %get-tuple-element.159), channel_id=1, source_target_pairs={{0,8},{2,10},{4,12},{6,14},{8,0},{10,2},{12,4},{14,6},{16,24},{18,... | collective-permute-start | bytes 4718600 | tf_op jit(solution)/shard_map/ppermute | solution.py:602
  339.2 86.5 %collective-permute-start.8 = (bf16[256,3072]{1,0:T(8,128)(2,1)}, bf16[256,3072]{1,0:T(8,128)(2,1)}, u32[]{:S(2)}, u32[]{:S(2)}) collective-permute-start(bf16[256,3072]{1,0:T(8,128)(2,1)} %get-tuple-element.162), channel_id=1, source_target_pairs={{0,4},{2,6},{4,0},{6,2},{8,12},{10,14},{12,8},{14,10},{16,20},{18,... | collective-permute-start | bytes 4718600 | tf_op jit(solution)/shard_map/ppermute | solution.py:602
  378.8 67.4 %collective-permute-start.14 = (bf16[512,1280]{1,0:T(8,128)(2,1)}, bf16[512,1280]{1,0:T(8,128)(2,1)}, u32[]{:S(2)}, u32[]{:S(2)}) collective-permute-start(bf16[512,1280]{1,0:T(8,128)(2,1)} %get-tuple-element.186), channel_id=1, source_target_pairs={{0,4},{2,6},{4,0},{6,2},{8,12},{10,14},{12,8},{14,10},{16,20},{18,... | collective-permute-start | bytes 3932168 | tf_op jit(solution)/shard_map/ppermute | solution.py:602
  384.6 58.8 %collective-permute-start.15 = (bf16[128,3072]{1,0:T(8,128)(2,1)}, bf16[128,3072]{1,0:T(8,128)(2,1)}, u32[]{:S(2)}, u32[]{:S(2)}) collective-permute-start(bf16[128,3072]{1,0:T(8,128)(2,1)} %get-tuple-element.176), channel_id=1, source_target_pairs={{0,16},{2,18},{4,20},{6,22},{8,24},{10,26},{12,28},{14,30},{16,0},... | collective-permute-start | bytes 2359304 | tf_op jit(solution)/shard_map/ppermute | solution.py:602
  389.5 77.3 %collective-permute-start.13 = (bf16[256,3072]{1,0:T(8,128)(2,1)}, bf16[256,3072]{1,0:T(8,128)(2,1)S(1)}, u32[]{:S(2)}, u32[]{:S(2)}) collective-permute-start(bf16[256,3072]{1,0:T(8,128)(2,1)} %get-tuple-element.178), channel_id=1, source_target_pairs={{0,8},{2,10},{4,12},{6,14},{8,0},{10,2},{12,4},{14,6},{16,24},{18,... | collective-permute-start | bytes 4718600 | tf_op jit(solution)/shard_map/ppermute | solution.py:602
  390.0 35.7 %copy-start.12 = (bf16[256,3072]{1,0:T(8,128)(2,1)S(1)}, bf16[256,3072]{1,0:T(8,128)(2,1)}, u32[]{:S(2)}) copy-start(bf16[256,3072]{1,0:T(8,128)(2,1)} %get-tuple-element.161.keep_low.keep_high) | copy-start | bytes 4718596
  428.7 42.1 %collective-permute-start.12 = (bf16[128,3072]{1,0:T(8,128)(2,1)}, bf16[128,3072]{1,0:T(8,128)(2,1)}, u32[]{:S(2)}, u32[]{:S(2)}) collective-permute-start(bf16[128,3072]{1,0:T(8,128)(2,1)} %get-tuple-element.183), channel_id=1, source_target_pairs={{0,16},{2,18},{4,20},{6,22},{8,24},{10,26},{12,28},{14,30},{16,0},... | collective-permute-start | bytes 2359304 | tf_op jit(solution)/shard_map/ppermute | solution.py:602
  443.0 45.4 %collective-permute-start.17 = (bf16[704,1280]{1,0:T(8,128)(2,1)}, bf16[704,1280]{1,0:T(8,128)(2,1)S(1)}, u32[]{:S(2)}, u32[]{:S(2)}) collective-permute-start(bf16[704,1280]{1,0:T(8,128)(2,1)} %get-tuple-element.206), channel_id=1, source_target_pairs={{0,4},{2,6},{4,0},{6,2},{8,12},{10,14},{12,8},{14,10},{16,20},{18,... | collective-permute-start | bytes 5406728 | tf_op jit(solution)/shard_map/ppermute | solution.py:602
  448.6 35.9 %collective-permute-start.18 = (bf16[256,1280]{1,0:T(8,128)(2,1)}, bf16[256,1280]{1,0:T(8,128)(2,1)}, u32[]{:S(2)}, u32[]{:S(2)}) collective-permute-start(bf16[256,1280]{1,0:T(8,128)(2,1)} %get-tuple-element.195), channel_id=1, source_target_pairs={{0,8},{2,10},{4,12},{6,14},{8,0},{10,2},{12,4},{14,6},{16,24},{18,... | collective-permute-start | bytes 1966088 | tf_op jit(solution)/shard_map/ppermute | solution.py:602
  465.3 47.3 %collective-permute-start.19 = (bf16[512,2048]{1,0:T(8,128)(2,1)}, bf16[512,2048]{1,0:T(8,128)(2,1)}, u32[]{:S(2)}, u32[]{:S(2)}) collective-permute-start(bf16[512,2048]{1,0:T(8,128)(2,1)} %two_back.6), channel_id=1, source_target_pairs={{0,1},{1,0},{2,3},{3,2},{4,5},{5,4},{6,7},{7,6},{8,9},{9,8},{10,11... | collective-permute-start | bytes 6291464 | tf_op jit(solution)/shard_map/ppermute | solution.py:597
  468.2 55.3 %collective-permute-start.23 = (bf16[128,3072]{1,0:T(8,128)(2,1)}, bf16[128,3072]{1,0:T(8,128)(2,1)}, u32[]{:S(2)}, u32[]{:S(2)}) collective-permute-start(bf16[128,3072]{1,0:T(8,128)(2,1)} %get-tuple-element.199), channel_id=1, source_target_pairs={{0,16},{2,18},{4,20},{6,22},{8,24},{10,26},{12,28},{14,30},{16,0},... | collective-permute-start | bytes 2359304 | tf_op jit(solution)/shard_map/ppermute | solution.py:602
  473.6 12.4 %copy-start.21 = (bf16[256,1280]{1,0:T(8,128)(2,1)S(1)}, bf16[256,1280]{1,0:T(8,128)(2,1)}, u32[]{:S(2)}) copy-start(bf16[256,1280]{1,0:T(8,128)(2,1)} %get-tuple-element.207.keep_low.keep_high) | copy-start | bytes 1966084
  484.5 37.2 %collective-permute-start.16 = (bf16[512,1280]{1,0:T(8,128)(2,1)}, bf16[512,1280]{1,0:T(8,128)(2,1)S(1)}, u32[]{:S(2)}, u32[]{:S(2)}) collective-permute-start(bf16[512,1280]{1,0:T(8,128)(2,1)} %get-tuple-element.204), channel_id=1, source_target_pairs={{0,4},{2,6},{4,0},{6,2},{8,12},{10,14},{12,8},{14,10},{16,20},{18,... | collective-permute-start | bytes 3932168 | tf_op jit(solution)/shard_map/ppermute | solution.py:602
  488.0 38.4 %collective-permute-start.22 = (bf16[128,1280]{1,0:T(8,128)(2,1)}, bf16[128,1280]{1,0:T(8,128)(2,1)S(1)}, u32[]{:S(2)}, u32[]{:S(2)}) collective-permute-start(bf16[128,1280]{1,0:T(8,128)(2,1)} %get-tuple-element.209), channel_id=1, source_target_pairs={{0,16},{2,18},{4,20},{6,22},{8,24},{10,26},{12,28},{14,30},{16,0},... | collective-permute-start | bytes 983048 | tf_op jit(solution)/shard_map/ppermute | solution.py:602
  489.8 42.8 %collective-permute-start.21 = (bf16[352,1280]{1,0:T(8,128)(2,1)}, bf16[352,1280]{1,0:T(8,128)(2,1)S(1)}, u32[]{:S(2)}, u32[]{:S(2)}) collective-permute-start(bf16[352,1280]{1,0:T(8,128)(2,1)} %get-tuple-element.211), channel_id=1, source_target_pairs={{0,8},{2,10},{4,12},{6,14},{8,0},{10,2},{12,4},{14,6},{16,24},{18,... | collective-permute-start | bytes 2703368 | tf_op jit(solution)/shard_map/ppermute | solution.py:602
  501.2 12.9 %copy-start.38 = (bf16[1,512,2048]{2,1,0:T(8,128)(2,1)S(1)}, bf16[1,512,2048]{2,1,0:T(8,128)(2,1)}, u32[]{:S(2)}) copy-start(bf16[1,512,2048]{2,1,0:T(8,128)(2,1)} %param.15) | copy-start | bytes 6291460
  501.2 12.9 %copy-start.48 = (f32[1,2048]{1,0:T(1,128)S(1)}, f32[1,2048]{1,0:T(1,128)}, u32[]{:S(2)}) copy-start(f32[1,2048]{1,0:T(1,128)} %copy-done.47) | copy-start | bytes 24580
  512.6 52.6 %collective-permute-start.24 = (bf16[512,2048]{1,0:T(8,128)(2,1)}, bf16[512,2048]{1,0:T(8,128)(2,1)}, u32[]{:S(2)}, u32[]{:S(2)}) collective-permute-start(bf16[512,2048]{1,0:T(8,128)(2,1)} %convolution_convert_fusion.1), channel_id=1, source_target_pairs={{0,1},{1,0},{2,3},{3,2},{4,5},{5,4},{6,7},{7,6},{8,9},{9,8},{10,11... | collective-permute-start | bytes 6291464 | tf_op jit(solution)/shard_map/ppermute | solution.py:597
  523.0 30.5 %collective-permute-start.20 = (bf16[256,1280]{1,0:T(8,128)(2,1)}, bf16[256,1280]{1,0:T(8,128)(2,1)S(1)}, u32[]{:S(2)}, u32[]{:S(2)}) collective-permute-start(bf16[256,1280]{1,0:T(8,128)(2,1)} %get-tuple-element.217), channel_id=1, source_target_pairs={{0,8},{2,10},{4,12},{6,14},{8,0},{10,2},{12,4},{14,6},{16,24},{18,... | collective-permute-start | bytes 1966088 | tf_op jit(solution)/shard_map/ppermute | solution.py:602
  527.3 26.2 %copy-start.22 = (bf16[256,1280]{1,0:T(8,128)(2,1)S(1)}, bf16[256,1280]{1,0:T(8,128)(2,1)}, u32[]{:S(2)}) copy-start(bf16[256,1280]{1,0:T(8,128)(2,1)} %get-tuple-element.216.keep_low.keep_high) | copy-start | bytes 1966084
  532.6 22.7 %copy-start.61 = (bf16[512,3072]{1,0:T(8,128)(2,1)S(1)}, bf16[512,3072]{1,0:T(8,128)(2,1)}, u32[]{:S(2)}) copy-start(bf16[512,3072]{1,0:T(8,128)(2,1)} %get-tuple-element.227.right_own) | copy-start | bytes 9437188
  533.7 35.7 %collective-permute-start.25 = (bf16[176,1280]{1,0:T(8,128)(2,1)}, bf16[176,1280]{1,0:T(8,128)(2,1)S(1)}, u32[]{:S(2)}, u32[]{:S(2)}) collective-permute-start(bf16[176,1280]{1,0:T(8,128)(2,1)} %get-tuple-element.224), channel_id=1, source_target_pairs={{0,16},{2,18},{4,20},{6,22},{8,24},{10,26},{12,28},{14,30},{16,0},... | collective-permute-start | bytes 1351688 | tf_op jit(solution)/shard_map/ppermute | solution.py:602
  554.5 20.3 %collective-permute-start.26 = (bf16[128,1280]{1,0:T(8,128)(2,1)}, bf16[128,1280]{1,0:T(8,128)(2,1)}, u32[]{:S(2)}, u32[]{:S(2)}) collective-permute-start(bf16[128,1280]{1,0:T(8,128)(2,1)} %get-tuple-element.226), channel_id=1, source_target_pairs={{0,16},{2,18},{4,20},{6,22},{8,24},{10,26},{12,28},{14,30},{16,0},... | collective-permute-start | bytes 983048 | tf_op jit(solution)/shard_map/ppermute | solution.py:602
  569.5 4.9 collective-permute-start.27
  570.1 11.6 %copy-start.1 = (bf16[2,10,256,256]{3,2,1,0:T(8,128)(2,1)S(1)}, bf16[2,10,256,256]{3,2,1,0:T(8,128)(2,1)}, u32[]{:S(2)}) copy-start(bf16[2,10,256,256]{3,2,1,0:T(8,128)(2,1)} %param.24) | copy-start | bytes 7864324
  577.5 3.6 collective-permute-start.28
  (50 other events, 224.2 us)

commit v7 on v6

--- a/solution.py
+++ b/solution.py
@@ -746,7 +746,7 @@
         order = [block_at(spot, stage_bits(count, "X" in CROSSED)) for spot in range(count)]
         chosen = jnp.bitwise_xor(jnp.array(order), me)[:, None] % (count // 2) == jnp.arange(count // 2)[None, :]
         sums = matmul(chosen.astype(BF16), sums.astype(BF16).reshape(count // 2, -1)).reshape(count, 8, each)
-        sums = jnp.pad(sums.astype(BF16), ((0, 0), (0, 8), (0, width - each)))
+        sums = jnp.pad(sums.astype(BF16), ((0, 0), (0, 0), (0, width - each)))
         at["extra"] = jnp.concatenate([gate_sums, sums], axis=1)
         return grads[0]
 
@@ -834,9 +834,9 @@
     down_grad, gate_grad, up_grad, out_grad, x_grad, y_grad = (grads[letter] for letter in "DGUOXY")
     x_grad = x_grad[:block]
     low, high = jnp.where(first_place, mine, others), jnp.where(first_place, others, mine)
-    both = jnp.stack([low[:-16], high[:-16]]).astype(F32).reshape(2, 2, -1, heads, gates.shape[-1])
+    both = jnp.stack([low[:-8], high[:-8]]).astype(F32).reshape(2, 2, -1, heads, gates.shape[-1])
     block_sums = jnp.transpose(both, (1, 0, 3, 2, 4)).reshape(2, 2 * heads, -1, gates.shape[-1])
-    small = jnp.where(me < count // 2, low[-16:-8], high[-16:-8])[:, :each].astype(F32)
+    small = jnp.where(me < count // 2, low[-8:], high[-8:])[:, :each].astype(F32)
 
     return (
         layer_out[None],

time: 588 us -> 587 us (level)
  no operation moved by 1% of the time
where the time goes in v7:
time: 587 us; the launch traced here: 582 us
  Pallas kernels  321 us (55%)
  waiting for transfers between devices  88.2 us (15%)
  matrix products  73.4 us (13%)
  other arithmetic  35.4 us (6%)
  starting transfers between devices  33.4 us (6%)
  local copies, waits for them, and re-layouts  27.9 us (5%)
    pallas_call x6, Pallas kernels, weight_grad(): pl.pallas_call(functools.partial(weight_grad_kernel, more), grid=(4,), in...  99.5 us
    ppermute x11, waiting for transfers between devices, swap(): return lax.ppermute(value, 'tp', [(0, 1), (1, 0)])  59.7 us
    pallas_call x4, Pallas kernels, two_back(): pl.pallas_call(two_back_kernel, grid=(cols // step,), in_specs=[left, rig...  54.9 us
    pallas_call x2, Pallas kernels, feed(): pl.pallas_call(functools.partial(feed_kernel, bits, sub), grid=(cols // w...  51.3 us
    dot_general x9, matrix products, matmul(): return jnp.dot(first_mat, second_mat, preferred_element_type=jnp.float32)  49.4 us
    pallas_call x1, Pallas kernels, rec_bwd(): pl.pallas_call(functools.partial(rec_bwd_kernel, count, stage_bits(count,...  33.9 us
    ppermute x18, waiting for transfers between devices, flip(): lax.ppermute(value, 'dp', [(source, source ^ bit) for source in range(cou...  28.6 us
    pallas_call x2, Pallas kernels, pull(): pl.pallas_call(functools.partial(pull_kernel, bits), grid=(cols // wide,)...  27.8 us
  transfers between devices with their start and end apart: 29, of which 9 were waited for; matrix products, arithmetic and copies ran while one was open for 20% of the time, Pallas kernels for 55%

profile of v7, /device:TPU:0, one launch (start us, length us, event | category | flops | bytes accessed | tf_op | source)
XLA Modules:
  0.0 581.8 jit_solution(7856251263538821932)
XLA Ops:
  0.7 3.0 collective-permute-start.1
  10.4 7.7 %fusion.38.by_own = f32[512,1280]{1,0:T(8,128)} fusion(bf16[512,2048]{1,0:T(8,128)(2,1)S(1)} %fusion.5.first, bf16[2048,1280]{1,0:T(8,128)(2,1)} %second_w.7), kind=kOutput, calls=%fused_computation.95 | convolution fusion | flops 2684354560 | bytes 9961472 | tf_op jit(solution)/shard_map/dot_general | solution.py:882
  18.1 4.0 convolution_convert_fusion.5.bx_own
  22.0 11.9 %fusion.39.grad_hidden = f32[512,3072]{1,0:T(8,128)} fusion(bf16[512,2048]{1,0:T(8,128)(2,1)S(1)} %bitcast.61, bf16[3072,2048]{1,0:T(8,128)(2,1)} %param.28), kind=kOutput, calls=%fused_computation.96 | convolution fusion | flops 6442450944 | bytes 20971520 | tf_op jit(solution)/shard_map/dot_general | solution.py:892
  36.2 16.4 %collective-permute-done.tokens = bf16[512,2048]{1,0:T(8,128)(2,1)} collective-permute-done((bf16[512,2048]{1,0:T(8,128)(2,1)}, bf16[512,2048]{1,0:T(8,128)(2,1)}, u32[]{:S(2)}, u32[]{:S(2)}) %collective-permute-start) | collective-permute-done | bytes 2097184 | tf_op jit(solution)/shard_map/ppermute | solution.py:597
  57.0 7.0 %fusion.40.by_oth = f32[512,1280]{1,0:T(8,128)} fusion(bf16[512,2048]{1,0:T(8,128)(2,1)S(1)} %fusion.2.second, bf16[2048,1280]{1,0:T(8,128)(2,1)} %second_w.7), kind=kOutput, calls=%fused_computation.97 | convolution fusion | flops 2684354560 | bytes 9961472 | tf_op jit(solution)/shard_map/dot_general | solution.py:882
  64.0 2.9 convolution_convert_fusion.4.bx_oth
  67.4 23.3 %rec_fwd.1 = (bf16[512,1280]{1,0:T(8,128)(2,1)S(1)}, bf16[512,1280]{1,0:T(8,128)(2,1)S(1)}, f32[64,16,1280]{2,1,0:T(8,128)}, f32[64,16,1280]{2,1,0:T(8,128)}, f3...) custom-call(bf16[512,1280]{1,0:T(8,128)(2,1)S(1)} %copy-done.23, ...), custom_call_target="tpu_custom_call" | custom-call | flops 1473249280 | bytes 34078720 | tf_op jit(solution)/shard_map/rec_fwd/pallas_call | solution.py:267
  90.8 3.1 convolution_convert_fusion.3.part
  94.1 4.2 convolution_convert_fusion.2.part
  100.3 12.1 %fusion.41.grad_hidden = f32[512,3072]{1,0:T(8,128)} fusion(bf16[512,2048]{1,0:T(8,128)(2,1)} %collective-permute-done.3.second.cot, bf16[3072,2048]{1,0:T(8,128)(2,1)} %param.28), kind=kOutput, calls=%fused_computation.98 | convolution fusion | flops 6442450944 | bytes 20971520 | tf_op jit(solution)/shard_map/dot_general | solution.py:892
  112.3 2.9 arrange.2
  119.4 23.3 %collective-permute-done.2.other = bf16[512,2048]{1,0:T(8,128)(2,1)} collective-permute-done((bf16[512,2048]{1,0:T(8,128)(2,1)S(1)}, bf16[512,2048]{1,0:T(8,128)(2,1)}, u32[]{:S(2)}, u32[]{:S(2)}) %collective-permute-start.2) | collective-permute-done | bytes 2097184 | tf_op jit(solution)/shard_map/ppermute | solution.py:597
  142.7 25.6 %feed.2 = (f32[512,2048]{1,0:T(8,128)}, bf16[512,2048]{1,0:T(8,128)(2,1)}, bf16[512,3072]{1,0:T(8,128)(2,1)}, bf16[512,3072]{1,0:T(8,128)(2,1)}, bf16[512,3072]{1,0:T(8,128)(2,1)}) custom-call(bf16[512,2048]{1,0:T(8,128)(2,1)} %bitcast.64, bf16[512,2048]{1,0:T(8,128)(2,1)} %convolution_convert_fusion.2.part, bf16[512,2048]{1,0:T(8,128)(2,1)} %collective-permute-done.2.other, ...), custom_call_target="tpu_custom_call" | custom-call | flops 12884901888 | bytes 44040192 | tf_op jit(solution)/shard_map/feed/pallas_call | solution.py:511
  170.2 18.6 %two_back.4.back = bf16[512,2048]{1,0:T(8,128)(2,1)} custom-call(bf16[512,3072]{1,0:T(8,128)(2,1)S(1)} %copy-done.36, bf16[2048,3072]{1,0:T(8,128)(2,1)} %first_w.5, bf16[512,3072]{1,0:T(8,128)(2,1)} %get-tuple-element.139.second.right_own, bf16[2048,3072]{1,0:T(8,128)(2,1)} %second_w.5), custom_call_target="tpu_custom_call" | custom-call | flops 12884901888 | bytes 31457280 | tf_op jit(solution)/shard_map/two_back/pallas_call | solution.py:582
  190.3 25.6 %feed.3 = (f32[512,2048]{1,0:T(8,128)}, bf16[512,2048]{1,0:T(8,128)(2,1)}, bf16[512,3072]{1,0:T(8,128)(2,1)}, bf16[512,3072]{1,0:T(8,128)(2,1)}, bf16[512,3072]{1,0:T(8,128)(2,1)}) custom-call(bf16[512,2048]{1,0:T(8,128)(2,1)} %collective-permute-done.tokens, bf16[512,2048]{1,0:T(8,128)(2,1)} %copy-done.58, bf16[512,2048]{1,0:T(8,128)(2,1)} %copy-done.59, ...), custom_call_target="tpu_custom_call" | custom-call | flops 12884901888 | bytes 44040192 | tf_op jit(solution)/shard_map/feed/pallas_call | solution.py:511
  215.9 21.8 %weight_grad.6 = (bf16[512,3072]{1,0:T(8,128)(2,1)}, bf16[512,3072]{1,0:T(8,128)(2,1)}) custom-call(bf16[512,2048]{1,0:T(8,128)(2,1)} %copy-done.27, bf16[512,2048]{1,0:T(8,128)(2,1)} %copy-done.27, bf16[512,2048]{1,0:T(8,128)(2,1)} %copy-done.28, bf16[512,2048]{1,0:T(8,128)(2,1)} %copy-done.28, bf16[512,3072]{1,0:T(8,128)(2,1)} %get-tuple-element.227.right_own, ...), custom_call_target="tpu_custom_call" | custom-call | flops 12884901888 | bytes 25165824 | tf_op jit(solution)/shard_map/weight_grad/pallas_call | solution.py:441
  239.9 22.2 %weight_grad.7 = (bf16[512,3072]{1,0:T(8,128)(2,1)}, bf16[512,3072]{1,0:T(8,128)(2,1)}) custom-call(bf16[512,2048]{1,0:T(8,128)(2,1)} %get-tuple-element.152.own_a.own_b, bf16[512,2048]{1,0:T(8,128)(2,1)} %get-tuple-element.152.own_a.own_b, bf16[512,2048]{1,0:T(8,128)(2,1)} %get-tuple-element.146.oth_a.oth_b, ...), custom_call_target="tpu_custom_call" | custom-call | flops 7730940928 | bytes 15099494 | tf_op jit(solution)/shard_map/weight_grad/pallas_call | solution.py:441
  263.7 21.6 %weight_grad.8 = (bf16[512,3072]{1,0:T(8,128)(2,1)}, bf16[512,3072]{1,0:T(8,128)(2,1)}) custom-call(bf16[512,2048]{1,0:T(8,128)(2,1)} %get-tuple-element.152.own_a.own_b, bf16[512,2048]{1,0:T(8,128)(2,1)} %get-tuple-element.152.own_a.own_b, bf16[512,2048]{1,0:T(8,128)(2,1)} %get-tuple-element.146.oth_a.oth_b, ...), custom_call_target="tpu_custom_call" | custom-call | flops 7730940928 | bytes 15099494 | tf_op jit(solution)/shard_map/weight_grad/pallas_call | solution.py:441
  287.8 18.4 %two_back.5.back = bf16[512,2048]{1,0:T(8,128)(2,1)} custom-call(bf16[512,3072]{1,0:T(8,128)(2,1)S(1)} %copy-done.18, bf16[2048,3072]{1,0:T(8,128)(2,1)} %first_w.5, bf16[512,3072]{1,0:T(8,128)(2,1)} %get-tuple-element.153.right_oth.second, bf16[2048,3072]{1,0:T(8,128)(2,1)} %second_w.5), custom_call_target="tpu_custom_call" | custom-call | flops 7730940928 | bytes 18874368 | tf_op jit(solution)/shard_map/two_back/pallas_call | solution.py:582
  307.7 14.1 %pull.2 = (f32[512,2048]{1,0:T(8,128)}, bf16[512,2048]{1,0:T(8,128)(2,1)}, f32[512,1280]{1,0:T(8,128)}) custom-call(f32[512,2048]{1,0:T(8,128)} %get-tuple-element.151.middle, bf16[512,2048]{1,0:T(8,128)(2,1)} %two_back.5.back, bf16[512,2048]{1,0:T(8,128)(2,1)} %collective-permute-done.7.other, bf16[512,2048]{1,0:T(8,128)(2,1)} %collective-permute-done.3.second.cot, ...), custom_call_target="tpu_custom_call" | custom-call | flops 16106127360 | bytes 116391936 | tf_op jit(solution)/shard_map/pull/pallas_call | solution.py:551
  321.8 3.9 halve.12
  326.2 7.2 %collective-permute-done.5.received_low.received_high = bf16[512,3072]{1,0:T(8,128)(2,1)} collective-permute-done((bf16[512,3072]{1,0:T(8,128)(2,1)}, bf16[512,3072]{1,0:T(8,128)(2,1)}, u32[]{:S(2)}, u32[]{:S(2)}) %collective-permute-start.5) | collective-permute-done | bytes 3145760 | tf_op jit(solution)/shard_map/ppermute | solution.py:602
  335.3 3.9 halve.13
  339.6 14.7 %collective-permute-done.9.other = bf16[512,2048]{1,0:T(8,128)(2,1)} collective-permute-done((bf16[512,2048]{1,0:T(8,128)(2,1)}, bf16[512,2048]{1,0:T(8,128)(2,1)}, u32[]{:S(2)}, u32[]{:S(2)}) %collective-permute-start.9) | collective-permute-done | bytes 2097184 | tf_op jit(solution)/shard_map/ppermute | solution.py:597
  354.3 13.7 %pull.3 = (f32[512,2048]{1,0:T(8,128)}, bf16[512,2048]{1,0:T(8,128)(2,1)}, f32[512,1280]{1,0:T(8,128)}) custom-call(f32[512,2048]{1,0:T(8,128)} %get-tuple-element.135.middle, bf16[512,2048]{1,0:T(8,128)(2,1)} %two_back.4.back, bf16[512,2048]{1,0:T(8,128)(2,1)} %collective-permute-done.9.other, bf16[512,2048]{1,0:T(8,128)(2,1)} %bitcast.60, ...), custom_call_target="tpu_custom_call" | custom-call | flops 2684354560 | bytes 19398656 | tf_op jit(solution)/shard_map/pull/pallas_call | solution.py:551
  368.0 10.8 %weight_grad.9 = (bf16[512,1280]{1,0:T(8,128)(2,1)}, bf16[512,1280]{1,0:T(8,128)(2,1)}) custom-call(bf16[512,2048]{1,0:T(8,128)(2,1)} %get-tuple-element.172.own_a.own_b, bf16[512,2048]{1,0:T(8,128)(2,1)} %get-tuple-element.172.own_a.own_b, bf16[512,2048]{1,0:T(8,128)(2,1)} %get-tuple-element.173.oth_a.oth_b, ...), custom_call_target="tpu_custom_call" | custom-call | flops 5368709120 | bytes 10485760 | tf_op jit(solution)/shard_map/weight_grad/pallas_call | solution.py:441
  381.8 2.9 halve.14
  384.6 2.6 collective-permute-start.15
  390.0 33.9 %rec_bwd.1 = (bf16[512,1280]{1,0:T(8,128)(2,1)S(1)}, bf16[512,1280]{1,0:T(8,128)(2,1)}, bf16[512,1280]{1,0:T(8,128)(2,1)}, bf16[512,1280]{1,0:T(8,128)(2,1)}, bf...) custom-call(bf16[512,1280]{1,0:T(8,128)(2,1)} %convolution_convert_fusion.5.bx_own, bf16[512,1280]{1,0:T(8,128)(2,1)} %copy-done.24, ...), custom_call_target="tpu_custom_call" | custom-call | flops 2880962560 | bytes 44564480 | tf_op jit(solution)/shard_map/rec_bwd/pallas_call | solution.py:296
  425.7 2.9 halve.16
  430.3 12.2 %weight_grad.10 = (bf16[672,1280]{1,0:T(8,128)(2,1)}, bf16[672,1280]{1,0:T(8,128)(2,1)}) custom-call(bf16[512,2048]{1,0:T(8,128)(2,1)} %copy-done.25, bf16[512,2048]{1,0:T(8,128)(2,1)} %copy-done.25, bf16[512,2048]{1,0:T(8,128)(2,1)} %copy-done.26, bf16[512,2048]{1,0:T(8,128)(2,1)} %copy-done.26, bf16[512,1280]{1,0:T(8,128)(2,1)} %copy-done.29, ...), custom_call_target="tpu_custom_call" | custom-call | flops 5368709120 | bytes 10485760 | tf_op jit(solution)/shard_map/weight_grad/pallas_call | solution.py:441
  443.0 2.7 add_bitcast_fusion
  445.7 2.5 halve.17
  449.9 3.0 copy.61
  455.5 9.3 %two_back.6 = bf16[512,2048]{1,0:T(8,128)(2,1)} custom-call(bf16[512,1280]{1,0:T(8,128)(2,1)S(1)} %copy-done.33, bf16[2048,1280]{1,0:T(8,128)(2,1)} %first_w.7, bf16[512,1280]{1,0:T(8,128)(2,1)S(1)} %copy-done.32, bf16[2048,1280]{1,0:T(8,128)(2,1)} %second_w.7), custom_call_target="tpu_custom_call" | custom-call | flops 5368709120 | bytes 13107200 | tf_op jit(solution)/shard_map/two_back/pallas_call | solution.py:582
  467.7 2.6 collective-permute-start.23
  470.4 2.8 multiply_reduce_fusion.1
  473.2 10.9 %weight_grad.11 = (bf16[512,1280]{1,0:T(8,128)(2,1)}, bf16[512,1280]{1,0:T(8,128)(2,1)}) custom-call(bf16[512,2048]{1,0:T(8,128)(2,1)} %copy-done.25, bf16[512,2048]{1,0:T(8,128)(2,1)} %copy-done.25, bf16[512,2048]{1,0:T(8,128)(2,1)} %copy-done.26, bf16[512,2048]{1,0:T(8,128)(2,1)} %copy-done.26, bf16[512,1280]{1,0:T(8,128)(2,1)} %get-tuple-element.202.right_own.second, ...), custom_call_target="tpu_custom_call" | custom-call | flops 5368709120 | bytes 10485760 | tf_op jit(solution)/shard_map/weight_grad/pallas_call | solution.py:441
  490.1 10.6 %convolution_convert_fusion.1 = bf16[512,2048]{1,0:T(8,128)(2,1)} fusion(bf16[512,3072]{1,0:T(8,128)(2,1)S(1)} %copy-done.62, bf16[3072,2048]{1,0:T(8,128)(2,1)} %param.28), kind=kOutput, calls=%fused_computation.20 | convolution fusion | flops 6443499520 | bytes 17825792 | tf_op jit(solution)/shard_map/dot_general | solution.py:882
  500.7 8.6 %two_back.7 = bf16[512,2048]{1,0:T(8,128)(2,1)S(1)} custom-call(bf16[512,1280]{1,0:T(8,128)(2,1)S(1)} %copy-done.30, bf16[2048,1280]{1,0:T(8,128)(2,1)} %first_w.7, bf16[512,1280]{1,0:T(8,128)(2,1)S(1)} %copy-done.31, bf16[2048,1280]{1,0:T(8,128)(2,1)} %second_w.7), custom_call_target="tpu_custom_call" | custom-call | flops 5368709120 | bytes 13107200 | tf_op jit(solution)/shard_map/two_back/pallas_call | solution.py:582
  509.4 2.8 collective-permute-done.19
  513.6 2.6 fusion.6
  516.3 5.0 fusion.8
  523.0 2.9 multiply_reduce_fusion
  534.4 19.1 %collective-permute-done.20.received_low.received_high = bf16[256,1280]{1,0:T(8,128)(2,1)S(1)} collective-permute-done((bf16[256,1280]{1,0:T(8,128)(2,1)}, bf16[256,1280]{1,0:T(8,128)(2,1)S(1)}, u32[]{:S(2)}, u32[]{:S(2)}) %collective-permute-start.20) | collective-permute-done | bytes 655392 | tf_op jit(solution)/shard_map/ppermute | solution.py:602
  555.3 9.8 %convolution_convert_fusion = bf16[512,2048]{1,0:T(8,128)(2,1)S(1)} fusion(bf16[512,3072]{1,0:T(8,128)(2,1)S(1)} %copy-done.61, bf16[3072,2048]{1,0:T(8,128)(2,1)} %param.28), kind=kOutput, calls=%fused_computation.19 | convolution fusion | flops 6443499520 | bytes 17825792 | tf_op jit(solution)/shard_map/dot_general | solution.py:882
  565.1 4.1 add_convert_fusion
  (260 shorter events, 82.2 us)
Async XLA Ops:
  0.6 33.5 %copy-start = (bf16[2,10,256,256]{3,2,1,0:T(8,128)(2,1)S(1)}, bf16[2,10,256,256]{3,2,1,0:T(8,128)(2,1)}, u32[]{:S(2)}) copy-start(bf16[2,10,256,256]{3,2,1,0:T(8,128)(2,1)} %param.24) | copy-start | bytes 7864324
  0.7 34.7 %collective-permute-start.1 = (s32[512]{0:T(512)}, s32[512]{0:T(512)S(1)}, u32[]{:S(2)}, u32[]{:S(2)}) collective-permute-start(s32[512]{0:T(512)} %bitcast.83), channel_id=1, source_target_pairs={{0,1},{1,0},{2,3},{3,2},{4,5},{5,4},{6,7},{7,6},{8,9},{9,8},{10,11... | collective-permute-start | bytes 6152 | tf_op jit(solution)/shard_map/ppermute | solution.py:597
  3.7 48.9 %collective-permute-start = (bf16[512,2048]{1,0:T(8,128)(2,1)}, bf16[512,2048]{1,0:T(8,128)(2,1)}, u32[]{:S(2)}, u32[]{:S(2)}) collective-permute-start(bf16[512,2048]{1,0:T(8,128)(2,1)} %bitcast.63), channel_id=1, source_target_pairs={{0,1},{1,0},{2,3},{3,2},{4,5},{5,4},{6,7},{7,6},{8,9},{9,8},{10,11... | collective-permute-start | bytes 6291464 | tf_op jit(solution)/shard_map/ppermute | solution.py:597
  3.8 96.5 %collective-permute-start.3 = (bf16[512,2048]{1,0:T(8,128)(2,1)}, bf16[512,2048]{1,0:T(8,128)(2,1)}, u32[]{:S(2)}, u32[]{:S(2)}) collective-permute-start(bf16[512,2048]{1,0:T(8,128)(2,1)} %bitcast.59), channel_id=1, source_target_pairs={{0,1},{1,0},{2,3},{3,2},{4,5},{5,4},{6,7},{7,6},{8,9},{9,8},{10,11... | collective-permute-start | bytes 6291464 | tf_op jit(solution)/shard_map/ppermute | solution.py:597
  9.2 45.4 %copy-start.47 = (f32[1,2048]{1,0:T(1,128)}, f32[1,2048]{1,0:T(1,128)S(1)}, u32[]{:S(2)}) copy-start(f32[1,2048]{1,0:T(1,128)S(1)} %get-tuple-element.313) | copy-start | bytes 24580
  22.0 11.9 %copy-start.51 = (f32[2560]{0:T(1024)S(1)}, f32[2560]{0:T(1024)}, u32[]{:S(2)}) copy-start(f32[2560]{0:T(1024)} %param.23) | copy-start | bytes 30724
  22.0 11.9 %copy-start.49 = (f32[4,2560]{1,0:T(4,128)S(1)}, f32[4,2560]{1,0:T(4,128)}, u32[]{:S(2)}) copy-start(f32[4,2560]{1,0:T(4,128)} %param.21) | copy-start | bytes 122884
  22.0 12.0 %copy-start.50 = (f32[3,2560]{1,0:T(4,128)S(1)}, f32[3,2560]{1,0:T(4,128)}, u32[]{:S(2)}) copy-start(f32[3,2560]{1,0:T(4,128)} %param.22) | copy-start | bytes 92164
  57.0 33.8 %slice-start = ((s8[5242880]{0:T(1024)(128)(4,1)}), s8[4194304]{0:T(1024)(128)(4,1)S(1)}, s32[]{:S(2)}) async-start(s8[5242880]{0:T(1024)(128)(4,1)} %bitcast.65), calls=%async_computation | async-start | bytes 8388608
  64.0 26.8 %slice-start.1 = ((s8[5242880]{0:T(1024)(128)(4,1)}), s8[1048576]{0:T(1024)(128)(4,1)S(1)}, s32[]{:S(2)}) async-start(s8[5242880]{0:T(1024)(128)(4,1)} %bitcast.65), calls=%async_computation.1 | async-start | bytes 2097152
  66.9 23.9 %copy-start.24 = (bf16[512,1280]{1,0:T(8,128)(2,1)}, bf16[512,1280]{1,0:T(8,128)(2,1)S(1)}, u32[]{:S(2)}) copy-start(bf16[512,1280]{1,0:T(8,128)(2,1)S(1)} %convolution_convert_fusion.4.bx_oth) | copy-start | bytes 3932164
  67.4 23.3 %copy-start.10 = (f32[3,67,16,128]{3,2,1,0:T(8,128)}, f32[3,67,16,128]{3,2,1,0:T(8,128)S(1)}, u32[]{:S(2)}) copy-start(f32[3,67,16,128]{3,2,1,0:T(8,128)S(1)} %broadcast_in_dim.11.mask_ref) | copy-start | bytes 4939780
  94.0 48.7 %collective-permute-start.2 = (bf16[512,2048]{1,0:T(8,128)(2,1)S(1)}, bf16[512,2048]{1,0:T(8,128)(2,1)}, u32[]{:S(2)}, u32[]{:S(2)}) collective-permute-start(bf16[512,2048]{1,0:T(8,128)(2,1)S(1)} %convolution_convert_fusion.3.part), channel_id=1, source_target_pairs={{0,1},{1,0},{2,3},{3,2},{4,5},{5,4},{6,7},{7,6},{8,9},{9,8},{10,11... | collective-permute-start | bytes 6291464 | tf_op jit(solution)/shard_map/ppermute | solution.py:597
  98.3 14.0 %copy-start.6 = (bf16[1,512,2048]{2,1,0:T(8,128)(2,1)S(1)}, bf16[1,512,2048]{2,1,0:T(8,128)(2,1)}, u32[]{:S(2)}) copy-start(bf16[1,512,2048]{2,1,0:T(8,128)(2,1)} %param.16) | copy-start | bytes 6291460
  98.3 90.6 %collective-permute-start.4 = (bf16[512,2048]{1,0:T(8,128)(2,1)}, bf16[512,2048]{1,0:T(8,128)(2,1)S(1)}, u32[]{:S(2)}, u32[]{:S(2)}) collective-permute-start(bf16[512,2048]{1,0:T(8,128)(2,1)} %convolution_convert_fusion.2.part), channel_id=1, source_target_pairs={{0,1},{1,0},{2,3},{3,2},{4,5},{5,4},{6,7},{7,6},{8,9},{9,8},{10,11... | collective-permute-start | bytes 6291464 | tf_op jit(solution)/shard_map/ppermute | solution.py:597
  115.2 27.5 %copy-start.28 = (bf16[512,2048]{1,0:T(8,128)(2,1)}, bf16[512,2048]{1,0:T(8,128)(2,1)S(1)}, u32[]{:S(2)}) copy-start(bf16[512,2048]{1,0:T(8,128)(2,1)S(1)} %get-tuple-element.143.oth_a.oth_b) | copy-start | bytes 6291460
  188.9 118.8 %collective-permute-start.7 = (bf16[512,2048]{1,0:T(8,128)(2,1)}, bf16[512,2048]{1,0:T(8,128)(2,1)}, u32[]{:S(2)}, u32[]{:S(2)}) collective-permute-start(bf16[512,2048]{1,0:T(8,128)(2,1)} %two_back.4.back), channel_id=1, source_target_pairs={{0,1},{1,0},{2,3},{3,2},{4,5},{5,4},{6,7},{7,6},{8,9},{9,8},{10,11... | collective-permute-start | bytes 6291464 | tf_op jit(solution)/shard_map/ppermute | solution.py:597
  237.7 84.1 %collective-permute-start.6 = (bf16[512,3072]{1,0:T(8,128)(2,1)}, bf16[512,3072]{1,0:T(8,128)(2,1)}, u32[]{:S(2)}, u32[]{:S(2)}) collective-permute-start(bf16[512,3072]{1,0:T(8,128)(2,1)} %get-tuple-element.150), channel_id=1, source_target_pairs={{0,4},{2,6},{4,0},{6,2},{8,12},{10,14},{12,8},{14,10},{16,20},{18,... | collective-permute-start | bytes 9437192 | tf_op jit(solution)/shard_map/ppermute | solution.py:602
  262.1 71.3 %collective-permute-start.5 = (bf16[512,3072]{1,0:T(8,128)(2,1)}, bf16[512,3072]{1,0:T(8,128)(2,1)}, u32[]{:S(2)}, u32[]{:S(2)}) collective-permute-start(bf16[512,3072]{1,0:T(8,128)(2,1)} %get-tuple-element.149), channel_id=1, source_target_pairs={{0,8},{2,10},{4,12},{6,14},{8,0},{10,2},{12,4},{14,6},{16,24},{18,... | collective-permute-start | bytes 9437192 | tf_op jit(solution)/shard_map/ppermute | solution.py:602
  285.3 101.9 %collective-permute-start.10 = (bf16[512,3072]{1,0:T(8,128)(2,1)}, bf16[512,3072]{1,0:T(8,128)(2,1)S(1)}, u32[]{:S(2)}, u32[]{:S(2)}) collective-permute-start(bf16[512,3072]{1,0:T(8,128)(2,1)} %get-tuple-element.169), channel_id=1, source_target_pairs={{0,4},{2,6},{4,0},{6,2},{8,12},{10,14},{12,8},{14,10},{16,20},{18,... | collective-permute-start | bytes 9437192 | tf_op jit(solution)/shard_map/ppermute | solution.py:602
  306.2 48.1 %collective-permute-start.9 = (bf16[512,2048]{1,0:T(8,128)(2,1)}, bf16[512,2048]{1,0:T(8,128)(2,1)}, u32[]{:S(2)}, u32[]{:S(2)}) collective-permute-start(bf16[512,2048]{1,0:T(8,128)(2,1)} %two_back.5.back), channel_id=1, source_target_pairs={{0,1},{1,0},{2,3},{3,2},{4,5},{5,4},{6,7},{7,6},{8,9},{9,8},{10,11... | collective-permute-start | bytes 6291464 | tf_op jit(solution)/shard_map/ppermute | solution.py:597
  307.7 14.1 %copy-start.4 = (bf16[512,3072]{1,0:T(8,128)(2,1)S(1)}, bf16[512,3072]{1,0:T(8,128)(2,1)}, u32[]{:S(2)}) copy-start(bf16[512,3072]{1,0:T(8,128)(2,1)} %get-tuple-element.144.keep_low.keep_high) | copy-start | bytes 9437188
  325.7 54.6 %collective-permute-start.11 = (bf16[256,3072]{1,0:T(8,128)(2,1)}, bf16[256,3072]{1,0:T(8,128)(2,1)}, u32[]{:S(2)}, u32[]{:S(2)}) collective-permute-start(bf16[256,3072]{1,0:T(8,128)(2,1)} %get-tuple-element.159), channel_id=1, source_target_pairs={{0,8},{2,10},{4,12},{6,14},{8,0},{10,2},{12,4},{14,6},{16,24},{18,... | collective-permute-start | bytes 4718600 | tf_op jit(solution)/shard_map/ppermute | solution.py:602
  339.2 86.5 %collective-permute-start.8 = (bf16[256,3072]{1,0:T(8,128)(2,1)}, bf16[256,3072]{1,0:T(8,128)(2,1)}, u32[]{:S(2)}, u32[]{:S(2)}) collective-permute-start(bf16[256,3072]{1,0:T(8,128)(2,1)} %get-tuple-element.162), channel_id=1, source_target_pairs={{0,4},{2,6},{4,0},{6,2},{8,12},{10,14},{12,8},{14,10},{16,20},{18,... | collective-permute-start | bytes 4718600 | tf_op jit(solution)/shard_map/ppermute | solution.py:602
  378.8 66.9 %collective-permute-start.14 = (bf16[512,1280]{1,0:T(8,128)(2,1)}, bf16[512,1280]{1,0:T(8,128)(2,1)}, u32[]{:S(2)}, u32[]{:S(2)}) collective-permute-start(bf16[512,1280]{1,0:T(8,128)(2,1)} %get-tuple-element.186), channel_id=1, source_target_pairs={{0,4},{2,6},{4,0},{6,2},{8,12},{10,14},{12,8},{14,10},{16,20},{18,... | collective-permute-start | bytes 3932168 | tf_op jit(solution)/shard_map/ppermute | solution.py:602
  384.6 58.4 %collective-permute-start.15 = (bf16[128,3072]{1,0:T(8,128)(2,1)}, bf16[128,3072]{1,0:T(8,128)(2,1)}, u32[]{:S(2)}, u32[]{:S(2)}) collective-permute-start(bf16[128,3072]{1,0:T(8,128)(2,1)} %get-tuple-element.176), channel_id=1, source_target_pairs={{0,16},{2,18},{4,20},{6,22},{8,24},{10,26},{12,28},{14,30},{16,0},... | collective-permute-start | bytes 2359304 | tf_op jit(solution)/shard_map/ppermute | solution.py:602
  389.5 76.8 %collective-permute-start.13 = (bf16[256,3072]{1,0:T(8,128)(2,1)}, bf16[256,3072]{1,0:T(8,128)(2,1)S(1)}, u32[]{:S(2)}, u32[]{:S(2)}) collective-permute-start(bf16[256,3072]{1,0:T(8,128)(2,1)} %get-tuple-element.178), channel_id=1, source_target_pairs={{0,8},{2,10},{4,12},{6,14},{8,0},{10,2},{12,4},{14,6},{16,24},{18,... | collective-permute-start | bytes 4718600 | tf_op jit(solution)/shard_map/ppermute | solution.py:602
  390.0 35.7 %copy-start.12 = (bf16[256,3072]{1,0:T(8,128)(2,1)S(1)}, bf16[256,3072]{1,0:T(8,128)(2,1)}, u32[]{:S(2)}) copy-start(bf16[256,3072]{1,0:T(8,128)(2,1)} %get-tuple-element.161.keep_low.keep_high) | copy-start | bytes 4718596
  428.7 41.7 %collective-permute-start.12 = (bf16[128,3072]{1,0:T(8,128)(2,1)}, bf16[128,3072]{1,0:T(8,128)(2,1)}, u32[]{:S(2)}, u32[]{:S(2)}) collective-permute-start(bf16[128,3072]{1,0:T(8,128)(2,1)} %get-tuple-element.183), channel_id=1, source_target_pairs={{0,16},{2,18},{4,20},{6,22},{8,24},{10,26},{12,28},{14,30},{16,0},... | collective-permute-start | bytes 2359304 | tf_op jit(solution)/shard_map/ppermute | solution.py:602
  442.5 45.4 %collective-permute-start.17 = (bf16[672,1280]{1,0:T(8,128)(2,1)}, bf16[672,1280]{1,0:T(8,128)(2,1)S(1)}, u32[]{:S(2)}, u32[]{:S(2)}) collective-permute-start(bf16[672,1280]{1,0:T(8,128)(2,1)} %get-tuple-element.206), channel_id=1, source_target_pairs={{0,4},{2,6},{4,0},{6,2},{8,12},{10,14},{12,8},{14,10},{16,20},{18,... | collective-permute-start | bytes 5160968 | tf_op jit(solution)/shard_map/ppermute | solution.py:602
  448.2 35.9 %collective-permute-start.18 = (bf16[256,1280]{1,0:T(8,128)(2,1)}, bf16[256,1280]{1,0:T(8,128)(2,1)}, u32[]{:S(2)}, u32[]{:S(2)}) collective-permute-start(bf16[256,1280]{1,0:T(8,128)(2,1)} %get-tuple-element.195), channel_id=1, source_target_pairs={{0,8},{2,10},{4,12},{6,14},{8,0},{10,2},{12,4},{14,6},{16,24},{18,... | collective-permute-start | bytes 1966088 | tf_op jit(solution)/shard_map/ppermute | solution.py:602
  464.8 47.3 %collective-permute-start.19 = (bf16[512,2048]{1,0:T(8,128)(2,1)}, bf16[512,2048]{1,0:T(8,128)(2,1)}, u32[]{:S(2)}, u32[]{:S(2)}) collective-permute-start(bf16[512,2048]{1,0:T(8,128)(2,1)} %two_back.6), channel_id=1, source_target_pairs={{0,1},{1,0},{2,3},{3,2},{4,5},{5,4},{6,7},{7,6},{8,9},{9,8},{10,11... | collective-permute-start | bytes 6291464 | tf_op jit(solution)/shard_map/ppermute | solution.py:597
  467.7 55.3 %collective-permute-start.23 = (bf16[128,3072]{1,0:T(8,128)(2,1)}, bf16[128,3072]{1,0:T(8,128)(2,1)}, u32[]{:S(2)}, u32[]{:S(2)}) collective-permute-start(bf16[128,3072]{1,0:T(8,128)(2,1)} %get-tuple-element.199), channel_id=1, source_target_pairs={{0,16},{2,18},{4,20},{6,22},{8,24},{10,26},{12,28},{14,30},{16,0},... | collective-permute-start | bytes 2359304 | tf_op jit(solution)/shard_map/ppermute | solution.py:602
  473.2 12.4 %copy-start.21 = (bf16[256,1280]{1,0:T(8,128)(2,1)S(1)}, bf16[256,1280]{1,0:T(8,128)(2,1)}, u32[]{:S(2)}) copy-start(bf16[256,1280]{1,0:T(8,128)(2,1)} %get-tuple-element.207.keep_low.keep_high) | copy-start | bytes 1966084
  484.1 37.2 %collective-permute-start.16 = (bf16[512,1280]{1,0:T(8,128)(2,1)}, bf16[512,1280]{1,0:T(8,128)(2,1)S(1)}, u32[]{:S(2)}, u32[]{:S(2)}) collective-permute-start(bf16[512,1280]{1,0:T(8,128)(2,1)} %get-tuple-element.204), channel_id=1, source_target_pairs={{0,4},{2,6},{4,0},{6,2},{8,12},{10,14},{12,8},{14,10},{16,20},{18,... | collective-permute-start | bytes 3932168 | tf_op jit(solution)/shard_map/ppermute | solution.py:602
  487.6 38.4 %collective-permute-start.22 = (bf16[128,1280]{1,0:T(8,128)(2,1)}, bf16[128,1280]{1,0:T(8,128)(2,1)S(1)}, u32[]{:S(2)}, u32[]{:S(2)}) collective-permute-start(bf16[128,1280]{1,0:T(8,128)(2,1)} %get-tuple-element.209), channel_id=1, source_target_pairs={{0,16},{2,18},{4,20},{6,22},{8,24},{10,26},{12,28},{14,30},{16,0},... | collective-permute-start | bytes 983048 | tf_op jit(solution)/shard_map/ppermute | solution.py:602
  489.3 41.9 %collective-permute-start.21 = (bf16[336,1280]{1,0:T(8,128)(2,1)}, bf16[336,1280]{1,0:T(8,128)(2,1)S(1)}, u32[]{:S(2)}, u32[]{:S(2)}) collective-permute-start(bf16[336,1280]{1,0:T(8,128)(2,1)} %get-tuple-element.211), channel_id=1, source_target_pairs={{0,8},{2,10},{4,12},{6,14},{8,0},{10,2},{12,4},{14,6},{16,24},{18,... | collective-permute-start | bytes 2580488 | tf_op jit(solution)/shard_map/ppermute | solution.py:602
  500.7 12.9 %copy-start.38 = (bf16[1,512,2048]{2,1,0:T(8,128)(2,1)S(1)}, bf16[1,512,2048]{2,1,0:T(8,128)(2,1)}, u32[]{:S(2)}) copy-start(bf16[1,512,2048]{2,1,0:T(8,128)(2,1)} %param.15) | copy-start | bytes 6291460
  500.7 12.9 %copy-start.48 = (f32[1,2048]{1,0:T(1,128)S(1)}, f32[1,2048]{1,0:T(1,128)}, u32[]{:S(2)}) copy-start(f32[1,2048]{1,0:T(1,128)} %copy-done.47) | copy-start | bytes 24580
  512.2 52.9 %collective-permute-start.24 = (bf16[512,2048]{1,0:T(8,128)(2,1)}, bf16[512,2048]{1,0:T(8,128)(2,1)}, u32[]{:S(2)}, u32[]{:S(2)}) collective-permute-start(bf16[512,2048]{1,0:T(8,128)(2,1)} %convolution_convert_fusion.1), channel_id=1, source_target_pairs={{0,1},{1,0},{2,3},{3,2},{4,5},{5,4},{6,7},{7,6},{8,9},{9,8},{10,11... | collective-permute-start | bytes 6291464 | tf_op jit(solution)/shard_map/ppermute | solution.py:597
  522.6 31.0 %collective-permute-start.20 = (bf16[256,1280]{1,0:T(8,128)(2,1)}, bf16[256,1280]{1,0:T(8,128)(2,1)S(1)}, u32[]{:S(2)}, u32[]{:S(2)}) collective-permute-start(bf16[256,1280]{1,0:T(8,128)(2,1)} %get-tuple-element.217), channel_id=1, source_target_pairs={{0,8},{2,10},{4,12},{6,14},{8,0},{10,2},{12,4},{14,6},{16,24},{18,... | collective-permute-start | bytes 1966088 | tf_op jit(solution)/shard_map/ppermute | solution.py:602
  526.9 26.7 %copy-start.22 = (bf16[256,1280]{1,0:T(8,128)(2,1)S(1)}, bf16[256,1280]{1,0:T(8,128)(2,1)}, u32[]{:S(2)}) copy-start(bf16[256,1280]{1,0:T(8,128)(2,1)} %get-tuple-element.216.keep_low.keep_high) | copy-start | bytes 1966084
  531.3 24.0 %copy-start.61 = (bf16[512,3072]{1,0:T(8,128)(2,1)S(1)}, bf16[512,3072]{1,0:T(8,128)(2,1)}, u32[]{:S(2)}) copy-start(bf16[512,3072]{1,0:T(8,128)(2,1)} %get-tuple-element.227.right_own) | copy-start | bytes 9437188
  532.3 36.9 %collective-permute-start.25 = (bf16[168,1280]{1,0:T(8,128)(2,1)}, bf16[168,1280]{1,0:T(8,128)(2,1)S(1)}, u32[]{:S(2)}, u32[]{:S(2)}) collective-permute-start(bf16[168,1280]{1,0:T(8,128)(2,1)} %get-tuple-element.224), channel_id=1, source_target_pairs={{0,16},{2,18},{4,20},{6,22},{8,24},{10,26},{12,28},{14,30},{16,0},... | collective-permute-start | bytes 1290248 | tf_op jit(solution)/shard_map/ppermute | solution.py:602
  554.4 19.9 %collective-permute-start.26 = (bf16[128,1280]{1,0:T(8,128)(2,1)}, bf16[128,1280]{1,0:T(8,128)(2,1)}, u32[]{:S(2)}, u32[]{:S(2)}) collective-permute-start(bf16[128,1280]{1,0:T(8,128)(2,1)} %get-tuple-element.226), channel_id=1, source_target_pairs={{0,16},{2,18},{4,20},{6,22},{8,24},{10,26},{12,28},{14,30},{16,0},... | collective-permute-start | bytes 983048 | tf_op jit(solution)/shard_map/ppermute | solution.py:602
  569.3 4.7 collective-permute-start.27
  569.9 11.4 %copy-start.1 = (bf16[2,10,256,256]{3,2,1,0:T(8,128)(2,1)S(1)}, bf16[2,10,256,256]{3,2,1,0:T(8,128)(2,1)}, u32[]{:S(2)}) copy-start(bf16[2,10,256,256]{3,2,1,0:T(8,128)(2,1)} %param.24) | copy-start | bytes 7864324
  577.1 3.6 collective-permute-start.28
  (50 other events, 223.0 us)
